TPU v7x, 32 devices: a whole 2x2x4 slice. The times are simulated.
32 devices in a mesh: expert: 8 (over y, x, core), hidden: 4 (over z).
Axes of the slice: x: 2, y: 2, z: 4, core: 2. Of those that a mesh axis runs over, the one named last changes fastest.
Arguments:
- x_in: bfloat16 [2, 8, 1024, 1024], P(None, 'expert', 'hidden'), may hold values from -6 to 6
- cotangent: bfloat16 [2, 8, 1024, 1024], P(None, 'expert', 'hidden'), may hold values from -6 to 6
- segment_ids: int32 [2, 8, 1024], P(None, 'expert'), may hold values from -1 to 8, as said below
- routes: int32 [2, 8, 1024, 2], P(None, 'expert', 'hidden'), may hold values from 0 to 15, all different within a row; in each aligned block of 256 rows (0 to 255, 256 to 511, ..., all dimensions but the last counted through in order) at most 40 rows name the same one
- qkv_weight: bfloat16 [3, 1024, 1024], P(None, None, 'hidden'), may hold values from -0.1875 to 0.1875
- out_weight: bfloat16 [1024, 1024], P('hidden'), may hold values from -0.75 to 0.75
- bias_table: bfloat16 [32, 16], P(None, 'hidden'), may hold values from -4 to 4
- attn_gain: bfloat16 [1024], replicated, may hold values from 0.5 to 1.5
- moe_gain: bfloat16 [1024], replicated, may hold values from 0.5 to 1.5
- router_weight: bfloat16 [1024, 16], replicated, may hold values from -0.375 to 0.375
- gate_weight: bfloat16 [16, 1024, 2816], P('expert', None, 'hidden'), may hold values from -0.1875 to 0.1875
- up_weight: bfloat16 [16, 1024, 2816], P('expert', None, 'hidden'), may hold values from -0.1875 to 0.1875
- down_weight: bfloat16 [16, 2816, 1024], P('expert', 'hidden'), may hold values from -0.21875 to 0.21875
Outputs:
- block_out: bfloat16 [2, 8, 1024, 1024], P(None, 'expert', 'hidden')
- x_grad: bfloat16 [2, 8, 1024, 1024], P(None, 'expert', 'hidden')
- qkv_grad: float32 [3, 1024, 1024], P(None, None, 'hidden')
- out_grad: float32 [1024, 1024], P('hidden')
- bias_grad: float32 [32, 16], P(None, 'hidden')
- attn_gain_grad: float32 [1024], replicated
- moe_gain_grad: float32 [1024], replicated
- router_grad: float32 [1024, 16], replicated
- gate_grad: float32 [16, 1024, 2816], P('expert', None, 'hidden')
- up_grad: float32 [16, 1024, 2816], P('expert', None, 'hidden')
- down_grad: float32 [16, 2816, 1024], P('expert', 'hidden')
Inputs may be any that keep to these rules, and one draw needn't show every extreme that they name: `segment_ids`: within each row, slots are numbered by item 0, 1, 2, ... in order; the first item of every row has 512 slots, every item 64 to 512; slots after the last whole item are -1. In the first row of the first micro-batch every item after the first has 64 slots. Item numbers serve only for comparison. `routes`: the two experts of a slot differ. In each aligned block of 256 slots (the slots of one row held by one index of hidden), no expert is named by more than 40 slots, a bound that some block reaches.
All inputs are finite; a program needn't handle non-finite values.
Results may differ from a plain program's by a relative error of at most 0.023.
Values may be sent and summed in bfloat16 or wider, within the bound.
A program may use at most 320 MiB of HBM per device.

v0:
```python
import jax
import jax.numpy as jnp
from jax import lax
from jax.sharding import PartitionSpec as P

EPSILON = 1e-06
PRECISE = lax.Precision.HIGHEST
LIMITS = (12, 16, 23, 32, 46, 64, 91)
MASKED = -1000000000.0


def bucket_of(distance):
    magnitude = jnp.abs(distance)
    far_bucket = jnp.full(magnitude.shape, 8, jnp.int32)
    for threshold in LIMITS:
        far_bucket = far_bucket + (magnitude >= threshold).astype(jnp.int32)
    return jnp.where(magnitude < 8, magnitude, far_bucket) + 16 * (distance > 0).astype(jnp.int32)


def normed(values, gain):
    return values * lax.rsqrt(jnp.mean(values * values, axis=-1, keepdims=True) + EPSILON) * gain


def geglu(gate_act, up_act):
    return jax.nn.gelu(gate_act, approximate=True) * up_act


def whole_rows(values):
    return lax.all_gather(values, "hidden", axis=1, tiled=True)


def own_rows(values):
    return lax.psum_scatter(values, "hidden", scatter_dimension=1, tiled=True)


def to_experts(buffer_in):
    arrived = lax.all_to_all(buffer_in, "expert", split_axis=0, concat_axis=1, tiled=True)
    return lax.all_gather(arrived, "hidden", axis=1, tiled=True)


def from_experts(partial_terms):
    summed = lax.psum_scatter(
        partial_terms.astype(jnp.bfloat16), "hidden", scatter_dimension=1, tiled=True
    )
    return lax.all_to_all(summed, "expert", split_axis=1, concat_axis=0, tiled=True)


def bucket_sums(grad_scores, query_start, bucket_count):
    heads_here, rows_block, key_count = grad_scores.shape
    flipped = grad_scores[:, :, ::-1]
    padded = jnp.pad(flipped, ((0, 0), (0, 0), (0, rows_block)))
    sheared = padded.reshape(heads_here, rows_block * (key_count + rows_block))
    sheared = sheared[:, : rows_block * (key_count + rows_block - 1)].reshape(
        heads_here, rows_block, key_count + rows_block - 1
    )
    per_distance = jnp.sum(sheared, axis=1)
    distance = key_count - 1 - query_start - jnp.arange(key_count + rows_block - 1, dtype=jnp.int32)
    onehot_bucket = (
        bucket_of(distance)[:, None] == jnp.arange(bucket_count, dtype=jnp.int32)[None, :]
    ).astype(jnp.float32)
    return jnp.einsum("hj,jb->bh", per_distance, onehot_bucket, precision=PRECISE)


def block_bias(table_rows, query_start, rows_block, key_count):
    bucket_count, heads_here = table_rows.shape
    line_len = rows_block + key_count + 1
    distance = jnp.arange(line_len, dtype=jnp.int32) - rows_block - query_start
    onehot_bucket = (
        bucket_of(distance)[:, None] == jnp.arange(bucket_count, dtype=jnp.int32)[None, :]
    ).astype(jnp.float32)
    per_distance = jnp.dot(onehot_bucket, table_rows, precision=PRECISE).T
    tiled = jnp.broadcast_to(per_distance[:, None, :], (heads_here, rows_block, line_len))
    tiled = tiled.reshape(heads_here, rows_block * line_len)[:, : rows_block * (line_len - 1)]
    tiled = tiled.reshape(heads_here, rows_block, line_len - 1)
    return tiled[:, :, rows_block : rows_block + key_count]


def shards(
    x_in,
    cotangent,
    segment_ids,
    routes,
    qkv_weight,
    out_weight,
    bias_table,
    attn_gain,
    moe_gain,
    router_weight,
    gate_weight,
    up_weight,
    down_weight,
):
    micro_count, row_count, shard_len, width = x_in.shape
    slot_count = segment_ids.shape[2]
    head_cols = out_weight.shape[0]
    bucket_count, heads_here = bias_table.shape
    head_size = head_cols // heads_here
    expert_count = router_weight.shape[1]
    capacity = max(2, (10 * shard_len + 4 * expert_count - 1) // (4 * expert_count))
    buffer_rows = expert_count * row_count * capacity
    token_count = row_count * shard_len
    block_rows = min(512, slot_count)
    score_scale = head_size ** (-0.5)
    hidden_index = lax.axis_index("hidden")
    table_rows = bias_table.astype(jnp.float32)
    attn_gain_f = attn_gain.astype(jnp.float32)
    moe_gain_f = moe_gain.astype(jnp.float32)
    block_starts = list(range(0, slot_count, block_rows))
    block_biases = []
    for block_start in block_starts:
        block_biases.append(block_bias(table_rows, block_start, block_rows, slot_count))
    expert_ids = jnp.arange(expert_count, dtype=jnp.int32)
    buffer_ids = jnp.arange(buffer_rows, dtype=jnp.int32)
    used_gate, used_up, used_down = (gate_weight, up_weight, down_weight)
    grad_qkv = jnp.zeros(qkv_weight.shape, jnp.float32)
    grad_out = jnp.zeros(out_weight.shape, jnp.float32)
    grad_table = jnp.zeros(bias_table.shape, jnp.float32)
    grad_attn_gain = jnp.zeros(attn_gain.shape, jnp.float32)
    grad_moe_gain = jnp.zeros(moe_gain.shape, jnp.float32)
    grad_router = jnp.zeros(router_weight.shape, jnp.float32)
    grad_gate = jnp.zeros(used_gate.shape, jnp.float32)
    grad_up = jnp.zeros(used_up.shape, jnp.float32)
    grad_down = jnp.zeros(used_down.shape, jnp.float32)
    outputs_list = []
    input_grads = []
    for micro_batch in range(micro_count):
        x_now = x_in[micro_batch].astype(jnp.float32)
        seg_now = segment_ids[micro_batch]
        own_seg = lax.dynamic_slice_in_dim(seg_now, hidden_index * shard_len, shard_len, 1)
        live_now = (own_seg >= 0).reshape(token_count)
        normed_one, norm_one_back = jax.vjp(normed, x_now, attn_gain_f)
        gathered = whole_rows(normed_one.astype(jnp.bfloat16))
        row_index = 0
        row_in = gathered[row_index]
        projected = jnp.einsum(
            "sd,tdf->tsf", row_in, qkv_weight, preferred_element_type=jnp.float32
        ).astype(jnp.bfloat16)
        split_heads = projected.reshape(3, slot_count, heads_here, head_size).transpose(0, 2, 1, 3)
        query_heads = split_heads[0]
        key_heads = split_heads[1]
        value_heads = split_heads[2]
        same_item = seg_now[row_index][:, None] == seg_now[row_index][None, :]
        head_blocks = []
        log_totals = []
        for block_index, block_start in enumerate(block_starts):
            query_block = query_heads[:, block_start : block_start + block_rows]
            scores = (
                jnp.einsum(
                    "hqe,hke->hqk", query_block, key_heads, preferred_element_type=jnp.float32
                )
                * score_scale
            )
            scores = jnp.where(
                same_item[None, block_start : block_start + block_rows],
                scores + block_biases[block_index],
                MASKED,
            )
            top_score = jnp.max(scores, axis=-1, keepdims=True)
            weights = jnp.exp(scores - top_score)
            totals = jnp.sum(weights, axis=-1, keepdims=True)
            probability = weights / totals
            log_totals.append(top_score + jnp.log(totals))
            head_blocks.append(
                jnp.einsum(
                    "hqk,hke->hqe",
                    probability.astype(jnp.bfloat16),
                    value_heads,
                    preferred_element_type=jnp.float32,
                )
            )
        heads_out = (
            jnp.concatenate(head_blocks, axis=1)
            .transpose(1, 0, 2)
            .reshape(slot_count, head_cols)
            .astype(jnp.bfloat16)
        )
        attn_terms = [jnp.dot(heads_out, out_weight, preferred_element_type=jnp.float32)]
        kept_rows = [
            (row_in, query_heads, key_heads, value_heads, heads_out, log_totals, same_item)
        ]
        attn_out = own_rows(jnp.stack(attn_terms))
        first_sum = x_now + attn_out
        normed_two, norm_two_back = jax.vjp(normed, first_sum, moe_gain_f)
        token_rows = normed_two.astype(jnp.bfloat16).reshape(token_count, width)
        logits = jnp.dot(token_rows, router_weight, preferred_element_type=jnp.float32)
        route_now = routes[micro_batch].reshape(token_count, 2)
        route_onehot = (route_now[:, :, None] == expert_ids).astype(jnp.float32)
        live_float = live_now.astype(jnp.float32)

        def gating(logit_values):
            router_probs = jax.nn.softmax(logit_values, axis=-1)
            picked_probs = jnp.sum(router_probs[:, None, :] * route_onehot, axis=-1)
            return picked_probs / jnp.sum(picked_probs, axis=1, keepdims=True) * live_float[:, None]

        gates, gating_back = jax.vjp(gating, logits)
        chosen = route_onehot.astype(jnp.int32) * live_now[:, None, None].astype(jnp.int32)
        chosen_rows = chosen.reshape(row_count, shard_len * 2, expert_count)
        earlier = jnp.cumsum(chosen_rows, axis=1) - chosen_rows
        position = jnp.sum(earlier * chosen_rows, axis=-1).reshape(token_count, 2)
        row_of = (jnp.arange(token_count, dtype=jnp.int32) // shard_len)[:, None]
        slot_now = jnp.where(
            live_now[:, None], route_now * (row_count * capacity) + row_of * capacity + position, -1
        )
        onehot_slot = (slot_now[:, :, None] == buffer_ids).astype(jnp.bfloat16)
        dispatched = jnp.einsum(
            "tks,td->sd", onehot_slot, token_rows, preferred_element_type=jnp.float32
        )
        dispatched = dispatched.astype(jnp.bfloat16).reshape(
            expert_count, row_count * capacity, width
        )
        expert_in = to_experts(dispatched)
        gate_act = jnp.einsum(
            "erd,edf->erf", expert_in, used_gate, preferred_element_type=jnp.float32
        )
        up_act = jnp.einsum("erd,edf->erf", expert_in, used_up, preferred_element_type=jnp.float32)
        hidden_act, glu_back = jax.vjp(geglu, gate_act, up_act)
        hidden_low = hidden_act.astype(jnp.bfloat16)
        expert_terms = jnp.einsum(
            "erf,efd->erd", hidden_low, used_down, preferred_element_type=jnp.float32
        )
        expert_out = from_experts(expert_terms).reshape(buffer_rows, width)
        picked_out = jnp.einsum(
            "tks,sd->tkd", onehot_slot, expert_out, preferred_element_type=jnp.float32
        )
        mixed = jnp.sum(gates[:, :, None] * picked_out, axis=1)
        outputs_list.append(
            (first_sum + mixed.reshape(row_count, shard_len, width)).astype(jnp.bfloat16)
        )
        grad_block = cotangent[micro_batch].astype(jnp.float32)
        grad_flat = grad_block.reshape(token_count, width)
        grad_gates = jnp.sum(grad_flat[:, None, :] * picked_out, axis=-1)
        grad_buffer = jnp.einsum(
            "tks,tkd->sd",
            onehot_slot.astype(jnp.float32),
            gates[:, :, None] * grad_flat[:, None, :],
            precision=PRECISE,
        )
        grad_buffer = grad_buffer.astype(jnp.bfloat16).reshape(
            expert_count, row_count * capacity, width
        )
        grad_expert_out = to_experts(grad_buffer)
        grad_down = grad_down + jnp.einsum(
            "erf,erd->efd", hidden_low, grad_expert_out, preferred_element_type=jnp.float32
        )
        grad_hidden = jnp.einsum(
            "erd,efd->erf", grad_expert_out, used_down, preferred_element_type=jnp.float32
        )
        grad_gate_act, grad_up_act = glu_back(grad_hidden)
        grad_gate_low = grad_gate_act.astype(jnp.bfloat16)
        grad_up_low = grad_up_act.astype(jnp.bfloat16)
        grad_gate = grad_gate + jnp.einsum(
            "erd,erf->edf", expert_in, grad_gate_low, preferred_element_type=jnp.float32
        )
        grad_up = grad_up + jnp.einsum(
            "erd,erf->edf", expert_in, grad_up_low, preferred_element_type=jnp.float32
        )
        grad_in_terms = jnp.einsum(
            "erf,edf->erd", grad_gate_low, used_gate, preferred_element_type=jnp.float32
        )
        grad_in_terms = grad_in_terms + jnp.einsum(
            "erf,edf->erd", grad_up_low, used_up, preferred_element_type=jnp.float32
        )
        grad_expert_in = from_experts(grad_in_terms).reshape(buffer_rows, width)
        grad_tokens = jnp.einsum(
            "tks,sd->td", onehot_slot, grad_expert_in, preferred_element_type=jnp.float32
        )
        (grad_logits,) = gating_back(grad_gates)
        grad_logits_low = grad_logits.astype(jnp.bfloat16)
        grad_router = grad_router + jnp.einsum(
            "td,te->de", token_rows, grad_logits_low, preferred_element_type=jnp.float32
        )
        grad_tokens = grad_tokens + jnp.einsum(
            "te,de->td", grad_logits_low, router_weight, preferred_element_type=jnp.float32
        )
        grad_sum_part, moe_gain_part = norm_two_back(
            grad_tokens.reshape(row_count, shard_len, width)
        )
        grad_moe_gain = grad_moe_gain + moe_gain_part
        grad_first_sum = grad_block + grad_sum_part
        grad_gathered = whole_rows(grad_first_sum.astype(jnp.bfloat16))
        row_index = 0
        row_in, query_heads, key_heads, value_heads, heads_out, log_totals, same_item = kept_rows[
            row_index
        ]
        row_grad = grad_gathered[row_index]
        grad_out = grad_out + jnp.einsum(
            "sf,sd->fd", heads_out, row_grad, preferred_element_type=jnp.float32
        )
        grad_heads = jnp.einsum(
            "sd,fd->sf", row_grad, out_weight, preferred_element_type=jnp.float32
        ).astype(jnp.bfloat16)
        grad_heads = grad_heads.reshape(slot_count, heads_here, head_size).transpose(1, 0, 2)
        grad_query_blocks = []
        grad_keys = jnp.zeros(key_heads.shape, jnp.float32)
        grad_values = jnp.zeros(value_heads.shape, jnp.float32)
        for block_index, block_start in enumerate(block_starts):
            query_block = query_heads[:, block_start : block_start + block_rows]
            scores = (
                jnp.einsum(
                    "hqe,hke->hqk", query_block, key_heads, preferred_element_type=jnp.float32
                )
                * score_scale
            )
            scores = jnp.where(
                same_item[None, block_start : block_start + block_rows],
                scores + block_biases[block_index],
                MASKED,
            )
            probability = jnp.exp(scores - log_totals[block_index])
            grad_head_block = grad_heads[:, block_start : block_start + block_rows]
            grad_prob = jnp.einsum(
                "hqe,hke->hqk", grad_head_block, value_heads, preferred_element_type=jnp.float32
            )
            inner = jnp.sum(probability * grad_prob, axis=-1, keepdims=True)
            grad_scores = (probability * (grad_prob - inner)).astype(jnp.bfloat16)
            grad_query_blocks.append(
                jnp.einsum(
                    "hqk,hke->hqe", grad_scores, key_heads, preferred_element_type=jnp.float32
                )
                * score_scale
            )
            grad_keys = (
                grad_keys
                + jnp.einsum(
                    "hqk,hqe->hke", grad_scores, query_block, preferred_element_type=jnp.float32
                )
                * score_scale
            )
            grad_values = grad_values + jnp.einsum(
                "hqk,hqe->hke",
                probability.astype(jnp.bfloat16),
                grad_head_block,
                preferred_element_type=jnp.float32,
            )
            grad_table = grad_table + bucket_sums(
                grad_scores.astype(jnp.float32), block_start, bucket_count
            )
        grad_query = jnp.concatenate(grad_query_blocks, axis=1)
        grad_proj = jnp.stack([grad_query, grad_keys, grad_values]).transpose(0, 2, 1, 3)
        grad_proj = grad_proj.reshape(3, slot_count, head_cols).astype(jnp.bfloat16)
        grad_qkv = grad_qkv + jnp.einsum(
            "sd,tsf->tdf", row_in, grad_proj, preferred_element_type=jnp.float32
        )
        input_terms = [
            jnp.einsum("tsf,tdf->sd", grad_proj, qkv_weight, preferred_element_type=jnp.float32)
        ]
        grad_normed_one = own_rows(jnp.stack(input_terms))
        grad_x_part, attn_gain_part = norm_one_back(grad_normed_one)
        grad_attn_gain = grad_attn_gain + attn_gain_part
        input_grads.append((grad_first_sum + grad_x_part).astype(jnp.bfloat16))
    grad_qkv, grad_out, grad_table = (
        lax.psum(grad_qkv.astype(jnp.bfloat16), "expert").astype(jnp.float32),
        lax.psum(grad_out.astype(jnp.bfloat16), "expert").astype(jnp.float32),
        lax.psum(grad_table.astype(jnp.bfloat16), "expert").astype(jnp.float32),
    )
    grad_router, grad_attn_gain, grad_moe_gain = lax.psum(
        (grad_router, grad_attn_gain, grad_moe_gain), ("expert", "hidden")
    )
    return (
        jnp.stack(outputs_list),
        jnp.stack(input_grads),
        grad_qkv,
        grad_out,
        grad_table,
        grad_attn_gain,
        grad_moe_gain,
        grad_router,
        grad_gate,
        grad_up,
        grad_down,
    )


def solution(mesh):
    return jax.shard_map(
        shards,
        mesh=mesh,
        in_specs=(
            P(None, "expert", "hidden", None),
            P(None, "expert", "hidden", None),
            P(None, "expert", None),
            P(None, "expert", "hidden", None),
            P(None, None, "hidden"),
            P("hidden", None),
            P(None, "hidden"),
            P(),
            P(),
            P(),
            P("expert", None, "hidden"),
            P("expert", None, "hidden"),
            P("expert", "hidden", None),
        ),
        out_specs=(
            P(None, "expert", "hidden", None),
            P(None, "expert", "hidden", None),
            P(None, None, "hidden"),
            P("hidden", None),
            P(None, "hidden"),
            P(),
            P(),
            P(),
            P("expert", None, "hidden"),
            P("expert", None, "hidden"),
            P("expert", "hidden", None),
        ),
        check_vma=False,
    )
```

profile of v0, /device:TPU:0, one launch (start us, length us, event | category | flops | bytes accessed | tf_op | source)
XLA Modules:
  0.0 2079.5 jit_solution(12845445553664772072)
XLA Ops:
  23.7 20.2 reshape.1272
  43.9 15.0 reshape.1215
  59.0 10.9 slice.169
  69.9 13.3 copy.228
  89.0 20.3 reshape.1274
  109.3 15.0 reshape.1213
  134.7 13.2 copy.229
  210.9 42.8 %reduce-scatter.13.cloned.1.call-done = f32[1,256,1024]{2,1,0:T(8,128)} async-done(((f32[1,1024,1024]{2,1,0:T(8,128)}), f32[1,256,1024]{2,1,0:T(8,128)}) %reduce-scatter.13.cloned.1.call-update) | async-done | bytes 1048592 | tf_op jit(solution)/shard_map/reduce_scatter | solution.py:33
  253.7 80.1 %reduce-scatter.9.cloned.1.call-done = f32[1,256,1024]{2,1,0:T(8,128)} async-done(((f32[1,1024,1024]{2,1,0:T(8,128)}), f32[1,256,1024]{2,1,0:T(8,128)}) %reduce-scatter.9.cloned.1.call-update) | async-done | bytes 1048592 | tf_op jit(solution)/shard_map/reduce_scatter | solution.py:33
  339.4 21.6 %all_to_all.132 = bf16[16,40,1024]{2,1,0:T(8,128)(2,1)S(1)} all-to-all(bf16[16,40,1024]{2,1,0:T(8,128)(2,1)S(1)} %bitcast.443), channel_id=1, replica_groups=mesh['expert'=8,'hidden'=4] {'expert'}, dimensions={0} | all-to-all | bytes 2621440 | tf_op jit(solution)/shard_map/all_to_all | solution.py:37
  371.9 20.6 all_to_all.133
  394.0 65.2 %all-gather.11.cloned.1.call-done = bf16[2,1280,1024]{2,1,0:T(8,128)(2,1)} async-done(((bf16[2,320,1024]{2,1,0:T(8,128)(2,1)}), bf16[2,1280,1024]{2,1,0:T(8,128)(2,1)}) %all-gather.11.cloned.1.call-update) | async-done | bytes 5242896 | tf_op jit(solution)/shard_map/all_gather | solution.py:38
  459.1 10.6 fusion.239
  475.6 82.0 %all-gather.17.cloned.1.call-done = bf16[2,1280,1024]{2,1,0:T(8,128)(2,1)} async-done(((bf16[2,320,1024]{2,1,0:T(8,128)(2,1)}), bf16[2,1280,1024]{2,1,0:T(8,128)(2,1)}) %all-gather.17.cloned.1.call-update) | async-done | bytes 5242896 | tf_op jit(solution)/shard_map/all_gather | solution.py:38
  557.6 15.1 multiply_convert_fusion.5
  581.0 11.4 fusion.242
  600.9 72.1 %reduce-scatter.11.cloned.1.call-done = bf16[2,320,1024]{2,1,0:T(8,128)(2,1)} async-done(((bf16[2,1280,1024]{2,1,0:T(8,128)(2,1)}), bf16[2,320,1024]{2,1,0:T(8,128)(2,1)}) %reduce-scatter.11.cloned.1.call-update) | async-done | bytes 1310736 | tf_op jit(solution)/shard_map/reduce_scatter | solution.py:42
  682.2 88.0 %reduce-scatter.17.cloned.1.call-done = bf16[2,320,1024]{2,1,0:T(8,128)(2,1)} async-done(((bf16[2,1280,1024]{2,1,0:T(8,128)(2,1)}), bf16[2,320,1024]{2,1,0:T(8,128)(2,1)}) %reduce-scatter.17.cloned.1.call-update) | async-done | bytes 1310736 | tf_op jit(solution)/shard_map/reduce_scatter | solution.py:42
  784.6 11.9 all-to-all-done.5
  801.7 20.6 all_to_all.134
  828.6 20.6 all_to_all.135
  850.6 69.7 %all-gather.15.cloned.1.call-done = bf16[2,1280,1024]{2,1,0:T(8,128)(2,1)} async-done(((bf16[2,320,1024]{2,1,0:T(8,128)(2,1)}), bf16[2,1280,1024]{2,1,0:T(8,128)(2,1)}) %all-gather.15.cloned.1.call-update) | async-done | bytes 5242896 | tf_op jit(solution)/shard_map/all_gather | solution.py:38
  920.4 10.6 fusion.241
  936.9 81.9 %all-gather.21.cloned.1.call-done = bf16[2,1280,1024]{2,1,0:T(8,128)(2,1)} async-done(((bf16[2,320,1024]{2,1,0:T(8,128)(2,1)}), bf16[2,1280,1024]{2,1,0:T(8,128)(2,1)}) %all-gather.21.cloned.1.call-update) | async-done | bytes 5242896 | tf_op jit(solution)/shard_map/all_gather | solution.py:38
  1018.8 15.2 multiply_convert_fusion.4
  1061.2 72.9 %reduce-scatter.15.cloned.1.call-done = bf16[2,320,1024]{2,1,0:T(8,128)(2,1)} async-done(((bf16[2,1280,1024]{2,1,0:T(8,128)(2,1)}), bf16[2,320,1024]{2,1,0:T(8,128)(2,1)}) %reduce-scatter.15.cloned.1.call-update) | async-done | bytes 1310736 | tf_op jit(solution)/shard_map/reduce_scatter | solution.py:42
  1141.5 89.6 %reduce-scatter.21.cloned.1.call-done = bf16[2,320,1024]{2,1,0:T(8,128)(2,1)} async-done(((bf16[2,1280,1024]{2,1,0:T(8,128)(2,1)}), bf16[2,320,1024]{2,1,0:T(8,128)(2,1)}) %reduce-scatter.21.cloned.1.call-update) | async-done | bytes 1310736 | tf_op jit(solution)/shard_map/reduce_scatter | solution.py:42
  1243.1 14.2 all-to-all-done.7
  1264.0 43.8 %all-gather.23.cloned.1.call-done = bf16[1,1024,1024]{2,1,0:T(8,128)(2,1)} async-done(((bf16[1,256,1024]{2,1,0:T(8,128)(2,1)}), bf16[1,1024,1024]{2,1,0:T(8,128)(2,1)}) %all-gather.23.cloned.1.call-update) | async-done | bytes 2097168 | tf_op jit(solution)/shard_map/all_gather | solution.py:29
  1333.0 21.5 %all-gather.19.cloned.1.call-done = bf16[1,1024,1024]{2,1,0:T(8,128)(2,1)} async-done(((bf16[1,256,1024]{2,1,0:T(8,128)(2,1)}), bf16[1,1024,1024]{2,1,0:T(8,128)(2,1)}) %all-gather.19.cloned.1.call-update) | async-done | bytes 2097168 | tf_op jit(solution)/shard_map/all_gather | solution.py:29
  1470.1 63.8 %rev.15 = f32[4,512,1024]{2,1,0:T(8,128)} reverse(bf16[4,512,1024]{2,1,0:T(8,128)(2,1)} %copy-done.8), dimensions={2} | reverse | bytes 12582912 | tf_op jit(solution)/shard_map/rev | solution.py:50
  1533.9 63.8 %rev.14 = f32[4,512,1024]{2,1,0:T(8,128)} reverse(bf16[4,512,1024]{2,1,0:T(8,128)(2,1)} %copy-done.6), dimensions={2} | reverse | bytes 12582912 | tf_op jit(solution)/shard_map/rev | solution.py:50
  1597.8 63.7 %rev.13 = f32[4,512,1024]{2,1,0:T(8,128)} reverse(bf16[4,512,1024]{2,1,0:T(8,128)(2,1)} %copy-done.9), dimensions={2} | reverse | bytes 12582912 | tf_op jit(solution)/shard_map/rev | solution.py:50
  1661.5 63.7 %rev.12 = f32[4,512,1024]{2,1,0:T(8,128)} reverse(bf16[4,512,1024]{2,1,0:T(8,128)(2,1)} %multiply_convert_fusion.3), dimensions={2} | reverse | bytes 12582912 | tf_op jit(solution)/shard_map/rev | solution.py:50
  1735.0 14.9 copy.219
  1755.1 14.2 reshape.1282
  1769.2 19.8 reshape.1251
  1798.7 14.7 copy.218
  1818.5 14.2 reshape.1280
  1832.8 19.9 reshape.1249
  1873.1 14.7 copy.217
  1893.2 14.2 reshape.1278
  1907.3 19.6 reshape.1247
  1942.0 14.9 copy.216
  1962.1 14.2 reshape.1276
  1976.3 19.8 reshape.1245
  2003.6 13.5 psum.44
  2032.8 38.0 %all-reduce.4 = (f32[1024]{0:T(1024)}, f32[1024]{0:T(1024)}) all-reduce(f32[1024]{0:T(1024)S(1)} %add.595, f32[1024]{0:T(1024)S(1)} %copy-done.99), channel_id=1, replica_groups=mesh['expert'=8,'hidden'=4] {'expert','hidden'}, use_global_device_ids=true, to_apply=%region_63.64 | all-reduce | flops 2048 | bytes 16384 | tf_op jit(solution)/shard_map/psum | solution.py:356
  (605 shorter events, 470.9 us)
Async XLA Ops:
  7.2 550.4 %copy-start = (bf16[2,704,1024]{2,1,0:T(8,128)(2,1)S(1)}, bf16[2,704,1024]{2,1,0:T(8,128)(2,1)}, u32[]{:S(2)}) copy-start(bf16[2,704,1024]{2,1,0:T(8,128)(2,1)} %param.25) | copy-start | bytes 8650756
  7.2 140.7 %all-gather.13.cloned.1.call-start = ((), (), s32[]{:S(2)}) async-start(), calls=%async_computation.20 | async-start | bytes 2621440 | tf_op jit(solution)/shard_map/all_gather | solution.py:29
  12.7 163.2 %all-gather.9.cloned.1.call-start = ((), (), s32[]{:S(2)}) async-start(), calls=%async_computation.16 | async-start | bytes 2621440 | tf_op jit(solution)/shard_map/all_gather | solution.py:29
  13.4 240.3 %reduce-scatter.13.cloned.1.call-start = ((), (), s32[]{:S(2)}) async-start(), calls=%async_computation.21 | async-start | bytes 5242880 | tf_op jit(solution)/shard_map/reduce_scatter | solution.py:33
  174.3 159.6 %reduce-scatter.9.cloned.1.call-start = ((), (), s32[]{:S(2)}) async-start(), calls=%async_computation.17 | async-start | bytes 5242880 | tf_op jit(solution)/shard_map/reduce_scatter | solution.py:33
  203.0 256.2 %all-gather.11.cloned.1.call-start = ((), (), s32[]{:S(2)}) async-start(), calls=%async_computation.18 | async-start | bytes 6553600 | tf_op jit(solution)/shard_map/all_gather | solution.py:38
  203.0 135.8 %copy-start.64 = (f32[1024]{0:T(1024)}, f32[1024]{0:T(1024)S(1)}, u32[]{:S(2)}) copy-start(f32[1024]{0:T(1024)S(1)} %convert_element_type.704) | copy-start | bytes 12292
  203.2 134.3 %copy-start.51 = (s32[1,1,256,2]{3,2,1,0:T(8,128)}, s32[1,1,256,2]{3,2,1,0:T(8,128)S(1)}, u32[]{:S(2)}) copy-start(s32[1,1,256,2]{3,2,1,0:T(8,128)S(1)} %copy.212) | copy-start | bytes 6148
  209.9 43.8 %copy-start.120 = (s32[256,2]{0,1:T(2,128)}, s32[256,2]{0,1:T(2,128)S(1)}, u32[]{:S(2)}) copy-start(s32[256,2]{0,1:T(2,128)S(1)} %copy.178) | copy-start | bytes 6148
  338.9 27.3 %copy-start.21 = (bf16[256,1024]{1,0:T(8,128)(2,1)}, bf16[256,1024]{1,0:T(8,128)(2,1)S(1)}, u32[]{:S(2)}) copy-start(bf16[256,1024]{1,0:T(8,128)(2,1)S(1)} %fusion.137) | copy-start | bytes 1572868
  362.2 195.4 %all-gather.17.cloned.1.call-start = ((), (), s32[]{:S(2)}) async-start(), calls=%async_computation.24 | async-start | bytes 6553600 | tf_op jit(solution)/shard_map/all_gather | solution.py:38
  366.1 27.6 %copy-start.59 = (f32[256,1024]{1,0:T(8,128)}, f32[256,1024]{1,0:T(8,128)S(1)}, u32[]{:S(2)}) copy-start(f32[256,1024]{1,0:T(8,128)S(1)} %get-tuple-element.118) | copy-start | bytes 3145732
  393.7 279.3 %reduce-scatter.11.cloned.1.call-start = ((), (), s32[]{:S(2)}) async-start(), calls=%async_computation.19 | async-start | bytes 6553600 | tf_op jit(solution)/shard_map/reduce_scatter | solution.py:42
  580.7 189.5 %reduce-scatter.17.cloned.1.call-start = ((), (), s32[]{:S(2)}) async-start(), calls=%async_computation.25 | async-start | bytes 6553600 | tf_op jit(solution)/shard_map/reduce_scatter | solution.py:42
  600.9 80.2 %copy-start.63 = (s32[256,2]{1,0:T(8,128)S(1)}, s32[256,2]{1,0:T(8,128)}, u32[]{:S(2)}) copy-start(s32[256,2]{1,0:T(8,128)} %get-tuple-element.132) | copy-start | bytes 6148
  600.9 177.7 %copy-start.106 = (f32[256]{0:T(256)S(1)}, f32[256]{0:T(256)}, u32[]{:S(2)}) copy-start(f32[256]{0:T(256)} %get-tuple-element.120) | copy-start | bytes 3076
  676.7 104.2 %copy-start.121 = (s32[256,2]{0,1:T(2,128)S(1)}, s32[256,2]{0,1:T(2,128)}, u32[]{:S(2)}) copy-start(s32[256,2]{0,1:T(2,128)} %copy-done.120) | copy-start | bytes 6148
  676.7 97.2 %all-to-all-start.1 = ((bf16[2,320,1024]{2,0,1:T(2,128)(2,1)}), bf16[2,320,1024]{2,0,1:T(2,128)(2,1)}, u32[]{:S(2)}, u32[]{:S(2)}) async-start(bf16[2,320,1024]{2,0,1:T(2,128)(2,1)} %copy.180), calls=%async_computation.3 | async-start | bytes 2621440 | tf_op jit(solution)/shard_map/all_to_all | solution.py:45
  681.2 89.0 %copy-start.118 = (s32[256,2]{0,1:T(2,128)}, s32[256,2]{0,1:T(2,128)S(1)}, u32[]{:S(2)}) copy-start(s32[256,2]{0,1:T(2,128)S(1)} %copy.190) | copy-start | bytes 6148
  773.9 22.5 %all-to-all-start.5 = ((bf16[2,320,1024]{2,0,1:T(2,128)(2,1)}), bf16[2,320,1024]{2,0,1:T(2,128)(2,1)}, u32[]{:S(2)}, u32[]{:S(2)}) async-start(bf16[2,320,1024]{2,0,1:T(2,128)(2,1)} %copy.196), calls=%async_computation.10 | async-start | bytes 2621440 | tf_op jit(solution)/shard_map/all_to_all | solution.py:45
  778.2 142.2 %all-gather.15.cloned.1.call-start = ((), (), s32[]{:S(2)}) async-start(), calls=%async_computation.22 | async-start | bytes 6553600 | tf_op jit(solution)/shard_map/all_gather | solution.py:38
  799.3 24.1 %copy-start.17 = (f32[256,1024]{1,0:T(8,128)}, f32[256,1024]{1,0:T(8,128)S(1)}, u32[]{:S(2)}) copy-start(f32[256,1024]{1,0:T(8,128)S(1)} %convolution_add_fusion.4) | copy-start | bytes 3145732
  801.1 27.5 %copy-start.23 = (bf16[256,1024]{1,0:T(8,128)(2,1)}, bf16[256,1024]{1,0:T(8,128)(2,1)S(1)}, u32[]{:S(2)}) copy-start(bf16[256,1024]{1,0:T(8,128)(2,1)S(1)} %get-tuple-element.128) | copy-start | bytes 1572868
  801.1 23.6 %copy-start.100 = (f32[256]{0:T(256)S(1)}, f32[256]{0:T(256)}, u32[]{:S(2)}) copy-start(f32[256]{0:T(256)} %get-tuple-element.135) | copy-start | bytes 3076
  801.1 23.6 %copy-start.119 = (s32[256,2]{0,1:T(2,128)S(1)}, s32[256,2]{0,1:T(2,128)}, u32[]{:S(2)}) copy-start(s32[256,2]{0,1:T(2,128)} %copy-done.118) | copy-start | bytes 6148
  823.5 195.4 %all-gather.21.cloned.1.call-start = ((), (), s32[]{:S(2)}) async-start(), calls=%async_computation.28 | async-start | bytes 6553600 | tf_op jit(solution)/shard_map/all_gather | solution.py:38
  850.4 283.7 %reduce-scatter.15.cloned.1.call-start = ((), (), s32[]{:S(2)}) async-start(), calls=%async_computation.23 | async-start | bytes 6553600 | tf_op jit(solution)/shard_map/reduce_scatter | solution.py:42
  1041.8 189.3 %reduce-scatter.21.cloned.1.call-start = ((), (), s32[]{:S(2)}) async-start(), calls=%async_computation.29 | async-start | bytes 6553600 | tf_op jit(solution)/shard_map/reduce_scatter | solution.py:42
  1061.2 80.3 %copy-start.109 = (f32[256]{0:T(256)S(1)}, f32[256]{0:T(256)}, u32[]{:S(2)}) copy-start(f32[256]{0:T(256)} %copy-done.108) | copy-start | bytes 3076
  1137.8 97.0 %all-to-all-start.3 = ((bf16[2,320,1024]{2,0,1:T(2,128)(2,1)}), bf16[2,320,1024]{2,0,1:T(2,128)(2,1)S(1)}, u32[]{:S(2)}, u32[]{:S(2)}) async-start(bf16[2,320,1024]{2,0,1:T(2,128)(2,1)} %copy.192), calls=%async_computation.7 | async-start | bytes 2621440 | tf_op jit(solution)/shard_map/all_to_all | solution.py:45
  1141.5 119.6 %copy-start.114 = (f32[256]{0:T(256)}, f32[256]{0:T(256)S(1)}, u32[]{:S(2)}) copy-start(f32[256]{0:T(256)S(1)} %multiply_multiply_fusion.9) | copy-start | bytes 3076
  1234.8 22.5 %all-to-all-start.7 = ((bf16[2,320,1024]{2,0,1:T(2,128)(2,1)}), bf16[2,320,1024]{2,0,1:T(2,128)(2,1)}, u32[]{:S(2)}, u32[]{:S(2)}) async-start(bf16[2,320,1024]{2,0,1:T(2,128)(2,1)} %copy.201), calls=%async_computation.14 | async-start | bytes 2621440 | tf_op jit(solution)/shard_map/all_to_all | solution.py:45
  1239.1 68.7 %all-gather.23.cloned.1.call-start = ((), (), s32[]{:S(2)}) async-start(), calls=%async_computation.30 | async-start | bytes 2621440 | tf_op jit(solution)/shard_map/all_gather | solution.py:29
  1261.1 46.7 %copy-start.54 = (bf16[256,1024]{1,0:T(8,128)(2,1)S(1)}, bf16[256,1024]{1,0:T(8,128)(2,1)}, u32[]{:S(2)}) copy-start(bf16[256,1024]{1,0:T(8,128)(2,1)} %param.18) | copy-start | bytes 1572868
  1262.9 47.3 %copy-start.34 = (bf16[1024,3,256]{0,2,1:T(8,128)(2,1)S(1)}, bf16[1024,3,256]{0,2,1:T(8,128)(2,1)}, u32[]{:S(2)}) copy-start(bf16[1024,3,256]{0,2,1:T(8,128)(2,1)} %copy-done.33) | copy-start | bytes 4718596
  1263.0 91.5 %all-gather.19.cloned.1.call-start = ((), (), s32[]{:S(2)}) async-start(), calls=%async_computation.26 | async-start | bytes 2621440 | tf_op jit(solution)/shard_map/all_gather | solution.py:29
  1263.5 754.2 %all-reduce.11.cloned.1.call-start = ((), (), s32[]{:S(2)}) async-start(), calls=%async_computation.33 | async-start | bytes 4194304 | tf_op jit(solution)/shard_map/psum | solution.py:352
  1327.3 27.2 %copy-start.55 = (bf16[256,1024]{1,0:T(8,128)(2,1)S(1)}, bf16[256,1024]{1,0:T(8,128)(2,1)}, u32[]{:S(2)}) copy-start(bf16[256,1024]{1,0:T(8,128)(2,1)} %param.18) | copy-start | bytes 1572868
  1414.2 608.7 %reduce-scatter.23.cloned.1.call-start = ((), (), s32[]{:S(2)}) async-start(), calls=%async_computation.31 | async-start | bytes 5242880 | tf_op jit(solution)/shard_map/reduce_scatter | solution.py:33
  1420.3 602.7 %reduce-scatter.19.cloned.1.call-start = ((), (), s32[]{:S(2)}) async-start(), calls=%async_computation.27 | async-start | bytes 5242880 | tf_op jit(solution)/shard_map/reduce_scatter | solution.py:33
  1425.6 645.2 %all-reduce.9.cloned.1.call-start = ((), (), s32[]{:S(2)}) async-start(), calls=%async_computation.32 | async-start | bytes 131072 | tf_op jit(solution)/shard_map/psum | solution.py:356
  2001.6 23.8 %copy-start.113 = (f32[256]{0:T(256)S(1)}, f32[256]{0:T(256)}, u32[]{:S(2)}) copy-start(f32[256]{0:T(256)} %copy-done.112) | copy-start | bytes 3076
  2001.6 23.8 %copy-start.111 = (f32[256]{0:T(256)S(1)}, f32[256]{0:T(256)}, u32[]{:S(2)}) copy-start(f32[256]{0:T(256)} %copy-done.110) | copy-start | bytes 3076
  2001.6 23.8 %copy-start.15 = (f32[1,256,1024]{2,1,0:T(8,128)S(1)}, f32[1,256,1024]{2,1,0:T(8,128)}, u32[]{:S(2)}) copy-start(f32[1,256,1024]{2,1,0:T(8,128)} %get-tuple-element.121) | copy-start | bytes 3145732
  2001.6 23.8 %copy-start.66 = (f32[1024]{0:T(1024)S(1)}, f32[1024]{0:T(1024)}, u32[]{:S(2)}) copy-start(f32[1024]{0:T(1024)} %copy-done.64) | copy-start | bytes 12292
  2001.6 23.8 %copy-start.92 = (f32[256]{0:T(256)S(1)}, f32[256]{0:T(256)}, u32[]{:S(2)}) copy-start(f32[256]{0:T(256)} %fusion.223) | copy-start | bytes 3076
  2001.6 23.8 %copy-start.117 = (f32[256]{0:T(256)S(1)}, f32[256]{0:T(256)}, u32[]{:S(2)}) copy-start(f32[256]{0:T(256)} %copy-done.116) | copy-start | bytes 3076
  2027.7 44.6 %copy-start.1 = (bf16[2,704,1024]{2,1,0:T(8,128)(2,1)S(1)}, bf16[2,704,1024]{2,1,0:T(8,128)(2,1)}, u32[]{:S(2)}) copy-start(bf16[2,704,1024]{2,1,0:T(8,128)(2,1)} %param.25) | copy-start | bytes 8650756
  (135 other events, 962.1 us)
Sparse Core Ops, SparseCore 0:
  12.8 48.6 all-gather.12
  63.6 44.6 all-gather.8
  174.4 79.2 reduce-scatter.12
  256.5 77.2 reduce-scatter.8
  362.3 96.7 all-gather.10
  461.1 96.4 all-gather.16
  580.8 92.1 reduce-scatter.10
  675.9 94.2 reduce-scatter.16
  823.6 96.7 all-gather.14
  922.4 96.4 all-gather.20
  1041.9 92.1 reduce-scatter.14
  1136.8 94.2 reduce-scatter.20
  1263.1 44.6 all-gather.22
  1309.8 44.6 all-gather.18
  1414.3 60.2 all-reduce.10
  1476.8 75.9 reduce-scatter.22
  1555.1 77.2 reduce-scatter.18
  1638.4 118.2 all-reduce.8
where the time goes:
time: 2120 us; the launch traced here: 2080 us
  waiting for transfers between devices  837 us (39%)
  local copies, waits for them, and re-layouts  688 us (32%)
  matrix products  296 us (14%)
  blocking collectives  135 us (6%)
  other arithmetic  87.3 us (4%)
    reduce_scatter x4, waiting for transfers between devices, from_experts(): lax.psum_scatter(partial_terms.astype(jnp.bfloat16), 'hidden', scatter_di...  323 us
    all_gather x4, waiting for transfers between devices, to_experts(): return lax.all_gather(arrived, 'hidden', axis=1, tiled=True)  299 us
    rev x4, local copies, waits for them, and re-layouts, bucket_sums(): flipped = grad_scores[:, :, ::-1]  255 us
    unnamed x342, local copies, waits for them, and re-layouts  238 us
    reduce_scatter x4, waiting for transfers between devices, own_rows(): return lax.psum_scatter(values, 'hidden', scatter_dimension=1, tiled=True)  123 us
    all_to_all x4, blocking collectives, to_experts(): lax.all_to_all(buffer_in, 'expert', split_axis=0, concat_axis=1, tiled=True)  83.4 us
    reshape x4, local copies, waits for them, and re-layouts, bucket_sums(): sheared[:, :rows_block * (key_count + rows_block - 1)]  79.2 us
    all_gather x4, waiting for transfers between devices, whole_rows(): return lax.all_gather(values, 'hidden', axis=1, tiled=True)  65.3 us
  transfers between devices with their start and end apart: 22, of which 14 were waited for; matrix products, arithmetic and copies ran while one was open for 45% of the time, Pallas kernels for 0%

commit v1 on v0

v1 whole, which is shorter than its diff:
```python
import functools

import jax
import jax.numpy as jnp
from jax import lax
from jax.experimental import pallas as pl
from jax.experimental.pallas import tpu as pltpu
from jax.sharding import PartitionSpec as P

EPSILON = 1e-06
PRECISE = lax.Precision.HIGHEST
LIMITS = (12, 16, 23, 32, 46, 64, 91)
MASKED = -1000000000.0
FIRST_ITEM = 512
GELU_C = 0.7978845608028654
GELU_A = 0.044715
VMEM_LIMIT = 60 * 1024 * 1024
F32 = jnp.float32
BF16 = jnp.bfloat16


def mm(a, b):
    return lax.dot_general(a, b, (((1,), (0,)), ((), ())), preferred_element_type=F32)


def mm_nt(a, b):
    return lax.dot_general(a, b, (((1,), (1,)), ((), ())), preferred_element_type=F32)


def mm_tn(a, b):
    return lax.dot_general(a, b, (((0,), (0,)), ((), ())), preferred_element_type=F32)


def bucket_of(distance):
    magnitude = jnp.abs(distance)
    far_bucket = jnp.full(magnitude.shape, 8, jnp.int32)
    for threshold in LIMITS:
        far_bucket = far_bucket + (magnitude >= threshold).astype(jnp.int32)
    return jnp.where(magnitude < 8, magnitude, far_bucket) + 16 * (distance > 0).astype(jnp.int32)


def bucket_onehot(half, bucket_count):
    lane = jnp.arange(2 * half, dtype=jnp.int32)
    distance = jnp.where(lane < half, lane, lane - 2 * half)
    return (
        bucket_of(distance)[:, None] == jnp.arange(bucket_count, dtype=jnp.int32)[None, :]
    ).astype(F32)


def bias_kernel(line_ref, out_ref):
    half = out_ref.shape[2]
    line = jnp.broadcast_to(line_ref[0], (16, 2 * half))
    row = lax.broadcasted_iota(jnp.int32, (16, 2 * half), 0)
    base = jnp.zeros((16, 2 * half), F32)
    for r in range(16):
        base = jnp.where(row == r, pltpu.roll(line, r, 1) if r else line, base)

    def body(a, carry):
        start = pl.multiple_of(a * 16, 16)
        moved = pltpu.roll(base, start, 1)
        out_ref[0, pl.ds(start, 16), :] = moved[:, :half].astype(out_ref.dtype)
        return carry

    lax.fori_loop(0, half // 16, body, 0)


def position_bias(line, half):
    heads = line.shape[0]
    return pl.pallas_call(
        bias_kernel,
        grid=(heads,),
        out_shape=jax.ShapeDtypeStruct((heads, half, half), BF16),
        in_specs=[pl.BlockSpec((1, 1, 2 * half), lambda h: (h, 0, 0))],
        out_specs=pl.BlockSpec((1, half, half), lambda h: (h, 0, 0)),
        compiler_params=pltpu.CompilerParams(vmem_limit_bytes=VMEM_LIMIT),
        name="position_bias",
    )(line.reshape(heads, 1, 2 * half))


def attend_kernel(scale, tile, qkv_ref, bias_ref, seg_row_ref, seg_col_ref, prob_ref, out_ref):
    heads, half = bias_ref.shape[0], bias_ref.shape[1]
    size = out_ref.shape[1] // heads
    seg_row = seg_row_ref[...]
    for head in range(heads):
        cols = slice(head * size, (head + 1) * size)
        keys = qkv_ref[1, :, cols]
        values = qkv_ref[2, :, cols]
        for start in range(0, half, tile):
            rows = slice(start, start + tile)
            scores = mm_nt(qkv_ref[0, rows, cols], keys) * scale
            scores = scores + bias_ref[head, rows, :].astype(F32)
            scores = jnp.where(seg_col_ref[rows, :] == seg_row, scores, MASKED)
            top = jnp.max(scores, axis=-1, keepdims=True)
            weights = jnp.exp(scores - top)
            inverse = 1.0 / jnp.sum(weights, axis=-1, keepdims=True)
            prob = (weights * inverse).astype(BF16)
            prob_ref[0, head, rows, :] = prob
            out_ref[rows, cols] = mm(prob, values).astype(BF16)


def attend(qkv, bias, seg, scale):
    heads, half = bias.shape[0], bias.shape[1]
    slots, cols = qkv.shape[1], qkv.shape[2]
    parts = slots // half
    return pl.pallas_call(
        functools.partial(attend_kernel, scale, min(128, half)),
        grid=(parts,),
        out_shape=(
            jax.ShapeDtypeStruct((parts, heads, half, half), BF16),
            jax.ShapeDtypeStruct((slots, cols), BF16),
        ),
        in_specs=[
            pl.BlockSpec((3, half, cols), lambda p: (0, p, 0)),
            pl.BlockSpec((heads, half, half), lambda p: (0, 0, 0)),
            pl.BlockSpec((1, half), lambda p: (0, p)),
            pl.BlockSpec((half, 1), lambda p: (p, 0)),
        ],
        out_specs=(
            pl.BlockSpec((1, heads, half, half), lambda p: (p, 0, 0, 0)),
            pl.BlockSpec((half, cols), lambda p: (p, 0)),
        ),
        compiler_params=pltpu.CompilerParams(vmem_limit_bytes=VMEM_LIMIT),
        cost_estimate=pl.CostEstimate(
            flops=4 * slots * half * cols,
            bytes_accessed=parts * heads * half * half * 3 + slots * cols * 8,
            transcendentals=parts * heads * half * half,
        ),
        name="attend",
    )(qkv, bias, seg.reshape(1, slots), seg.reshape(slots, 1))


def attend_back_kernel(
    scale, tile, qkv_ref, prob_ref, grad_ref, dproj_ref, line_ref, total_ref, ds_ref
):
    heads, half = prob_ref.shape[1], prob_ref.shape[2]
    size = grad_ref.shape[1] // heads
    part = pl.program_id(0)

    @pl.when(part == 0)
    def _():
        total_ref[...] = jnp.zeros_like(total_ref)

    for head in range(heads):
        cols = slice(head * size, (head + 1) * size)
        values = qkv_ref[2, :, cols]
        for start in range(0, half, tile):
            rows = slice(start, start + tile)
            prob = prob_ref[0, head, rows, :].astype(F32)
            dprob = mm_nt(grad_ref[rows, cols], values)
            inner = jnp.sum(prob * dprob, axis=-1, keepdims=True)
            dscore = (prob * (dprob - inner)).astype(BF16)
            ds_ref[rows, :] = dscore
            total_ref[head, rows, :] += dscore.astype(F32)
        dscores = ds_ref[...]
        dproj_ref[0, :, cols] = (mm(dscores, qkv_ref[1, :, cols]) * scale).astype(BF16)
        dproj_ref[1, :, cols] = (mm_tn(dscores, qkv_ref[0, :, cols]) * scale).astype(BF16)
        dproj_ref[2, :, cols] = mm_tn(prob_ref[0, head], grad_ref[:, cols]).astype(BF16)

    @pl.when(part == pl.num_programs(0) - 1)
    def _():
        row = lax.broadcasted_iota(jnp.int32, (8, 2 * half), 0)
        for head in range(heads):

            def body(a, carry):
                start = pl.multiple_of(a * 8, 8)
                block = total_ref[head, pl.ds(start, 8), :]
                block = jnp.concatenate([block, jnp.zeros_like(block)], axis=1)
                return carry + pltpu.roll(block, 2 * half - start, 1)

            found = lax.fori_loop(0, half // 8, body, jnp.zeros((8, 2 * half), F32))
            line = jnp.zeros((1, 2 * half), F32)
            for r in range(8):
                moved = pltpu.roll(found, 2 * half - r, 1) if r else found
                line = line + jnp.sum(jnp.where(row == r, moved, 0.0), axis=0, keepdims=True)
            line_ref[head : head + 1, :] = line


def attend_back(qkv, prob, grad_heads, scale):
    parts, heads, half = prob.shape[:3]
    slots, cols = grad_heads.shape
    return pl.pallas_call(
        functools.partial(attend_back_kernel, scale, min(128, half)),
        grid=(parts,),
        out_shape=(
            jax.ShapeDtypeStruct((3, slots, cols), BF16),
            jax.ShapeDtypeStruct((heads, 2 * half), F32),
        ),
        in_specs=[
            pl.BlockSpec((3, half, cols), lambda p: (0, p, 0)),
            pl.BlockSpec((1, heads, half, half), lambda p: (p, 0, 0, 0)),
            pl.BlockSpec((half, cols), lambda p: (p, 0)),
        ],
        out_specs=(
            pl.BlockSpec((3, half, cols), lambda p: (0, p, 0)),
            pl.BlockSpec((heads, 2 * half), lambda p: (0, 0)),
        ),
        scratch_shapes=[
            pltpu.VMEM((heads, half, half), F32),
            pltpu.VMEM((half, half), BF16),
        ],
        compiler_params=pltpu.CompilerParams(vmem_limit_bytes=VMEM_LIMIT),
        cost_estimate=pl.CostEstimate(
            flops=8 * slots * half * cols,
            bytes_accessed=parts * heads * half * half * 2 + slots * cols * 14,
            transcendentals=0,
        ),
        name="attend_back",
    )(qkv, prob, grad_heads)


def expert_kernel(x_ref, g_ref, wg_ref, wu_ref, wd_ref, y_ref, dx_ref, hid_ref, dga_ref, dup_ref):
    sources, _, cap, width = x_ref.shape
    rows = sources * cap
    x = x_ref[...].reshape(rows, width)
    g = g_ref[...].reshape(rows, width)
    gate = mm(x, wg_ref[0])
    up = mm(x, wu_ref[0])
    square = gate * gate
    bent = jnp.tanh(GELU_C * gate * (1.0 + GELU_A * square))
    half_gate = 0.5 * gate
    gelu = half_gate * (1.0 + bent)
    slope = 0.5 * (1.0 + bent) + half_gate * (1.0 - bent * bent) * (
        GELU_C * (1.0 + 3.0 * GELU_A * square)
    )
    hid = (gelu * up).astype(BF16)
    dhid = mm_nt(g, wd_ref[0])
    dga = (dhid * (up * slope)).astype(BF16)
    dup = (dhid * gelu).astype(BF16)
    hid_ref[0] = hid
    dga_ref[0] = dga
    dup_ref[0] = dup
    y_ref[...] = mm(hid, wd_ref[0]).astype(BF16).reshape(sources, 1, cap, width)
    dx = mm_nt(dga, wg_ref[0]) + mm_nt(dup, wu_ref[0])
    dx_ref[...] = dx.astype(BF16).reshape(sources, 1, cap, width)


def expert_pass(x, g, wg, wu, wd):
    sources, experts, cap, width = x.shape
    hidden = wg.shape[2]
    group = 2 if sources % 2 == 0 else 1
    tokens = pl.BlockSpec((group, 1, cap, width), lambda e, s: (s, e, 0, 0))
    wide = pl.BlockSpec((1, width, hidden), lambda e, s: (e, 0, 0))
    tall = pl.BlockSpec((1, hidden, width), lambda e, s: (e, 0, 0))
    acts = pl.BlockSpec((1, group * cap, hidden), lambda e, s: (e, s, 0))
    rows = sources * cap
    act_shape = jax.ShapeDtypeStruct((experts, rows, hidden), BF16)
    return pl.pallas_call(
        expert_kernel,
        grid=(experts, sources // group),
        out_shape=(
            jax.ShapeDtypeStruct(x.shape, BF16),
            jax.ShapeDtypeStruct(x.shape, BF16),
            act_shape,
            act_shape,
            act_shape,
        ),
        in_specs=[tokens, tokens, wide, wide, tall],
        out_specs=(tokens, tokens, acts, acts, acts),
        compiler_params=pltpu.CompilerParams(vmem_limit_bytes=VMEM_LIMIT),
        cost_estimate=pl.CostEstimate(
            flops=12 * experts * rows * width * hidden,
            bytes_accessed=8 * experts * rows * width + 6 * experts * hidden * (width + rows),
            transcendentals=experts * rows * hidden,
        ),
        name="expert_pass",
    )(x, g, wg, wu, wd)


def weight_kernel(*refs):
    count = (len(refs) - 3) // 5
    dwg_ref, dwu_ref, dwd_ref = refs[-3:]
    totals = [0.0, 0.0, 0.0]
    for index in range(count):
        x_ref, g_ref, hid_ref, dga_ref, dup_ref = refs[5 * index : 5 * index + 5]
        sources, _, cap, width = x_ref.shape
        x = x_ref[...].reshape(sources * cap, width)
        g = g_ref[...].reshape(sources * cap, width)
        totals[0] = totals[0] + mm_tn(x, dga_ref[0])
        totals[1] = totals[1] + mm_tn(x, dup_ref[0])
        totals[2] = totals[2] + mm_tn(hid_ref[0], g)
    dwg_ref[0] = totals[0]
    dwu_ref[0] = totals[1]
    dwd_ref[0] = totals[2]


def weight_pass(kept):
    sources, experts, cap, width = kept[0][0].shape
    rows, hidden = kept[0][2].shape[1:]
    block = 256 if width % 256 == 0 else width
    tokens = pl.BlockSpec((sources, 1, cap, block), lambda e, j: (0, e, 0, j))
    acts = pl.BlockSpec((1, rows, hidden), lambda e, j: (e, 0, 0))
    operands = []
    for arrays in kept:
        operands.extend(arrays)
    return pl.pallas_call(
        weight_kernel,
        grid=(experts, width // block),
        out_shape=(
            jax.ShapeDtypeStruct((experts, width, hidden), F32),
            jax.ShapeDtypeStruct((experts, width, hidden), F32),
            jax.ShapeDtypeStruct((experts, hidden, width), F32),
        ),
        in_specs=[tokens, tokens, acts, acts, acts] * len(kept),
        out_specs=(
            pl.BlockSpec((1, block, hidden), lambda e, j: (e, j, 0)),
            pl.BlockSpec((1, block, hidden), lambda e, j: (e, j, 0)),
            pl.BlockSpec((1, hidden, block), lambda e, j: (e, 0, j)),
        ),
        compiler_params=pltpu.CompilerParams(vmem_limit_bytes=VMEM_LIMIT),
        cost_estimate=pl.CostEstimate(
            flops=6 * len(kept) * experts * rows * width * hidden,
            bytes_accessed=len(kept) * experts * rows * (4 * width + 6 * hidden)
            + 12 * experts * width * hidden,
            transcendentals=0,
        ),
        name="weight_pass",
    )(*operands)


def norm_back(grad_out, unit, scale, gain):
    weighted = grad_out * gain
    grad_in = scale * (weighted - unit * jnp.mean(weighted * unit, axis=-1, keepdims=True))
    return grad_in, jnp.sum(grad_out * unit, axis=0)


def shards(
    x_in,
    cotangent,
    segment_ids,
    routes,
    qkv_weight,
    out_weight,
    bias_table,
    attn_gain,
    moe_gain,
    router_weight,
    gate_weight,
    up_weight,
    down_weight,
):
    micro_count, _, shard_len, width = x_in.shape
    slot_count = segment_ids.shape[2]
    head_cols = out_weight.shape[0]
    bucket_count, heads_here = bias_table.shape
    head_size = head_cols // heads_here
    expert_count = router_weight.shape[1]
    experts_here = gate_weight.shape[0]
    devices = expert_count // experts_here
    blocks = slot_count // shard_len
    capacity = max(2, (10 * shard_len + 4 * expert_count - 1) // (4 * expert_count))
    half = min(FIRST_ITEM, slot_count)
    scale = head_size ** (-0.5)
    hidden_index = lax.axis_index("hidden")
    own_start = hidden_index * shard_len
    attn_gain_f = attn_gain.astype(F32)
    moe_gain_f = moe_gain.astype(F32)
    onehot_bucket = bucket_onehot(half, bucket_count)
    line = jnp.einsum(
        "jb,bh->hj", onehot_bucket, bias_table.astype(F32), precision=PRECISE
    )
    bias = position_bias(line, half)
    expert_ids = jnp.arange(expert_count, dtype=jnp.int32)
    place_ids = jnp.arange(expert_count * capacity, dtype=jnp.int32)
    earlier_than = (
        jnp.arange(shard_len, dtype=jnp.int32)[:, None]
        < jnp.arange(shard_len, dtype=jnp.int32)[None, :]
    ).astype(BF16)
    all_routes = lax.all_gather(routes[:, 0], "hidden", axis=1, tiled=True)
    all_out_weight = lax.all_gather(out_weight, "hidden", axis=0, tiled=True)
    all_out_weight = all_out_weight.reshape(blocks, head_cols, width)

    def own(values):
        return lax.dynamic_slice_in_dim(values, own_start, shard_len, 0)

    def gather(values):
        return lax.all_gather(values, "hidden", axis=0, tiled=True)

    def scatter(values):
        return lax.psum_scatter(values.astype(BF16), "hidden", scatter_dimension=0, tiled=True)

    def exchange(buffer):
        return lax.all_to_all(buffer, "expert", split_axis=0, concat_axis=0, tiled=True)

    def to_buffer(rows):
        rows = rows.reshape(blocks, expert_count, capacity, width).transpose(1, 0, 2, 3)
        return rows.reshape(devices, experts_here * blocks * capacity, width)

    def from_buffer(buffer):
        rows = buffer.reshape(expert_count, blocks, capacity, width).transpose(1, 0, 2, 3)
        return rows.reshape(blocks, expert_count * capacity, width)

    def attention(micro):
        seg = segment_ids[micro, 0]
        gathered = gather(x_in[micro, 0])
        x_now = gathered.astype(F32)
        r1 = lax.rsqrt(jnp.mean(x_now * x_now, axis=-1, keepdims=True) + EPSILON)
        xn1 = (x_now * r1 * attn_gain_f).astype(BF16)
        qkv = jnp.einsum("sd,tdf->tsf", xn1, qkv_weight, preferred_element_type=F32).astype(BF16)
        prob, heads_out = attend(qkv, bias, seg, scale)
        all_heads = lax.all_gather(heads_out, "hidden", axis=0, tiled=False)
        return dict(seg=seg, gathered=gathered, xn1=xn1, qkv=qkv, prob=prob, heads=heads_out, all_heads=all_heads)

    def dispatch(micro, kept):
        attn = jnp.einsum(
            "hsf,hfd->sd", kept["all_heads"], all_out_weight, preferred_element_type=F32
        )
        h1 = kept["gathered"].astype(F32) + attn
        r2 = lax.rsqrt(jnp.mean(h1 * h1, axis=-1, keepdims=True) + EPSILON)
        xn2 = (h1 * r2 * moe_gain_f).astype(BF16)
        logits = jnp.dot(xn2, router_weight, preferred_element_type=F32)
        router = jax.nn.softmax(logits, axis=-1)
        route = all_routes[micro]
        live = kept["seg"] >= 0
        live_f = live.astype(F32)
        onehot = (route[:, :, None] == expert_ids).astype(F32)
        picked = jnp.sum(router[:, None, :] * onehot, axis=-1)
        total = jnp.sum(picked, axis=1, keepdims=True)
        gates = picked / total * live_f[:, None]
        chosen = (onehot * live_f[:, None, None]).reshape(blocks, shard_len, 2, expert_count)
        counted = jnp.sum(chosen, axis=2).astype(BF16)
        before = jnp.einsum("bte,tu->bue", counted, earlier_than, preferred_element_type=F32)
        position = jnp.sum(before[:, :, None, :] * chosen, axis=-1).astype(jnp.int32)
        route_b = route.reshape(blocks, shard_len, 2)
        place = jnp.where(
            live.reshape(blocks, shard_len)[:, :, None], route_b * capacity + position, -1
        )
        at_place = [place[:, None, :, k] == place_ids[None, :, None] for k in range(2)]
        placed = (at_place[0] | at_place[1]).astype(BF16)
        gates_b = gates.reshape(blocks, shard_len, 2)
        gate_place = sum(
            jnp.sum(jnp.where(at_place[k], gates_b[:, None, :, k], 0.0), axis=-1) for k in range(2)
        )
        xn2_b = xn2.reshape(blocks, shard_len, width)
        sent = jnp.einsum("bst,btd->bsd", placed, xn2_b, preferred_element_type=F32).astype(BF16)
        arrived = exchange(to_buffer(sent))
        dy = gather(cotangent[micro, 0])
        dy_b = dy.reshape(blocks, shard_len, width)
        dy_place = jnp.einsum("bst,btd->bsd", placed, dy_b, preferred_element_type=F32)
        sent_back = (dy_place * gate_place[:, :, None]).astype(BF16)
        arrived_back = exchange(to_buffer(sent_back))
        kept.update(
            h1=own(h1), r2=own(r2), xn2=own(xn2), router=own(router), picked=own(picked),
            total=own(total), onehot=own(onehot), live=own(live_f), placed=placed,
            place=place, at_place=at_place, gate_place=gate_place, dy_place=dy_place.astype(BF16),
            arrived=arrived, arrived_back=arrived_back,
        )

    def experts(micro, kept):
        shape = (devices, experts_here, blocks * capacity, width)
        x = kept["arrived"].reshape(shape)
        g = kept["arrived_back"].reshape(shape)
        y, dx, hid, dga, dup = expert_pass(x, g, gate_weight, up_weight, down_weight)
        kept["weights"] = (x, g, hid, dga, dup)
        kept["back_y"] = exchange(y.reshape(devices, -1, width))
        kept["back_dx"] = exchange(dx.reshape(devices, -1, width))

    def combine(micro, kept):
        y = from_buffer(kept["back_y"])
        y_f = y.astype(F32)
        scaled = (y_f * kept["gate_place"][:, :, None]).astype(BF16)
        mixed = jnp.einsum("bst,bsd->btd", kept["placed"], scaled, preferred_element_type=F32)
        mixed = scatter(mixed.reshape(slot_count, width))
        dgate_place = jnp.sum(y_f * kept["dy_place"].astype(F32), axis=-1)
        dgates = jnp.stack(
            [
                jnp.sum(jnp.where(kept["at_place"][k], dgate_place[:, :, None], 0.0), axis=1)
                for k in range(2)
            ],
            axis=-1,
        )
        dgates = lax.psum_scatter(
            dgates.reshape(slot_count, 2), "hidden", scatter_dimension=0, tiled=True
        )
        dx = from_buffer(kept["back_dx"])
        dxn2 = jnp.einsum("bst,bsd->btd", kept["placed"], dx, preferred_element_type=F32)
        dxn2 = scatter(dxn2.reshape(slot_count, width)).astype(F32)
        kept["block_out"] = (kept["h1"] + mixed.astype(F32)).astype(BF16)
        picked, total, router = kept["picked"], kept["total"], kept["router"]
        dgates = dgates * kept["live"][:, None]
        dpicked = dgates / total - jnp.sum(dgates * picked, axis=1, keepdims=True) / (total * total)
        drouter = jnp.sum(dpicked[:, :, None] * kept["onehot"], axis=1)
        dlogits = router * (drouter - jnp.sum(router * drouter, axis=-1, keepdims=True))
        dlogits = dlogits.astype(BF16)
        kept["router_grad"] = mm_tn(kept["xn2"], dlogits)
        dxn2 = dxn2 + mm_nt(dlogits, router_weight)
        unit = kept["h1"] * kept["r2"]
        part, kept["moe_gain_grad"] = norm_back(dxn2, unit, kept["r2"], moe_gain_f)
        kept["dh1"] = cotangent[micro, 0].astype(F32) + part
        kept["dattn"] = gather(kept["dh1"].astype(BF16))

    def attention_back(micro, kept):
        dattn = kept["dattn"]
        kept["out_grad"] = mm_tn(kept["heads"], dattn)
        dheads = mm_nt(dattn, out_weight).astype(BF16)
        dproj, bias_line = attend_back(kept["qkv"], kept["prob"], dheads, scale)
        kept["bias_line"] = bias_line
        dxn1 = jnp.einsum("tsf,tdf->sd", dproj, qkv_weight, preferred_element_type=F32)
        dxn1 = scatter(dxn1).astype(F32)
        kept["qkv_grad"] = jnp.einsum(
            "sd,tsf->tdf", kept["xn1"], dproj, preferred_element_type=F32
        )
        x_own = x_in[micro, 0].astype(F32)
        r1 = lax.rsqrt(jnp.mean(x_own * x_own, axis=-1, keepdims=True) + EPSILON)
        part, kept["attn_gain_grad"] = norm_back(dxn1, x_own * r1, r1, attn_gain_f)
        kept["x_grad"] = (kept["dh1"] + part).astype(BF16)

    states = []
    for micro in range(micro_count):
        states.append(attention(micro))
    for micro in range(micro_count):
        dispatch(micro, states[micro])
        experts(micro, states[micro])
    for micro in range(micro_count):
        combine(micro, states[micro])
        attention_back(micro, states[micro])
    dwg, dwu, dwd = weight_pass([state["weights"] for state in states])

    def added(name):
        total = states[0][name]
        for state in states[1:]:
            total = total + state[name]
        return total

    grad_table = jnp.einsum("hj,jb->bh", added("bias_line"), onehot_bucket, precision=PRECISE)
    grad_qkv, grad_out, grad_table = (
        lax.psum(added("qkv_grad").astype(BF16), "expert").astype(F32),
        lax.psum(added("out_grad").astype(BF16), "expert").astype(F32),
        lax.psum(grad_table.astype(BF16), "expert").astype(F32),
    )
    grad_router, grad_attn_gain, grad_moe_gain = lax.psum(
        (added("router_grad"), added("attn_gain_grad"), added("moe_gain_grad")),
        ("expert", "hidden"),
    )
    return (
        jnp.stack([state["block_out"] for state in states])[:, None],
        jnp.stack([state["x_grad"] for state in states])[:, None],
        grad_qkv,
        grad_out,
        grad_table,
        grad_attn_gain,
        grad_moe_gain,
        grad_router,
        dwg,
        dwu,
        dwd,
    )


def solution(mesh):
    return jax.shard_map(
        shards,
        mesh=mesh,
        in_specs=(
            P(None, "expert", "hidden", None),
            P(None, "expert", "hidden", None),
            P(None, "expert", None),
            P(None, "expert", "hidden", None),
            P(None, None, "hidden"),
            P("hidden", None),
            P(None, "hidden"),
            P(),
            P(),
            P(),
            P("expert", None, "hidden"),
            P("expert", None, "hidden"),
            P("expert", "hidden", None),
        ),
        out_specs=(
            P(None, "expert", "hidden", None),
            P(None, "expert", "hidden", None),
            P(None, None, "hidden"),
            P("hidden", None),
            P(None, "hidden"),
            P(),
            P(),
            P(),
            P("expert", None, "hidden"),
            P("expert", None, "hidden"),
            P("expert", "hidden", None),
        ),
        check_vma=False,
    )
```

time: 2120 us -> 1370 us (0.65); the launches traced: 2080 us -> 1360 us
  local copies, waits for them, and re-layouts: 688 us -> 76.9 us
  Pallas kernels: 0 us -> 206 us
  matrix products: 296 us -> 94.2 us
  waiting for transfers between devices: 837 us -> 760 us
  other arithmetic: 87.3 us -> 46.8 us
    rev x4 -> x0, local copies, waits for them, and re-layouts: 255 us -> none  [bucket_sums(): flipped = grad_scores[:, :, ::-1]]
    reduce_scatter x8 -> x6, waiting for transfers between devices: 445 us -> 201 us  [scatter(): lax.psum_scatter(values.astype(BF16), 'hidden', scatter_dimension=0, tile...]
    pallas_call x0 -> x8, Pallas kernels: none -> 206 us  [the longest x2 63.7 us: expert_pass(): pl.pallas_call(expert_kernel, grid=(experts, sources // group), out_shape...]
    unnamed x342 -> x94, local copies, waits for them, and re-layouts: 238 us -> 32.7 us
    dot_general x74 -> x28, matrix products: 296 us -> 93.9 us  [the longest x2 12.6 us: dispatch(): jnp.einsum('hsf,hfd->sd', kept['all_heads'], all_out_weight, preferred_el...]
    all_to_all x4 -> x7, waiting for transfers between devices: 26 us -> 180 us  [exchange(): lax.all_to_all(buffer, 'expert', split_axis=0, concat_axis=0, tiled=True)]
    reshape x10 -> x3, local copies, waits for them, and re-layouts: 110 us -> 9.54 us  [the longest x2 8.92 us: from_buffer(): buffer.reshape(expert_count, blocks, capacity, width).transpose(1, 0, 2, 3)]
    psum x2, waiting for transfers between devices: 0.01 us -> 78.7 us  [the longest x1 78.7 us: shards(): lax.psum((added('router_grad'), added('attn_gain_grad'), added('moe_gain_...]
  transfers between devices with their start and end apart: 22 -> 26, of which waited for: 14 -> 23; matrix products, arithmetic and copies ran while one was open for 45% -> 13% of each run, Pallas kernels for 0% -> 13%
where the time goes in v1:
time: 1370 us; the launch traced here: 1360 us
  waiting for transfers between devices  760 us (55%)
  Pallas kernels  206 us (15%)
  blocking collectives  131 us (10%)
  matrix products  94.2 us (7%)
  local copies, waits for them, and re-layouts  76.9 us (6%)
  other arithmetic  46.8 us (3%)
  starting transfers between devices  34.7 us (3%)
  between operations  15.5 us (1%)
    reduce_scatter x6, waiting for transfers between devices, scatter(): lax.psum_scatter(values.astype(BF16), 'hidden', scatter_dimension=0, tile...  201 us
    all_gather x6, waiting for transfers between devices, gather(): return lax.all_gather(values, 'hidden', axis=0, tiled=True)  200 us
    all_to_all x7, waiting for transfers between devices, exchange(): lax.all_to_all(buffer, 'expert', split_axis=0, concat_axis=0, tiled=True)  180 us
    all_gather x2, waiting for transfers between devices, attention(): all_heads = lax.all_gather(heads_out, 'hidden', axis=0, tiled=False)  85.1 us
    psum x1, waiting for transfers between devices, shards(): lax.psum((added('router_grad'), added('attn_gain_grad'), added('moe_gain_...  78.7 us
    all_to_all x1, blocking collectives, exchange(): lax.all_to_all(buffer, 'expert', split_axis=0, concat_axis=0, tiled=True)  64.8 us
    pallas_call x2, Pallas kernels, expert_pass(): pl.pallas_call(expert_kernel, grid=(experts, sources // group), out_shape...  63.7 us
    pallas_call x2, Pallas kernels, attend_back(): pl.pallas_call(functools.partial(attend_back_kernel, scale, min(128, half...  62.5 us
  transfers between devices with their start and end apart: 26, of which 23 were waited for; matrix products, arithmetic and copies ran while one was open for 13% of the time, Pallas kernels for 13%

profile of v1, /device:TPU:0, one launch (start us, length us, event | category | flops | bytes accessed | tf_op | source)
XLA Modules:
  0.0 1364.5 jit_solution(6339079748083183733)
XLA Ops:
  13.8 13.0 position_bias.1.bias_ref
  26.8 32.1 %all-gather.23.cloned.1.call-done = bf16[1,1,1024,1024]{3,2,1,0:T(8,128)(2,1)} async-done(((bf16[1,1,256,1024]{3,2,1,0:T(8,128)(2,1)}), bf16[1,1,1024,1024]{3,2,1,0:T(8,128)(2,1)}) %all-gather.23.cloned.1.call-update) | async-done | bytes 2097168 | tf_op jit(solution)/shard_map/all_gather | solution.py:376
  65.6 15.5 %attend.2 = (bf16[2,4,512,512]{3,2,1,0:T(8,128)(2,1)}, bf16[1024,256]{1,0:T(8,128)(2,1)}) custom-call(bf16[3,1024,256]{2,1,0:T(8,128)(2,1)} %fusion.14.qkv_ref, bf16[4,512,512]{2,1,0:T(8,128)(2,1)} %position_bias.1.bias_ref, s32[1,1024]{1,0:T(1,128)} %get-tuple-element.156.seg_row_ref, s32[1024,1]{1,0:T(8,128)} %copy.127.seg_col_ref), custom_call_target="tpu_custom_call" | custom-call | flops 536870912 | bytes 8388608 | tf_op jit(solution)/shard_map/attend/pallas_call | solution.py:105
  82.4 23.6 %all-gather.29.cloned.1.call-done = bf16[1,1,1024,1024]{3,2,1,0:T(8,128)(2,1)} async-done(((bf16[1,1,256,1024]{3,2,1,0:T(8,128)(2,1)}), bf16[1,1,1024,1024]{3,2,1,0:T(8,128)(2,1)}) %all-gather.29.cloned.1.call-update) | async-done | bytes 2097168 | tf_op jit(solution)/shard_map/all_gather | solution.py:376
  112.8 15.5 %attend.3 = (bf16[2,4,512,512]{3,2,1,0:T(8,128)(2,1)}, bf16[1024,256]{1,0:T(8,128)(2,1)}) custom-call(bf16[3,1024,256]{2,1,0:T(8,128)(2,1)} %fusion.15.qkv_ref, bf16[4,512,512]{2,1,0:T(8,128)(2,1)} %position_bias.1.bias_ref, s32[1,1024]{1,0:T(1,128)} %get-tuple-element.155.seg_row_ref, s32[1024,1]{1,0:T(8,128)} %copy.135.seg_col_ref), custom_call_target="tpu_custom_call" | custom-call | flops 536870912 | bytes 8388608 | tf_op jit(solution)/shard_map/attend/pallas_call | solution.py:105
  128.4 12.1 all-gather.2
  140.8 11.9 all-gather.17.cloned.1.call-done
  152.7 46.2 %all-gather.25.cloned.1.call-done = bf16[4096,256]{1,0:T(8,128)(2,1)} async-done(((bf16[1024,256]{1,0:T(8,128)(2,1)}), bf16[4096,256]{1,0:T(8,128)(2,1)}) %all-gather.25.cloned.1.call-update) | async-done | bytes 2097168 | tf_op jit(solution)/shard_map/all_gather | solution.py:400
  198.9 7.2 multiply_reduce_fusion.1
  206.1 38.9 %all-gather.31.cloned.1.call-done = bf16[4096,256]{1,0:T(8,128)(2,1)} async-done(((bf16[1024,256]{1,0:T(8,128)(2,1)}), bf16[4096,256]{1,0:T(8,128)(2,1)}) %all-gather.31.cloned.1.call-update) | async-done | bytes 2097168 | tf_op jit(solution)/shard_map/all_gather | solution.py:400
  245.0 5.5 multiply_reduce_fusion
  270.1 53.6 %all-to-all-done.3 = bf16[8,320,1024]{2,1,0:T(8,128)(2,1)} async-done(((bf16[8,320,1024]{2,1,0:T(8,128)(2,1)}), bf16[8,320,1024]{2,1,0:T(8,128)(2,1)}, u32[]{:S(2)}, u32[]{:S(2)}) %all-to-all-start.3) | async-done | bytes 5242912 | tf_op jit(solution)/shard_map/all_to_all | solution.py:382
  332.8 43.4 %all-gather.27.cloned.1.call-done = bf16[1,1,1024,1024]{3,2,1,0:T(8,128)(2,1)} async-done(((bf16[1,1,256,1024]{3,2,1,0:T(8,128)(2,1)}), bf16[1,1,1024,1024]{3,2,1,0:T(8,128)(2,1)}) %all-gather.27.cloned.1.call-update) | async-done | bytes 2097168 | tf_op jit(solution)/shard_map/all_gather | solution.py:376
  376.2 5.1 multiply_convert_fusion.1
  397.4 44.1 %all-gather.33.cloned.1.call-done = bf16[1,1,1024,1024]{3,2,1,0:T(8,128)(2,1)} async-done(((bf16[1,1,256,1024]{3,2,1,0:T(8,128)(2,1)}), bf16[1,1,1024,1024]{3,2,1,0:T(8,128)(2,1)}) %all-gather.33.cloned.1.call-update) | async-done | bytes 2097168 | tf_op jit(solution)/shard_map/all_gather | solution.py:376
  441.6 5.1 multiply_convert_fusion
  453.8 5.0 all-to-all-start.4
  468.1 31.8 %expert_pass.2 = (bf16[8,2,160,1024]{3,2,1,0:T(8,128)(2,1)}, bf16[8,2,160,1024]{3,2,1,0:T(8,128)(2,1)}, bf16[2,1280,704]{2,1,0:T(8,128)(2,1)}, bf16[2,1280,704]{2,1,0:T(8,128)(2,1)}, bf16[2,1280,704]{2,1,0:T(8,128)(2,1)}) custom-call(bf16[8,2,160,1024]{3,2,1,0:T(8,128)(2,1)} %bitcast.19.x_ref.refs_0_, bf16[8,2,160,1024]{3,2,1,0:T(8,128)(2,1)} %bitcast.27.g_ref.refs_1_, ...), custom_call_target="tpu_custom_call" | custom-call | flops 22145925120 | bytes 40435712 | tf_op jit(solution)/shard_map/expert_pass/pallas_call | solution.py:247
  499.9 19.3 %all-to-all-done.4 = bf16[8,320,1024]{2,1,0:T(8,128)(2,1)} async-done(((bf16[8,320,1024]{2,1,0:T(8,128)(2,1)}), bf16[8,320,1024]{2,1,0:T(8,128)(2,1)}, u32[]{:S(2)}, u32[]{:S(2)}) %all-to-all-start.4) | async-done | bytes 5242912 | tf_op jit(solution)/shard_map/all_to_all | solution.py:382
  523.9 31.9 %expert_pass.3 = (bf16[8,2,160,1024]{3,2,1,0:T(8,128)(2,1)}, bf16[8,2,160,1024]{3,2,1,0:T(8,128)(2,1)}, bf16[2,1280,704]{2,1,0:T(8,128)(2,1)}, bf16[2,1280,704]{2,1,0:T(8,128)(2,1)}, bf16[2,1280,704]{2,1,0:T(8,128)(2,1)}) custom-call(bf16[8,2,160,1024]{3,2,1,0:T(8,128)(2,1)} %bitcast.51.x_ref.refs_5_, bf16[8,2,160,1024]{3,2,1,0:T(8,128)(2,1)} %bitcast.59.g_ref.refs_6_, ...), custom_call_target="tpu_custom_call" | custom-call | flops 22145925120 | bytes 40435712 | tf_op jit(solution)/shard_map/expert_pass/pallas_call | solution.py:247
  555.8 28.5 %all-to-all-done.2 = bf16[8,320,1024]{2,1,0:T(8,128)(2,1)} async-done(((bf16[8,320,1024]{2,1,0:T(8,128)(2,1)}), bf16[8,320,1024]{2,1,0:T(8,128)(2,1)}, u32[]{:S(2)}, u32[]{:S(2)}) %all-to-all-start.2) | async-done | bytes 5242912 | tf_op jit(solution)/shard_map/all_to_all | solution.py:382
  584.3 64.8 %all_to_all.40 = bf16[8,320,1024]{2,1,0:T(8,128)(2,1)} all-to-all(bf16[8,320,1024]{2,1,0:T(8,128)(2,1)} %bitcast.279), channel_id=1, replica_groups=mesh['expert'=8,'hidden'=4] {'expert'}, dimensions={0} | all-to-all | bytes 10485760 | tf_op jit(solution)/shard_map/all_to_all | solution.py:382
  653.8 7.8 copy.134
  661.6 9.6 fusion.3
  673.3 7.8 copy.142
  681.1 33.1 %all-to-all-done.7 = bf16[8,320,1024]{2,1,0:T(8,128)(2,1)} async-done(((bf16[8,320,1024]{2,1,0:T(8,128)(2,1)}), bf16[8,320,1024]{2,1,0:T(8,128)(2,1)}, u32[]{:S(2)}, u32[]{:S(2)}) %all-to-all-start.7) | async-done | bytes 5242912 | tf_op jit(solution)/shard_map/all_to_all | solution.py:382
  719.0 9.6 fusion.1
  729.6 5.6 copy.144
  736.4 5.9 convolution_convert_fusion.2
  742.3 37.0 %all-to-all-done.6 = bf16[8,320,1024]{2,1,0:T(8,128)(2,1)} async-done(((bf16[8,320,1024]{2,1,0:T(8,128)(2,1)}), bf16[8,320,1024]{2,1,0:T(8,128)(2,1)}, u32[]{:S(2)}, u32[]{:S(2)}) %all-to-all-start.6) | async-done | bytes 5242912 | tf_op jit(solution)/shard_map/all_to_all | solution.py:382
  788.6 13.6 reduce-scatter.21.cloned.1.call-done
  803.6 44.8 %reduce-scatter.17.cloned.1.call-done = bf16[256,1024]{1,0:T(8,128)(2,1)} async-done(((bf16[1024,1024]{1,0:T(8,128)(2,1)}), bf16[256,1024]{1,0:T(8,128)(2,1)}) %reduce-scatter.17.cloned.1.call-update) | async-done | bytes 524304 | tf_op jit(solution)/shard_map/reduce_scatter | solution.py:379
  855.5 44.4 %all-gather.21.cloned.1.call-done = bf16[1024,1024]{1,0:T(8,128)(2,1)} async-done(((bf16[256,1024]{1,0:T(8,128)(2,1)}), bf16[1024,1024]{1,0:T(8,128)(2,1)}) %all-gather.21.cloned.1.call-update) | async-done | bytes 2097168 | tf_op jit(solution)/shard_map/all_gather | solution.py:376
  903.1 31.1 %attend_back.3 = (bf16[3,1024,256]{2,1,0:T(8,128)(2,1)}, f32[4,1024]{1,0:T(4,128)}) custom-call(bf16[3,1024,256]{2,1,0:T(8,128)(2,1)} %fusion.15.qkv_ref, bf16[2,4,512,512]{3,2,1,0:T(8,128)(2,1)} %get-tuple-element.40.prob_ref, bf16[1024,256]{1,0:T(8,128)(2,1)} %convolution_convert_fusion.8.grad_ref), custom_call_target="tpu_custom_call" | custom-call | flops 1073741824 | bytes 7864320 | tf_op jit(solution)/shard_map/attend_back/pallas_call | solution.py:181
  934.1 12.6 all-gather.19.cloned.1.call-done
  949.9 31.4 %attend_back.2 = (bf16[3,1024,256]{2,1,0:T(8,128)(2,1)}, f32[4,1024]{1,0:T(4,128)}) custom-call(bf16[3,1024,256]{2,1,0:T(8,128)(2,1)} %fusion.14.qkv_ref, bf16[2,4,512,512]{3,2,1,0:T(8,128)(2,1)} %get-tuple-element.37.prob_ref, bf16[1024,256]{1,0:T(8,128)(2,1)} %convolution_convert_fusion.9.grad_ref), custom_call_target="tpu_custom_call" | custom-call | flops 1073741824 | bytes 7864320 | tf_op jit(solution)/shard_map/attend_back/pallas_call | solution.py:181
  999.2 6.0 convolution_convert_fusion.5
  1005.3 6.0 convolution_convert_fusion.4
  1012.8 36.0 %weight_pass.1 = (f32[2,1024,704]{2,1,0:T(8,128)}, f32[2,1024,704]{2,1,0:T(8,128)}, f32[2,704,1024]{2,1,0:T(8,128)}) custom-call(bf16[8,2,160,1024]{3,2,1,0:T(8,128)(2,1)} %bitcast.19.x_ref.refs_0_, bf16[8,2,160,1024]{3,2,1,0:T(8,128)(2,1)} %bitcast.27.g_ref.refs_1_, bf16[2,1280,704]{2,1,0:T(8,128)(2,1)} %get-tuple-element.44.refs_2_, ...), custom_call_target="tpu_custom_call" | custom-call | flops 22145925120 | bytes 59899904 | tf_op jit(solution)/shard_map/weight_pass/pallas_call | solution.py:295
  1048.8 6.4 copy.150
  1055.2 6.5 copy.151
  1065.2 14.0 %psum.44 = bf16[32,4]{0,1:T(4,128)(2,1)S(1)} all-reduce(bf16[32,4]{0,1:T(4,128)(2,1)S(1)} %convolution_convert_fusion.10), channel_id=1, replica_groups=mesh['expert'=8,'hidden'=4] {'expert'}, use_global_device_ids=true, to_apply=%region_48.49 | all-reduce | flops 128 | bytes 512 | tf_op jit(solution)/shard_map/psum | solution.py:528
  1085.0 11.6 reduce-scatter.23.cloned.1.call-done
  1096.6 45.5 %reduce-scatter.19.cloned.1.call-done = bf16[256,1024]{1,0:T(8,128)(2,1)} async-done(((bf16[1024,1024]{1,0:T(8,128)(2,1)}), bf16[256,1024]{1,0:T(8,128)(2,1)}) %reduce-scatter.19.cloned.1.call-update) | async-done | bytes 524304 | tf_op jit(solution)/shard_map/reduce_scatter | solution.py:379
  1144.1 43.4 %reduce-scatter.13.cloned.1.call-done = bf16[256,1024]{1,0:T(8,128)(2,1)} async-done(((bf16[1024,1024]{1,0:T(8,128)(2,1)}), bf16[256,1024]{1,0:T(8,128)(2,1)}) %reduce-scatter.13.cloned.1.call-update) | async-done | bytes 524304 | tf_op jit(solution)/shard_map/reduce_scatter | solution.py:379
  1191.0 41.9 %reduce-scatter.15.cloned.1.call-done = bf16[256,1024]{1,0:T(8,128)(2,1)} async-done(((bf16[1024,1024]{1,0:T(8,128)(2,1)}), bf16[256,1024]{1,0:T(8,128)(2,1)}) %reduce-scatter.15.cloned.1.call-update) | async-done | bytes 524304 | tf_op jit(solution)/shard_map/reduce_scatter | solution.py:379
  1237.7 39.6 %all-reduce = (f32[1024]{0:T(1024)}, f32[1024]{0:T(1024)}) all-reduce(f32[1024]{0:T(1024)S(1)} %add.272, f32[1024]{0:T(1024)S(1)} %add.273), channel_id=1, replica_groups=mesh['expert'=8,'hidden'=4] {'expert','hidden'}, use_global_device_ids=true, to_apply=%region_51.52 | all-reduce | flops 2048 | bytes 16384 | tf_op jit(solution)/shard_map/psum | solution.py:530
  1277.3 78.7 %all-reduce.5.cloned.1.call-done = f32[1024,16]{0,1:T(8,128)} async-done(((f32[1024,16]{0,1:T(8,128)}), f32[1024,16]{0,1:T(8,128)}) %all-reduce.5.cloned.1.call-update) | async-done | bytes 65552 | tf_op jit(solution)/shard_map/psum | solution.py:530
  (257 shorter events, 164.8 us)
Async XLA Ops:
  7.2 53.9 %copy-start = (bf16[3,1024,256]{2,1,0:T(8,128)(2,1)S(1)}, bf16[3,1024,256]{2,1,0:T(8,128)(2,1)}, u32[]{:S(2)}) copy-start(bf16[3,1024,256]{2,1,0:T(8,128)(2,1)} %param.17) | copy-start | bytes 4718596
  7.2 4.0 copy-start.29
  7.2 4.0 copy-start.35
  7.2 5.0 copy-start.21
  7.2 51.7 %all-gather.23.cloned.1.call-start = ((), (), s32[]{:S(2)}) async-start(), calls=%async_computation.26 | async-start | bytes 2621440 | tf_op jit(solution)/shard_map/all_gather | solution.py:376
  9.6 96.4 %all-gather.29.cloned.1.call-start = ((), (), s32[]{:S(2)}) async-start(), calls=%async_computation.29 | async-start | bytes 2621440 | tf_op jit(solution)/shard_map/all_gather | solution.py:376
  10.4 142.3 %all-gather.17.cloned.1.call-start = ((), (), s32[]{:S(2)}) async-start(), calls=%async_computation.16 | async-start | bytes 2621440 | tf_op jit(solution)/shard_map/all_gather | solution.py:369
  11.1 187.8 %all-gather.25.cloned.1.call-start = ((), (), s32[]{:S(2)}) async-start(), calls=%async_computation.27 | async-start | bytes 2621440 | tf_op jit(solution)/shard_map/all_gather | solution.py:400
  11.2 96.9 %copy-start.19 = (f32[1024]{0:T(1024)}, f32[1024]{0:T(1024)S(1)}, u32[]{:S(2)}) copy-start(f32[1024]{0:T(1024)S(1)} %convert_element_type.317) | copy-start | bytes 12292
  61.1 4.6 copy-start.25
  81.1 163.8 %all-gather.31.cloned.1.call-start = ((), (), s32[]{:S(2)}) async-start(), calls=%async_computation.30 | async-start | bytes 2621440 | tf_op jit(solution)/shard_map/all_gather | solution.py:400
  108.1 4.6 copy-start.27
  112.8 15.6 %copy-start.30 = (bf16[1024]{0:T(1024)(128)(2,1)S(1)}, bf16[1024]{0:T(1024)(128)(2,1)}, u32[]{:S(2)}) copy-start(bf16[1024]{0:T(1024)(128)(2,1)} %param.21) | copy-start | bytes 6148
  112.8 15.7 %copy-start.22 = (s32[2,1,256,2]{2,3,1,0:T(2,128)S(1)}, s32[2,1,256,2]{2,3,1,0:T(2,128)}, u32[]{:S(2)}) copy-start(s32[2,1,256,2]{2,3,1,0:T(2,128)} %param.16) | copy-start | bytes 12292
  245.0 5.5 copy-start.5
  250.4 2.6 copy-start.4
  258.4 65.3 %all-to-all-start.3 = ((bf16[8,320,1024]{2,1,0:T(8,128)(2,1)}), bf16[8,320,1024]{2,1,0:T(8,128)(2,1)}, u32[]{:S(2)}, u32[]{:S(2)}) async-start(bf16[8,320,1024]{2,1,0:T(8,128)(2,1)} %bitcast.268), calls=%async_computation.4 | async-start | bytes 10485760 | tf_op jit(solution)/shard_map/all_to_all | solution.py:382
  323.6 4.9 copy-start.6
  323.6 65.2 %all-to-all-start = ((bf16[8,320,1024]{2,1,0:T(8,128)(2,1)}), bf16[8,320,1024]{2,1,0:T(8,128)(2,1)}, u32[]{:S(2)}, u32[]{:S(2)}) async-start(bf16[8,320,1024]{2,1,0:T(8,128)(2,1)} %bitcast.266), calls=%async_computation | async-start | bytes 10485760 | tf_op jit(solution)/shard_map/all_to_all | solution.py:382
  328.5 47.8 %all-gather.27.cloned.1.call-start = ((), (), s32[]{:S(2)}) async-start(), calls=%async_computation.28 | async-start | bytes 2621440 | tf_op jit(solution)/shard_map/all_gather | solution.py:376
  388.8 65.0 %all-to-all-start.1 = ((bf16[8,320,1024]{2,1,0:T(8,128)(2,1)}), bf16[8,320,1024]{2,1,0:T(8,128)(2,1)}, u32[]{:S(2)}, u32[]{:S(2)}) async-start(bf16[8,320,1024]{2,1,0:T(8,128)(2,1)} %bitcast.267), calls=%async_computation.1 | async-start | bytes 10485760 | tf_op jit(solution)/shard_map/all_to_all | solution.py:382
  393.5 48.1 %all-gather.33.cloned.1.call-start = ((), (), s32[]{:S(2)}) async-start(), calls=%async_computation.31 | async-start | bytes 2621440 | tf_op jit(solution)/shard_map/all_gather | solution.py:376
  453.8 65.4 %all-to-all-start.4 = ((bf16[8,320,1024]{2,1,0:T(8,128)(2,1)}), bf16[8,320,1024]{2,1,0:T(8,128)(2,1)}, u32[]{:S(2)}, u32[]{:S(2)}) async-start(bf16[8,320,1024]{2,1,0:T(8,128)(2,1)} %bitcast.269), calls=%async_computation.5 | async-start | bytes 10485760 | tf_op jit(solution)/shard_map/all_to_all | solution.py:382
  519.2 65.0 %all-to-all-start.2 = ((bf16[8,320,1024]{2,1,0:T(8,128)(2,1)}), bf16[8,320,1024]{2,1,0:T(8,128)(2,1)}, u32[]{:S(2)}, u32[]{:S(2)}) async-start(bf16[8,320,1024]{2,1,0:T(8,128)(2,1)} %bitcast.277), calls=%async_computation.2 | async-start | bytes 10485760 | tf_op jit(solution)/shard_map/all_to_all | solution.py:382
  649.1 65.0 %all-to-all-start.7 = ((bf16[8,320,1024]{2,1,0:T(8,128)(2,1)}), bf16[8,320,1024]{2,1,0:T(8,128)(2,1)}, u32[]{:S(2)}, u32[]{:S(2)}) async-start(bf16[8,320,1024]{2,1,0:T(8,128)(2,1)} %bitcast.276), calls=%async_computation.11 | async-start | bytes 10485760 | tf_op jit(solution)/shard_map/all_to_all | solution.py:382
  653.8 132.5 %reduce-scatter.25.cloned.1.call-start = ((), (), s32[]{:S(2)}) async-start(), calls=%async_computation.32 | async-start | bytes 655360
  714.1 65.2 %all-to-all-start.6 = ((bf16[8,320,1024]{2,1,0:T(8,128)(2,1)}), bf16[8,320,1024]{2,1,0:T(8,128)(2,1)}, u32[]{:S(2)}, u32[]{:S(2)}) async-start(bf16[8,320,1024]{2,1,0:T(8,128)(2,1)} %bitcast.275), calls=%async_computation.8 | async-start | bytes 10485760 | tf_op jit(solution)/shard_map/all_to_all | solution.py:382
  719.0 68.3 %reduce-scatter.27.cloned.1.call-start = ((), (), s32[]{:S(2)}) async-start(), calls=%async_computation.33 | async-start | bytes 655360
  736.3 65.9 %reduce-scatter.21.cloned.1.call-start = ((), (), s32[]{:S(2)}) async-start(), calls=%async_computation.22 | async-start | bytes 2621440 | tf_op jit(solution)/shard_map/reduce_scatter | solution.py:379
  742.3 106.2 %reduce-scatter.17.cloned.1.call-start = ((), (), s32[]{:S(2)}) async-start(), calls=%async_computation.19 | async-start | bytes 2621440 | tf_op jit(solution)/shard_map/reduce_scatter | solution.py:379
  786.0 113.9 %all-gather.21.cloned.1.call-start = ((), (), s32[]{:S(2)}) async-start(), calls=%async_computation.23 | async-start | bytes 2621440 | tf_op jit(solution)/shard_map/all_gather | solution.py:376
  803.6 50.9 %copy-start.3 = (f32[256,1024]{1,0:T(8,128)}, f32[256,1024]{1,0:T(8,128)S(1)}, u32[]{:S(2)}) copy-start(f32[256,1024]{1,0:T(8,128)S(1)} %convolution_add_fusion) | copy-start | bytes 3145732
  850.9 3.6 copy-start.8
  851.0 48.9 %copy-start.18 = (bf16[256,1024]{1,0:T(8,128)(2,1)S(1)}, bf16[256,1024]{1,0:T(8,128)(2,1)}, u32[]{:S(2)}) copy-start(bf16[256,1024]{1,0:T(8,128)(2,1)} %param.18) | copy-start | bytes 1572868
  854.5 92.2 %all-gather.19.cloned.1.call-start = ((), (), s32[]{:S(2)}) async-start(), calls=%async_computation.20 | async-start | bytes 2621440 | tf_op jit(solution)/shard_map/all_gather | solution.py:376
  855.3 224.5 %all-reduce.7.cloned.1.call-start = ((), (), s32[]{:S(2)}) async-start(), calls=%async_computation.34 | async-start | bytes 4194304 | tf_op jit(solution)/shard_map/psum | solution.py:526
  949.9 31.5 %copy-start.9 = (bf16[1024,1024]{1,0:T(8,128)(2,1)S(1)}, bf16[1024,1024]{1,0:T(8,128)(2,1)}, u32[]{:S(2)}) copy-start(bf16[1024,1024]{1,0:T(8,128)(2,1)} %all-gather.19.cloned.1.call-done) | copy-start | bytes 6291460
  990.9 105.7 %reduce-scatter.23.cloned.1.call-start = ((), (), s32[]{:S(2)}) async-start(), calls=%async_computation.24 | async-start | bytes 2621440 | tf_op jit(solution)/shard_map/reduce_scatter | solution.py:379
  994.2 147.9 %reduce-scatter.19.cloned.1.call-start = ((), (), s32[]{:S(2)}) async-start(), calls=%async_computation.21 | async-start | bytes 2621440 | tf_op jit(solution)/shard_map/reduce_scatter | solution.py:379
  999.2 188.3 %reduce-scatter.13.cloned.1.call-start = ((), (), s32[]{:S(2)}) async-start(), calls=%async_computation.17 | async-start | bytes 2621440 | tf_op jit(solution)/shard_map/reduce_scatter | solution.py:379
  1005.2 227.7 %reduce-scatter.15.cloned.1.call-start = ((), (), s32[]{:S(2)}) async-start(), calls=%async_computation.18 | async-start | bytes 2621440 | tf_op jit(solution)/shard_map/reduce_scatter | solution.py:379
  1011.3 344.7 %all-reduce.5.cloned.1.call-start = ((), (), s32[]{:S(2)}) async-start(), calls=%async_computation.25 | async-start | bytes 131072 | tf_op jit(solution)/shard_map/psum | solution.py:530
  1055.2 9.6 copy-start.24
  1055.2 9.6 copy-start.33
  1055.2 9.6 copy-start.34
  1144.1 88.9 %copy-start.13 = (bf16[256,1024]{1,0:T(8,128)(2,1)S(1)}, bf16[256,1024]{1,0:T(8,128)(2,1)}, u32[]{:S(2)}) copy-start(bf16[256,1024]{1,0:T(8,128)(2,1)} %reduce-scatter.23.cloned.1.call-done) | copy-start | bytes 1572868
  1232.9 2.6 copy-start.15
  1232.9 3.6 copy-start.14
  (14 other events, 24.9 us)
Sparse Core Ops, SparseCore 0:
  10.2 48.7 all-gather.22
  61.1 44.8 all-gather.28
  107.6 45.0 all-gather.16
  154.1 44.6 all-gather.24
  200.3 44.6 all-gather.30
  331.1 45.0 all-gather.26
  396.5 45.0 all-gather.32
  673.4 20.5 reduce-scatter.24
  736.4 20.8 reduce-scatter.26
  760.0 42.1 reduce-scatter.20
  805.2 43.1 reduce-scatter.16
  854.6 45.2 all-gather.20
  902.1 44.6 all-gather.18
  991.0 60.3 all-reduce.6
  1053.5 43.0 reduce-scatter.22
  1098.9 43.1 reduce-scatter.18
  1144.2 43.1 reduce-scatter.12
  1189.7 43.1 reduce-scatter.14
  1239.1 116.8 all-reduce.4

commit v2 on v1

--- a/solution.py
+++ b/solution.py
@@ -208,11 +208,129 @@
     )(qkv, prob, grad_heads)
 
 
-def expert_kernel(x_ref, g_ref, wg_ref, wu_ref, wd_ref, y_ref, dx_ref, hid_ref, dga_ref, dup_ref):
+def spread(rows, place0, place1, count):
+    ids = lax.broadcasted_iota(jnp.int32, (count, rows.shape[0]), 0)
+    hit = (ids == place0) | (ids == place1)
+    return mm(jnp.where(hit, 1.0, 0.0).astype(BF16), rows)
+
+
+def spread_kernel(rows_ref, place_ref, out_ref):
+    experts, _, cap, width = out_ref.shape
+    placed = spread(rows_ref[...], place_ref[0:1, :], place_ref[1:2, :], experts * cap)
+    out_ref[...] = placed.astype(BF16).reshape(experts, 1, cap, width)
+
+
+def spread_rows(rows, place, experts, cap, shard_len):
+    slots, width = rows.shape
+    blocks = slots // shard_len
+    return pl.pallas_call(
+        spread_kernel,
+        grid=(blocks,),
+        out_shape=jax.ShapeDtypeStruct((experts, blocks, cap, width), BF16),
+        in_specs=[
+            pl.BlockSpec((shard_len, width), lambda b: (b, 0)),
+            pl.BlockSpec((2, shard_len), lambda b: (0, b)),
+        ],
+        out_specs=pl.BlockSpec((experts, 1, cap, width), lambda b: (0, b, 0, 0)),
+        compiler_params=pltpu.CompilerParams(vmem_limit_bytes=VMEM_LIMIT),
+        cost_estimate=pl.CostEstimate(
+            flops=2 * experts * cap * slots * width,
+            bytes_accessed=2 * slots * width + 2 * experts * blocks * cap * width,
+            transcendentals=0,
+        ),
+        name="spread_rows",
+    )(rows, place)
+
+
+def project_kernel(heads_ref, weight_ref, x_ref, gain_ref, place_ref, h1_ref, out_ref):
+    experts, _, cap, width = out_ref.shape
+    h1 = x_ref[...].astype(F32)
+    for group in range(heads_ref.shape[0]):
+        h1 = h1 + mm(heads_ref[group], weight_ref[group])
+    h1_ref[...] = h1
+    scale = lax.rsqrt(jnp.mean(h1 * h1, axis=-1, keepdims=True) + EPSILON)
+    tokens = (h1 * scale * gain_ref[...]).astype(BF16)
+    placed = spread(tokens, place_ref[0:1, :], place_ref[1:2, :], experts * cap)
+    out_ref[...] = placed.astype(BF16).reshape(experts, 1, cap, width)
+
+
+def project_and_spread(heads, weight, x, gain, place, experts, cap, shard_len):
+    slots, width = x.shape
+    blocks = slots // shard_len
+    groups, _, cols = heads.shape
+    return pl.pallas_call(
+        project_kernel,
+        grid=(blocks,),
+        out_shape=(
+            jax.ShapeDtypeStruct((slots, width), F32),
+            jax.ShapeDtypeStruct((experts, blocks, cap, width), BF16),
+        ),
+        in_specs=[
+            pl.BlockSpec((groups, shard_len, cols), lambda b: (0, b, 0)),
+            pl.BlockSpec((groups, cols, width), lambda b: (0, 0, 0)),
+            pl.BlockSpec((shard_len, width), lambda b: (b, 0)),
+            pl.BlockSpec((1, width), lambda b: (0, 0)),
+            pl.BlockSpec((2, shard_len), lambda b: (0, b)),
+        ],
+        out_specs=(
+            pl.BlockSpec((shard_len, width), lambda b: (b, 0)),
+            pl.BlockSpec((experts, 1, cap, width), lambda b: (0, b, 0, 0)),
+        ),
+        compiler_params=pltpu.CompilerParams(vmem_limit_bytes=VMEM_LIMIT),
+        cost_estimate=pl.CostEstimate(
+            flops=2 * slots * width * (width + experts * cap),
+            bytes_accessed=10 * slots * width + 2 * experts * blocks * cap * width,
+            transcendentals=0,
+        ),
+        name="project_and_spread",
+    )(heads, weight, x, gain.reshape(1, width), place)
+
+
+def collect_kernel(rows_ref, place_ref, out_ref):
+    experts, _, cap, width = rows_ref.shape
+    tokens = out_ref.shape[0]
+    ids = lax.broadcasted_iota(jnp.int32, (tokens, experts * cap), 1)
+    hit = (ids == place_ref[:, 0:1]) | (ids == place_ref[:, 1:2])
+    rows = rows_ref[...].reshape(experts * cap, width)
+    out_ref[...] = mm(jnp.where(hit, 1.0, 0.0).astype(BF16), rows).astype(BF16)
+
+
+def collect_rows(rows, place, shard_len):
+    experts, blocks, cap, width = rows.shape
+    slots = blocks * shard_len
+    return pl.pallas_call(
+        collect_kernel,
+        grid=(blocks,),
+        out_shape=jax.ShapeDtypeStruct((slots, width), BF16),
+        in_specs=[
+            pl.BlockSpec((experts, 1, cap, width), lambda b: (0, b, 0, 0)),
+            pl.BlockSpec((shard_len, 2), lambda b: (b, 0)),
+        ],
+        out_specs=pl.BlockSpec((shard_len, width), lambda b: (b, 0)),
+        compiler_params=pltpu.CompilerParams(vmem_limit_bytes=VMEM_LIMIT),
+        cost_estimate=pl.CostEstimate(
+            flops=2 * experts * cap * slots * width,
+            bytes_accessed=2 * slots * width + 2 * experts * blocks * cap * width,
+            transcendentals=0,
+        ),
+        name="collect_rows",
+    )(rows, place)
+
+
+def expert_kernel(
+    x_ref, dy_ref, pair_ref, wr_ref, wg_ref, wu_ref, wd_ref,
+    y_ref, dx_ref, g_ref, hid_ref, dga_ref, dup_ref, dlog_ref,
+):
     sources, _, cap, width = x_ref.shape
     rows = sources * cap
     x = x_ref[...].reshape(rows, width)
-    g = g_ref[...].reshape(rows, width)
+    dy = dy_ref[...].reshape(rows, width).astype(F32)
+    pair = pair_ref[...].reshape(rows, pair_ref.shape[3])
+    margin = jnp.sum(mm(x, wr_ref[...]) * pair, axis=-1, keepdims=True)
+    own_gate = 1.0 / (1.0 + jnp.exp(-margin))
+    other_gate = 1.0 / (1.0 + jnp.exp(margin))
+    g = (own_gate * dy).astype(BF16)
+    g_ref[0] = g
     gate = mm(x, wg_ref[0])
     up = mm(x, wu_ref[0])
     square = gate * gate
@@ -229,66 +347,92 @@
     hid_ref[0] = hid
     dga_ref[0] = dga
     dup_ref[0] = dup
-    y_ref[...] = mm(hid, wd_ref[0]).astype(BF16).reshape(sources, 1, cap, width)
-    dx = mm_nt(dga, wg_ref[0]) + mm_nt(dup, wu_ref[0])
+    y = mm(hid, wd_ref[0])
+    dgate = jnp.sum(y * dy, axis=-1, keepdims=True)
+    y_ref[...] = (y * own_gate).astype(BF16).reshape(sources, 1, cap, width)
+    dlog = (dgate * own_gate * other_gate * pair).astype(BF16)
+    dlog_ref[0] = dlog
+    dx = mm_nt(dga, wg_ref[0]) + mm_nt(dup, wu_ref[0]) + mm_nt(dlog, wr_ref[...])
     dx_ref[...] = dx.astype(BF16).reshape(sources, 1, cap, width)
 
 
-def expert_pass(x, g, wg, wu, wd):
+def expert_pass(x, dy, pair, wr, wg, wu, wd):
     sources, experts, cap, width = x.shape
     hidden = wg.shape[2]
+    choices = wr.shape[1]
     group = 2 if sources % 2 == 0 else 1
+    rows = sources * cap
     tokens = pl.BlockSpec((group, 1, cap, width), lambda e, s: (s, e, 0, 0))
     wide = pl.BlockSpec((1, width, hidden), lambda e, s: (e, 0, 0))
     tall = pl.BlockSpec((1, hidden, width), lambda e, s: (e, 0, 0))
-    acts = pl.BlockSpec((1, group * cap, hidden), lambda e, s: (e, s, 0))
-    rows = sources * cap
-    act_shape = jax.ShapeDtypeStruct((experts, rows, hidden), BF16)
+
+    def acts(cols):
+        return pl.BlockSpec((1, group * cap, cols), lambda e, s: (e, s, 0))
+
+    def act_shape(cols):
+        return jax.ShapeDtypeStruct((experts, rows, cols), BF16)
+
     return pl.pallas_call(
         expert_kernel,
         grid=(experts, sources // group),
         out_shape=(
             jax.ShapeDtypeStruct(x.shape, BF16),
             jax.ShapeDtypeStruct(x.shape, BF16),
-            act_shape,
-            act_shape,
-            act_shape,
-        ),
-        in_specs=[tokens, tokens, wide, wide, tall],
-        out_specs=(tokens, tokens, acts, acts, acts),
+            act_shape(width),
+            act_shape(hidden),
+            act_shape(hidden),
+            act_shape(hidden),
+            act_shape(choices),
+        ),
+        in_specs=[
+            tokens,
+            tokens,
+            pl.BlockSpec((group, 1, cap, choices), lambda e, s: (s, e, 0, 0)),
+            pl.BlockSpec((width, choices), lambda e, s: (0, 0)),
+            wide,
+            wide,
+            tall,
+        ],
+        out_specs=(
+            tokens, tokens, acts(width), acts(hidden), acts(hidden), acts(hidden), acts(choices)
+        ),
         compiler_params=pltpu.CompilerParams(vmem_limit_bytes=VMEM_LIMIT),
         cost_estimate=pl.CostEstimate(
             flops=12 * experts * rows * width * hidden,
-            bytes_accessed=8 * experts * rows * width + 6 * experts * hidden * (width + rows),
+            bytes_accessed=10 * experts * rows * width + 6 * experts * hidden * (width + rows),
             transcendentals=experts * rows * hidden,
         ),
         name="expert_pass",
-    )(x, g, wg, wu, wd)
+    )(x, dy, pair, wr, wg, wu, wd)
 
 
 def weight_kernel(*refs):
-    count = (len(refs) - 3) // 5
-    dwg_ref, dwu_ref, dwd_ref = refs[-3:]
-    totals = [0.0, 0.0, 0.0]
+    count = (len(refs) - 4) // 6
+    dwr_ref, dwg_ref, dwu_ref, dwd_ref = refs[-4:]
+    totals = [0.0, 0.0, 0.0, 0.0]
     for index in range(count):
-        x_ref, g_ref, hid_ref, dga_ref, dup_ref = refs[5 * index : 5 * index + 5]
+        x_ref, g_ref, hid_ref, dga_ref, dup_ref, dlog_ref = refs[6 * index : 6 * index + 6]
         sources, _, cap, width = x_ref.shape
         x = x_ref[...].reshape(sources * cap, width)
-        g = g_ref[...].reshape(sources * cap, width)
-        totals[0] = totals[0] + mm_tn(x, dga_ref[0])
-        totals[1] = totals[1] + mm_tn(x, dup_ref[0])
-        totals[2] = totals[2] + mm_tn(hid_ref[0], g)
-    dwg_ref[0] = totals[0]
-    dwu_ref[0] = totals[1]
-    dwd_ref[0] = totals[2]
+        totals[0] = totals[0] + mm_tn(x, dlog_ref[0])
+        totals[1] = totals[1] + mm_tn(x, dga_ref[0])
+        totals[2] = totals[2] + mm_tn(x, dup_ref[0])
+        totals[3] = totals[3] + mm_tn(hid_ref[0], g_ref[0])
+    dwr_ref[0] = totals[0]
+    dwg_ref[0] = totals[1]
+    dwu_ref[0] = totals[2]
+    dwd_ref[0] = totals[3]
 
 
 def weight_pass(kept):
     sources, experts, cap, width = kept[0][0].shape
     rows, hidden = kept[0][2].shape[1:]
+    choices = kept[0][5].shape[2]
     block = 256 if width % 256 == 0 else width
     tokens = pl.BlockSpec((sources, 1, cap, block), lambda e, j: (0, e, 0, j))
+    grads = pl.BlockSpec((1, rows, block), lambda e, j: (e, 0, j))
     acts = pl.BlockSpec((1, rows, hidden), lambda e, j: (e, 0, 0))
+    logs = pl.BlockSpec((1, rows, choices), lambda e, j: (e, 0, 0))
     operands = []
     for arrays in kept:
         operands.extend(arrays)
@@ -296,12 +440,14 @@
         weight_kernel,
         grid=(experts, width // block),
         out_shape=(
+            jax.ShapeDtypeStruct((experts, width, choices), F32),
             jax.ShapeDtypeStruct((experts, width, hidden), F32),
             jax.ShapeDtypeStruct((experts, width, hidden), F32),
             jax.ShapeDtypeStruct((experts, hidden, width), F32),
         ),
-        in_specs=[tokens, tokens, acts, acts, acts] * len(kept),
+        in_specs=[tokens, grads, acts, acts, acts, logs] * len(kept),
         out_specs=(
+            pl.BlockSpec((1, block, choices), lambda e, j: (e, j, 0)),
             pl.BlockSpec((1, block, hidden), lambda e, j: (e, j, 0)),
             pl.BlockSpec((1, block, hidden), lambda e, j: (e, j, 0)),
             pl.BlockSpec((1, hidden, block), lambda e, j: (e, 0, j)),
@@ -365,9 +511,10 @@
         jnp.arange(shard_len, dtype=jnp.int32)[:, None]
         < jnp.arange(shard_len, dtype=jnp.int32)[None, :]
     ).astype(BF16)
-    all_routes = lax.all_gather(routes[:, 0], "hidden", axis=1, tiled=True)
-    all_out_weight = lax.all_gather(out_weight, "hidden", axis=0, tiled=True)
-    all_out_weight = all_out_weight.reshape(blocks, head_cols, width)
+    expert_index = lax.axis_index("expert")
+    token_shape = (devices, experts_here, blocks * capacity, width)
+    flat_shape = (devices, experts_here * blocks * capacity, width)
+    place_shape = (expert_count, blocks, capacity, width)
 
     def own(values):
         return lax.dynamic_slice_in_dim(values, own_start, shard_len, 0)
@@ -381,110 +528,79 @@
     def exchange(buffer):
         return lax.all_to_all(buffer, "expert", split_axis=0, concat_axis=0, tiled=True)
 
-    def to_buffer(rows):
-        rows = rows.reshape(blocks, expert_count, capacity, width).transpose(1, 0, 2, 3)
-        return rows.reshape(devices, experts_here * blocks * capacity, width)
-
-    def from_buffer(buffer):
-        rows = buffer.reshape(expert_count, blocks, capacity, width).transpose(1, 0, 2, 3)
-        return rows.reshape(blocks, expert_count * capacity, width)
-
-    def attention(micro):
-        seg = segment_ids[micro, 0]
+    def placing():
+        route = lax.all_gather(routes[:, 0], "hidden", axis=1, tiled=True)
+        route = route.reshape(micro_count, blocks, shard_len, 2)
+        live = (segment_ids[:, 0] >= 0).reshape(micro_count, blocks, shard_len)
+        chosen = (route[..., None] == expert_ids).astype(F32)
+        chosen = chosen * live[..., None, None].astype(F32)
+        counted = jnp.sum(chosen, axis=3).astype(BF16)
+        before = jnp.einsum("mbte,tu->mbue", counted, earlier_than, preferred_element_type=F32)
+        position = jnp.sum(before[:, :, :, None, :] * chosen, axis=-1).astype(jnp.int32)
+        place = jnp.where(live[..., None], route * capacity + position, -1)
+        other = jnp.full((micro_count, blocks, expert_count * capacity), -1, jnp.int32)
+        for k in range(2):
+            hit = place[:, :, None, :, k] == place_ids[None, None, :, None]
+            found = jnp.max(jnp.where(hit, route[:, :, None, :, 1 - k], -1), axis=-1)
+            other = jnp.maximum(other, found)
+        other = other.reshape(micro_count, blocks, devices, experts_here, capacity)
+        other = exchange(other.transpose(2, 0, 3, 1, 4))
+        other = other.transpose(1, 0, 2, 3, 4)
+        other = other.reshape(micro_count, devices, experts_here, blocks * capacity)
+        me = expert_index * experts_here + jnp.arange(experts_here, dtype=jnp.int32)
+        plus = me[None, None, :, None, None] == expert_ids
+        minus = other[..., None] == expert_ids
+        pair = plus.astype(F32) - minus.astype(F32)
+        pair = jnp.where(other[..., None] >= 0, pair, 0.0).astype(BF16)
+        place = place.reshape(micro_count, slot_count, 2)
+        return place, place.transpose(0, 2, 1), pair
+
+    place_cols, place_rows, pairs = placing()
+    all_out_weight = lax.all_gather(out_weight, "hidden", axis=0, tiled=False)
+
+    def send_back(micro, kept):
+        dy = gather(cotangent[micro, 0])
+        sent = spread_rows(dy, place_rows[micro], expert_count, capacity, shard_len)
+        kept["dy"] = exchange(sent.reshape(flat_shape)).reshape(token_shape)
+
+    def attention(micro, kept):
         gathered = gather(x_in[micro, 0])
         x_now = gathered.astype(F32)
         r1 = lax.rsqrt(jnp.mean(x_now * x_now, axis=-1, keepdims=True) + EPSILON)
         xn1 = (x_now * r1 * attn_gain_f).astype(BF16)
         qkv = jnp.einsum("sd,tdf->tsf", xn1, qkv_weight, preferred_element_type=F32).astype(BF16)
-        prob, heads_out = attend(qkv, bias, seg, scale)
+        prob, heads_out = attend(qkv, bias, segment_ids[micro, 0], scale)
         all_heads = lax.all_gather(heads_out, "hidden", axis=0, tiled=False)
-        return dict(seg=seg, gathered=gathered, xn1=xn1, qkv=qkv, prob=prob, heads=heads_out, all_heads=all_heads)
-
-    def dispatch(micro, kept):
-        attn = jnp.einsum(
-            "hsf,hfd->sd", kept["all_heads"], all_out_weight, preferred_element_type=F32
+        kept.update(
+            gathered=gathered, r1=r1, xn1=xn1, qkv=qkv, prob=prob, heads=heads_out,
+            all_heads=all_heads,
         )
-        h1 = kept["gathered"].astype(F32) + attn
+
+    def send(micro, kept):
+        h1, sent = project_and_spread(
+            kept["all_heads"], all_out_weight, kept["gathered"], moe_gain_f, place_rows[micro],
+            expert_count, capacity, shard_len,
+        )
+        kept["h1"] = own(h1)
+        kept["x"] = exchange(sent.reshape(flat_shape)).reshape(token_shape)
+
+    def experts(micro, kept):
+        y, dx, g, hid, dga, dup, dlog = expert_pass(
+            kept["x"], kept["dy"], pairs[micro], router_weight, gate_weight, up_weight, down_weight
+        )
+        kept["weights"] = (kept["x"], g, hid, dga, dup, dlog)
+        kept["back_dx"] = exchange(dx.reshape(flat_shape)).reshape(place_shape)
+        kept["back_y"] = exchange(y.reshape(flat_shape)).reshape(place_shape)
+
+    def finish(micro, kept):
+        mixed = scatter(collect_rows(kept["back_y"], place_cols[micro], shard_len))
+        kept["block_out"] = (kept["h1"] + mixed.astype(F32)).astype(BF16)
+
+    def combine(micro, kept):
+        dxn2 = scatter(collect_rows(kept["back_dx"], place_cols[micro], shard_len)).astype(F32)
+        h1 = kept["h1"]
         r2 = lax.rsqrt(jnp.mean(h1 * h1, axis=-1, keepdims=True) + EPSILON)
-        xn2 = (h1 * r2 * moe_gain_f).astype(BF16)
-        logits = jnp.dot(xn2, router_weight, preferred_element_type=F32)
-        router = jax.nn.softmax(logits, axis=-1)
-        route = all_routes[micro]
-        live = kept["seg"] >= 0
-        live_f = live.astype(F32)
-        onehot = (route[:, :, None] == expert_ids).astype(F32)
-        picked = jnp.sum(router[:, None, :] * onehot, axis=-1)
-        total = jnp.sum(picked, axis=1, keepdims=True)
-        gates = picked / total * live_f[:, None]
-        chosen = (onehot * live_f[:, None, None]).reshape(blocks, shard_len, 2, expert_count)
-        counted = jnp.sum(chosen, axis=2).astype(BF16)
-        before = jnp.einsum("bte,tu->bue", counted, earlier_than, preferred_element_type=F32)
-        position = jnp.sum(before[:, :, None, :] * chosen, axis=-1).astype(jnp.int32)
-        route_b = route.reshape(blocks, shard_len, 2)
-        place = jnp.where(
-            live.reshape(blocks, shard_len)[:, :, None], route_b * capacity + position, -1
-        )
-        at_place = [place[:, None, :, k] == place_ids[None, :, None] for k in range(2)]
-        placed = (at_place[0] | at_place[1]).astype(BF16)
-        gates_b = gates.reshape(blocks, shard_len, 2)
-        gate_place = sum(
-            jnp.sum(jnp.where(at_place[k], gates_b[:, None, :, k], 0.0), axis=-1) for k in range(2)
-        )
-        xn2_b = xn2.reshape(blocks, shard_len, width)
-        sent = jnp.einsum("bst,btd->bsd", placed, xn2_b, preferred_element_type=F32).astype(BF16)
-        arrived = exchange(to_buffer(sent))
-        dy = gather(cotangent[micro, 0])
-        dy_b = dy.reshape(blocks, shard_len, width)
-        dy_place = jnp.einsum("bst,btd->bsd", placed, dy_b, preferred_element_type=F32)
-        sent_back = (dy_place * gate_place[:, :, None]).astype(BF16)
-        arrived_back = exchange(to_buffer(sent_back))
-        kept.update(
-            h1=own(h1), r2=own(r2), xn2=own(xn2), router=own(router), picked=own(picked),
-            total=own(total), onehot=own(onehot), live=own(live_f), placed=placed,
-            place=place, at_place=at_place, gate_place=gate_place, dy_place=dy_place.astype(BF16),
-            arrived=arrived, arrived_back=arrived_back,
-        )
-
-    def experts(micro, kept):
-        shape = (devices, experts_here, blocks * capacity, width)
-        x = kept["arrived"].reshape(shape)
-        g = kept["arrived_back"].reshape(shape)
-        y, dx, hid, dga, dup = expert_pass(x, g, gate_weight, up_weight, down_weight)
-        kept["weights"] = (x, g, hid, dga, dup)
-        kept["back_y"] = exchange(y.reshape(devices, -1, width))
-        kept["back_dx"] = exchange(dx.reshape(devices, -1, width))
-
-    def combine(micro, kept):
-        y = from_buffer(kept["back_y"])
-        y_f = y.astype(F32)
-        scaled = (y_f * kept["gate_place"][:, :, None]).astype(BF16)
-        mixed = jnp.einsum("bst,bsd->btd", kept["placed"], scaled, preferred_element_type=F32)
-        mixed = scatter(mixed.reshape(slot_count, width))
-        dgate_place = jnp.sum(y_f * kept["dy_place"].astype(F32), axis=-1)
-        dgates = jnp.stack(
-            [
-                jnp.sum(jnp.where(kept["at_place"][k], dgate_place[:, :, None], 0.0), axis=1)
-                for k in range(2)
-            ],
-            axis=-1,
-        )
-        dgates = lax.psum_scatter(
-            dgates.reshape(slot_count, 2), "hidden", scatter_dimension=0, tiled=True
-        )
-        dx = from_buffer(kept["back_dx"])
-        dxn2 = jnp.einsum("bst,bsd->btd", kept["placed"], dx, preferred_element_type=F32)
-        dxn2 = scatter(dxn2.reshape(slot_count, width)).astype(F32)
-        kept["block_out"] = (kept["h1"] + mixed.astype(F32)).astype(BF16)
-        picked, total, router = kept["picked"], kept["total"], kept["router"]
-        dgates = dgates * kept["live"][:, None]
-        dpicked = dgates / total - jnp.sum(dgates * picked, axis=1, keepdims=True) / (total * total)
-        drouter = jnp.sum(dpicked[:, :, None] * kept["onehot"], axis=1)
-        dlogits = router * (drouter - jnp.sum(router * drouter, axis=-1, keepdims=True))
-        dlogits = dlogits.astype(BF16)
-        kept["router_grad"] = mm_tn(kept["xn2"], dlogits)
-        dxn2 = dxn2 + mm_nt(dlogits, router_weight)
-        unit = kept["h1"] * kept["r2"]
-        part, kept["moe_gain_grad"] = norm_back(dxn2, unit, kept["r2"], moe_gain_f)
+        part, kept["moe_gain_grad"] = norm_back(dxn2, h1 * r2, r2, moe_gain_f)
         kept["dh1"] = cotangent[micro, 0].astype(F32) + part
         kept["dattn"] = gather(kept["dh1"].astype(BF16))
 
@@ -494,26 +610,29 @@
         dheads = mm_nt(dattn, out_weight).astype(BF16)
         dproj, bias_line = attend_back(kept["qkv"], kept["prob"], dheads, scale)
         kept["bias_line"] = bias_line
-        dxn1 = jnp.einsum("tsf,tdf->sd", dproj, qkv_weight, preferred_element_type=F32)
-        dxn1 = scatter(dxn1).astype(F32)
         kept["qkv_grad"] = jnp.einsum(
             "sd,tsf->tdf", kept["xn1"], dproj, preferred_element_type=F32
         )
+        dxn1 = jnp.einsum("tsf,tdf->sd", dproj, qkv_weight, preferred_element_type=F32)
+        unit = kept["gathered"].astype(F32) * kept["r1"]
+        kept["attn_gain_grad"] = jnp.sum(dxn1 * unit, axis=0)
+        dxn1 = scatter(dxn1).astype(F32)
         x_own = x_in[micro, 0].astype(F32)
         r1 = lax.rsqrt(jnp.mean(x_own * x_own, axis=-1, keepdims=True) + EPSILON)
-        part, kept["attn_gain_grad"] = norm_back(dxn1, x_own * r1, r1, attn_gain_f)
+        part, _ = norm_back(dxn1, x_own * r1, r1, attn_gain_f)
         kept["x_grad"] = (kept["dh1"] + part).astype(BF16)
 
-    states = []
+    states = [dict() for _ in range(micro_count)]
     for micro in range(micro_count):
-        states.append(attention(micro))
-    for micro in range(micro_count):
-        dispatch(micro, states[micro])
+        attention(micro, states[micro])
+        send_back(micro, states[micro])
+        send(micro, states[micro])
         experts(micro, states[micro])
     for micro in range(micro_count):
         combine(micro, states[micro])
         attention_back(micro, states[micro])
-    dwg, dwu, dwd = weight_pass([state["weights"] for state in states])
+        finish(micro, states[micro])
+    dwr, dwg, dwu, dwd = weight_pass([state["weights"] for state in states])
 
     def added(name):
         total = states[0][name]
@@ -521,14 +640,19 @@
             total = total + state[name]
         return total
 
+    def expert_sum(values):
+        shape, count = values.shape, values.size // devices
+        pieces = exchange(values.astype(BF16).reshape(devices, count // width, width))
+        piece = jnp.sum(pieces.astype(F32), axis=0).astype(BF16)
+        whole = lax.all_gather(piece, "expert", axis=0, tiled=True)
+        return whole.astype(F32).reshape(shape)
+
+    grad_qkv = expert_sum(added("qkv_grad"))
+    grad_out = expert_sum(added("out_grad"))
     grad_table = jnp.einsum("hj,jb->bh", added("bias_line"), onehot_bucket, precision=PRECISE)
-    grad_qkv, grad_out, grad_table = (
-        lax.psum(added("qkv_grad").astype(BF16), "expert").astype(F32),
-        lax.psum(added("out_grad").astype(BF16), "expert").astype(F32),
-        lax.psum(grad_table.astype(BF16), "expert").astype(F32),
-    )
+    grad_table = lax.psum(grad_table.astype(BF16), "expert").astype(F32)
     grad_router, grad_attn_gain, grad_moe_gain = lax.psum(
-        (added("router_grad"), added("attn_gain_grad"), added("moe_gain_grad")),
+        (jnp.sum(dwr, axis=0), added("attn_gain_grad"), added("moe_gain_grad")),
         ("expert", "hidden"),
     )
     return (

time: 1370 us -> 1190 us (0.87)
  waiting for transfers between devices: 760 us -> 647 us
  Pallas kernels: 206 us -> 268 us
  matrix products: 94.2 us -> 37.6 us
  blocking collectives: 131 us -> 80.7 us
  local copies, waits for them, and re-layouts: 76.9 us -> 45.2 us
  starting transfers between devices: 34.7 us -> 50.4 us
    psum x2 -> x1, waiting for transfers between devices: 78.7 us -> 1.59 us  [shards(): lax.psum((jnp.sum(dwr, axis=0), added('attn_gain_grad'), added('moe_gain_...]
    all_to_all x1 -> x0, blocking collectives: 64.8 us -> none  [exchange(): lax.all_to_all(buffer, 'expert', split_axis=0, concat_axis=0, tiled=True)]
    dot_general x12 -> x1, matrix products: 54 us -> 0.17 us  [placing(): jnp.einsum('mbte,tu->mbue', counted, earlier_than, preferred_element_type...]
    pallas_call x0 -> x8, Pallas kernels: none -> 51.3 us  [the longest x4 23.1 us: collect_rows(): pl.pallas_call(collect_kernel, grid=(blocks,), out_shape=jax.ShapeDtypeSt...]
    reduce_scatter x6, waiting for transfers between devices: 201 us -> 158 us  [scatter(): lax.psum_scatter(values.astype(BF16), 'hidden', scatter_dimension=0, tile...]
    all_gather x6, waiting for transfers between devices: 200 us -> 161 us  [gather(): return lax.all_gather(values, 'hidden', axis=0, tiled=True)]
    all_gather x1 -> x2, waiting for transfers between devices: 11.9 us -> 34.8 us  [the longest x1 34.8 us: shards(): all_out_weight = lax.all_gather(out_weight, 'hidden', axis=0, tiled=False)]
    all_to_all x7 -> x11, waiting for transfers between devices: 180 us -> 198 us  [exchange(): lax.all_to_all(buffer, 'expert', split_axis=0, concat_axis=0, tiled=True)]
  transfers between devices with their start and end apart: 26 -> 28, of which waited for: 23 -> 19; matrix products, arithmetic and copies ran while one was open for 13% -> 8% of each run, Pallas kernels for 13% -> 20%
where the time goes in v2:
time: 1190 us; the launch traced here: 1180 us
  waiting for transfers between devices  647 us (54%)
  Pallas kernels  268 us (23%)
  blocking collectives  80.7 us (7%)
  starting transfers between devices  50.4 us (4%)
  local copies, waits for them, and re-layouts  45.2 us (4%)
  other arithmetic  40 us (3%)
  matrix products  37.6 us (3%)
  between operations  15.2 us (1%)
    all_to_all x11, waiting for transfers between devices, exchange(): lax.all_to_all(buffer, 'expert', split_axis=0, concat_axis=0, tiled=True)  198 us
    all_gather x6, waiting for transfers between devices, gather(): return lax.all_gather(values, 'hidden', axis=0, tiled=True)  161 us
    reduce_scatter x6, waiting for transfers between devices, scatter(): lax.psum_scatter(values.astype(BF16), 'hidden', scatter_dimension=0, tile...  158 us
    all_gather x2, waiting for transfers between devices, attention(): all_heads = lax.all_gather(heads_out, 'hidden', axis=0, tiled=False)  90.9 us
    pallas_call x2, Pallas kernels, expert_pass(): pl.pallas_call(expert_kernel, grid=(experts, sources // group), out_shape...  71.5 us
    pallas_call x2, Pallas kernels, attend_back(): pl.pallas_call(functools.partial(attend_back_kernel, scale, min(128, half...  62.5 us
    all_to_all x11, starting transfers between devices, exchange(): lax.all_to_all(buffer, 'expert', split_axis=0, concat_axis=0, tiled=True)  49.3 us
    psum x1, blocking collectives, shards(): lax.psum((jnp.sum(dwr, axis=0), added('attn_gain_grad'), added('moe_gain_...  41.6 us
  transfers between devices with their start and end apart: 28, of which 19 were waited for; matrix products, arithmetic and copies ran while one was open for 8% of the time, Pallas kernels for 20%

profile of v2, /device:TPU:0, one launch (start us, length us, event | category | flops | bytes accessed | tf_op | source)
XLA Modules:
  0.0 1183.2 jit_solution(15203970475387664890)
XLA Ops:
  11.6 13.7 %all-gather.3 = s32[2,1,1024,2]{2,3,0,1:T(2,128)S(1)} all-gather(s32[2,1,256,2]{2,3,0,1:T(2,128)S(1)} %bitcast.214), channel_id=5, replica_groups=mesh['expert'=8,'hidden'=4] {'hidden'}, dimensions={2}, use_global_device_ids=true | all-gather | bytes 20480 | tf_op jit(solution)/shard_map/all_gather | solution.py:532
  33.3 25.6 %all-gather.31.cloned.1.call-done = bf16[1,1,1024,1024]{3,2,1,0:T(8,128)(2,1)} async-done(((bf16[1,1,256,1024]{3,2,1,0:T(8,128)(2,1)}), bf16[1,1,1024,1024]{3,2,1,0:T(8,128)(2,1)}) %all-gather.31.cloned.1.call-update) | async-done | bytes 2097168 | tf_op jit(solution)/shard_map/all_gather | solution.py:523
  58.9 5.3 spread_rows.2
  64.3 4.8 all-to-all-start.1
  70.2 13.0 %position_bias.1.bias_ref = bf16[4,512,512]{2,1,0:T(8,128)(2,1)} custom-call(f32[4,1,1024]{2,1,0:T(1,128)} %reshape.264.line_ref), custom_call_target="tpu_custom_call" | custom-call | tf_op jit(solution)/shard_map/position_bias/pallas_call | solution.py:69
  84.8 21.2 %all-gather.25.cloned.1.call-done = bf16[1,1,1024,1024]{3,2,1,0:T(8,128)(2,1)} async-done(((bf16[1,1,256,1024]{3,2,1,0:T(8,128)(2,1)}), bf16[1,1,1024,1024]{3,2,1,0:T(8,128)(2,1)}) %all-gather.25.cloned.1.call-update) | async-done | bytes 2097168 | tf_op jit(solution)/shard_map/all_gather | solution.py:523
  112.7 15.5 %attend.2 = (bf16[2,4,512,512]{3,2,1,0:T(8,128)(2,1)}, bf16[1024,256]{1,0:T(8,128)(2,1)}) custom-call(bf16[3,1024,256]{2,1,0:T(8,128)(2,1)} %fusion.12.qkv_ref, bf16[4,512,512]{2,1,0:T(8,128)(2,1)} %position_bias.1.bias_ref, s32[1,1024]{1,0:T(1,128)} %get-tuple-element.158.seg_row_ref, s32[1024,1]{1,0:T(8,128)} %copy.115.seg_col_ref), custom_call_target="tpu_custom_call" | custom-call | flops 536870912 | bytes 8388608 | tf_op jit(solution)/shard_map/attend/pallas_call | solution.py:105
  128.2 24.7 %all-gather.37.cloned.1.call-done = bf16[1,1,1024,1024]{3,2,1,0:T(8,128)(2,1)} async-done(((bf16[1,1,256,1024]{3,2,1,0:T(8,128)(2,1)}), bf16[1,1,1024,1024]{3,2,1,0:T(8,128)(2,1)}) %all-gather.37.cloned.1.call-update) | async-done | bytes 2097168 | tf_op jit(solution)/shard_map/all_gather | solution.py:523
  152.9 5.3 spread_rows.3
  158.2 4.8 all-to-all-start.5
  164.2 34.8 %all-gather.29.cloned.1.call-done = bf16[1024,1024]{1,0:T(8,128)(2,1)} async-done(((bf16[256,1024]{1,0:T(8,128)(2,1)}), bf16[1024,1024]{1,0:T(8,128)(2,1)}) %all-gather.29.cloned.1.call-update) | async-done | bytes 2097168 | tf_op jit(solution)/shard_map/all_gather | solution.py:559
  199.0 46.1 %all-gather.27.cloned.1.call-done = bf16[4096,256]{1,0:T(8,128)(2,1)} async-done(((bf16[1024,256]{1,0:T(8,128)(2,1)}), bf16[4096,256]{1,0:T(8,128)(2,1)}) %all-gather.27.cloned.1.call-update) | async-done | bytes 2097168 | tf_op jit(solution)/shard_map/all_gather | solution.py:573
  245.1 8.8 project_and_spread.2
  253.8 4.7 all-to-all-start
  259.6 32.1 %all-gather.33.cloned.1.call-done = bf16[1,1,1024,1024]{3,2,1,0:T(8,128)(2,1)} async-done(((bf16[1,1,256,1024]{3,2,1,0:T(8,128)(2,1)}), bf16[1,1,1024,1024]{3,2,1,0:T(8,128)(2,1)}) %all-gather.33.cloned.1.call-update) | async-done | bytes 2097168 | tf_op jit(solution)/shard_map/all_gather | solution.py:523
  298.4 15.3 %attend.3 = (bf16[2,4,512,512]{3,2,1,0:T(8,128)(2,1)}, bf16[1024,256]{1,0:T(8,128)(2,1)}) custom-call(bf16[3,1024,256]{2,1,0:T(8,128)(2,1)} %fusion.13.qkv_ref, bf16[4,512,512]{2,1,0:T(8,128)(2,1)} %position_bias.1.bias_ref, s32[1,1024]{1,0:T(1,128)} %get-tuple-element.159.seg_row_ref, s32[1024,1]{1,0:T(8,128)} %copy.127.seg_col_ref), custom_call_target="tpu_custom_call" | custom-call | flops 536870912 | bytes 8388608 | tf_op jit(solution)/shard_map/attend/pallas_call | solution.py:105
  313.8 44.8 %all-gather.35.cloned.1.call-done = bf16[4096,256]{1,0:T(8,128)(2,1)} async-done(((bf16[1024,256]{1,0:T(8,128)(2,1)}), bf16[4096,256]{1,0:T(8,128)(2,1)}) %all-gather.35.cloned.1.call-update) | async-done | bytes 2097168 | tf_op jit(solution)/shard_map/all_gather | solution.py:573
  358.6 8.8 project_and_spread.3
  367.3 5.1 all-to-all-start.4
  387.3 35.7 %expert_pass.2 = (bf16[8,2,160,1024]{3,2,1,0:T(8,128)(2,1)}, bf16[8,2,160,1024]{3,2,1,0:T(8,128)(2,1)}, bf16[2,1280,1024]{2,1,0:T(8,128)(2,1)}, bf16[2,1280,704]...) custom-call(bf16[8,2,160,1024]{3,2,1,0:T(8,128)(2,1)} %bitcast.19.x_, ...), custom_call_target="tpu_custom_call" | custom-call | flops 22145925120 | bytes 45678592 | tf_op jit(solution)/shard_map/expert_pass/pallas_call | solution.py:375
  423.1 9.7 all-to-all-done.4
  432.8 4.7 all-to-all-start.7
  437.5 35.7 %expert_pass.3 = (bf16[8,2,160,1024]{3,2,1,0:T(8,128)(2,1)}, bf16[8,2,160,1024]{3,2,1,0:T(8,128)(2,1)}, bf16[2,1280,1024]{2,1,0:T(8,128)(2,1)}, bf16[2,1280,704]...) custom-call(bf16[8,2,160,1024]{3,2,1,0:T(8,128)(2,1)} %bitcast.41.x_, ...), custom_call_target="tpu_custom_call" | custom-call | flops 22145925120 | bytes 45678592 | tf_op jit(solution)/shard_map/expert_pass/pallas_call | solution.py:375
  473.2 24.6 %all-to-all-done.7 = bf16[8,320,1024]{2,1,0:T(8,128)(2,1)} async-done(((bf16[8,320,1024]{2,1,0:T(8,128)(2,1)}), bf16[8,320,1024]{2,1,0:T(8,128)(2,1)}, u32[]{:S(2)}, u32[]{:S(2)}) %all-to-all-start.7) | async-done | bytes 5242912 | tf_op jit(solution)/shard_map/all_to_all | solution.py:529
  503.6 5.7 collect_rows.6
  510.4 52.5 %all-to-all-done.8 = bf16[8,320,1024]{2,1,0:T(8,128)(2,1)} async-done(((bf16[8,320,1024]{2,1,0:T(8,128)(2,1)}), bf16[8,320,1024]{2,1,0:T(8,128)(2,1)}, u32[]{:S(2)}, u32[]{:S(2)}) %all-to-all-start.8) | async-done | bytes 5242912 | tf_op jit(solution)/shard_map/all_to_all | solution.py:529
  562.8 5.7 collect_rows.7
  571.5 38.0 %reduce-scatter.15.cloned.1.call-done = bf16[256,1024]{1,0:T(8,128)(2,1)} async-done(((bf16[1024,1024]{1,0:T(8,128)(2,1)}), bf16[256,1024]{1,0:T(8,128)(2,1)}) %reduce-scatter.15.cloned.1.call-update) | async-done | bytes 524304 | tf_op jit(solution)/shard_map/reduce_scatter | solution.py:526
  616.0 44.7 %all-gather.21.cloned.1.call-done = bf16[1024,1024]{1,0:T(8,128)(2,1)} async-done(((bf16[256,1024]{1,0:T(8,128)(2,1)}), bf16[1024,1024]{1,0:T(8,128)(2,1)}) %all-gather.21.cloned.1.call-update) | async-done | bytes 2097168 | tf_op jit(solution)/shard_map/all_gather | solution.py:523
  663.9 31.1 %attend_back.3 = (bf16[3,1024,256]{2,1,0:T(8,128)(2,1)}, f32[4,1024]{1,0:T(4,128)}) custom-call(bf16[3,1024,256]{2,1,0:T(8,128)(2,1)} %fusion.13.qkv_ref, bf16[2,4,512,512]{3,2,1,0:T(8,128)(2,1)} %get-tuple-element.53.prob_ref, bf16[1024,256]{1,0:T(8,128)(2,1)} %convolution_convert_fusion.2.grad_ref), custom_call_target="tpu_custom_call" | custom-call | flops 1073741824 | bytes 7864320 | tf_op jit(solution)/shard_map/attend_back/pallas_call | solution.py:181
  695.0 12.4 %all-gather.19.cloned.1.call-done = bf16[1024,1024]{1,0:T(8,128)(2,1)} async-done(((bf16[256,1024]{1,0:T(8,128)(2,1)}), bf16[1024,1024]{1,0:T(8,128)(2,1)}) %all-gather.19.cloned.1.call-update) | async-done | bytes 2097168 | tf_op jit(solution)/shard_map/all_gather | solution.py:523
  710.6 31.4 %attend_back.2 = (bf16[3,1024,256]{2,1,0:T(8,128)(2,1)}, f32[4,1024]{1,0:T(4,128)}) custom-call(bf16[3,1024,256]{2,1,0:T(8,128)(2,1)} %fusion.12.qkv_ref, bf16[2,4,512,512]{3,2,1,0:T(8,128)(2,1)} %get-tuple-element.50.prob_ref, bf16[1024,256]{1,0:T(8,128)(2,1)} %convolution_convert_fusion.3.grad_ref), custom_call_target="tpu_custom_call" | custom-call | flops 1073741824 | bytes 7864320 | tf_op jit(solution)/shard_map/attend_back/pallas_call | solution.py:181
  756.6 38.5 %weight_pass.1 = (f32[2,1024,16]{2,1,0:T(8,128)}, f32[2,1024,704]{2,1,0:T(8,128)}, f32[2,1024,704]{2,1,0:T(8,128)}, f32[2,704,1024]{2,1,0:T(8,128)}) custom-call(bf16[8,2,160,1024]{3,2,1,0:T(8,128)(2,1)} %bitcast.19.x_ref.refs_0_, bf16[2,1280,1024]{2,1,0:T(8,128)(2,1)} %get-tuple-element.57.refs_1_, bf16[2,1280,704]{2,1,0:T(8,128)(2,1)} %get-tuple-element.58.refs_2_, ...), custom_call_target="tpu_custom_call" | custom-call | flops 22145925120 | bytes 59899904 | tf_op jit(solution)/shard_map/weight_pass/pallas_call | solution.py:439
  798.4 5.9 bitcast_convert_fusion
  804.3 4.8 all-to-all-start.6
  813.7 56.6 %all-to-all-done.6 = bf16[8,320,1024]{2,1,0:T(8,128)(2,1)} async-done(((bf16[8,320,1024]{2,1,0:T(8,128)(2,1)}), bf16[8,320,1024]{2,1,0:T(8,128)(2,1)}, u32[]{:S(2)}, u32[]{:S(2)}) %all-to-all-start.6) | async-done | bytes 5242912 | tf_op jit(solution)/shard_map/all_to_all | solution.py:529
  870.3 4.7 all-to-all-start.3
  875.1 5.7 collect_rows.5
  880.8 55.0 %all-to-all-done.3 = bf16[8,320,1024]{2,1,0:T(8,128)(2,1)} async-done(((bf16[8,320,1024]{2,1,0:T(8,128)(2,1)}), bf16[8,320,1024]{2,1,0:T(8,128)(2,1)}, u32[]{:S(2)}, u32[]{:S(2)}) %all-to-all-start.3) | async-done | bytes 5242912 | tf_op jit(solution)/shard_map/all_to_all | solution.py:529
  935.9 6.0 collect_rows.4
  942.2 6.4 copy.138
  948.6 6.4 copy.139
  970.0 14.6 %psum.28 = bf16[32,4]{0,1:T(4,128)(2,1)S(1)} all-reduce(bf16[32,4]{0,1:T(4,128)(2,1)S(1)} %convolution_convert_fusion.4), channel_id=1, replica_groups=mesh['expert'=8,'hidden'=4] {'expert'}, use_global_device_ids=true, to_apply=%region_22.23 | all-reduce | flops 128 | bytes 512 | tf_op jit(solution)/shard_map/psum | solution.py:653
  988.7 41.6 %all-reduce = (f32[1024]{0:T(1024)}, f32[1024]{0:T(1024)}) all-reduce(f32[1024]{0:T(1024)S(1)} %add.217, f32[1024]{0:T(1024)S(1)} %add.218), channel_id=1, replica_groups=mesh['expert'=8,'hidden'=4] {'expert','hidden'}, use_global_device_ids=true, to_apply=%region_25.26 | all-reduce | flops 2048 | bytes 16384 | tf_op jit(solution)/shard_map/psum | solution.py:654
  1030.4 10.9 all_gather.59
  1046.5 34.4 %reduce-scatter.13.cloned.1.call-done = bf16[256,1024]{1,0:T(8,128)(2,1)} async-done(((bf16[1024,1024]{1,0:T(8,128)(2,1)}), bf16[256,1024]{1,0:T(8,128)(2,1)}) %reduce-scatter.13.cloned.1.call-update) | async-done | bytes 524304 | tf_op jit(solution)/shard_map/reduce_scatter | solution.py:526
  1082.6 43.7 %reduce-scatter.9.cloned.1.call-done = bf16[256,1024]{1,0:T(8,128)(2,1)} async-done(((bf16[1024,1024]{1,0:T(8,128)(2,1)}), bf16[256,1024]{1,0:T(8,128)(2,1)}) %reduce-scatter.9.cloned.1.call-update) | async-done | bytes 524304 | tf_op jit(solution)/shard_map/reduce_scatter | solution.py:526
  1129.7 42.0 %reduce-scatter.7.cloned.1.call-done = bf16[256,1024]{1,0:T(8,128)(2,1)} async-done(((bf16[1024,1024]{1,0:T(8,128)(2,1)}), bf16[256,1024]{1,0:T(8,128)(2,1)}) %reduce-scatter.7.cloned.1.call-update) | async-done | bytes 524304 | tf_op jit(solution)/shard_map/reduce_scatter | solution.py:526
  (199 shorter events, 124.7 us)
Async XLA Ops:
  7.2 100.9 %copy-start = (bf16[3,1024,256]{2,1,0:T(8,128)(2,1)S(1)}, bf16[3,1024,256]{2,1,0:T(8,128)(2,1)}, u32[]{:S(2)}) copy-start(bf16[3,1024,256]{2,1,0:T(8,128)(2,1)} %param.17) | copy-start | bytes 4718596
  7.2 4.3 copy-start.17
  7.2 4.4 copy-start.18
  7.2 51.7 %all-gather.31.cloned.1.call-start = ((), (), s32[]{:S(2)}) async-start(), calls=%async_computation.30 | async-start | bytes 2621440 | tf_op jit(solution)/shard_map/all_gather | solution.py:523
  9.7 96.3 %all-gather.25.cloned.1.call-start = ((), (), s32[]{:S(2)}) async-start(), calls=%async_computation.27 | async-start | bytes 2621440 | tf_op jit(solution)/shard_map/all_gather | solution.py:523
  10.8 142.1 %all-gather.37.cloned.1.call-start = ((), (), s32[]{:S(2)}) async-start(), calls=%async_computation.33 | async-start | bytes 2621440 | tf_op jit(solution)/shard_map/all_gather | solution.py:523
  28.4 35.9 %all-to-all-start.2 = ((s32[8,1,640]{2,1,0:T(1,128)}), s32[8,1,640]{2,1,0:T(1,128)S(1)}, u32[]{:S(2)}, u32[]{:S(2)}) async-start(s32[8,1,640]{2,1,0:T(1,128)} %reshape.309), calls=%async_computation.2 | async-start | bytes 40960 | tf_op jit(solution)/shard_map/all_to_all | solution.py:529
  32.1 166.8 %all-gather.29.cloned.1.call-start = ((), (), s32[]{:S(2)}) async-start(), calls=%async_computation.29 | async-start | bytes 2621440 | tf_op jit(solution)/shard_map/all_gather | solution.py:559
  64.2 4.9 copy-start.21
  64.2 4.9 copy-start.27
  64.3 93.9 %all-to-all-start.1 = ((bf16[8,320,1024]{2,1,0:T(8,128)(2,1)}), bf16[8,320,1024]{2,1,0:T(8,128)(2,1)}, u32[]{:S(2)}, u32[]{:S(2)}) async-start(bf16[8,320,1024]{2,1,0:T(8,128)(2,1)} %bitcast.188), calls=%async_computation.1 | async-start | bytes 10485760 | tf_op jit(solution)/shard_map/all_to_all | solution.py:529
  69.1 176.0 %all-gather.27.cloned.1.call-start = ((), (), s32[]{:S(2)}) async-start(), calls=%async_computation.28 | async-start | bytes 2621440 | tf_op jit(solution)/shard_map/all_gather | solution.py:573
  69.2 43.5 %copy-start.19 = (s32[1024]{0:T(1024)}, s32[1024]{0:T(1024)S(1)}, u32[]{:S(2)}) copy-start(s32[1024]{0:T(1024)S(1)} %fusion.62) | copy-start | bytes 12292
  158.2 5.4 copy-start.22
  158.2 95.6 %all-to-all-start.5 = ((bf16[8,320,1024]{2,1,0:T(8,128)(2,1)}), bf16[8,320,1024]{2,1,0:T(8,128)(2,1)}, u32[]{:S(2)}, u32[]{:S(2)}) async-start(bf16[8,320,1024]{2,1,0:T(8,128)(2,1)} %bitcast.189), calls=%async_computation.6 | async-start | bytes 10485760 | tf_op jit(solution)/shard_map/all_to_all | solution.py:529
  163.0 128.7 %all-gather.33.cloned.1.call-start = ((), (), s32[]{:S(2)}) async-start(), calls=%async_computation.31 | async-start | bytes 2621440 | tf_op jit(solution)/shard_map/all_gather | solution.py:523
  253.8 113.5 %all-to-all-start = ((bf16[8,320,1024]{2,1,0:T(8,128)(2,1)}), bf16[8,320,1024]{2,1,0:T(8,128)(2,1)}, u32[]{:S(2)}, u32[]{:S(2)}) async-start(bf16[8,320,1024]{2,1,0:T(8,128)(2,1)} %bitcast.195), calls=%async_computation | async-start | bytes 10485760 | tf_op jit(solution)/shard_map/all_to_all | solution.py:529
  258.5 100.0 %all-gather.35.cloned.1.call-start = ((), (), s32[]{:S(2)}) async-start(), calls=%async_computation.32 | async-start | bytes 2621440 | tf_op jit(solution)/shard_map/all_gather | solution.py:573
  367.3 5.1 copy-start.16
  367.3 65.4 %all-to-all-start.4 = ((bf16[8,320,1024]{2,1,0:T(8,128)(2,1)}), bf16[8,320,1024]{2,1,0:T(8,128)(2,1)}, u32[]{:S(2)}, u32[]{:S(2)}) async-start(bf16[8,320,1024]{2,1,0:T(8,128)(2,1)} %bitcast.194), calls=%async_computation.5 | async-start | bytes 10485760 | tf_op jit(solution)/shard_map/all_to_all | solution.py:529
  432.8 65.0 %all-to-all-start.7 = ((bf16[8,320,1024]{2,1,0:T(8,128)(2,1)}), bf16[8,320,1024]{2,1,0:T(8,128)(2,1)}, u32[]{:S(2)}, u32[]{:S(2)}) async-start(bf16[8,320,1024]{2,1,0:T(8,128)(2,1)} %bitcast.197), calls=%async_computation.9 | async-start | bytes 10485760 | tf_op jit(solution)/shard_map/all_to_all | solution.py:529
  497.8 65.0 %all-to-all-start.8 = ((bf16[8,320,1024]{2,1,0:T(8,128)(2,1)}), bf16[8,320,1024]{2,1,0:T(8,128)(2,1)}, u32[]{:S(2)}, u32[]{:S(2)}) async-start(bf16[8,320,1024]{2,1,0:T(8,128)(2,1)} %bitcast.196), calls=%async_computation.12 | async-start | bytes 10485760 | tf_op jit(solution)/shard_map/all_to_all | solution.py:529
  502.5 69.0 %reduce-scatter.11.cloned.1.call-start = ((), (), s32[]{:S(2)}) async-start(), calls=%async_computation.19 | async-start | bytes 2621440 | tf_op jit(solution)/shard_map/reduce_scatter | solution.py:526
  509.3 100.2 %reduce-scatter.15.cloned.1.call-start = ((), (), s32[]{:S(2)}) async-start(), calls=%async_computation.22 | async-start | bytes 2621440 | tf_op jit(solution)/shard_map/reduce_scatter | solution.py:526
  568.5 41.0 %copy-start.15 = (f32[1024]{0:T(1024)S(1)}, f32[1024]{0:T(1024)}, u32[]{:S(2)}) copy-start(f32[1024]{0:T(1024)} %convert_element_type.225) | copy-start | bytes 12292
  568.5 43.5 %copy-start.3 = (bf16[2,1,256,1024]{3,2,1,0:T(8,128)(2,1)S(1)}, bf16[2,1,256,1024]{3,2,1,0:T(8,128)(2,1)}, u32[]{:S(2)}) copy-start(bf16[2,1,256,1024]{3,2,1,0:T(8,128)(2,1)} %param.14) | copy-start | bytes 3145732
  568.5 92.2 %all-gather.21.cloned.1.call-start = ((), (), s32[]{:S(2)}) async-start(), calls=%async_computation.23 | async-start | bytes 2621440 | tf_op jit(solution)/shard_map/all_gather | solution.py:523
  571.5 40.6 %copy-start.6 = (bf16[256,1024]{1,0:T(8,128)(2,1)S(1)}, bf16[256,1024]{1,0:T(8,128)(2,1)}, u32[]{:S(2)}) copy-start(bf16[256,1024]{1,0:T(8,128)(2,1)} %reduce-scatter.11.cloned.1.call-done) | copy-start | bytes 1572868
  615.3 92.1 %all-gather.19.cloned.1.call-start = ((), (), s32[]{:S(2)}) async-start(), calls=%async_computation.20 | async-start | bytes 2621440 | tf_op jit(solution)/shard_map/all_gather | solution.py:523
  663.9 43.5 %copy-start.14 = (bf16[256,1024]{1,0:T(8,128)(2,1)S(1)}, bf16[256,1024]{1,0:T(8,128)(2,1)}, u32[]{:S(2)}) copy-start(bf16[256,1024]{1,0:T(8,128)(2,1)} %param.18) | copy-start | bytes 1572868
  710.6 31.4 %copy-start.4 = (bf16[1,1,1024,1024]{3,2,1,0:T(8,128)(2,1)S(1)}, bf16[1,1,1024,1024]{3,2,1,0:T(8,128)(2,1)}, u32[]{:S(2)}) copy-start(bf16[1,1,1024,1024]{3,2,1,0:T(8,128)(2,1)} %all-gather.25.cloned.1.call-done) | copy-start | bytes 6291460
  742.0 3.5 copy-start.5
  742.0 3.5 copy-start.24
  752.8 44.5 %all-to-all-start.9 = ((bf16[8,96,1024]{2,1,0:T(8,128)(2,1)}), bf16[8,96,1024]{2,1,0:T(8,128)(2,1)S(1)}, u32[]{:S(2)}, u32[]{:S(2)}) async-start(bf16[8,96,1024]{2,1,0:T(8,128)(2,1)} %reshape.282), calls=%async_computation.15 | async-start | bytes 3145728 | tf_op jit(solution)/shard_map/all_to_all | solution.py:529
  756.5 200.1 %all-reduce.3.cloned.1.call-start = ((), (), s32[]{:S(2)}) async-start(), calls=%async_computation.26 | async-start | bytes 1048576 | tf_op jit(solution)/shard_map/psum | solution.py:654
  797.3 245.1 %all-gather.23.cloned.1.call-start = ((), (), s32[]{:S(2)}) async-start(), calls=%async_computation.25 | async-start | bytes 1769472 | tf_op jit(solution)/shard_map/all_gather | solution.py:647
  798.3 248.2 %reduce-scatter.17.cloned.1.call-start = ((), (), s32[]{:S(2)}) async-start(), calls=%async_computation.24 | async-start | bytes 2621440 | tf_op jit(solution)/shard_map/reduce_scatter | solution.py:526
  804.3 4.9 copy-start.23
  804.3 66.0 %all-to-all-start.6 = ((bf16[8,320,1024]{2,1,0:T(8,128)(2,1)}), bf16[8,320,1024]{2,1,0:T(8,128)(2,1)}, u32[]{:S(2)}, u32[]{:S(2)}) async-start(bf16[8,320,1024]{2,1,0:T(8,128)(2,1)} %bitcast.193), calls=%async_computation.7 | async-start | bytes 10485760 | tf_op jit(solution)/shard_map/all_to_all | solution.py:529
  809.1 271.7 %reduce-scatter.13.cloned.1.call-start = ((), (), s32[]{:S(2)}) async-start(), calls=%async_computation.21 | async-start | bytes 2621440 | tf_op jit(solution)/shard_map/reduce_scatter | solution.py:526
  870.3 65.5 %all-to-all-start.3 = ((bf16[8,320,1024]{2,1,0:T(8,128)(2,1)}), bf16[8,320,1024]{2,1,0:T(8,128)(2,1)}, u32[]{:S(2)}, u32[]{:S(2)}) async-start(bf16[8,320,1024]{2,1,0:T(8,128)(2,1)} %bitcast.192), calls=%async_computation.3 | async-start | bytes 10485760 | tf_op jit(solution)/shard_map/all_to_all | solution.py:529
  875.0 251.3 %reduce-scatter.9.cloned.1.call-start = ((), (), s32[]{:S(2)}) async-start(), calls=%async_computation.18 | async-start | bytes 2621440 | tf_op jit(solution)/shard_map/reduce_scatter | solution.py:526
  880.8 290.9 %reduce-scatter.7.cloned.1.call-start = ((), (), s32[]{:S(2)}) async-start(), calls=%async_computation.17 | async-start | bytes 2621440 | tf_op jit(solution)/shard_map/reduce_scatter | solution.py:526
  935.9 6.1 copy-start.2
  948.6 9.9 copy-start.9
  962.5 67.8 %all-to-all-start.10 = ((bf16[8,32,1024]{2,1,0:T(8,128)(2,1)}), bf16[8,32,1024]{2,1,0:T(8,128)(2,1)S(1)}, u32[]{:S(2)}, u32[]{:S(2)}) async-start(bf16[8,32,1024]{2,1,0:T(8,128)(2,1)} %bitcast.204), calls=%async_computation.16 | async-start | bytes 1048576 | tf_op jit(solution)/shard_map/all_to_all | solution.py:529
  966.1 3.5 copy-start.25
  1082.6 89.1 %copy-start.7 = (bf16[256,1024]{1,0:T(8,128)(2,1)S(1)}, bf16[256,1024]{1,0:T(8,128)(2,1)}, u32[]{:S(2)}) copy-start(bf16[256,1024]{1,0:T(8,128)(2,1)} %reduce-scatter.11.cloned.1.call-done) | copy-start | bytes 1572868
  (8 other events, 23.2 us)
Sparse Core Ops, SparseCore 0:
  10.2 48.6 all-gather.30
  61.1 44.9 all-gather.24
  108.2 44.6 all-gather.36
  154.3 44.6 all-gather.28
  200.4 44.6 all-gather.26
  247.1 44.6 all-gather.32
  313.9 44.6 all-gather.34
  509.4 42.9 reduce-scatter.10
  568.7 40.7 reduce-scatter.14
  615.4 45.2 all-gather.20
  662.9 44.5 all-gather.18
  797.4 159.1 all-reduce.2
  958.7 29.6 all-gather.22
  990.6 44.7 reduce-scatter.16
  1037.6 43.2 reduce-scatter.12
  1083.1 43.1 reduce-scatter.8
  1128.4 43.1 reduce-scatter.6

commit v3 on v2

v3 whole, which is shorter than its diff:
```python
import functools

import jax
import jax.numpy as jnp
from jax import lax
from jax.experimental import pallas as pl
from jax.experimental.pallas import tpu as pltpu
from jax.sharding import PartitionSpec as P

EPSILON = 1e-06
PRECISE = lax.Precision.HIGHEST
LIMITS = (12, 16, 23, 32, 46, 64, 91)
MASKED = -1000000000.0
GELU_C = 0.7978845608028654
GELU_A = 0.044715
VMEM_LIMIT = 60 * 1024 * 1024
F32 = jnp.float32
BF16 = jnp.bfloat16


def mm(a, b):
    return lax.dot_general(a, b, (((1,), (0,)), ((), ())), preferred_element_type=F32)


def mm_nt(a, b):
    return lax.dot_general(a, b, (((1,), (1,)), ((), ())), preferred_element_type=F32)


def mm_tn(a, b):
    return lax.dot_general(a, b, (((0,), (0,)), ((), ())), preferred_element_type=F32)


def bucket_of(distance):
    magnitude = jnp.abs(distance)
    far_bucket = jnp.full(magnitude.shape, 8, jnp.int32)
    for threshold in LIMITS:
        far_bucket = far_bucket + (magnitude >= threshold).astype(jnp.int32)
    return jnp.where(magnitude < 8, magnitude, far_bucket) + 16 * (distance > 0).astype(jnp.int32)


def bucket_onehot(half, bucket_count):
    lane = jnp.arange(2 * half, dtype=jnp.int32)
    distance = jnp.where(lane < half, lane, lane - 2 * half)
    return (
        bucket_of(distance)[:, None] == jnp.arange(bucket_count, dtype=jnp.int32)[None, :]
    ).astype(F32)


TILE = 128


def bias_kernel(line_ref, out_ref):
    length = out_ref.shape[2]
    line = jnp.broadcast_to(line_ref[0], (8, length))
    row = lax.broadcasted_iota(jnp.int32, (8, length), 0)
    sheet = line
    for r in range(1, 8):
        sheet = jnp.where(row == r, pltpu.roll(line, r, 1), sheet)
    while sheet.shape[0] < TILE:
        sheet = jnp.concatenate([sheet, pltpu.roll(sheet, sheet.shape[0], 1)], axis=0)
    out_ref[0] = sheet.astype(out_ref.dtype)


def position_bias(line):
    heads, length = line.shape
    return pl.pallas_call(
        bias_kernel,
        grid=(heads,),
        out_shape=jax.ShapeDtypeStruct((heads, TILE, length), BF16),
        in_specs=[pl.BlockSpec((1, 1, length), lambda h: (h, 0, 0))],
        out_specs=pl.BlockSpec((1, TILE, length), lambda h: (h, 0, 0)),
        compiler_params=pltpu.CompilerParams(vmem_limit_bytes=VMEM_LIMIT),
        name="position_bias",
    )(line.reshape(heads, 1, length))


def unit_rows(x):
    x = x.astype(F32)
    return x * lax.rsqrt(jnp.mean(x * x, axis=-1, keepdims=True) + EPSILON)


def attend_kernel(
    scale, x_ref, gain_ref, own_ref, other_ref, bias_ref, seg_row_ref, seg_col_ref,
    qkv_ref, prob_ref, out_ref, xn_ref,
):
    heads, length = bias_ref.shape[0], bias_ref.shape[2]
    half = x_ref.shape[0]
    size = out_ref.shape[1] // heads
    group = pl.program_id(0)

    @pl.when(group == 0)
    def _():
        xn_ref[...] = (unit_rows(x_ref[...]) * gain_ref[...]).astype(BF16)
        for t in range(3):
            qkv_ref[0, t] = mm(xn_ref[...], own_ref[t]).astype(BF16)

    @pl.when(group > 0)
    def _():
        for t in range(3):
            qkv_ref[0, t] = mm(xn_ref[...], other_ref[t]).astype(BF16)

    seg_row = seg_row_ref[...]
    for head in range(heads):
        cols = slice(head * size, (head + 1) * size)
        keys = qkv_ref[0, 1, :, cols]
        values = qkv_ref[0, 2, :, cols]
        for start in range(0, half, TILE):
            rows = slice(start, start + TILE)
            scores = mm_nt(qkv_ref[0, 0, rows, cols], keys) * scale
            shift = bias_ref[head, :, : half - start]
            if start:
                shift = jnp.concatenate([bias_ref[head, :, length - start :], shift], axis=1)
            scores = scores + shift.astype(F32)
            scores = jnp.where(seg_col_ref[rows, :] == seg_row, scores, MASKED)
            top = jnp.max(scores, axis=-1, keepdims=True)
            weights = jnp.exp(scores - top)
            inverse = 1.0 / jnp.sum(weights, axis=-1, keepdims=True)
            prob = (weights * inverse).astype(BF16)
            prob_ref[0, head, rows, :] = prob
            out_ref[rows, cols] = mm(prob, values).astype(BF16)


def attend(x, gain, own_weight, other_weight, bias, seg, scale):
    half, width = x.shape
    cols = own_weight.shape[2]
    groups = 2
    heads = bias.shape[0] // groups
    return pl.pallas_call(
        functools.partial(attend_kernel, scale),
        grid=(groups,),
        out_shape=(
            jax.ShapeDtypeStruct((groups, 3, half, cols), BF16),
            jax.ShapeDtypeStruct((groups, heads, half, half), BF16),
            jax.ShapeDtypeStruct((half, groups * cols), BF16),
        ),
        in_specs=[
            pl.BlockSpec((half, width), lambda p: (0, 0)),
            pl.BlockSpec((1, width), lambda p: (0, 0)),
            pl.BlockSpec((3, width, cols), lambda p: (0, 0, 0)),
            pl.BlockSpec((3, width, cols), lambda p: (0, 0, 0)),
            pl.BlockSpec((heads,) + bias.shape[1:], lambda p: (p, 0, 0)),
            pl.BlockSpec((1, half), lambda p: (0, 0)),
            pl.BlockSpec((half, 1), lambda p: (0, 0)),
        ],
        out_specs=(
            pl.BlockSpec((1, 3, half, cols), lambda p: (p, 0, 0, 0)),
            pl.BlockSpec((1, heads, half, half), lambda p: (p, 0, 0, 0)),
            pl.BlockSpec((half, cols), lambda p: (0, p)),
        ),
        scratch_shapes=[pltpu.VMEM((half, width), BF16)],
        compiler_params=pltpu.CompilerParams(vmem_limit_bytes=VMEM_LIMIT),
        cost_estimate=pl.CostEstimate(
            flops=groups * half * cols * (6 * width + 4 * half),
            bytes_accessed=3 * groups * heads * half * half + 16 * width * cols,
            transcendentals=groups * heads * half * half,
        ),
        name="attend",
    )(x, gain, own_weight, other_weight, bias, seg.reshape(1, half), seg.reshape(half, 1))


def attend_back_kernel(
    scale, x_ref, gain_ref, own_ref, other_ref, qkv_ref, prob_ref, grad_ref,
    dxn_ref, dw_ref, line_ref, dgain_ref, sheet_ref, ds_ref, dproj_ref, xn_ref, total_ref,
):
    heads, half = prob_ref.shape[1], prob_ref.shape[2]
    size = grad_ref.shape[1] // heads
    length = sheet_ref.shape[1]
    group = pl.program_id(0)

    @pl.when(group == 0)
    def _():
        xn_ref[...] = (unit_rows(x_ref[...]) * gain_ref[...]).astype(BF16)

    for head in range(heads):
        cols = slice(head * size, (head + 1) * size)
        values = qkv_ref[0, 2, :, cols]
        sheet_ref[...] = jnp.zeros_like(sheet_ref)
        for start in range(0, half, TILE):
            rows = slice(start, start + TILE)
            prob = prob_ref[0, head, rows, :].astype(F32)
            dprob = mm_nt(grad_ref[rows, cols], values)
            inner = jnp.sum(prob * dprob, axis=-1, keepdims=True)
            dscore = (prob * (dprob - inner)).astype(BF16)
            ds_ref[rows, :] = dscore
            dscore = dscore.astype(F32)
            sheet_ref[:, : half - start] += dscore[:, start:]
            if start:
                sheet_ref[:, length - start :] += dscore[:, :start]
        dscores = ds_ref[...]
        dproj_ref[0, :, cols] = (mm(dscores, qkv_ref[0, 1, :, cols]) * scale).astype(BF16)
        dproj_ref[1, :, cols] = (mm_tn(dscores, qkv_ref[0, 0, :, cols]) * scale).astype(BF16)
        dproj_ref[2, :, cols] = mm_tn(prob_ref[0, head], grad_ref[:, cols]).astype(BF16)
        sheet = sheet_ref[...]
        while sheet.shape[0] > 8:
            upper = sheet.shape[0] // 2
            sheet = sheet[:upper] + pltpu.roll(sheet[upper:], length - upper, 1)
        row = lax.broadcasted_iota(jnp.int32, (8, length), 0)
        line = jnp.zeros((1, length), F32)
        for r in range(8):
            moved = pltpu.roll(sheet, length - r, 1) if r else sheet
            line = line + jnp.sum(jnp.where(row == r, moved, 0.0), axis=0, keepdims=True)
        line_ref[0, head : head + 1, :] = line

    def products(weight_ref):
        dxn = mm_nt(dproj_ref[0], weight_ref[0])
        for t in range(1, 3):
            dxn = dxn + mm_nt(dproj_ref[t], weight_ref[t])
        return dxn

    grads = [mm_tn(xn_ref[...], dproj_ref[t]).astype(BF16) for t in range(3)]
    grads = jnp.concatenate(grads, axis=0)
    dw_ref[...] = grads.reshape(dw_ref.shape)

    @pl.when(group == 0)
    def _():
        total_ref[...] = products(own_ref)

    @pl.when(group > 0)
    def _():
        total = total_ref[...] + products(other_ref)
        dgain_ref[...] = jnp.sum(total * unit_rows(x_ref[...]), axis=0, keepdims=True)
        dxn_ref[...] = total.astype(BF16)


def attend_back(x, gain, own_weight, other_weight, qkv, prob, grad_heads, scale, pieces):
    groups, heads, half = prob.shape[:3]
    width, cols = own_weight.shape[1:]
    length = 2 * half
    return pl.pallas_call(
        functools.partial(attend_back_kernel, scale),
        grid=(groups,),
        out_shape=(
            jax.ShapeDtypeStruct((half, width), BF16),
            jax.ShapeDtypeStruct((pieces, groups, 3 * width // pieces, cols), BF16),
            jax.ShapeDtypeStruct((groups, heads, length), F32),
            jax.ShapeDtypeStruct((1, width), F32),
        ),
        in_specs=[
            pl.BlockSpec((half, width), lambda p: (0, 0)),
            pl.BlockSpec((1, width), lambda p: (0, 0)),
            pl.BlockSpec((3, width, cols), lambda p: (0, 0, 0)),
            pl.BlockSpec((3, width, cols), lambda p: (0, 0, 0)),
            pl.BlockSpec((1, 3, half, cols), lambda p: (p, 0, 0, 0)),
            pl.BlockSpec((1, heads, half, half), lambda p: (p, 0, 0, 0)),
            pl.BlockSpec((half, cols), lambda p: (0, p)),
        ],
        out_specs=(
            pl.BlockSpec((half, width), lambda p: (0, 0)),
            pl.BlockSpec((pieces, 1, 3 * width // pieces, cols), lambda p: (0, p, 0, 0)),
            pl.BlockSpec((1, heads, length), lambda p: (p, 0, 0)),
            pl.BlockSpec((1, width), lambda p: (0, 0)),
        ),
        scratch_shapes=[
            pltpu.VMEM((TILE, length), F32),
            pltpu.VMEM((half, half), BF16),
            pltpu.VMEM((3, half, cols), BF16),
            pltpu.VMEM((half, width), BF16),
            pltpu.VMEM((half, width), F32),
        ],
        compiler_params=pltpu.CompilerParams(vmem_limit_bytes=VMEM_LIMIT),
        cost_estimate=pl.CostEstimate(
            flops=groups * half * cols * (12 * width + 8 * half),
            bytes_accessed=2 * groups * heads * half * half + 24 * width * cols,
            transcendentals=0,
        ),
        name="attend_back",
    )(x, gain, own_weight, other_weight, qkv, prob, grad_heads)


def project_kernel(part_ref, heads_ref, weight_ref, x_ref, gain_ref, h1_ref, xn_ref):
    members, _, both = heads_ref.shape
    cols = weight_ref.shape[1]
    part = part_ref[0]
    h1 = x_ref[...].astype(F32)
    for member in range(members):
        for j in range(both // cols):
            index = lax.rem(part + j, 2) * members + member
            h1 = h1 + mm(heads_ref[member, :, j * cols : (j + 1) * cols], weight_ref[index])
    h1_ref[...] = h1
    xn_ref[...] = (unit_rows(h1) * gain_ref[...]).astype(BF16)


def project(part, heads, weight, x, gain):
    slots, width = x.shape
    whole = pl.BlockSpec(memory_space=pltpu.VMEM)
    return pl.pallas_call(
        project_kernel,
        out_shape=(
            jax.ShapeDtypeStruct((slots, width), F32),
            jax.ShapeDtypeStruct((slots, width), BF16),
        ),
        in_specs=[pl.BlockSpec(memory_space=pltpu.SMEM)] + [whole] * 4,
        out_specs=(whole, whole),
        compiler_params=pltpu.CompilerParams(vmem_limit_bytes=VMEM_LIMIT),
        cost_estimate=pl.CostEstimate(
            flops=2 * slots * width * width,
            bytes_accessed=10 * slots * width + 2 * width * width,
            transcendentals=0,
        ),
        name="project",
    )(part, heads, weight, x, gain)


def turn_kernel(part_ref, grad_ref, h1_ref, dy_ref, gain_ref, weight_ref,
                dh1_ref, dattn_ref, dheads_ref, dgain_ref):
    members, _, both = dheads_ref.shape
    cols = weight_ref.shape[1]
    part = part_ref[0]
    grad = grad_ref[...].astype(F32)
    h1 = h1_ref[...]
    scale = lax.rsqrt(jnp.mean(h1 * h1, axis=-1, keepdims=True) + EPSILON)
    unit = h1 * scale
    dgain_ref[...] = jnp.sum(grad * unit, axis=0, keepdims=True)
    weighted = grad * gain_ref[...]
    inner = jnp.mean(weighted * unit, axis=-1, keepdims=True)
    dh1 = dy_ref[...].astype(F32) + scale * (weighted - unit * inner)
    dh1_ref[...] = dh1
    dattn = dh1.astype(BF16)
    dattn_ref[...] = dattn
    for member in range(members):
        for j in range(both // cols):
            index = lax.rem(part + j, 2) * members + member
            dheads = mm_nt(dattn, weight_ref[index])
            dheads_ref[member, :, j * cols : (j + 1) * cols] = dheads.astype(BF16)


def turn(part, grad, h1, dy, gain, weight, members):
    slots, width = h1.shape
    both = 2 * weight.shape[1]
    whole = pl.BlockSpec(memory_space=pltpu.VMEM)
    return pl.pallas_call(
        turn_kernel,
        out_shape=(
            jax.ShapeDtypeStruct((slots, width), F32),
            jax.ShapeDtypeStruct((slots, width), BF16),
            jax.ShapeDtypeStruct((members, slots, both), BF16),
            jax.ShapeDtypeStruct((1, width), F32),
        ),
        in_specs=[pl.BlockSpec(memory_space=pltpu.SMEM)] + [whole] * 5,
        out_specs=(whole,) * 4,
        compiler_params=pltpu.CompilerParams(vmem_limit_bytes=VMEM_LIMIT),
        cost_estimate=pl.CostEstimate(
            flops=2 * slots * width * width,
            bytes_accessed=16 * slots * width + 2 * width * width,
            transcendentals=0,
        ),
        name="turn",
    )(part, grad, h1, dy, gain, weight)


def spread(rows, place0, place1, count):
    ids = lax.broadcasted_iota(jnp.int32, (count, rows.shape[0]), 0)
    hit = (ids == place0) | (ids == place1)
    return mm(jnp.where(hit, 1.0, 0.0).astype(BF16), rows)


def spread_kernel(rows_ref, place_ref, out_ref):
    experts, _, cap, width = out_ref.shape
    placed = spread(rows_ref[...], place_ref[0:1, :], place_ref[1:2, :], experts * cap)
    out_ref[...] = placed.astype(BF16).reshape(experts, 1, cap, width)


def spread_rows(rows, place, experts, cap, shard_len):
    slots, width = rows.shape
    blocks = slots // shard_len
    return pl.pallas_call(
        spread_kernel,
        grid=(blocks,),
        out_shape=jax.ShapeDtypeStruct((experts, blocks, cap, width), BF16),
        in_specs=[
            pl.BlockSpec((shard_len, width), lambda b: (b, 0)),
            pl.BlockSpec((2, shard_len), lambda b: (0, b)),
        ],
        out_specs=pl.BlockSpec((experts, 1, cap, width), lambda b: (0, b, 0, 0)),
        compiler_params=pltpu.CompilerParams(vmem_limit_bytes=VMEM_LIMIT),
        cost_estimate=pl.CostEstimate(
            flops=2 * experts * cap * slots * width,
            bytes_accessed=2 * slots * width + 2 * experts * blocks * cap * width,
            transcendentals=0,
        ),
        name="spread_rows",
    )(rows, place)


def collect_kernel(rows_ref, place_ref, out_ref):
    experts, _, cap, width = rows_ref.shape
    tokens = out_ref.shape[0]
    ids = lax.broadcasted_iota(jnp.int32, (tokens, experts * cap), 1)
    hit = (ids == place_ref[:, 0:1]) | (ids == place_ref[:, 1:2])
    rows = rows_ref[...].reshape(experts * cap, width)
    out_ref[...] = mm(jnp.where(hit, 1.0, 0.0).astype(BF16), rows).astype(BF16)


def collect_rows(rows, place, shard_len):
    experts, blocks, cap, width = rows.shape
    slots = blocks * shard_len
    return pl.pallas_call(
        collect_kernel,
        grid=(blocks,),
        out_shape=jax.ShapeDtypeStruct((slots, width), BF16),
        in_specs=[
            pl.BlockSpec((experts, 1, cap, width), lambda b: (0, b, 0, 0)),
            pl.BlockSpec((shard_len, 2), lambda b: (b, 0)),
        ],
        out_specs=pl.BlockSpec((shard_len, width), lambda b: (b, 0)),
        compiler_params=pltpu.CompilerParams(vmem_limit_bytes=VMEM_LIMIT),
        cost_estimate=pl.CostEstimate(
            flops=2 * experts * cap * slots * width,
            bytes_accessed=2 * slots * width + 2 * experts * blocks * cap * width,
            transcendentals=0,
        ),
        name="collect_rows",
    )(rows, place)


def expert_kernel(
    x_ref, dy_ref, pair_ref, wr_ref, wg_ref, wu_ref, wd_ref,
    y_ref, dx_ref, g_ref, hid_ref, dga_ref, dup_ref, dlog_ref,
):
    sources, _, cap, width = x_ref.shape
    rows = sources * cap
    x = x_ref[...].reshape(rows, width)
    dy = dy_ref[...].reshape(rows, width).astype(F32)
    pair = pair_ref[...].reshape(rows, pair_ref.shape[3])
    margin = jnp.sum(mm(x, wr_ref[...]) * pair, axis=-1, keepdims=True)
    own_gate = 1.0 / (1.0 + jnp.exp(-margin))
    other_gate = 1.0 / (1.0 + jnp.exp(margin))
    g = (own_gate * dy).astype(BF16)
    g_ref[0] = g
    gate = mm(x, wg_ref[0])
    up = mm(x, wu_ref[0])
    square = gate * gate
    bent = jnp.tanh(GELU_C * gate * (1.0 + GELU_A * square))
    half_gate = 0.5 * gate
    gelu = half_gate * (1.0 + bent)
    slope = 0.5 * (1.0 + bent) + half_gate * (1.0 - bent * bent) * (
        GELU_C * (1.0 + 3.0 * GELU_A * square)
    )
    hid = (gelu * up).astype(BF16)
    dhid = mm_nt(g, wd_ref[0])
    dga = (dhid * (up * slope)).astype(BF16)
    dup = (dhid * gelu).astype(BF16)
    hid_ref[0] = hid
    dga_ref[0] = dga
    dup_ref[0] = dup
    y = mm(hid, wd_ref[0])
    dgate = jnp.sum(y * dy, axis=-1, keepdims=True)
    y_ref[...] = (y * own_gate).astype(BF16).reshape(sources, 1, cap, width)
    dlog = (dgate * own_gate * other_gate * pair).astype(BF16)
    dlog_ref[0] = dlog
    dx = mm_nt(dga, wg_ref[0]) + mm_nt(dup, wu_ref[0]) + mm_nt(dlog, wr_ref[...])
    dx_ref[...] = dx.astype(BF16).reshape(sources, 1, cap, width)


def expert_pass(x, dy, pair, wr, wg, wu, wd):
    sources, experts, cap, width = x.shape
    hidden = wg.shape[2]
    choices = wr.shape[1]
    group = 2 if sources % 2 == 0 else 1
    rows = sources * cap
    tokens = pl.BlockSpec((group, 1, cap, width), lambda e, s: (s, e, 0, 0))
    wide = pl.BlockSpec((1, width, hidden), lambda e, s: (e, 0, 0))
    tall = pl.BlockSpec((1, hidden, width), lambda e, s: (e, 0, 0))

    def acts(cols):
        return pl.BlockSpec((1, group * cap, cols), lambda e, s: (e, s, 0))

    def act_shape(cols):
        return jax.ShapeDtypeStruct((experts, rows, cols), BF16)

    return pl.pallas_call(
        expert_kernel,
        grid=(experts, sources // group),
        out_shape=(
            jax.ShapeDtypeStruct(x.shape, BF16),
            jax.ShapeDtypeStruct(x.shape, BF16),
            act_shape(width),
            act_shape(hidden),
            act_shape(hidden),
            act_shape(hidden),
            act_shape(choices),
        ),
        in_specs=[
            tokens,
            tokens,
            pl.BlockSpec((group, 1, cap, choices), lambda e, s: (s, e, 0, 0)),
            pl.BlockSpec((width, choices), lambda e, s: (0, 0)),
            wide,
            wide,
            tall,
        ],
        out_specs=(
            tokens, tokens, acts(width), acts(hidden), acts(hidden), acts(hidden), acts(choices)
        ),
        compiler_params=pltpu.CompilerParams(vmem_limit_bytes=VMEM_LIMIT),
        cost_estimate=pl.CostEstimate(
            flops=12 * experts * rows * width * hidden,
            bytes_accessed=10 * experts * rows * width + 6 * experts * hidden * (width + rows),
            transcendentals=experts * rows * hidden,
        ),
        name="expert_pass",
    )(x, dy, pair, wr, wg, wu, wd)


def weight_kernel(*refs):
    count = (len(refs) - 4) // 6
    dwr_ref, dwg_ref, dwu_ref, dwd_ref = refs[-4:]
    totals = [0.0, 0.0, 0.0, 0.0]
    for index in range(count):
        x_ref, g_ref, hid_ref, dga_ref, dup_ref, dlog_ref = refs[6 * index : 6 * index + 6]
        sources, _, cap, width = x_ref.shape
        x = x_ref[...].reshape(sources * cap, width)
        totals[0] = totals[0] + mm_tn(x, dlog_ref[0])
        totals[1] = totals[1] + mm_tn(x, dga_ref[0])
        totals[2] = totals[2] + mm_tn(x, dup_ref[0])
        totals[3] = totals[3] + mm_tn(hid_ref[0], g_ref[0])
    dwr_ref[0] = totals[0]
    dwg_ref[0] = totals[1]
    dwu_ref[0] = totals[2]
    dwd_ref[0] = totals[3]


def weight_pass(kept):
    sources, experts, cap, width = kept[0][0].shape
    rows, hidden = kept[0][2].shape[1:]
    choices = kept[0][5].shape[2]
    block = 256 if width % 256 == 0 else width
    tokens = pl.BlockSpec((sources, 1, cap, block), lambda e, j: (0, e, 0, j))
    grads = pl.BlockSpec((1, rows, block), lambda e, j: (e, 0, j))
    acts = pl.BlockSpec((1, rows, hidden), lambda e, j: (e, 0, 0))
    logs = pl.BlockSpec((1, rows, choices), lambda e, j: (e, 0, 0))
    operands = []
    for arrays in kept:
        operands.extend(arrays)
    return pl.pallas_call(
        weight_kernel,
        grid=(experts, width // block),
        out_shape=(
            jax.ShapeDtypeStruct((experts, width, choices), F32),
            jax.ShapeDtypeStruct((experts, width, hidden), F32),
            jax.ShapeDtypeStruct((experts, width, hidden), F32),
            jax.ShapeDtypeStruct((experts, hidden, width), F32),
        ),
        in_specs=[tokens, grads, acts, acts, acts, logs] * len(kept),
        out_specs=(
            pl.BlockSpec((1, block, choices), lambda e, j: (e, j, 0)),
            pl.BlockSpec((1, block, hidden), lambda e, j: (e, j, 0)),
            pl.BlockSpec((1, block, hidden), lambda e, j: (e, j, 0)),
            pl.BlockSpec((1, hidden, block), lambda e, j: (e, 0, j)),
        ),
        compiler_params=pltpu.CompilerParams(vmem_limit_bytes=VMEM_LIMIT),
        cost_estimate=pl.CostEstimate(
            flops=6 * len(kept) * experts * rows * width * hidden,
            bytes_accessed=len(kept) * experts * rows * (4 * width + 6 * hidden)
            + 12 * experts * width * hidden,
            transcendentals=0,
        ),
        name="weight_pass",
    )(*operands)


def after(values, *others):
    return lax.optimization_barrier((values,) + others)[0]


def shards(
    x_in,
    cotangent,
    segment_ids,
    routes,
    qkv_weight,
    out_weight,
    bias_table,
    attn_gain,
    moe_gain,
    router_weight,
    gate_weight,
    up_weight,
    down_weight,
):
    micro_count, _, shard_len, width = x_in.shape
    slot_count = segment_ids.shape[2]
    head_cols = out_weight.shape[0]
    bucket_count, heads_here = bias_table.shape
    head_size = head_cols // heads_here
    expert_count = router_weight.shape[1]
    experts_here = gate_weight.shape[0]
    devices = expert_count // experts_here
    blocks = slot_count // shard_len
    members = blocks // 2
    half = slot_count // 2
    capacity = max(2, (10 * shard_len + 4 * expert_count - 1) // (4 * expert_count))
    scale = head_size ** (-0.5)
    hidden_index = lax.axis_index("hidden")
    expert_index = lax.axis_index("expert")
    part = hidden_index // members
    part_ref = part.reshape(1).astype(jnp.int32)
    attn_gain_f = attn_gain.astype(F32).reshape(1, width)
    moe_gain_f = moe_gain.astype(F32).reshape(1, width)
    token_shape = (devices, experts_here, blocks * capacity, width)
    flat_shape = (devices, experts_here * blocks * capacity, width)
    place_shape = (expert_count, blocks, capacity, width)
    half_groups = [list(range(p * members, (p + 1) * members)) for p in range(2)]
    across = [(z, (z + members) % blocks) for z in range(blocks)]

    def exchange(buffer):
        return lax.all_to_all(buffer, "expert", split_axis=0, concat_axis=0, tiled=True)

    def to_all(values, axis, count, groups=None):
        copies = jnp.broadcast_to(values[None], (count,) + values.shape)
        return lax.all_to_all(
            copies, axis, split_axis=0, concat_axis=0, tiled=True, axis_index_groups=groups
        )

    def swap_half(buffer):
        return lax.all_to_all(
            buffer, "hidden", split_axis=0, concat_axis=0, tiled=True,
            axis_index_groups=half_groups,
        )

    def gather(values):
        return lax.all_gather(values, "hidden", axis=0, tiled=True)

    def scatter(values):
        return lax.psum_scatter(values.astype(BF16), "hidden", scatter_dimension=0, tiled=True)

    def my_piece(flat):
        rows = flat.shape[0] // devices
        return lax.dynamic_slice_in_dim(flat, expert_index * rows, rows, 0)

    def placing():
        expert_ids = jnp.arange(expert_count, dtype=jnp.int32)
        place_ids = jnp.arange(expert_count * capacity, dtype=jnp.int32)
        slot = jnp.arange(shard_len, dtype=jnp.int32)
        earlier_than = (slot[:, None] < slot[None, :]).astype(BF16)
        route = to_all(routes[:, 0], "hidden", blocks)
        route = route.transpose(1, 0, 2, 3)
        live = (segment_ids[:, 0] >= 0).reshape(micro_count, blocks, shard_len)
        chosen = (route[..., None] == expert_ids).astype(F32)
        chosen = chosen * live[..., None, None].astype(F32)
        counted = jnp.sum(chosen, axis=3).astype(BF16)
        before = jnp.einsum("mbte,tu->mbue", counted, earlier_than, preferred_element_type=F32)
        position = jnp.sum(before[:, :, :, None, :] * chosen, axis=-1).astype(jnp.int32)
        place = jnp.where(live[..., None], route * capacity + position, -1)
        other = jnp.full((micro_count, blocks, expert_count * capacity), -1, jnp.int32)
        for k in range(2):
            hit = place[:, :, None, :, k] == place_ids[None, None, :, None]
            found = jnp.max(jnp.where(hit, route[:, :, None, :, 1 - k], -1), axis=-1)
            other = jnp.maximum(other, found)
        other = other.reshape(micro_count, blocks, devices, experts_here, capacity)
        other = exchange(other.transpose(2, 0, 3, 1, 4))
        other = other.transpose(1, 0, 2, 3, 4)
        other = other.reshape(micro_count, devices, experts_here, blocks * capacity)
        me = expert_index * experts_here + jnp.arange(experts_here, dtype=jnp.int32)
        plus = me[None, None, :, None, None] == expert_ids
        minus = other[..., None] == expert_ids
        pair = plus.astype(F32) - minus.astype(F32)
        pair = jnp.where(other[..., None] >= 0, pair, 0.0).astype(BF16)
        place = place.reshape(micro_count, slot_count, 2)
        return place, place.transpose(0, 2, 1), pair

    states = [dict() for _ in range(micro_count)]

    piece = lax.ppermute(my_piece(qkv_weight.reshape(3 * width, head_cols)), "hidden", across)
    other_qkv = to_all(piece, "expert", devices).reshape(qkv_weight.shape)
    piece = to_all(my_piece(out_weight), "hidden", blocks)
    all_out = to_all(piece, "expert", devices)
    all_out = all_out.transpose(1, 0, 2, 3).reshape(blocks, head_cols, width)
    tables = jnp.concatenate(
        [bias_table, lax.ppermute(bias_table, "hidden", across)], axis=1
    ).astype(F32)
    onehot_bucket = bucket_onehot(half, bucket_count)
    bias = position_bias(jnp.einsum("jb,bh->hj", onehot_bucket, tables, precision=PRECISE))
    place_cols, place_rows, pairs = placing()

    def pair_x(micro, kept):
        kept["x_half"] = to_all(x_in[micro, 0], "hidden", members, half_groups).reshape(half, width)

    def attention(micro, kept):
        seg = lax.dynamic_slice_in_dim(segment_ids[micro, 0], part * half, half, 0)
        qkv, prob, heads = attend(
            kept["x_half"], attn_gain_f, qkv_weight, other_qkv, bias, seg, scale
        )
        kept.update(qkv=qkv, prob=prob, heads=heads)
        own_heads = swap_half(heads.reshape(members, shard_len, 2 * head_cols))
        kept["h1"], kept["xn2"] = project(part_ref, own_heads, all_out, x_in[micro, 0], moe_gain_f)

    def spread(rows, micro):
        sent = spread_rows(rows, place_rows[micro], expert_count, capacity, shard_len)
        return sent.reshape(flat_shape)

    def experts(micro, kept):
        y, dx, g, hid, dga, dup, dlog = expert_pass(
            kept["x"], kept["dy"], pairs[micro], router_weight, gate_weight, up_weight, down_weight
        )
        kept["weights"] = (kept["x"], g, hid, dga, dup, dlog)
        kept["y_sent"] = y.reshape(flat_shape)
        kept["dx_sent"] = dx.reshape(flat_shape)

    def combine(micro, kept):
        part_sum = collect_rows(kept["dx_back"], place_cols[micro], shard_len)
        kept["dxn2"] = scatter(part_sum)

    def attention_back(micro, kept):
        dh1, dattn, dheads, kept["moe_gain_grad"] = turn(
            part_ref, kept["dxn2"], kept["h1"], cotangent[micro, 0], moe_gain_f, all_out, members
        )
        dheads = swap_half(dheads).reshape(half, 2 * head_cols)
        dattn = to_all(dattn, "hidden", members, half_groups).reshape(half, width)
        dxn1, kept["qkv_grad"], kept["line"], kept["attn_gain_grad"] = attend_back(
            kept["x_half"], attn_gain_f, qkv_weight, other_qkv, kept["qkv"], kept["prob"], dheads,
            scale, devices,
        )
        kept["dxn1"] = dxn1
        kept["out_grad"] = mm_tn(kept["heads"], dattn).astype(BF16)
        dxn1 = swap_half(dxn1.reshape(members, shard_len, width))
        dxn1 = jnp.sum(dxn1.astype(F32), axis=0)
        x_own = x_in[micro, 0].astype(F32)
        r1 = lax.rsqrt(jnp.mean(x_own * x_own, axis=-1, keepdims=True) + EPSILON)
        unit = x_own * r1
        weighted = dxn1 * attn_gain_f
        inner = jnp.mean(weighted * unit, axis=-1, keepdims=True)
        kept["x_grad"] = (dh1 + r1 * (weighted - unit * inner)).astype(BF16)

    def finish(micro, kept):
        mixed = scatter(collect_rows(kept["y_back"], place_cols[micro], shard_len))
        kept["block_out"] = (kept["h1"] + mixed.astype(F32)).astype(BF16)

    first, last = states[0], states[-1]
    for micro in range(micro_count):
        pair_x(micro, states[micro])
    first["dy_all"] = gather(cotangent[0, 0])
    attention(0, first)
    first["dy"] = exchange(spread(first["dy_all"], 0)).reshape(token_shape)
    first["xn2_all"] = gather(first["xn2"])
    first["x"] = exchange(spread(first["xn2_all"], 0)).reshape(token_shape)
    behind = first["xn2_all"]
    for micro in range(1, micro_count):
        state = states[micro]
        attention(micro, state)
        state["xn2_all"] = gather(after(state["xn2"], behind))
        state["x"] = exchange(spread(state["xn2_all"], micro)).reshape(token_shape)
        state["dy_all"] = gather(after(cotangent[micro, 0], state["xn2_all"]))
        state["dy"] = exchange(spread(state["dy_all"], micro)).reshape(token_shape)
        behind = state["dy_all"]
    for micro in range(micro_count):
        state = states[micro]
        experts(micro, state)
        sent = state["dx_sent"]
        if micro + 1 < micro_count:
            sent = after(sent, states[micro + 1]["dy"])
        state["dx_back"] = exchange(sent).reshape(place_shape)
    for micro in range(micro_count):
        state = states[micro]
        state["y_back"] = exchange(after(state["y_sent"], last["dx_back"])).reshape(place_shape)
    for micro in range(micro_count):
        combine(micro, states[micro])
        attention_back(micro, states[micro])
    for micro in range(micro_count):
        finish(micro, states[micro])
    kept = [state["weights"] for state in states]
    kept[-1] = tuple(after(list(kept[-1]), last["dxn1"]))
    dwr, dwg, dwu, dwd = weight_pass(kept)

    def added(name):
        total = states[0][name].astype(F32)
        for state in states[1:]:
            total = total + state[name].astype(F32)
        return total

    def both_halves(pieces):
        total = jnp.sum(pieces.astype(F32), axis=0)
        moved = lax.ppermute(total[1].astype(BF16), "hidden", across)
        piece = (total[0] + moved.astype(F32)).astype(BF16)
        return to_all(piece, "expert", devices)

    grad_qkv = both_halves(exchange(added("qkv_grad").astype(BF16)))
    grad_qkv = grad_qkv.astype(F32).reshape(qkv_weight.shape)
    grad_out = added("out_grad").astype(BF16).reshape(2, devices, head_cols // devices, width)
    grad_out = both_halves(exchange(grad_out.transpose(1, 0, 2, 3)))
    grad_out = grad_out.astype(F32).reshape(out_weight.shape)
    lines = added("line").reshape(2 * heads_here, 2 * half)
    table = jnp.einsum("hj,jb->hb", lines, onehot_bucket, precision=PRECISE)
    table = table.reshape(2, heads_here * bucket_count)
    mine = jnp.arange(blocks, dtype=jnp.int32)[:, None]
    table = jnp.where(mine == hidden_index, table[0], 0.0) + jnp.where(
        mine == (hidden_index + members) % blocks, table[1], 0.0
    )
    small = jnp.concatenate(
        [
            jnp.sum(dwr, axis=0).reshape(-1),
            added("attn_gain_grad").reshape(-1),
            added("moe_gain_grad").reshape(-1),
            table.reshape(-1),
        ]
    ).reshape(-1, 128)
    small = jnp.sum(to_all(small, "expert", devices), axis=0)
    small = jnp.sum(to_all(small, "hidden", blocks), axis=0).reshape(-1)
    sizes = (width * expert_count, width, width)
    grad_router = small[: sizes[0]].reshape(width, expert_count)
    grad_attn_gain = small[sizes[0] : sizes[0] + width]
    grad_moe_gain = small[sizes[0] + width : sizes[0] + 2 * width]
    table = small[sizes[0] + 2 * width :].reshape(blocks, heads_here, bucket_count)
    grad_table = lax.dynamic_index_in_dim(table, hidden_index, 0, keepdims=False).T
    return (
        jnp.stack([state["block_out"] for state in states])[:, None],
        jnp.stack([state["x_grad"] for state in states])[:, None],
        grad_qkv,
        grad_out,
        grad_table,
        grad_attn_gain,
        grad_moe_gain,
        grad_router,
        dwg,
        dwu,
        dwd,
    )


def solution(mesh):
    return jax.shard_map(
        shards,
        mesh=mesh,
        in_specs=(
            P(None, "expert", "hidden", None),
            P(None, "expert", "hidden", None),
            P(None, "expert", None),
            P(None, "expert", "hidden", None),
            P(None, None, "hidden"),
            P("hidden", None),
            P(None, "hidden"),
            P(),
            P(),
            P(),
            P("expert", None, "hidden"),
            P("expert", None, "hidden"),
            P("expert", "hidden", None),
        ),
        out_specs=(
            P(None, "expert", "hidden", None),
            P(None, "expert", "hidden", None),
            P(None, None, "hidden"),
            P("hidden", None),
            P(None, "hidden"),
            P(),
            P(),
            P(),
            P("expert", None, "hidden"),
            P("expert", None, "hidden"),
            P("expert", "hidden", None),
        ),
        check_vma=False,
    )
```

time: 1190 us -> 1020 us (0.86)
  waiting for transfers between devices: 647 us -> 480 us
  starting transfers between devices: 50.4 us -> 110 us
  matrix products: 37.6 us -> 3.7 us
  blocking collectives: 80.7 us -> 60.8 us
  Pallas kernels: 268 us -> 251 us
    all_gather x4 -> x0, waiting for transfers between devices: 126 us -> none  [the longest x2 90.9 us: attention(): all_heads = lax.all_gather(heads_out, 'hidden', axis=0, tiled=False)]
    all_to_all x0 -> x15, waiting for transfers between devices: none -> 90.4 us  [the longest x10 63.9 us: to_all(): lax.all_to_all(copies, axis, split_axis=0, concat_axis=0, tiled=True, axi...]
    reduce_scatter x6 -> x4, waiting for transfers between devices: 158 us -> 81.3 us  [scatter(): lax.psum_scatter(values.astype(BF16), 'hidden', scatter_dimension=0, tile...]
    all_gather x6 -> x4, waiting for transfers between devices: 161 us -> 94.4 us  [gather(): return lax.all_gather(values, 'hidden', axis=0, tiled=True)]
    all_to_all x0 -> x3, blocking collectives: none -> 60.8 us  [the longest x2 33.5 us: to_all(): lax.all_to_all(copies, axis, split_axis=0, concat_axis=0, tiled=True, axi...]
    all_to_all x0 -> x15, starting transfers between devices: none -> 58.1 us  [the longest x10 40.5 us: to_all(): lax.all_to_all(copies, axis, split_axis=0, concat_axis=0, tiled=True, axi...]
    psum x2 -> x0, blocking collectives: 56.1 us -> none  [the longest x1 41.6 us: shards(): lax.psum((jnp.sum(dwr, axis=0), added('attn_gain_grad'), added('moe_gain_...]
    ppermute x0 -> x4, waiting for transfers between devices: none -> 35.6 us  [the longest x2 24.4 us: both_halves(): moved = lax.ppermute(total[1].astype(BF16), 'hidden', across)]
  transfers between devices with their start and end apart: 28 -> 38, of which waited for: 19 -> 26; matrix products, arithmetic and copies ran while one was open for 8% -> 8% of each run, Pallas kernels for 20% -> 25%
where the time goes in v3:
time: 1020 us; the launch traced here: 1010 us
  waiting for transfers between devices  480 us (47%)
  Pallas kernels  251 us (25%)
  starting transfers between devices  110 us (11%)
  blocking collectives  60.8 us (6%)
  local copies, waits for them, and re-layouts  57 us (6%)
  other arithmetic  32 us (3%)
  between operations  15.5 us (2%)
    all_to_all x11, waiting for transfers between devices, exchange(): lax.all_to_all(buffer, 'expert', split_axis=0, concat_axis=0, tiled=True)  178 us
    all_gather x4, waiting for transfers between devices, gather(): return lax.all_gather(values, 'hidden', axis=0, tiled=True)  94.4 us
    reduce_scatter x4, waiting for transfers between devices, scatter(): lax.psum_scatter(values.astype(BF16), 'hidden', scatter_dimension=0, tile...  81.3 us
    pallas_call x2, Pallas kernels, expert_pass(): pl.pallas_call(expert_kernel, grid=(experts, sources // group), out_shape...  71.5 us
    all_to_all x10, waiting for transfers between devices, to_all(): lax.all_to_all(copies, axis, split_axis=0, concat_axis=0, tiled=True, axi...  63.9 us
    all_to_all x11, starting transfers between devices, exchange(): lax.all_to_all(buffer, 'expert', split_axis=0, concat_axis=0, tiled=True)  50 us
    all_to_all x10, starting transfers between devices, to_all(): lax.all_to_all(copies, axis, split_axis=0, concat_axis=0, tiled=True, axi...  40.5 us
    pallas_call x1, Pallas kernels, weight_pass(): pl.pallas_call(weight_kernel, grid=(experts, width // block), out_shape=(...  38.5 us
  transfers between devices with their start and end apart: 38, of which 26 were waited for; matrix products, arithmetic and copies ran while one was open for 8% of the time, Pallas kernels for 25%

profile of v3, /device:TPU:0, one launch (start us, length us, event | category | flops | bytes accessed | tf_op | source)
XLA Modules:
  0.0 1010.0 jit_solution(328517125989880690)
XLA Ops:
  8.6 6.3 all-to-all-start.5
  14.9 5.6 all-to-all-done.5
  25.9 6.6 all-to-all-done.3
  38.2 11.2 %collective-permute-done = bf16[384,256]{1,0:T(8,128)(2,1)S(1)} collective-permute-done((bf16[384,256]{1,0:T(8,128)(2,1)S(1)}, bf16[384,256]{1,0:T(8,128)(2,1)S(1)}, u32[]{:S(2)}, u32[]{:S(2)}) %collective-permute-start) | collective-permute-done | bytes 196640 | tf_op jit(solution)/shard_map/ppermute | solution.py:664
  59.4 18.4 %all-to-all-done.1 = bf16[8,384,256]{2,1,0:T(8,128)(2,1)S(1)} async-done(((bf16[8,384,256]{2,1,0:T(8,128)(2,1)}), bf16[8,384,256]{2,1,0:T(8,128)(2,1)S(1)}, u32[]{:S(2)}, u32[]{:S(2)}) %all-to-all-start.1) | async-done | bytes 1572896 | tf_op jit(solution)/shard_map/all_to_all | solution.py:611
  89.7 5.9 position_bias.1.bias_ref
  96.0 18.4 %attend.2 = (bf16[2,3,512,256]{3,2,1,0:T(8,128)(2,1)}, bf16[2,4,512,512]{3,2,1,0:T(8,128)(2,1)}, bf16[512,512]{1,0:T(8,128)(2,1)}) custom-call(bf16[512,1024]{1,0:T(8,128)(2,1)} %bitcast.190, f32[1,1024]{1,0:T(1,128)} %bitcast.209, bf16[3,1024,256]{2,1,0:T(8,128)(2,1)} %own_ref.7, bf16[3,1024,256]{2,1,0:T(8,128)(2,1)} %bitcast.186, ...), custom_call_target="tpu_custom_call" | custom-call | flops 2147483648 | bytes 10485760 | tf_op jit(solution)/shard_map/attend/pallas_call | solution.py:128
  119.5 6.8 all-to-all-done.2.heads_ref
  137.6 6.7 all-to-all-done.9
  148.2 18.4 %attend.3 = (bf16[2,3,512,256]{3,2,1,0:T(8,128)(2,1)}, bf16[2,4,512,512]{3,2,1,0:T(8,128)(2,1)}, bf16[512,512]{1,0:T(8,128)(2,1)}) custom-call(bf16[512,1024]{1,0:T(8,128)(2,1)} %bitcast.192, f32[1,1024]{1,0:T(1,128)} %bitcast.210, bf16[3,1024,256]{2,1,0:T(8,128)(2,1)} %own_ref.7, bf16[3,1024,256]{2,1,0:T(8,128)(2,1)} %bitcast.187, ...), custom_call_target="tpu_custom_call" | custom-call | flops 2147483648 | bytes 10485760 | tf_op jit(solution)/shard_map/attend/pallas_call | solution.py:128
  170.7 5.3 spread_rows.5
  176.0 10.4 %all-to-all-done.10.heads_ref = bf16[2,256,512]{2,1,0:T(8,128)(2,1)S(1)} async-done(((bf16[2,256,512]{2,1,0:T(8,128)(2,1)}), bf16[2,256,512]{2,1,0:T(8,128)(2,1)S(1)}, u32[]{:S(2)}, u32[]{:S(2)}) %all-to-all-start.10) | async-done | bytes 524320 | tf_op jit(solution)/shard_map/all_to_all | solution.py:616
  195.7 46.5 %all-gather.8.cloned.1.call-done.rows_ref = bf16[1024,1024]{1,0:T(8,128)(2,1)} async-done(((bf16[256,1024]{1,0:T(8,128)(2,1)}), bf16[1024,1024]{1,0:T(8,128)(2,1)}) %all-gather.8.cloned.1.call-update) | async-done | bytes 2097168 | tf_op jit(solution)/shard_map/all_gather | solution.py:622
  242.2 5.3 spread_rows.6
  257.5 47.9 %all-gather.10.cloned.1.call-done.rows_ref = bf16[1024,1024]{1,0:T(8,128)(2,1)} async-done(((bf16[256,1024]{1,0:T(8,128)(2,1)}), bf16[1024,1024]{1,0:T(8,128)(2,1)}) %all-gather.10.cloned.1.call-update) | async-done | bytes 2097168 | tf_op jit(solution)/shard_map/all_gather | solution.py:622
  305.4 5.3 spread_rows.7
  310.7 6.6 all-to-all-done.11
  322.0 5.3 spread_rows.4
  327.3 55.0 %all-to-all-done.12 = bf16[8,320,1024]{2,1,0:T(8,128)(2,1)} async-done(((bf16[8,320,1024]{2,1,0:T(8,128)(2,1)}), bf16[8,320,1024]{2,1,0:T(8,128)(2,1)}, u32[]{:S(2)}, u32[]{:S(2)}) %all-to-all-start.12) | async-done | bytes 5242912 | tf_op jit(solution)/shard_map/all_to_all | solution.py:607
  382.4 5.3 all-to-all-start.6
  400.7 35.7 %expert_pass.3 = (bf16[8,2,160,1024]{3,2,1,0:T(8,128)(2,1)}, bf16[8,2,160,1024]{3,2,1,0:T(8,128)(2,1)}, bf16[2,1280,1024]{2,1,0:T(8,128)(2,1)}, bf16[2,1280,704]...) custom-call(bf16[8,2,160,1024]{3,2,1,0:T(8,128)(2,1)} %bitcast.37.x_, ...), custom_call_target="tpu_custom_call" | custom-call | flops 22145925120 | bytes 45678592 | tf_op jit(solution)/shard_map/expert_pass/pallas_call | solution.py:471
  436.4 11.6 %all-to-all-done.6 = bf16[8,320,1024]{2,1,0:T(8,128)(2,1)} async-done(((bf16[8,320,1024]{2,1,0:T(8,128)(2,1)}), bf16[8,320,1024]{2,1,0:T(8,128)(2,1)}, u32[]{:S(2)}, u32[]{:S(2)}) %all-to-all-start.6) | async-done | bytes 5242912 | tf_op jit(solution)/shard_map/all_to_all | solution.py:607
  452.7 35.8 %expert_pass.2 = (bf16[8,2,160,1024]{3,2,1,0:T(8,128)(2,1)}, bf16[8,2,160,1024]{3,2,1,0:T(8,128)(2,1)}, bf16[2,1280,1024]{2,1,0:T(8,128)(2,1)}, bf16[2,1280,704]...) custom-call(bf16[8,2,160,1024]{3,2,1,0:T(8,128)(2,1)} %bitcast.21.x_, ...), custom_call_target="tpu_custom_call" | custom-call | flops 22145925120 | bytes 45678592 | tf_op jit(solution)/shard_map/expert_pass/pallas_call | solution.py:471
  488.5 24.6 %all-to-all-done.13 = bf16[8,320,1024]{2,1,0:T(8,128)(2,1)} async-done(((bf16[8,320,1024]{2,1,0:T(8,128)(2,1)}), bf16[8,320,1024]{2,1,0:T(8,128)(2,1)}, u32[]{:S(2)}, u32[]{:S(2)}) %all-to-all-start.13) | async-done | bytes 5242912 | tf_op jit(solution)/shard_map/all_to_all | solution.py:607
  517.7 60.4 %all-to-all-done.16 = bf16[8,320,1024]{2,1,0:T(8,128)(2,1)} async-done(((bf16[8,320,1024]{2,1,0:T(8,128)(2,1)}), bf16[8,320,1024]{2,1,0:T(8,128)(2,1)}, u32[]{:S(2)}, u32[]{:S(2)}) %all-to-all-start.16) | async-done | bytes 5242912 | tf_op jit(solution)/shard_map/all_to_all | solution.py:607
  583.9 5.7 collect_rows.7
  589.6 44.4 %reduce-scatter.11.cloned.1.call-done.grad_ref = bf16[256,1024]{1,0:T(8,128)(2,1)} async-done(((bf16[1024,1024]{1,0:T(8,128)(2,1)}), bf16[256,1024]{1,0:T(8,128)(2,1)}) %reduce-scatter.11.cloned.1.call-update) | async-done | bytes 524304 | tf_op jit(solution)/shard_map/reduce_scatter | solution.py:625
  638.3 4.8 all-to-all-done.14
  647.7 5.7 collect_rows.6
  654.2 4.8 all-to-all-start.15
  659.1 36.8 %reduce-scatter.9.cloned.1.call-done.grad_ref = bf16[256,1024]{1,0:T(8,128)(2,1)} async-done(((bf16[1024,1024]{1,0:T(8,128)(2,1)}), bf16[256,1024]{1,0:T(8,128)(2,1)}) %reduce-scatter.9.cloned.1.call-update) | async-done | bytes 524304 | tf_op jit(solution)/shard_map/reduce_scatter | solution.py:625
  700.9 18.8 %attend_back.3 = (bf16[512,1024]{1,0:T(8,128)(2,1)}, bf16[8,2,384,256]{3,2,1,0:T(8,128)(2,1)}, f32[2,4,1024]{2,1,0:T(4,128)}, f32[1,1024]{1,0:T(1,128)}) custom-call(bf16[512,1024]{1,0:T(8,128)(2,1)} %bitcast.193, f32[1,1024]{1,0:T(1,128)} %bitcast.211, bf16[3,1024,256]{2,1,0:T(8,128)(2,1)} %own_ref.7, bf16[3,1024,256]{2,1,0:T(8,128)(2,1)} %bitcast.188, ...), custom_call_target="tpu_custom_call" | custom-call | flops 4294967296 | bytes 10485760 | tf_op jit(solution)/shard_map/attend_back/pallas_call | solution.py:229
  723.2 38.5 %weight_pass.1 = (f32[2,1024,16]{2,1,0:T(8,128)}, f32[2,1024,704]{2,1,0:T(8,128)}, f32[2,1024,704]{2,1,0:T(8,128)}, f32[2,704,1024]{2,1,0:T(8,128)}) custom-call(bf16[8,2,160,1024]{3,2,1,0:T(8,128)(2,1)} %bitcast.21.x_ref.refs_0_, bf16[2,1280,1024]{2,1,0:T(8,128)(2,1)} %get-tuple-element.95.refs_1_, bf16[2,1280,704]{2,1,0:T(8,128)(2,1)} %get-tuple-element.96.refs_2_, ...), custom_call_target="tpu_custom_call" | custom-call | flops 22145925120 | bytes 59899904 | tf_op jit(solution)/shard_map/weight_pass/pallas_call | solution.py:535
  766.7 18.8 %attend_back.2 = (bf16[512,1024]{1,0:T(8,128)(2,1)}, bf16[8,2,384,256]{3,2,1,0:T(8,128)(2,1)}, f32[2,4,1024]{2,1,0:T(4,128)}, f32[1,1024]{1,0:T(1,128)}) custom-call(bf16[512,1024]{1,0:T(8,128)(2,1)} %bitcast.191, f32[1,1024]{1,0:T(1,128)} %bitcast.212, bf16[3,1024,256]{2,1,0:T(8,128)(2,1)} %own_ref.7, bf16[3,1024,256]{2,1,0:T(8,128)(2,1)} %bitcast.189, ...), custom_call_target="tpu_custom_call" | custom-call | flops 4294967296 | bytes 10485760 | tf_op jit(solution)/shard_map/attend_back/pallas_call | solution.py:229
  788.2 14.2 %all_to_all.145 = f32[8,148,128]{2,1,0:T(8,128)S(1)} all-to-all(f32[8,148,128]{2,1,0:T(8,128)S(1)} %broadcast_in_dim.204), channel_id=1, replica_groups=mesh['expert'=8,'hidden'=4] {'expert'}, dimensions={0} | all-to-all | bytes 1212416 | tf_op jit(solution)/shard_map/all_to_all | solution.py:611
  808.0 5.7 collect_rows.4
  813.8 11.6 %all-to-all-done.24 = bf16[2,256,1024]{2,1,0:T(8,128)(2,1)} async-done(((bf16[2,256,1024]{2,1,0:T(8,128)(2,1)}), bf16[2,256,1024]{2,1,0:T(8,128)(2,1)}, u32[]{:S(2)}, u32[]{:S(2)}) %all-to-all-start.24) | async-done | bytes 1048608 | tf_op jit(solution)/shard_map/all_to_all | solution.py:611
  825.4 19.3 %all_to_all.146 = f32[4,148,128]{2,1,0:T(8,128)S(1)} all-to-all(f32[4,148,128]{2,1,0:T(8,128)S(1)} %broadcast_in_dim.205), channel_id=1, replica_groups=mesh['expert'=8,'hidden'=4] {'hidden'}, dimensions={0} | all-to-all | bytes 606208 | tf_op jit(solution)/shard_map/all_to_all | solution.py:611
  844.7 27.2 %all_to_all.147 = bf16[2,256,1024]{2,1,0:T(8,128)(2,1)} all-to-all(bf16[2,256,1024]{2,1,0:T(8,128)(2,1)} %bitcast.195), channel_id=1, replica_groups={{0,1},{2,3},{4,5},{6,7},{8,9},{10,11},{12,13},{14,15},{16,17},{18,19},{..., dimensions={0} | all-to-all | bytes 2097152 | tf_op jit(solution)/shard_map/all_to_all | solution.py:616
  879.4 9.3 all-to-all-done.20
  893.2 5.5 add_convert_fusion
  898.7 9.8 all-to-all-done.25
  914.3 5.8 collect_rows.5
  920.5 6.7 copy.154
  927.1 6.4 copy.155
  940.9 10.9 %collective-permute-done.3 = bf16[32,1024]{1,0:T(8,128)(2,1)S(1)} collective-permute-done((bf16[32,1024]{1,0:T(8,128)(2,1)S(1)}, bf16[32,1024]{1,0:T(8,128)(2,1)S(1)}, u32[]{:S(2)}, u32[]{:S(2)}) %collective-permute-start.3) | collective-permute-done | bytes 65568 | tf_op jit(solution)/shard_map/ppermute | solution.py:773
  959.1 13.6 %collective-permute-done.2 = bf16[384,256]{1,0:T(8,128)(2,1)S(1)} collective-permute-done((bf16[384,256]{1,0:T(8,128)(2,1)S(1)}, bf16[384,256]{1,0:T(8,128)(2,1)S(1)}, u32[]{:S(2)}, u32[]{:S(2)}) %collective-permute-start.2) | collective-permute-done | bytes 196640 | tf_op jit(solution)/shard_map/ppermute | solution.py:773
  986.5 12.9 %all-to-all-done.22 = bf16[8,384,256]{2,1,0:T(8,128)(2,1)} async-done(((bf16[8,384,256]{2,1,0:T(8,128)(2,1)}), bf16[8,384,256]{2,1,0:T(8,128)(2,1)}, u32[]{:S(2)}, u32[]{:S(2)}) %all-to-all-start.22) | async-done | bytes 1572896 | tf_op jit(solution)/shard_map/all_to_all | solution.py:611
  (237 shorter events, 191.9 us)
Async XLA Ops:
  8.6 11.9 %all-to-all-start.5 = ((s32[4,2,256,2]{2,1,3,0:T(2,128)}), s32[4,2,256,2]{2,1,3,0:T(2,128)S(1)}, u32[]{:S(2)}, u32[]{:S(2)}) async-start(s32[4,2,256,2]{2,1,3,0:T(2,128)} %broadcast_in_dim.180), calls=%async_computation.5 | async-start | bytes 32768 | tf_op jit(solution)/shard_map/all_to_all | solution.py:611
  21.2 11.3 %all-to-all-start.3 = ((bf16[4,32,1024]{2,1,0:T(8,128)(2,1)}), bf16[4,32,1024]{2,1,0:T(8,128)(2,1)S(1)}, u32[]{:S(2)}, u32[]{:S(2)}) async-start(bf16[4,32,1024]{2,1,0:T(8,128)(2,1)} %broadcast_in_dim.176), calls=%async_computation.3 | async-start | bytes 524288 | tf_op jit(solution)/shard_map/all_to_all | solution.py:611
  25.9 27.2 %copy-start.5 = (bf16[256,1024]{1,0:T(8,128)(2,1)}, bf16[256,1024]{1,0:T(8,128)(2,1)S(1)}, u32[]{:S(2)}) copy-start(bf16[256,1024]{1,0:T(8,128)(2,1)S(1)} %get-tuple-element.198.x_ref) | copy-start | bytes 1572868
  25.9 100.4 %copy-start.4 = (bf16[256,1024]{1,0:T(8,128)(2,1)}, bf16[256,1024]{1,0:T(8,128)(2,1)S(1)}, u32[]{:S(2)}) copy-start(bf16[256,1024]{1,0:T(8,128)(2,1)S(1)} %get-tuple-element.199.x_ref) | copy-start | bytes 1572868
  33.6 18.0 %all-to-all-start = ((bf16[2,256,1024]{2,1,0:T(8,128)(2,1)}), bf16[2,256,1024]{2,1,0:T(8,128)(2,1)S(1)}, u32[]{:S(2)}, u32[]{:S(2)}) async-start(bf16[2,256,1024]{2,1,0:T(8,128)(2,1)} %broadcast_in_dim.174), calls=%async_computation | async-start | bytes 2097152 | tf_op jit(solution)/shard_map/all_to_all | solution.py:611
  38.2 11.2 %collective-permute-start = (bf16[384,256]{1,0:T(8,128)(2,1)S(1)}, bf16[384,256]{1,0:T(8,128)(2,1)S(1)}, u32[]{:S(2)}, u32[]{:S(2)}) collective-permute-start(bf16[384,256]{1,0:T(8,128)(2,1)S(1)} %constant_dynamic-slice_fusion.3), channel_id=1, source_target_pairs={{0,2},{1,3},{2,0},{3,1},{4,6},{5,7},{6,4},{7,5},{8,10},{9,11},{10,... | collective-permute-start | bytes 589832 | tf_op jit(solution)/shard_map/ppermute | solution.py:664
  53.1 24.8 %all-to-all-start.1 = ((bf16[8,384,256]{2,1,0:T(8,128)(2,1)}), bf16[8,384,256]{2,1,0:T(8,128)(2,1)S(1)}, u32[]{:S(2)}, u32[]{:S(2)}) async-start(bf16[8,384,256]{2,1,0:T(8,128)(2,1)} %broadcast_in_dim.175), calls=%async_computation.1 | async-start | bytes 3145728 | tf_op jit(solution)/shard_map/all_to_all | solution.py:611
  56.8 113.9 %all-gather.12.cloned.1.call-start = ((), (), s32[]{:S(2)}) async-start(), calls=%async_computation.40 | async-start | bytes 2621440 | tf_op jit(solution)/shard_map/all_gather | solution.py:622
  59.4 24.0 %copy-start.31 = (bf16[32,4]{0,1:T(4,128)(2,1)S(1)}, bf16[32,4]{0,1:T(4,128)(2,1)}, u32[]{:S(2)}) copy-start(bf16[32,4]{0,1:T(4,128)(2,1)} %param.19) | copy-start | bytes 772
  59.4 25.2 %copy-start.29 = (bf16[1024]{0:T(1024)(128)(2,1)S(1)}, bf16[1024]{0:T(1024)(128)(2,1)}, u32[]{:S(2)}) copy-start(bf16[1024]{0:T(1024)(128)(2,1)} %param.20) | copy-start | bytes 6148
  59.4 25.8 %copy-start.30 = (bf16[1024]{0:T(1024)(128)(2,1)S(1)}, bf16[1024]{0:T(1024)(128)(2,1)}, u32[]{:S(2)}) copy-start(bf16[1024]{0:T(1024)(128)(2,1)} %param.21) | copy-start | bytes 6148
  59.4 26.4 %copy-start.26 = (s32[2,1,1024]{2,1,0:T(1,128)S(1)}, s32[2,1,1024]{2,1,0:T(1,128)}, u32[]{:S(2)}) copy-start(s32[2,1,1024]{2,1,0:T(1,128)} %param.15) | copy-start | bytes 24580
  79.7 34.7 %all-to-all-start.4 = ((bf16[8,4,32,1024]{3,2,1,0:T(8,128)(2,1)}), bf16[8,4,32,1024]{3,2,1,0:T(8,128)(2,1)S(1)}, u32[]{:S(2)}, u32[]{:S(2)}) async-start(bf16[8,4,32,1024]{3,2,1,0:T(8,128)(2,1)} %broadcast_in_dim.177), calls=%async_computation.4 | async-start | bytes 4194304 | tf_op jit(solution)/shard_map/all_to_all | solution.py:611
  83.3 5.4 collective-permute-start.1
  114.4 12.0 %all-to-all-start.2 = ((bf16[2,256,512]{2,1,0:T(8,128)(2,1)}), bf16[2,256,512]{2,1,0:T(8,128)(2,1)S(1)}, u32[]{:S(2)}, u32[]{:S(2)}) async-start(bf16[2,256,512]{2,1,0:T(8,128)(2,1)} %bitcast.197), calls=%async_computation.2 | async-start | bytes 1048576 | tf_op jit(solution)/shard_map/all_to_all | solution.py:616
  127.5 16.8 %all-to-all-start.9 = ((bf16[2,256,1024]{2,1,0:T(8,128)(2,1)}), bf16[2,256,1024]{2,1,0:T(8,128)(2,1)S(1)}, u32[]{:S(2)}, u32[]{:S(2)}) async-start(bf16[2,256,1024]{2,1,0:T(8,128)(2,1)} %broadcast_in_dim.191), calls=%async_computation.9 | async-start | bytes 2097152 | tf_op jit(solution)/shard_map/all_to_all | solution.py:611
  131.1 64.6 %all-gather.6.cloned.1.call-start = ((), (), s32[]{:S(2)}) async-start(), calls=%async_computation.33 | async-start | bytes 2621440 | tf_op jit(solution)/shard_map/all_gather | solution.py:622
  144.3 22.3 %all-to-all-start.8 = ((s32[8,1,640]{2,1,0:T(1,128)}), s32[8,1,640]{2,1,0:T(1,128)S(1)}, u32[]{:S(2)}, u32[]{:S(2)}) async-start(s32[8,1,640]{2,1,0:T(1,128)} %reshape.407), calls=%async_computation.8 | async-start | bytes 40960 | tf_op jit(solution)/shard_map/all_to_all | solution.py:607
  166.6 19.9 %all-to-all-start.10 = ((bf16[2,256,512]{2,1,0:T(8,128)(2,1)}), bf16[2,256,512]{2,1,0:T(8,128)(2,1)S(1)}, u32[]{:S(2)}, u32[]{:S(2)}) async-start(bf16[2,256,512]{2,1,0:T(8,128)(2,1)} %bitcast.198), calls=%async_computation.10 | async-start | bytes 1048576 | tf_op jit(solution)/shard_map/all_to_all | solution.py:616
  187.3 65.0 %all-to-all-start.7 = ((bf16[8,320,1024]{2,1,0:T(8,128)(2,1)}), bf16[8,320,1024]{2,1,0:T(8,128)(2,1)}, u32[]{:S(2)}, u32[]{:S(2)}) async-start(bf16[8,320,1024]{2,1,0:T(8,128)(2,1)} %bitcast.173), calls=%async_computation.7 | async-start | bytes 10485760 | tf_op jit(solution)/shard_map/all_to_all | solution.py:607
  192.0 50.3 %all-gather.8.cloned.1.call-start = ((), (), s32[]{:S(2)}) async-start(), calls=%async_computation.34 | async-start | bytes 2621440 | tf_op jit(solution)/shard_map/all_gather | solution.py:622
  252.3 65.0 %all-to-all-start.11 = ((bf16[8,320,1024]{2,1,0:T(8,128)(2,1)}), bf16[8,320,1024]{2,1,0:T(8,128)(2,1)}, u32[]{:S(2)}, u32[]{:S(2)}) async-start(bf16[8,320,1024]{2,1,0:T(8,128)(2,1)} %bitcast.174), calls=%async_computation.11 | async-start | bytes 10485760 | tf_op jit(solution)/shard_map/all_to_all | solution.py:607
  257.0 48.5 %all-gather.10.cloned.1.call-start = ((), (), s32[]{:S(2)}) async-start(), calls=%async_computation.35 | async-start | bytes 2621440 | tf_op jit(solution)/shard_map/all_gather | solution.py:622
  317.3 65.0 %all-to-all-start.12 = ((bf16[8,320,1024]{2,1,0:T(8,128)(2,1)}), bf16[8,320,1024]{2,1,0:T(8,128)(2,1)}, u32[]{:S(2)}, u32[]{:S(2)}) async-start(bf16[8,320,1024]{2,1,0:T(8,128)(2,1)} %bitcast.175), calls=%async_computation.12 | async-start | bytes 10485760 | tf_op jit(solution)/shard_map/all_to_all | solution.py:607
  382.4 65.7 %all-to-all-start.6 = ((bf16[8,320,1024]{2,1,0:T(8,128)(2,1)}), bf16[8,320,1024]{2,1,0:T(8,128)(2,1)}, u32[]{:S(2)}, u32[]{:S(2)}) async-start(bf16[8,320,1024]{2,1,0:T(8,128)(2,1)} %bitcast.172), calls=%async_computation.6 | async-start | bytes 10485760 | tf_op jit(solution)/shard_map/all_to_all | solution.py:607
  448.1 65.0 %all-to-all-start.13 = ((bf16[8,320,1024]{2,1,0:T(8,128)(2,1)}), bf16[8,320,1024]{2,1,0:T(8,128)(2,1)}, u32[]{:S(2)}, u32[]{:S(2)}) async-start(bf16[8,320,1024]{2,1,0:T(8,128)(2,1)} %bitcast.179), calls=%async_computation.13 | async-start | bytes 10485760 | tf_op jit(solution)/shard_map/all_to_all | solution.py:607
  513.1 65.0 %all-to-all-start.16 = ((bf16[8,320,1024]{2,1,0:T(8,128)(2,1)}), bf16[8,320,1024]{2,1,0:T(8,128)(2,1)}, u32[]{:S(2)}, u32[]{:S(2)}) async-start(bf16[8,320,1024]{2,1,0:T(8,128)(2,1)} %bitcast.180), calls=%async_computation.18 | async-start | bytes 10485760 | tf_op jit(solution)/shard_map/all_to_all | solution.py:607
  578.1 65.0 %all-to-all-start.14 = ((bf16[8,320,1024]{2,1,0:T(8,128)(2,1)}), bf16[8,320,1024]{2,1,0:T(8,128)(2,1)}, u32[]{:S(2)}, u32[]{:S(2)}) async-start(bf16[8,320,1024]{2,1,0:T(8,128)(2,1)} %bitcast.178), calls=%async_computation.14 | async-start | bytes 10485760 | tf_op jit(solution)/shard_map/all_to_all | solution.py:607
  582.8 51.2 %reduce-scatter.11.cloned.1.call-start = ((), (), s32[]{:S(2)}) async-start(), calls=%async_computation.39 | async-start | bytes 2621440 | tf_op jit(solution)/shard_map/reduce_scatter | solution.py:625
  643.1 10.3 %all-to-all-start.19 = ((bf16[2,256,512]{2,1,0:T(8,128)(2,1)}), bf16[2,256,512]{2,1,0:T(8,128)(2,1)S(1)}, u32[]{:S(2)}, u32[]{:S(2)}) async-start(bf16[2,256,512]{2,1,0:T(8,128)(2,1)} %get-tuple-element.89), calls=%async_computation.23 | async-start | bytes 1048576 | tf_op jit(solution)/shard_map/all_to_all | solution.py:616
  646.6 49.3 %reduce-scatter.9.cloned.1.call-start = ((), (), s32[]{:S(2)}) async-start(), calls=%async_computation.38 | async-start | bytes 2621440 | tf_op jit(solution)/shard_map/reduce_scatter | solution.py:625
  654.2 65.5 %all-to-all-start.15 = ((bf16[8,320,1024]{2,1,0:T(8,128)(2,1)}), bf16[8,320,1024]{2,1,0:T(8,128)(2,1)}, u32[]{:S(2)}, u32[]{:S(2)}) async-start(bf16[8,320,1024]{2,1,0:T(8,128)(2,1)} %bitcast.177), calls=%async_computation.16 | async-start | bytes 10485760 | tf_op jit(solution)/shard_map/all_to_all | solution.py:607
  659.0 41.2 %copy-start.27 = (f32[1,1024]{1,0:T(1,128)S(1)}, f32[1,1024]{1,0:T(1,128)}, u32[]{:S(2)}) copy-start(f32[1,1024]{1,0:T(1,128)} %get-tuple-element.115) | copy-start | bytes 12292
  719.7 42.1 %all-to-all-start.17 = ((bf16[2,256,512]{2,1,0:T(8,128)(2,1)}), bf16[2,256,512]{2,1,0:T(8,128)(2,1)S(1)}, u32[]{:S(2)}, u32[]{:S(2)}) async-start(bf16[2,256,512]{2,1,0:T(8,128)(2,1)} %get-tuple-element.84), calls=%async_computation.20 | async-start | bytes 1048576 | tf_op jit(solution)/shard_map/all_to_all | solution.py:616
  723.2 38.6 %copy-start.19 = (bf16[256,1024]{1,0:T(8,128)(2,1)S(1)}, bf16[256,1024]{1,0:T(8,128)(2,1)}, u32[]{:S(2)}) copy-start(bf16[256,1024]{1,0:T(8,128)(2,1)} %get-tuple-element.93) | copy-start | bytes 1572868
  762.9 25.2 %all-to-all-start.23 = ((bf16[2,256,1024]{2,1,0:T(8,128)(2,1)}), bf16[2,256,1024]{2,1,0:T(8,128)(2,1)S(1)}, u32[]{:S(2)}, u32[]{:S(2)}) async-start(bf16[2,256,1024]{2,1,0:T(8,128)(2,1)} %broadcast_in_dim.195), calls=%async_computation.27 | async-start | bytes 2097152 | tf_op jit(solution)/shard_map/all_to_all | solution.py:611
  766.7 20.6 %copy-start.28 = (f32[1,1024]{1,0:T(1,128)S(1)}, f32[1,1024]{1,0:T(1,128)}, u32[]{:S(2)}) copy-start(f32[1,1024]{1,0:T(1,128)} %get-tuple-element.113) | copy-start | bytes 12292
  803.5 21.8 %all-to-all-start.24 = ((bf16[2,256,1024]{2,1,0:T(8,128)(2,1)}), bf16[2,256,1024]{2,1,0:T(8,128)(2,1)}, u32[]{:S(2)}, u32[]{:S(2)}) async-start(bf16[2,256,1024]{2,1,0:T(8,128)(2,1)} %broadcast_in_dim.196), calls=%async_computation.28 | async-start | bytes 2097152 | tf_op jit(solution)/shard_map/all_to_all | solution.py:611
  807.9 175.0 %reduce-scatter.5.cloned.1.call-start = ((), (), s32[]{:S(2)}) async-start(), calls=%async_computation.36 | async-start | bytes 2621440 | tf_op jit(solution)/shard_map/reduce_scatter | solution.py:625
  844.7 33.0 %copy-start.20 = (bf16[512,512]{1,0:T(8,128)(2,1)S(1)}, bf16[512,512]{1,0:T(8,128)(2,1)}, u32[]{:S(2)}) copy-start(bf16[512,512]{1,0:T(8,128)(2,1)} %get-tuple-element.66) | copy-start | bytes 1572868
  871.9 16.8 %all-to-all-start.20 = ((bf16[2,256,1024]{2,1,0:T(8,128)(2,1)}), bf16[2,256,1024]{2,1,0:T(8,128)(2,1)S(1)}, u32[]{:S(2)}, u32[]{:S(2)}) async-start(bf16[2,256,1024]{2,1,0:T(8,128)(2,1)} %bitcast.60), calls=%async_computation.24 | async-start | bytes 2097152 | tf_op jit(solution)/shard_map/all_to_all | solution.py:616
  889.7 18.9 %all-to-all-start.25 = ((bf16[8,2,32,1024]{3,2,1,0:T(8,128)(2,1)}), bf16[8,2,32,1024]{3,2,1,0:T(8,128)(2,1)S(1)}, u32[]{:S(2)}, u32[]{:S(2)}) async-start(bf16[8,2,32,1024]{3,2,1,0:T(8,128)(2,1)} %bitcast.166), calls=%async_computation.29 | async-start | bytes 2097152 | tf_op jit(solution)/shard_map/all_to_all | solution.py:607
  909.5 42.4 %all-to-all-start.21 = ((bf16[8,2,384,256]{3,2,1,0:T(8,128)(2,1)}), bf16[8,2,384,256]{3,2,1,0:T(8,128)(2,1)}, u32[]{:S(2)}, u32[]{:S(2)}) async-start(bf16[8,2,384,256]{3,2,1,0:T(8,128)(2,1)} %add_convert_fusion), calls=%async_computation.25 | async-start | bytes 6291456 | tf_op jit(solution)/shard_map/all_to_all | solution.py:607
  914.0 70.1 %reduce-scatter.7.cloned.1.call-start = ((), (), s32[]{:S(2)}) async-start(), calls=%async_computation.37 | async-start | bytes 2621440 | tf_op jit(solution)/shard_map/reduce_scatter | solution.py:625
  940.7 11.1 %collective-permute-start.3 = (bf16[32,1024]{1,0:T(8,128)(2,1)S(1)}, bf16[32,1024]{1,0:T(8,128)(2,1)S(1)}, u32[]{:S(2)}, u32[]{:S(2)}) collective-permute-start(bf16[32,1024]{1,0:T(8,128)(2,1)S(1)} %fusion.32), channel_id=1, source_target_pairs={{0,2},{1,3},{2,0},{3,1},{4,6},{5,7},{6,4},{7,5},{8,10},{9,11},{10,... | collective-permute-start | bytes 196616 | tf_op jit(solution)/shard_map/ppermute | solution.py:773
  952.8 20.0 %all-to-all-start.26 = ((bf16[8,32,1024]{2,1,0:T(8,128)(2,1)}), bf16[8,32,1024]{2,1,0:T(8,128)(2,1)S(1)}, u32[]{:S(2)}, u32[]{:S(2)}) async-start(bf16[8,32,1024]{2,1,0:T(8,128)(2,1)} %broadcast_in_dim.197), calls=%async_computation.30 | async-start | bytes 1048576 | tf_op jit(solution)/shard_map/all_to_all | solution.py:611
  959.0 13.7 %collective-permute-start.2 = (bf16[384,256]{1,0:T(8,128)(2,1)S(1)}, bf16[384,256]{1,0:T(8,128)(2,1)S(1)}, u32[]{:S(2)}, u32[]{:S(2)}) collective-permute-start(bf16[384,256]{1,0:T(8,128)(2,1)S(1)} %fusion.29), channel_id=1, source_target_pairs={{0,2},{1,3},{2,0},{3,1},{4,6},{5,7},{6,4},{7,5},{8,10},{9,11},{10,... | collective-permute-start | bytes 589832 | tf_op jit(solution)/shard_map/ppermute | solution.py:773
  974.0 25.3 %all-to-all-start.22 = ((bf16[8,384,256]{2,1,0:T(8,128)(2,1)}), bf16[8,384,256]{2,1,0:T(8,128)(2,1)}, u32[]{:S(2)}, u32[]{:S(2)}) async-start(bf16[8,384,256]{2,1,0:T(8,128)(2,1)} %broadcast_in_dim.194), calls=%async_computation.26 | async-start | bytes 3145728 | tf_op jit(solution)/shard_map/all_to_all | solution.py:611
  (22 other events, 136.2 us)
Sparse Core Ops, SparseCore 0:
  59.8 46.6 all-gather.11
  135.0 49.7 all-gather.5
  195.9 46.2 all-gather.7
  259.1 46.3 all-gather.9
  589.7 44.2 reduce-scatter.10
  653.5 42.3 reduce-scatter.8
  813.9 57.7 reduce-scatter.4
  920.3 44.0 reduce-scatter.6

commit v4 on v3

--- a/solution.py
+++ b/solution.py
@@ -413,93 +413,178 @@
     )(rows, place)
 
 
+def bits_of(count):
+    return [1 << b for b in range(count.bit_length() - 1)]
+
+
+def partner_of(me, step, count):
+    found = 0
+    for bit in bits_of(count):
+        found = found + bit * lax.rem(me // bit + step // bit, 2)
+    return found
+
+
 def expert_kernel(
-    x_ref, dy_ref, pair_ref, wr_ref, wg_ref, wu_ref, wd_ref,
-    y_ref, dx_ref, g_ref, hid_ref, dga_ref, dup_ref, dlog_ref,
+    sent_ref, dy_ref, pair_ref, wr_ref, wg_ref, wu_ref, wd_ref,
+    back_ref, y_ref, x_ref, g_ref, hid_ref, dga_ref, dup_ref, dlog_ref,
+    got_ref, dx_ref, stage_ref, x_send, x_recv, dx_send, dx_recv, own_sem, stage_sem,
 ):
-    sources, _, cap, width = x_ref.shape
-    rows = sources * cap
-    x = x_ref[...].reshape(rows, width)
-    dy = dy_ref[...].reshape(rows, width).astype(F32)
-    pair = pair_ref[...].reshape(rows, pair_ref.shape[3])
-    margin = jnp.sum(mm(x, wr_ref[...]) * pair, axis=-1, keepdims=True)
-    own_gate = 1.0 / (1.0 + jnp.exp(-margin))
-    other_gate = 1.0 / (1.0 + jnp.exp(margin))
-    g = (own_gate * dy).astype(BF16)
-    g_ref[0] = g
-    gate = mm(x, wg_ref[0])
-    up = mm(x, wu_ref[0])
-    square = gate * gate
-    bent = jnp.tanh(GELU_C * gate * (1.0 + GELU_A * square))
-    half_gate = 0.5 * gate
-    gelu = half_gate * (1.0 + bent)
-    slope = 0.5 * (1.0 + bent) + half_gate * (1.0 - bent * bent) * (
-        GELU_C * (1.0 + 3.0 * GELU_A * square)
-    )
-    hid = (gelu * up).astype(BF16)
-    dhid = mm_nt(g, wd_ref[0])
-    dga = (dhid * (up * slope)).astype(BF16)
-    dup = (dhid * gelu).astype(BF16)
-    hid_ref[0] = hid
-    dga_ref[0] = dga
-    dup_ref[0] = dup
-    y = mm(hid, wd_ref[0])
-    dgate = jnp.sum(y * dy, axis=-1, keepdims=True)
-    y_ref[...] = (y * own_gate).astype(BF16).reshape(sources, 1, cap, width)
-    dlog = (dgate * own_gate * other_gate * pair).astype(BF16)
-    dlog_ref[0] = dlog
-    dx = mm_nt(dga, wg_ref[0]) + mm_nt(dup, wu_ref[0]) + mm_nt(dlog, wr_ref[...])
-    dx_ref[...] = dx.astype(BF16).reshape(sources, 1, cap, width)
-
-
-def expert_pass(x, dy, pair, wr, wg, wu, wd):
-    sources, experts, cap, width = x.shape
+    devices, experts, cap, width = sent_ref.shape
+    step = pl.program_id(0)
+    me = lax.axis_index("expert")
+    line = lax.axis_index("hidden")
+
+    def x_copy(s):
+        peer = partner_of(me, s, devices)
+        return pltpu.make_async_remote_copy(
+            src_ref=sent_ref.at[peer], dst_ref=got_ref.at[s], send_sem=x_send.at[s],
+            recv_sem=x_recv.at[s], device_id=(peer, line), device_id_type=pl.DeviceIdType.MESH,
+        )
+
+    def dx_copy(s):
+        peer = partner_of(me, s, devices)
+        return pltpu.make_async_remote_copy(
+            src_ref=dx_ref.at[s], dst_ref=back_ref.at[me], send_sem=dx_send.at[s],
+            recv_sem=dx_recv.at[s], device_id=(peer, line), device_id_type=pl.DeviceIdType.MESH,
+        )
+
+    def y_copy(s):
+        source = partner_of(me, s, devices)
+        slot = lax.rem(s, 2)
+        return pltpu.make_async_copy(stage_ref.at[slot], y_ref.at[source], stage_sem.at[slot])
+
+    def work(s):
+        source = partner_of(me, s, devices)
+        slot = lax.rem(s, 2)
+        for e in range(experts):
+            x = got_ref[s, e]
+            dy = dy_ref[source, e].astype(F32)
+            pair = pair_ref[source, e].astype(F32)
+            margin = jnp.sum(mm(x, wr_ref[...]) * pair, axis=-1, keepdims=True)
+            own_gate = 1.0 / (1.0 + jnp.exp(-margin))
+            other_gate = 1.0 / (1.0 + jnp.exp(margin))
+            g = (own_gate * dy).astype(BF16)
+            x_ref[0, e] = x
+            g_ref[0, e] = g
+            gate = mm(x, wg_ref[e])
+            up = mm(x, wu_ref[e])
+            square = gate * gate
+            bent = jnp.tanh(GELU_C * gate * (1.0 + GELU_A * square))
+            half_gate = 0.5 * gate
+            gelu = half_gate * (1.0 + bent)
+            slope = 0.5 * (1.0 + bent) + half_gate * (1.0 - bent * bent) * (
+                GELU_C * (1.0 + 3.0 * GELU_A * square)
+            )
+            hid = (gelu * up).astype(BF16)
+            dhid = mm_nt(g, wd_ref[e])
+            dga = (dhid * (up * slope)).astype(BF16)
+            dup = (dhid * gelu).astype(BF16)
+            hid_ref[0, e] = hid
+            dga_ref[0, e] = dga
+            dup_ref[0, e] = dup
+            y = mm(hid, wd_ref[e])
+            dgate = jnp.sum(y * dy, axis=-1, keepdims=True)
+            stage_ref[slot, e] = (y * own_gate).astype(BF16)
+            dlog = (dgate * own_gate * other_gate * pair).astype(BF16)
+            dlog_ref[0, e] = dlog
+            dx = mm_nt(dga, wg_ref[e]) + mm_nt(dup, wu_ref[e]) + mm_nt(dlog, wr_ref[...])
+            dx_ref[s, e] = dx.astype(BF16)
+
+    @pl.when(step == 0)
+    def _():
+        barrier = pltpu.get_barrier_semaphore()
+        for s in range(1, devices):
+            pl.semaphore_signal(
+                barrier, inc=1, device_id=(partner_of(me, s, devices), line),
+                device_id_type=pl.DeviceIdType.MESH,
+            )
+        pl.semaphore_wait(barrier, devices - 1)
+        for s in range(devices - 1, 0, -1):
+            x_copy(s).start()
+        own = pltpu.make_async_copy(sent_ref.at[me], got_ref.at[0], own_sem)
+        own.start()
+        own.wait()
+
+    @pl.when(step > 0)
+    def _():
+        x_copy(step).wait_recv()
+
+    @pl.when(step > 1)
+    def _():
+        y_copy(step - 2).wait()
+
+    work(step)
+    y_copy(step).start()
+
+    @pl.when(step > 0)
+    def _():
+        dx_copy(step).start()
+
+    @pl.when(step == devices - 1)
+    def _():
+        own = pltpu.make_async_copy(dx_ref.at[0], back_ref.at[me], own_sem)
+        own.start()
+        own.wait()
+        y_copy(devices - 2).wait()
+        y_copy(devices - 1).wait()
+        for s in range(1, devices):
+            x_copy(s).wait_send()
+            dx_copy(s).wait_send()
+            dx_copy(s).wait_recv()
+
+
+def expert_pass(sent, dy, pair, wr, wg, wu, wd, identity):
+    devices, experts, cap, width = sent.shape
     hidden = wg.shape[2]
     choices = wr.shape[1]
-    group = 2 if sources % 2 == 0 else 1
-    rows = sources * cap
-    tokens = pl.BlockSpec((group, 1, cap, width), lambda e, s: (s, e, 0, 0))
-    wide = pl.BlockSpec((1, width, hidden), lambda e, s: (e, 0, 0))
-    tall = pl.BlockSpec((1, hidden, width), lambda e, s: (e, 0, 0))
-
-    def acts(cols):
-        return pl.BlockSpec((1, group * cap, cols), lambda e, s: (e, s, 0))
-
-    def act_shape(cols):
-        return jax.ShapeDtypeStruct((experts, rows, cols), BF16)
-
+    any_space = pl.BlockSpec(memory_space=pl.ANY)
+
+    def whole(shape):
+        return pl.BlockSpec(shape, lambda s: (0,) * len(shape), pipeline_mode=pl.Buffered(1))
+
+    def block(cols):
+        return pl.BlockSpec((1, experts, cap, cols), lambda s: (s, 0, 0, 0))
+
+    def kept(cols):
+        return jax.ShapeDtypeStruct((devices, experts, cap, cols), BF16)
+
+    rows = devices * cap
     return pl.pallas_call(
         expert_kernel,
-        grid=(experts, sources // group),
+        grid=(devices,),
         out_shape=(
-            jax.ShapeDtypeStruct(x.shape, BF16),
-            jax.ShapeDtypeStruct(x.shape, BF16),
-            act_shape(width),
-            act_shape(hidden),
-            act_shape(hidden),
-            act_shape(hidden),
-            act_shape(choices),
+            kept(width), kept(width), kept(width), kept(width), kept(hidden), kept(hidden),
+            kept(hidden), kept(choices),
         ),
         in_specs=[
-            tokens,
-            tokens,
-            pl.BlockSpec((group, 1, cap, choices), lambda e, s: (s, e, 0, 0)),
-            pl.BlockSpec((width, choices), lambda e, s: (0, 0)),
-            wide,
-            wide,
-            tall,
+            any_space, whole(dy.shape), whole(pair.shape), whole(wr.shape), whole(wg.shape),
+            whole(wu.shape), whole(wd.shape),
         ],
         out_specs=(
-            tokens, tokens, acts(width), acts(hidden), acts(hidden), acts(hidden), acts(choices)
-        ),
-        compiler_params=pltpu.CompilerParams(vmem_limit_bytes=VMEM_LIMIT),
+            any_space, any_space, block(width), block(width), block(hidden), block(hidden),
+            block(hidden), block(choices),
+        ),
+        scratch_shapes=[
+            pltpu.VMEM((devices, experts, cap, width), BF16),
+            pltpu.VMEM((devices, experts, cap, width), BF16),
+            pltpu.VMEM((2, experts, cap, width), BF16),
+            pltpu.SemaphoreType.DMA((devices,)),
+            pltpu.SemaphoreType.DMA((devices,)),
+            pltpu.SemaphoreType.DMA((devices,)),
+            pltpu.SemaphoreType.DMA((devices,)),
+            pltpu.SemaphoreType.DMA,
+            pltpu.SemaphoreType.DMA((2,)),
+        ],
+        compiler_params=pltpu.CompilerParams(
+            vmem_limit_bytes=VMEM_LIMIT, collective_id=identity, has_side_effects=True
+        ),
         cost_estimate=pl.CostEstimate(
             flops=12 * experts * rows * width * hidden,
-            bytes_accessed=10 * experts * rows * width + 6 * experts * hidden * (width + rows),
+            bytes_accessed=80 * experts * rows * width,
             transcendentals=experts * rows * hidden,
         ),
         name="expert_pass",
-    )(x, dy, pair, wr, wg, wu, wd)
+    )(sent, dy, pair, wr, wg, wu, wd)
 
 
 def weight_kernel(*refs):
@@ -507,13 +592,15 @@
     dwr_ref, dwg_ref, dwu_ref, dwd_ref = refs[-4:]
     totals = [0.0, 0.0, 0.0, 0.0]
     for index in range(count):
-        x_ref, g_ref, hid_ref, dga_ref, dup_ref, dlog_ref = refs[6 * index : 6 * index + 6]
-        sources, _, cap, width = x_ref.shape
-        x = x_ref[...].reshape(sources * cap, width)
-        totals[0] = totals[0] + mm_tn(x, dlog_ref[0])
-        totals[1] = totals[1] + mm_tn(x, dga_ref[0])
-        totals[2] = totals[2] + mm_tn(x, dup_ref[0])
-        totals[3] = totals[3] + mm_tn(hid_ref[0], g_ref[0])
+        blocks = [
+            ref[...].reshape(ref.shape[0] * ref.shape[2], ref.shape[3])
+            for ref in refs[6 * index : 6 * index + 6]
+        ]
+        x, g, hid, dga, dup, dlog = blocks
+        totals[0] = totals[0] + mm_tn(x, dlog)
+        totals[1] = totals[1] + mm_tn(x, dga)
+        totals[2] = totals[2] + mm_tn(x, dup)
+        totals[3] = totals[3] + mm_tn(hid, g)
     dwr_ref[0] = totals[0]
     dwg_ref[0] = totals[1]
     dwu_ref[0] = totals[2]
@@ -522,13 +609,13 @@
 
 def weight_pass(kept):
     sources, experts, cap, width = kept[0][0].shape
-    rows, hidden = kept[0][2].shape[1:]
-    choices = kept[0][5].shape[2]
+    hidden = kept[0][2].shape[3]
+    choices = kept[0][5].shape[3]
+    rows = sources * cap
     block = 256 if width % 256 == 0 else width
     tokens = pl.BlockSpec((sources, 1, cap, block), lambda e, j: (0, e, 0, j))
-    grads = pl.BlockSpec((1, rows, block), lambda e, j: (e, 0, j))
-    acts = pl.BlockSpec((1, rows, hidden), lambda e, j: (e, 0, 0))
-    logs = pl.BlockSpec((1, rows, choices), lambda e, j: (e, 0, 0))
+    acts = pl.BlockSpec((sources, 1, cap, hidden), lambda e, j: (0, e, 0, 0))
+    logs = pl.BlockSpec((sources, 1, cap, choices), lambda e, j: (0, e, 0, 0))
     operands = []
     for arrays in kept:
         operands.extend(arrays)
@@ -541,7 +628,7 @@
             jax.ShapeDtypeStruct((experts, width, hidden), F32),
             jax.ShapeDtypeStruct((experts, hidden, width), F32),
         ),
-        in_specs=[tokens, grads, acts, acts, acts, logs] * len(kept),
+        in_specs=[tokens, tokens, acts, acts, acts, logs] * len(kept),
         out_specs=(
             pl.BlockSpec((1, block, choices), lambda e, j: (e, j, 0)),
             pl.BlockSpec((1, block, hidden), lambda e, j: (e, j, 0)),
@@ -686,20 +773,25 @@
         kept["h1"], kept["xn2"] = project(part_ref, own_heads, all_out, x_in[micro, 0], moe_gain_f)
 
     def spread(rows, micro):
-        sent = spread_rows(rows, place_rows[micro], expert_count, capacity, shard_len)
-        return sent.reshape(flat_shape)
-
-    def experts(micro, kept):
-        y, dx, g, hid, dga, dup, dlog = expert_pass(
-            kept["x"], kept["dy"], pairs[micro], router_weight, gate_weight, up_weight, down_weight
+        return spread_rows(rows, place_rows[micro], expert_count, capacity, shard_len)
+
+    def send_dy(micro, kept):
+        sent = spread(kept["dy_all"], micro).reshape(flat_shape)
+        kept["dy"] = exchange(sent).reshape(token_shape)
+
+    def experts(micro, kept, *behind):
+        sent = spread(kept["xn2_all"], micro).reshape(token_shape)
+        back, y, x, g, hid, dga, dup, dlog = expert_pass(
+            after(sent, *behind), kept["dy"], pairs[micro], router_weight, gate_weight, up_weight,
+            down_weight, 1 + micro,
         )
-        kept["weights"] = (kept["x"], g, hid, dga, dup, dlog)
+        kept["weights"] = (x, g, hid, dga, dup, dlog)
         kept["y_sent"] = y.reshape(flat_shape)
-        kept["dx_sent"] = dx.reshape(flat_shape)
+        kept["dx_back"] = back.reshape(place_shape)
 
     def combine(micro, kept):
-        part_sum = collect_rows(kept["dx_back"], place_cols[micro], shard_len)
-        kept["dxn2"] = scatter(part_sum)
+        kept["dx_part"] = collect_rows(kept["dx_back"], place_cols[micro], shard_len)
+        kept["dxn2"] = scatter(kept["dx_part"])
 
     def attention_back(micro, kept):
         dh1, dattn, dheads, kept["moe_gain_grad"] = turn(
@@ -726,35 +818,29 @@
         mixed = scatter(collect_rows(kept["y_back"], place_cols[micro], shard_len))
         kept["block_out"] = (kept["h1"] + mixed.astype(F32)).astype(BF16)
 
-    first, last = states[0], states[-1]
-    for micro in range(micro_count):
-        pair_x(micro, states[micro])
-    first["dy_all"] = gather(cotangent[0, 0])
-    attention(0, first)
-    first["dy"] = exchange(spread(first["dy_all"], 0)).reshape(token_shape)
-    first["xn2_all"] = gather(first["xn2"])
-    first["x"] = exchange(spread(first["xn2_all"], 0)).reshape(token_shape)
-    behind = first["xn2_all"]
-    for micro in range(1, micro_count):
-        state = states[micro]
-        attention(micro, state)
-        state["xn2_all"] = gather(after(state["xn2"], behind))
-        state["x"] = exchange(spread(state["xn2_all"], micro)).reshape(token_shape)
-        state["dy_all"] = gather(after(cotangent[micro, 0], state["xn2_all"]))
-        state["dy"] = exchange(spread(state["dy_all"], micro)).reshape(token_shape)
-        behind = state["dy_all"]
+    last = states[-1]
+    behind = ()
     for micro in range(micro_count):
         state = states[micro]
-        experts(micro, state)
-        sent = state["dx_sent"]
-        if micro + 1 < micro_count:
-            sent = after(sent, states[micro + 1]["dy"])
-        state["dx_back"] = exchange(sent).reshape(place_shape)
+        pair_x(micro, state)
+        state["dy_all"] = gather(after(cotangent[micro, 0], *behind))
+        send_dy(micro, state)
+        behind = (state["dy_all"],)
+    for micro in range(micro_count):
+        state = states[micro]
+        state["x_half"] = after(state["x_half"], state["dy_all"])
+        attention(micro, state)
+        state["xn2_all"] = gather(after(state["xn2"], *behind))
+        behind = (state["xn2_all"],)
+    behind = ()
+    for micro in range(micro_count):
+        experts(micro, states[micro], *behind)
+        combine(micro, states[micro])
+        behind = (states[micro]["dx_part"],)
     for micro in range(micro_count):
         state = states[micro]
         state["y_back"] = exchange(after(state["y_sent"], last["dx_back"])).reshape(place_shape)
     for micro in range(micro_count):
-        combine(micro, states[micro])
         attention_back(micro, states[micro])
     for micro in range(micro_count):
         finish(micro, states[micro])

time: 1020 us -> 1050 us (1.029)
  Pallas kernels: 251 us -> 459 us
  waiting for transfers between devices: 480 us -> 325 us
  starting transfers between devices: 110 us -> 94.3 us
  blocking collectives: 60.8 us -> 45.2 us
    pallas_call x2, Pallas kernels: 71.5 us -> 280 us  [expert_pass(): pl.pallas_call(expert_kernel, grid=(devices,), out_shape=(kept(width), ke...]
    all_to_all x11 -> x7, waiting for transfers between devices: 178 us -> 72.5 us  [exchange(): lax.all_to_all(buffer, 'expert', split_axis=0, concat_axis=0, tiled=True)]
    all_gather x4, waiting for transfers between devices: 94.4 us -> 30.6 us  [gather(): return lax.all_gather(values, 'hidden', axis=0, tiled=True)]
    reduce_scatter x4, waiting for transfers between devices: 81.3 us -> 43.9 us  [scatter(): lax.psum_scatter(values.astype(BF16), 'hidden', scatter_dimension=0, tile...]
    ppermute x1, waiting for transfers between devices: 11.2 us -> 30.3 us  [shards(): lax.ppermute(my_piece(qkv_weight.reshape(3 * width, head_cols)), 'hidden'...]
    all_to_all x10, waiting for transfers between devices: 63.9 us -> 82.8 us  [to_all(): lax.all_to_all(copies, axis, split_axis=0, concat_axis=0, tiled=True, axi...]
    all_to_all x1, blocking collectives: 27.2 us -> 10.9 us  [swap_half(): lax.all_to_all(buffer, 'hidden', split_axis=0, concat_axis=0, tiled=True,...]
    all_to_all x11 -> x7, starting transfers between devices: 50 us -> 34.7 us  [exchange(): lax.all_to_all(buffer, 'expert', split_axis=0, concat_axis=0, tiled=True)]
  transfers between devices with their start and end apart: 38 -> 34, of which waited for: 26 -> 21; matrix products, arithmetic and copies ran while one was open for 8% -> 8% of each run, Pallas kernels for 25% -> 44%
where the time goes in v4:
time: 1050 us; the launch traced here: 1040 us
  Pallas kernels  459 us (44%)
  waiting for transfers between devices  325 us (31%)
  starting transfers between devices  94.3 us (9%)
  local copies, waits for them, and re-layouts  62.9 us (6%)
  blocking collectives  45.2 us (4%)
  other arithmetic  33.7 us (3%)
  between operations  15.3 us (1%)
    pallas_call x2, Pallas kernels, expert_pass(): pl.pallas_call(expert_kernel, grid=(devices,), out_shape=(kept(width), ke...  280 us
    all_to_all x10, waiting for transfers between devices, to_all(): lax.all_to_all(copies, axis, split_axis=0, concat_axis=0, tiled=True, axi...  82.8 us
    all_to_all x7, waiting for transfers between devices, exchange(): lax.all_to_all(buffer, 'expert', split_axis=0, concat_axis=0, tiled=True)  72.5 us
    reduce_scatter x4, waiting for transfers between devices, scatter(): lax.psum_scatter(values.astype(BF16), 'hidden', scatter_dimension=0, tile...  43.9 us
    all_to_all x10, starting transfers between devices, to_all(): lax.all_to_all(copies, axis, split_axis=0, concat_axis=0, tiled=True, axi...  40.8 us
    pallas_call x1, Pallas kernels, weight_pass(): pl.pallas_call(weight_kernel, grid=(experts, width // block), out_shape=(...  38.7 us
    all_to_all x5, waiting for transfers between devices, swap_half(): lax.all_to_all(buffer, 'hidden', split_axis=0, concat_axis=0, tiled=True,...  37.8 us
    pallas_call x2, Pallas kernels, attend_back(): pl.pallas_call(functools.partial(attend_back_kernel, scale), grid=(groups...  37.7 us
  transfers between devices with their start and end apart: 34, of which 21 were waited for; matrix products, arithmetic and copies ran while one was open for 8% of the time, Pallas kernels for 44%

profile of v4, /device:TPU:0, one launch (start us, length us, event | category | flops | bytes accessed | tf_op | source)
XLA Modules:
  0.0 1040.4 jit_solution(12088007049712508676)
XLA Ops:
  8.7 6.3 all-to-all-start.5
  15.8 4.8 all-to-all-done.5
  27.5 4.7 all-to-all-done.7
  37.6 7.8 all-to-all-done.3
  51.2 30.3 %collective-permute-done = bf16[384,256]{1,0:T(8,128)(2,1)} collective-permute-done((bf16[384,256]{1,0:T(8,128)(2,1)S(1)}, bf16[384,256]{1,0:T(8,128)(2,1)}, u32[]{:S(2)}, u32[]{:S(2)}) %collective-permute-start) | collective-permute-done | bytes 196640 | tf_op jit(solution)/shard_map/ppermute | solution.py:751
  81.4 13.1 %all-to-all-done = bf16[2,256,1024]{2,1,0:T(8,128)(2,1)S(1)} async-done(((bf16[2,256,1024]{2,1,0:T(8,128)(2,1)}), bf16[2,256,1024]{2,1,0:T(8,128)(2,1)S(1)}, u32[]{:S(2)}, u32[]{:S(2)}) %all-to-all-start) | async-done | bytes 1048608 | tf_op jit(solution)/shard_map/all_to_all | solution.py:698
  95.8 24.1 %all_to_all.125 = bf16[8,384,256]{2,1,0:T(8,128)(2,1)} all-to-all(bf16[8,384,256]{2,1,0:T(8,128)(2,1)S(1)} %broadcast_in_dim.175), channel_id=1, replica_groups=mesh['expert'=8,'hidden'=4] {'expert'}, dimensions={0} | all-to-all | bytes 3145728 | tf_op jit(solution)/shard_map/all_to_all | solution.py:698
  132.2 5.9 position_bias.1.bias_ref
  138.1 18.3 %attend.2 = (bf16[2,3,512,256]{3,2,1,0:T(8,128)(2,1)}, bf16[2,4,512,512]{3,2,1,0:T(8,128)(2,1)}, bf16[512,512]{1,0:T(8,128)(2,1)}) custom-call(bf16[512,1024]{1,0:T(8,128)(2,1)} %bitcast.184, f32[1,1024]{1,0:T(1,128)} %bitcast.205, bf16[3,1024,256]{2,1,0:T(8,128)(2,1)} %own_ref.7, bf16[3,1024,256]{2,1,0:T(8,128)(2,1)} %bitcast.180, ...), custom_call_target="tpu_custom_call" | custom-call | flops 2147483648 | bytes 10485760 | tf_op jit(solution)/shard_map/attend/pallas_call | solution.py:128
  160.5 5.3 spread_rows.5
  165.9 11.1 %all-to-all-done.2.heads_ref = bf16[2,256,512]{2,1,0:T(8,128)(2,1)S(1)} async-done(((bf16[2,256,512]{2,1,0:T(8,128)(2,1)}), bf16[2,256,512]{2,1,0:T(8,128)(2,1)S(1)}, u32[]{:S(2)}, u32[]{:S(2)}) %all-to-all-start.2) | async-done | bytes 524320 | tf_op jit(solution)/shard_map/all_to_all | solution.py:703
  177.8 4.6 all-to-all-start.6
  191.4 4.6 copy.140.wg_ref
  196.0 4.7 copy.141.wu_ref
  206.5 30.5 %all-gather.9.cloned.1.call-done.rows_ref = bf16[1024,1024]{1,0:T(8,128)(2,1)} async-done(((bf16[256,1024]{1,0:T(8,128)(2,1)}), bf16[1024,1024]{1,0:T(8,128)(2,1)}) %all-gather.9.cloned.1.call-update) | async-done | bytes 2097168 | tf_op jit(solution)/shard_map/all_gather | solution.py:709
  237.1 5.3 spread_rows.4
  247.5 139.5 %expert_pass.2 = (bf16[8,2,160,1024]{3,2,1,0:T(8,128)(2,1)}, bf16[8,2,160,1024]{3,2,1,0:T(8,128)(2,1)}, bf16[8,2,160,1024]{3,2,1,0:T(8,128)(2,1)}, bf16[8,2,160,...) custom-call(bf16[8,2,160,1024]{3,2,1,0:T(8,128)(2,1)} %bitcast.172, ...), custom_call_target="tpu_custom_call" | custom-call | flops 22145925120 | bytes 209715200 | tf_op jit(solution)/shard_map/expert_pass/pallas_call | solution.py:552
  387.0 5.7 collect_rows.4
  395.1 18.3 %attend.3 = (bf16[2,3,512,256]{3,2,1,0:T(8,128)(2,1)}, bf16[2,4,512,512]{3,2,1,0:T(8,128)(2,1)}, bf16[512,512]{1,0:T(8,128)(2,1)}) custom-call(bf16[512,1024]{1,0:T(8,128)(2,1)} %bitcast.187, f32[1,1024]{1,0:T(1,128)} %bitcast.206, bf16[3,1024,256]{2,1,0:T(8,128)(2,1)} %own_ref.7, bf16[3,1024,256]{2,1,0:T(8,128)(2,1)} %bitcast.181, ...), custom_call_target="tpu_custom_call" | custom-call | flops 2147483648 | bytes 10485760 | tf_op jit(solution)/shard_map/attend/pallas_call | solution.py:128
  417.0 5.4 spread_rows.7
  422.4 16.1 %all-to-all-done.9.heads_ref = bf16[2,256,512]{2,1,0:T(8,128)(2,1)S(1)} async-done(((bf16[2,256,512]{2,1,0:T(8,128)(2,1)}), bf16[2,256,512]{2,1,0:T(8,128)(2,1)S(1)}, u32[]{:S(2)}, u32[]{:S(2)}) %all-to-all-start.9) | async-done | bytes 524320 | tf_op jit(solution)/shard_map/all_to_all | solution.py:703
  439.2 4.6 all-to-all-start.10
  452.2 52.1 %all-to-all-done.10 = bf16[8,320,1024]{2,1,0:T(8,128)(2,1)} async-done(((bf16[8,320,1024]{2,1,0:T(8,128)(2,1)}), bf16[8,320,1024]{2,1,0:T(8,128)(2,1)}, u32[]{:S(2)}, u32[]{:S(2)}) %all-to-all-start.10) | async-done | bytes 5242912 | tf_op jit(solution)/shard_map/all_to_all | solution.py:694
  504.2 10.9 %all_to_all.126 = bf16[2,256,512]{2,1,0:T(8,128)(2,1)} all-to-all(bf16[2,256,512]{2,1,0:T(8,128)(2,1)} %get-tuple-element.92), channel_id=1, replica_groups={{0,1},{2,3},{4,5},{6,7},{8,9},{10,11},{12,13},{14,15},{16,17},{18,19},{..., dimensions={0} | all-to-all | bytes 1048576 | tf_op jit(solution)/shard_map/all_to_all | solution.py:703
  520.9 5.3 spread_rows.6
  526.2 18.9 %attend_back.2 = (bf16[512,1024]{1,0:T(8,128)(2,1)}, bf16[8,2,384,256]{3,2,1,0:T(8,128)(2,1)}, f32[2,4,1024]{2,1,0:T(4,128)}, f32[1,1024]{1,0:T(1,128)}) custom-call(bf16[512,1024]{1,0:T(8,128)(2,1)} %bitcast.185, f32[1,1024]{1,0:T(1,128)} %bitcast.207, bf16[3,1024,256]{2,1,0:T(8,128)(2,1)} %own_ref.7, bf16[3,1024,256]{2,1,0:T(8,128)(2,1)} %bitcast.182, ...), custom_call_target="tpu_custom_call" | custom-call | flops 4294967296 | bytes 10485760 | tf_op jit(solution)/shard_map/attend_back/pallas_call | solution.py:229
  549.7 140.5 %expert_pass.3 = (bf16[8,2,160,1024]{3,2,1,0:T(8,128)(2,1)}, bf16[8,2,160,1024]{3,2,1,0:T(8,128)(2,1)}, bf16[8,2,160,1024]{3,2,1,0:T(8,128)(2,1)}, bf16[8,2,160,...) custom-call(bf16[8,2,160,1024]{3,2,1,0:T(8,128)(2,1)} %bitcast.171, ...), custom_call_target="tpu_custom_call" | custom-call | flops 22145925120 | bytes 209715200 | tf_op jit(solution)/shard_map/expert_pass/pallas_call | solution.py:552
  691.1 4.7 all-to-all-start.11
  696.9 5.7 collect_rows.7
  702.6 43.9 %reduce-scatter.11.cloned.1.call-done.grad_ref = bf16[256,1024]{1,0:T(8,128)(2,1)} async-done(((bf16[1024,1024]{1,0:T(8,128)(2,1)}), bf16[256,1024]{1,0:T(8,128)(2,1)}) %reduce-scatter.11.cloned.1.call-update) | async-done | bytes 524304 | tf_op jit(solution)/shard_map/reduce_scatter | solution.py:712
  750.8 5.4 all-to-all-done.11
  759.7 6.5 all-to-all-done.15
  767.1 5.1 all-to-all-start.12
  772.2 18.8 %attend_back.3 = (bf16[512,1024]{1,0:T(8,128)(2,1)}, bf16[8,2,384,256]{3,2,1,0:T(8,128)(2,1)}, f32[2,4,1024]{2,1,0:T(4,128)}, f32[1,1024]{1,0:T(1,128)}) custom-call(bf16[512,1024]{1,0:T(8,128)(2,1)} %bitcast.188, f32[1,1024]{1,0:T(1,128)} %bitcast.208, bf16[3,1024,256]{2,1,0:T(8,128)(2,1)} %own_ref.7, bf16[3,1024,256]{2,1,0:T(8,128)(2,1)} %bitcast.183, ...), custom_call_target="tpu_custom_call" | custom-call | flops 4294967296 | bytes 10485760 | tf_op jit(solution)/shard_map/attend_back/pallas_call | solution.py:229
  792.3 38.7 %weight_pass.1 = (f32[2,1024,16]{2,1,0:T(8,128)}, f32[2,1024,704]{2,1,0:T(8,128)}, f32[2,1024,704]{2,1,0:T(8,128)}, f32[2,704,1024]{2,1,0:T(8,128)}) custom-call(bf16[8,2,160,1024]{3,2,1,0:T(8,128)(2,1)} %get-tuple-element.103.refs_0_, bf16[8,2,160,1024]{3,2,1,0:T(8,128)(2,1)} %get-tuple-element.104.refs_1_, ...), custom_call_target="tpu_custom_call" | custom-call | flops 22145925120 | bytes 59899904 | tf_op jit(solution)/shard_map/weight_pass/pallas_call | solution.py:622
  837.8 5.8 collect_rows.5
  843.6 5.0 all-to-all-done.23
  853.4 39.2 %all-to-all-done.20 = bf16[2,256,1024]{2,1,0:T(8,128)(2,1)S(1)} async-done(((bf16[2,256,1024]{2,1,0:T(8,128)(2,1)}), bf16[2,256,1024]{2,1,0:T(8,128)(2,1)S(1)}, u32[]{:S(2)}, u32[]{:S(2)}) %all-to-all-start.20) | async-done | bytes 1048608 | tf_op jit(solution)/shard_map/all_to_all | solution.py:698
  892.6 10.2 all_to_all.127
  916.8 7.5 all-to-all-start.21
  924.3 5.5 add_convert_fusion
  929.7 9.9 all-to-all-done.21
  945.1 5.7 collect_rows.6
  952.7 6.4 copy.154
  959.1 6.4 copy.155
  972.4 11.2 %collective-permute-done.3 = bf16[32,1024]{1,0:T(8,128)(2,1)S(1)} collective-permute-done((bf16[32,1024]{1,0:T(8,128)(2,1)S(1)}, bf16[32,1024]{1,0:T(8,128)(2,1)S(1)}, u32[]{:S(2)}, u32[]{:S(2)}) %collective-permute-start.3) | collective-permute-done | bytes 65568 | tf_op jit(solution)/shard_map/ppermute | solution.py:859
  990.8 12.6 %collective-permute-done.2 = bf16[384,256]{1,0:T(8,128)(2,1)S(1)} collective-permute-done((bf16[384,256]{1,0:T(8,128)(2,1)S(1)}, bf16[384,256]{1,0:T(8,128)(2,1)S(1)}, u32[]{:S(2)}, u32[]{:S(2)}) %collective-permute-start.2) | collective-permute-done | bytes 196640 | tf_op jit(solution)/shard_map/ppermute | solution.py:859
  1017.2 12.9 %all-to-all-done.18 = bf16[8,384,256]{2,1,0:T(8,128)(2,1)} async-done(((bf16[8,384,256]{2,1,0:T(8,128)(2,1)}), bf16[8,384,256]{2,1,0:T(8,128)(2,1)}, u32[]{:S(2)}, u32[]{:S(2)}) %all-to-all-start.18) | async-done | bytes 1572896 | tf_op jit(solution)/shard_map/all_to_all | solution.py:698
  (227 shorter events, 159.5 us)
Async XLA Ops:
  7.2 20.3 %copy-start = (bf16[256,1024]{1,0:T(8,128)(2,1)S(1)}, bf16[256,1024]{1,0:T(8,128)(2,1)}, u32[]{:S(2)}) copy-start(bf16[256,1024]{1,0:T(8,128)(2,1)} %param.18) | copy-start | bytes 1572868
  7.2 29.2 %copy-start.13 = (bf16[2,1,256,1024]{3,2,1,0:T(8,128)(2,1)S(1)}, bf16[2,1,256,1024]{3,2,1,0:T(8,128)(2,1)}, u32[]{:S(2)}) copy-start(bf16[2,1,256,1024]{3,2,1,0:T(8,128)(2,1)} %param.14) | copy-start | bytes 3145732
  7.2 30.3 %copy-start.2 = (bf16[2,1,256,1024]{3,2,1,0:T(8,128)(2,1)S(1)}, bf16[2,1,256,1024]{3,2,1,0:T(8,128)(2,1)}, u32[]{:S(2)}) copy-start(bf16[2,1,256,1024]{3,2,1,0:T(8,128)(2,1)} %param.13) | copy-start | bytes 3145732
  8.7 11.9 %all-to-all-start.5 = ((s32[4,2,256,2]{2,1,3,0:T(2,128)}), s32[4,2,256,2]{2,1,3,0:T(2,128)S(1)}, u32[]{:S(2)}, u32[]{:S(2)}) async-start(s32[4,2,256,2]{2,1,3,0:T(2,128)} %broadcast_in_dim.180), calls=%async_computation.5 | async-start | bytes 32768 | tf_op jit(solution)/shard_map/all_to_all | solution.py:698
  23.7 8.5 all-to-all-start.7
  33.0 12.5 %all-to-all-start.3 = ((bf16[4,32,1024]{2,1,0:T(8,128)(2,1)}), bf16[4,32,1024]{2,1,0:T(8,128)(2,1)S(1)}, u32[]{:S(2)}, u32[]{:S(2)}) async-start(bf16[4,32,1024]{2,1,0:T(8,128)(2,1)} %broadcast_in_dim.176), calls=%async_computation.3 | async-start | bytes 524288 | tf_op jit(solution)/shard_map/all_to_all | solution.py:698
  36.4 89.6 %all-gather.5.cloned.1.call-start = ((), (), s32[]{:S(2)}) async-start(), calls=%async_computation.29 | async-start | bytes 2621440 | tf_op jit(solution)/shard_map/all_gather | solution.py:709
  37.6 82.3 %copy-start.5 = (bf16[256,1024]{1,0:T(8,128)(2,1)}, bf16[256,1024]{1,0:T(8,128)(2,1)S(1)}, u32[]{:S(2)}) copy-start(bf16[256,1024]{1,0:T(8,128)(2,1)S(1)} %get-tuple-element.205.x_ref) | copy-start | bytes 1572868
  37.6 205.1 %copy-start.4 = (bf16[256,1024]{1,0:T(8,128)(2,1)}, bf16[256,1024]{1,0:T(8,128)(2,1)S(1)}, u32[]{:S(2)}) copy-start(bf16[256,1024]{1,0:T(8,128)(2,1)S(1)} %get-tuple-element.206.x_ref) | copy-start | bytes 1572868
  46.6 48.0 %all-to-all-start = ((bf16[2,256,1024]{2,1,0:T(8,128)(2,1)}), bf16[2,256,1024]{2,1,0:T(8,128)(2,1)S(1)}, u32[]{:S(2)}, u32[]{:S(2)}) async-start(bf16[2,256,1024]{2,1,0:T(8,128)(2,1)} %broadcast_in_dim.174), calls=%async_computation | async-start | bytes 2097152 | tf_op jit(solution)/shard_map/all_to_all | solution.py:698
  51.1 30.3 %collective-permute-start = (bf16[384,256]{1,0:T(8,128)(2,1)S(1)}, bf16[384,256]{1,0:T(8,128)(2,1)}, u32[]{:S(2)}, u32[]{:S(2)}) collective-permute-start(bf16[384,256]{1,0:T(8,128)(2,1)S(1)} %constant_dynamic-slice_fusion.3), channel_id=1, source_target_pairs={{0,2},{1,3},{2,0},{3,1},{4,6},{5,7},{6,4},{7,5},{8,10},{9,11},{10,... | collective-permute-start | bytes 589832 | tf_op jit(solution)/shard_map/ppermute | solution.py:751
  94.6 26.9 %copy-start.14 = (bf16[2,256,1024]{2,1,0:T(8,128)(2,1)}, bf16[2,256,1024]{2,1,0:T(8,128)(2,1)S(1)}, u32[]{:S(2)}) copy-start(bf16[2,256,1024]{2,1,0:T(8,128)(2,1)S(1)} %all-to-all-done) | copy-start | bytes 3145732
  121.5 34.9 %all-to-all-start.4 = ((bf16[8,4,32,1024]{3,2,1,0:T(8,128)(2,1)}), bf16[8,4,32,1024]{3,2,1,0:T(8,128)(2,1)}, u32[]{:S(2)}, u32[]{:S(2)}) async-start(bf16[8,4,32,1024]{3,2,1,0:T(8,128)(2,1)} %broadcast_in_dim.177), calls=%async_computation.4 | async-start | bytes 4194304 | tf_op jit(solution)/shard_map/all_to_all | solution.py:698
  125.9 64.7 %all-gather.7.cloned.1.call-start = ((), (), s32[]{:S(2)}) async-start(), calls=%async_computation.30 | async-start | bytes 2621440 | tf_op jit(solution)/shard_map/all_gather | solution.py:709
  126.6 4.5 collective-permute-start.1
  156.4 20.5 %all-to-all-start.2 = ((bf16[2,256,512]{2,1,0:T(8,128)(2,1)}), bf16[2,256,512]{2,1,0:T(8,128)(2,1)S(1)}, u32[]{:S(2)}, u32[]{:S(2)}) async-start(bf16[2,256,512]{2,1,0:T(8,128)(2,1)} %bitcast.193), calls=%async_computation.2 | async-start | bytes 1048576 | tf_op jit(solution)/shard_map/all_to_all | solution.py:703
  177.8 65.0 %all-to-all-start.6 = ((bf16[8,320,1024]{2,1,0:T(8,128)(2,1)}), bf16[8,320,1024]{2,1,0:T(8,128)(2,1)}, u32[]{:S(2)}, u32[]{:S(2)}) async-start(bf16[8,320,1024]{2,1,0:T(8,128)(2,1)} %bitcast.167), calls=%async_computation.6 | async-start | bytes 10485760 | tf_op jit(solution)/shard_map/all_to_all | solution.py:694
  182.4 54.7 %all-gather.9.cloned.1.call-start = ((), (), s32[]{:S(2)}) async-start(), calls=%async_computation.31 | async-start | bytes 2621440 | tf_op jit(solution)/shard_map/all_gather | solution.py:709
  243.9 150.3 %all-to-all-start.8 = ((bf16[2,256,1024]{2,1,0:T(8,128)(2,1)}), bf16[2,256,1024]{2,1,0:T(8,128)(2,1)S(1)}, u32[]{:S(2)}, u32[]{:S(2)}) async-start(bf16[2,256,1024]{2,1,0:T(8,128)(2,1)} %broadcast_in_dim.191), calls=%async_computation.8 | async-start | bytes 2097152 | tf_op jit(solution)/shard_map/all_to_all | solution.py:698
  247.5 200.4 %reduce-scatter.9.cloned.1.call-start = ((), (), s32[]{:S(2)}) async-start(), calls=%async_computation.35 | async-start | bytes 2621440 | tf_op jit(solution)/shard_map/reduce_scatter | solution.py:712
  413.5 25.0 %all-to-all-start.9 = ((bf16[2,256,512]{2,1,0:T(8,128)(2,1)}), bf16[2,256,512]{2,1,0:T(8,128)(2,1)S(1)}, u32[]{:S(2)}, u32[]{:S(2)}) async-start(bf16[2,256,512]{2,1,0:T(8,128)(2,1)} %bitcast.194), calls=%async_computation.9 | async-start | bytes 1048576 | tf_op jit(solution)/shard_map/all_to_all | solution.py:703
  439.2 65.0 %all-to-all-start.10 = ((bf16[8,320,1024]{2,1,0:T(8,128)(2,1)}), bf16[8,320,1024]{2,1,0:T(8,128)(2,1)}, u32[]{:S(2)}, u32[]{:S(2)}) async-start(bf16[8,320,1024]{2,1,0:T(8,128)(2,1)} %bitcast.168), calls=%async_computation.10 | async-start | bytes 10485760 | tf_op jit(solution)/shard_map/all_to_all | solution.py:694
  443.9 77.0 %all-gather.11.cloned.1.call-start = ((), (), s32[]{:S(2)}) async-start(), calls=%async_computation.32 | async-start | bytes 2621440 | tf_op jit(solution)/shard_map/all_gather | solution.py:709
  517.3 27.8 %all-to-all-start.19 = ((bf16[2,256,1024]{2,1,0:T(8,128)(2,1)}), bf16[2,256,1024]{2,1,0:T(8,128)(2,1)S(1)}, u32[]{:S(2)}, u32[]{:S(2)}) async-start(bf16[2,256,1024]{2,1,0:T(8,128)(2,1)} %broadcast_in_dim.195), calls=%async_computation.23 | async-start | bytes 2097152 | tf_op jit(solution)/shard_map/all_to_all | solution.py:698
  546.1 144.1 %all-to-all-start.14 = ((bf16[2,256,1024]{2,1,0:T(8,128)(2,1)}), bf16[2,256,1024]{2,1,0:T(8,128)(2,1)S(1)}, u32[]{:S(2)}, u32[]{:S(2)}) async-start(bf16[2,256,1024]{2,1,0:T(8,128)(2,1)} %bitcast.190), calls=%async_computation.17 | async-start | bytes 2097152 | tf_op jit(solution)/shard_map/all_to_all | solution.py:703
  691.1 65.1 %all-to-all-start.11 = ((bf16[8,320,1024]{2,1,0:T(8,128)(2,1)}), bf16[8,320,1024]{2,1,0:T(8,128)(2,1)}, u32[]{:S(2)}, u32[]{:S(2)}) async-start(bf16[8,320,1024]{2,1,0:T(8,128)(2,1)} %bitcast.169), calls=%async_computation.11 | async-start | bytes 10485760 | tf_op jit(solution)/shard_map/all_to_all | solution.py:694
  695.8 50.7 %reduce-scatter.11.cloned.1.call-start = ((), (), s32[]{:S(2)}) async-start(), calls=%async_computation.36 | async-start | bytes 2621440 | tf_op jit(solution)/shard_map/reduce_scatter | solution.py:712
  756.2 10.1 all-to-all-start.15
  759.7 12.5 %copy-start.25 = (f32[1,1024]{1,0:T(1,128)S(1)}, f32[1,1024]{1,0:T(1,128)}, u32[]{:S(2)}) copy-start(f32[1,1024]{1,0:T(1,128)} %get-tuple-element.124) | copy-start | bytes 12292
  759.7 12.5 %copy-start.26 = (f32[1,1024]{1,0:T(1,128)S(1)}, f32[1,1024]{1,0:T(1,128)}, u32[]{:S(2)}) copy-start(f32[1,1024]{1,0:T(1,128)} %get-tuple-element.125) | copy-start | bytes 12292
  767.1 65.6 %all-to-all-start.12 = ((bf16[8,320,1024]{2,1,0:T(8,128)(2,1)}), bf16[8,320,1024]{2,1,0:T(8,128)(2,1)}, u32[]{:S(2)}, u32[]{:S(2)}) async-start(bf16[8,320,1024]{2,1,0:T(8,128)(2,1)} %bitcast.170), calls=%async_computation.13 | async-start | bytes 10485760 | tf_op jit(solution)/shard_map/all_to_all | solution.py:694
  772.2 18.8 %copy-start.22 = (f32[2,4,1024]{2,1,0:T(4,128)S(1)}, f32[2,4,1024]{2,1,0:T(4,128)}, u32[]{:S(2)}) copy-start(f32[2,4,1024]{2,1,0:T(4,128)} %get-tuple-element.126) | copy-start | bytes 98308
  792.3 40.3 %copy-start.24 = (f32[1,1024]{1,0:T(1,128)S(1)}, f32[1,1024]{1,0:T(1,128)}, u32[]{:S(2)}) copy-start(f32[1,1024]{1,0:T(1,128)} %get-tuple-element.122) | copy-start | bytes 12292
  792.3 40.3 %copy-start.27 = (f32[1,1024]{1,0:T(1,128)S(1)}, f32[1,1024]{1,0:T(1,128)}, u32[]{:S(2)}) copy-start(f32[1,1024]{1,0:T(1,128)} %get-tuple-element.123) | copy-start | bytes 12292
  833.6 14.9 %all-to-all-start.23 = ((f32[8,148,128]{2,1,0:T(8,128)}), f32[8,148,128]{2,1,0:T(8,128)S(1)}, u32[]{:S(2)}, u32[]{:S(2)}) async-start(f32[8,148,128]{2,1,0:T(8,128)} %broadcast_in_dim.204), calls=%async_computation.27 | async-start | bytes 1245184 | tf_op jit(solution)/shard_map/all_to_all | solution.py:698
  837.7 175.9 %reduce-scatter.5.cloned.1.call-start = ((), (), s32[]{:S(2)}) async-start(), calls=%async_computation.33 | async-start | bytes 2621440 | tf_op jit(solution)/shard_map/reduce_scatter | solution.py:712
  837.8 10.8 %copy-start.18 = (bf16[256,1024]{1,0:T(8,128)(2,1)S(1)}, bf16[256,1024]{1,0:T(8,128)(2,1)}, u32[]{:S(2)}) copy-start(bf16[256,1024]{1,0:T(8,128)(2,1)} %get-tuple-element.102) | copy-start | bytes 1572868
  849.6 43.0 %all-to-all-start.20 = ((bf16[2,256,1024]{2,1,0:T(8,128)(2,1)}), bf16[2,256,1024]{2,1,0:T(8,128)(2,1)S(1)}, u32[]{:S(2)}, u32[]{:S(2)}) async-start(bf16[2,256,1024]{2,1,0:T(8,128)(2,1)} %broadcast_in_dim.196), calls=%async_computation.24 | async-start | bytes 2097152 | tf_op jit(solution)/shard_map/all_to_all | solution.py:698
  892.6 10.3 copy-start.17
  902.9 13.0 %all-to-all-start.16 = ((bf16[2,256,1024]{2,1,0:T(8,128)(2,1)}), bf16[2,256,1024]{2,1,0:T(8,128)(2,1)S(1)}, u32[]{:S(2)}, u32[]{:S(2)}) async-start(bf16[2,256,1024]{2,1,0:T(8,128)(2,1)} %bitcast.189), calls=%async_computation.20 | async-start | bytes 2097152 | tf_op jit(solution)/shard_map/all_to_all | solution.py:703
  916.8 22.9 %all-to-all-start.21 = ((bf16[8,2,32,1024]{3,2,1,0:T(8,128)(2,1)}), bf16[8,2,32,1024]{3,2,1,0:T(8,128)(2,1)S(1)}, u32[]{:S(2)}, u32[]{:S(2)}) async-start(bf16[8,2,32,1024]{3,2,1,0:T(8,128)(2,1)} %bitcast.179), calls=%async_computation.25 | async-start | bytes 2097152 | tf_op jit(solution)/shard_map/all_to_all | solution.py:694
  940.6 42.9 %all-to-all-start.17 = ((bf16[8,2,384,256]{3,2,1,0:T(8,128)(2,1)}), bf16[8,2,384,256]{3,2,1,0:T(8,128)(2,1)}, u32[]{:S(2)}, u32[]{:S(2)}) async-start(bf16[8,2,384,256]{3,2,1,0:T(8,128)(2,1)} %add_convert_fusion), calls=%async_computation.21 | async-start | bytes 6291456 | tf_op jit(solution)/shard_map/all_to_all | solution.py:694
  945.1 69.8 %reduce-scatter.7.cloned.1.call-start = ((), (), s32[]{:S(2)}) async-start(), calls=%async_computation.34 | async-start | bytes 2621440 | tf_op jit(solution)/shard_map/reduce_scatter | solution.py:712
  972.3 11.3 %collective-permute-start.3 = (bf16[32,1024]{1,0:T(8,128)(2,1)S(1)}, bf16[32,1024]{1,0:T(8,128)(2,1)S(1)}, u32[]{:S(2)}, u32[]{:S(2)}) collective-permute-start(bf16[32,1024]{1,0:T(8,128)(2,1)S(1)} %fusion.32), channel_id=1, source_target_pairs={{0,2},{1,3},{2,0},{3,1},{4,6},{5,7},{6,4},{7,5},{8,10},{9,11},{10,... | collective-permute-start | bytes 196616 | tf_op jit(solution)/shard_map/ppermute | solution.py:859
  984.4 19.0 %all-to-all-start.22 = ((bf16[8,32,1024]{2,1,0:T(8,128)(2,1)}), bf16[8,32,1024]{2,1,0:T(8,128)(2,1)S(1)}, u32[]{:S(2)}, u32[]{:S(2)}) async-start(bf16[8,32,1024]{2,1,0:T(8,128)(2,1)} %broadcast_in_dim.197), calls=%async_computation.26 | async-start | bytes 1048576 | tf_op jit(solution)/shard_map/all_to_all | solution.py:698
  990.7 12.7 %collective-permute-start.2 = (bf16[384,256]{1,0:T(8,128)(2,1)S(1)}, bf16[384,256]{1,0:T(8,128)(2,1)S(1)}, u32[]{:S(2)}, u32[]{:S(2)}) collective-permute-start(bf16[384,256]{1,0:T(8,128)(2,1)S(1)} %fusion.29), channel_id=1, source_target_pairs={{0,2},{1,3},{2,0},{3,1},{4,6},{5,7},{6,4},{7,5},{8,10},{9,11},{10,... | collective-permute-start | bytes 589832 | tf_op jit(solution)/shard_map/ppermute | solution.py:859
  1004.7 25.3 %all-to-all-start.18 = ((bf16[8,384,256]{2,1,0:T(8,128)(2,1)}), bf16[8,384,256]{2,1,0:T(8,128)(2,1)}, u32[]{:S(2)}, u32[]{:S(2)}) async-start(bf16[8,384,256]{2,1,0:T(8,128)(2,1)} %broadcast_in_dim.194), calls=%async_computation.22 | async-start | bytes 3145728 | tf_op jit(solution)/shard_map/all_to_all | solution.py:698
  1014.9 18.5 %copy-start.1 = (bf16[256,1024]{1,0:T(8,128)(2,1)S(1)}, bf16[256,1024]{1,0:T(8,128)(2,1)}, u32[]{:S(2)}) copy-start(bf16[256,1024]{1,0:T(8,128)(2,1)} %param.18) | copy-start | bytes 1572868
  (17 other events, 52.7 us)
Sparse Core Ops, SparseCore 0:
  38.8 59.4 all-gather.4
  128.3 47.3 all-gather.6
  190.7 46.3 all-gather.8
  392.8 49.4 reduce-scatter.8
  448.0 44.4 all-gather.10
  702.8 43.7 reduce-scatter.10
  843.7 55.0 reduce-scatter.4
  951.0 43.8 reduce-scatter.6

commit v5 on v4

v5 whole, which is shorter than its diff:
```python
import functools

import jax
import jax.numpy as jnp
from jax import lax
from jax.experimental import pallas as pl
from jax.experimental.pallas import tpu as pltpu
from jax.sharding import PartitionSpec as P

EPSILON = 1e-06
PRECISE = lax.Precision.HIGHEST
LIMITS = (12, 16, 23, 32, 46, 64, 91)
MASKED = -1000000000.0
GELU_C = 0.7978845608028654
GELU_A = 0.044715
VMEM_LIMIT = 60 * 1024 * 1024
F32 = jnp.float32
BF16 = jnp.bfloat16


def mm(a, b):
    return lax.dot_general(a, b, (((1,), (0,)), ((), ())), preferred_element_type=F32)


def mm_nt(a, b):
    return lax.dot_general(a, b, (((1,), (1,)), ((), ())), preferred_element_type=F32)


def mm_tn(a, b):
    return lax.dot_general(a, b, (((0,), (0,)), ((), ())), preferred_element_type=F32)


def bucket_of(distance):
    magnitude = jnp.abs(distance)
    far_bucket = jnp.full(magnitude.shape, 8, jnp.int32)
    for threshold in LIMITS:
        far_bucket = far_bucket + (magnitude >= threshold).astype(jnp.int32)
    return jnp.where(magnitude < 8, magnitude, far_bucket) + 16 * (distance > 0).astype(jnp.int32)


def bucket_onehot(half, bucket_count):
    lane = jnp.arange(2 * half, dtype=jnp.int32)
    distance = jnp.where(lane < half, lane, lane - 2 * half)
    return (
        bucket_of(distance)[:, None] == jnp.arange(bucket_count, dtype=jnp.int32)[None, :]
    ).astype(F32)


TILE = 128


def bias_kernel(line_ref, out_ref):
    length = out_ref.shape[2]
    line = jnp.broadcast_to(line_ref[0], (8, length))
    row = lax.broadcasted_iota(jnp.int32, (8, length), 0)
    sheet = line
    for r in range(1, 8):
        sheet = jnp.where(row == r, pltpu.roll(line, r, 1), sheet)
    while sheet.shape[0] < TILE:
        sheet = jnp.concatenate([sheet, pltpu.roll(sheet, sheet.shape[0], 1)], axis=0)
    out_ref[0] = sheet.astype(out_ref.dtype)


def position_bias(line):
    heads, length = line.shape
    return pl.pallas_call(
        bias_kernel,
        grid=(heads,),
        out_shape=jax.ShapeDtypeStruct((heads, TILE, length), BF16),
        in_specs=[pl.BlockSpec((1, 1, length), lambda h: (h, 0, 0))],
        out_specs=pl.BlockSpec((1, TILE, length), lambda h: (h, 0, 0)),
        compiler_params=pltpu.CompilerParams(vmem_limit_bytes=VMEM_LIMIT),
        name="position_bias",
    )(line.reshape(heads, 1, length))


def unit_rows(x):
    x = x.astype(F32)
    return x * lax.rsqrt(jnp.mean(x * x, axis=-1, keepdims=True) + EPSILON)


def remote(src, dst, send_sem, recv_sem, device):
    return pltpu.make_async_remote_copy(
        src_ref=src, dst_ref=dst, send_sem=send_sem, recv_sem=recv_sem,
        device_id=device, device_id_type=pl.DeviceIdType.MESH,
    )


def greet(devices):
    barrier = pltpu.get_barrier_semaphore()
    for device in devices:
        pl.semaphore_signal(
            barrier, inc=1, device_id=device, device_id_type=pl.DeviceIdType.MESH
        )
    pl.semaphore_wait(barrier, len(devices))


def bits_of(count):
    return [1 << b for b in range(count.bit_length() - 1)]


def partner_of(me, step, count):
    found = 0
    for bit in bits_of(count):
        found = found + bit * lax.rem(me // bit + step // bit, 2)
    return found


def any_space():
    return pl.BlockSpec(memory_space=pl.ANY)


def opening_kernel(
    micros, x_ref, qkv_ref, out_ref, routes_ref, table_ref,
    x_all, qkv_all, out_all, routes_all, table_all,
    x_send, x_recv, qkv_send, qkv_recv, out_send, out_recv, qkv_on_send, qkv_on_recv,
    out_on_send, out_on_recv, routes_send, routes_recv, table_send, table_recv, own_sem,
):
    devices, qkv_rows = qkv_all.shape[0], qkv_all.shape[1]
    blocks, out_rows = out_all.shape[0], out_all.shape[2]
    members = x_all.shape[1]
    me = lax.axis_index("expert")
    line = lax.axis_index("hidden")
    mine = lax.rem(line, members)
    base = line - mine
    others = [partner_of(me, s, devices) for s in range(1, devices)]
    along = [lax.rem(line + s, blocks) for s in range(1, blocks)]
    across = lax.rem(line + members, blocks)
    greet([(other, line) for other in others] + [(me, z) for z in along])
    own = [
        pltpu.make_async_copy(out_ref.at[pl.ds(me * out_rows, out_rows)], out_all.at[line, me], own_sem.at[0]),
        pltpu.make_async_copy(routes_ref, routes_all.at[line], own_sem.at[1]),
    ]
    for micro in range(micros):
        own.append(
            pltpu.make_async_copy(x_ref.at[micro], x_all.at[micro, mine], own_sem.at[2 + micro])
        )
    for copy in own:
        copy.start()
    first_qkv = remote(
        qkv_ref.at[pl.ds(me * qkv_rows, qkv_rows)], qkv_all.at[me], qkv_send, qkv_recv, (me, across)
    )
    first_qkv.start()
    first_out = []
    small = [remote(table_ref, table_all, table_send, table_recv, (me, across))]
    for s, z in enumerate(along):
        first_out.append(
            remote(
                out_ref.at[pl.ds(me * out_rows, out_rows)], out_all.at[line, me], out_send.at[s],
                out_recv.at[s], (me, z),
            )
        )
        small.append(
            remote(routes_ref, routes_all.at[line], routes_send.at[s], routes_recv.at[s], (me, z))
        )
    for copy in first_out + small:
        copy.start()
    xs = []
    for micro in range(micros):
        for s in range(1, members):
            peer = base + lax.rem(mine + s, members)
            xs.append(
                remote(
                    x_ref.at[micro], x_all.at[micro, mine], x_send.at[micro, s],
                    x_recv.at[micro, s], (me, peer),
                )
            )
    for copy in xs:
        copy.start()
    first_qkv.wait_recv()
    second = []
    for s, other in enumerate(others):
        second.append(
            remote(
                qkv_all.at[me], qkv_all.at[me], qkv_on_send.at[s], qkv_on_recv.at[s], (other, line)
            )
        )
        second[-1].start()
    own[0].wait()
    for copy in first_out:
        copy.wait_recv()
    for s, other in enumerate(others):
        second.append(
            remote(
                out_all.at[:, me], out_all.at[:, me], out_on_send.at[s], out_on_recv.at[s],
                (other, line),
            )
        )
        second[-1].start()
    for copy in own[1:]:
        copy.wait()
    first_qkv.wait_send()
    for copy in first_out:
        copy.wait_send()
    for copy in small + xs + second:
        copy.wait()


def opening(x, qkv, out, routes, table, devices, blocks, members):
    micros, shard_len, width = x.shape
    dma = pltpu.SemaphoreType.DMA
    return pl.pallas_call(
        functools.partial(opening_kernel, micros),
        out_shape=(
            jax.ShapeDtypeStruct((micros, members, shard_len, width), BF16),
            jax.ShapeDtypeStruct((devices, qkv.shape[0] // devices, qkv.shape[1]), BF16),
            jax.ShapeDtypeStruct((blocks, devices, out.shape[0] // devices, width), BF16),
            jax.ShapeDtypeStruct((blocks,) + routes.shape, jnp.int32),
            jax.ShapeDtypeStruct(table.shape, table.dtype),
        ),
        in_specs=[any_space()] * 5,
        out_specs=(any_space(),) * 5,
        scratch_shapes=[
            dma((micros, members)), dma((micros, members)), dma, dma, dma((blocks,)), dma((blocks,)),
            dma((devices,)), dma((devices,)), dma((devices,)), dma((devices,)), dma((blocks,)),
            dma((blocks,)), dma, dma, dma((2 + micros,)),
        ],
        compiler_params=pltpu.CompilerParams(collective_id=1, has_side_effects=True),
        cost_estimate=pl.CostEstimate(flops=0, bytes_accessed=60000000, transcendentals=0),
        name="opening",
    )(x, qkv, out, routes, table)


def unit_rows(x):
    x = x.astype(F32)
    return x * lax.rsqrt(jnp.mean(x * x, axis=-1, keepdims=True) + EPSILON)


def attend_kernel(
    scale, x_ref, gain_ref, own_ref, other_ref, bias_ref, seg_row_ref, seg_col_ref,
    out_ref, x_own_ref, moe_gain_ref,
    qkv_ref, prob_ref, heads_ref, h1_ref, xn2_ref,
    xn_ref, part_ref, got_ref, send_sem, recv_sem,
):
    micros, members, shard_len, both = got_ref.shape
    cols = both // 2
    heads, length = bias_ref.shape[0], bias_ref.shape[2]
    half = members * shard_len
    size = cols // heads
    micro, group = pl.program_id(0), pl.program_id(1)
    me = lax.axis_index("expert")
    line = lax.axis_index("hidden")
    mine = lax.rem(line, members)
    part = line // members
    base = line - mine

    def swap(m, s):
        peer = lax.rem(mine + s, members)
        return remote(
            part_ref.at[m, peer], got_ref.at[m, mine], send_sem.at[m, s], recv_sem.at[m, s],
            (me, base + peer),
        )

    @pl.when((micro == 0) & (group == 0))
    def _():
        greet([(me, base + lax.rem(mine + s, members)) for s in range(1, members)])

    @pl.when(group == 0)
    def _():
        xn_ref[...] = (unit_rows(x_ref[0]) * gain_ref[...]).astype(BF16)
        for t in range(3):
            qkv_ref[0, 0, t] = mm(xn_ref[...], own_ref[t]).astype(BF16)

    @pl.when(group > 0)
    def _():
        for t in range(3):
            qkv_ref[0, 0, t] = mm(xn_ref[...], other_ref[t]).astype(BF16)

    seg_row = seg_row_ref[0]
    for head in range(heads):
        inner = slice(head * size, (head + 1) * size)
        keys = qkv_ref[0, 0, 1, :, inner]
        values = qkv_ref[0, 0, 2, :, inner]
        for start in range(0, half, TILE):
            rows = slice(start, start + TILE)
            scores = mm_nt(qkv_ref[0, 0, 0, rows, inner], keys) * scale
            shift = bias_ref[head, :, : half - start]
            if start:
                shift = jnp.concatenate([bias_ref[head, :, length - start :], shift], axis=1)
            scores = scores + shift.astype(F32)
            scores = jnp.where(seg_col_ref[0, rows, :] == seg_row, scores, MASKED)
            top = jnp.max(scores, axis=-1, keepdims=True)
            weights = jnp.exp(scores - top)
            inverse = 1.0 / jnp.sum(weights, axis=-1, keepdims=True)
            prob = (weights * inverse).astype(BF16)
            prob_ref[0, 0, head, rows, :] = prob
            heads_ref[0, rows, inner] = mm(prob, values).astype(BF16)

    for g in range(2):

        @pl.when(group == g)
        def _(g=g):
            for member in range(members):
                rows = slice(member * shard_len, (member + 1) * shard_len)
                part_ref[micro, member, :, g * cols : (g + 1) * cols] = heads_ref[0, rows, :]

    @pl.when(group == 1)
    def _():
        got_ref[micro, mine] = part_ref[micro, mine]
        for s in range(1, members):
            swap(micro, s).start()

    @pl.when((micro == micros - 1) & (group == 1))
    def _():
        for m in range(micros):
            for s in range(1, members):
                swap(m, s).wait_recv()
            h1 = x_own_ref[m].astype(F32)
            for member in range(members):
                for j in range(2):
                    index = lax.rem(part + j, 2) * members + member
                    h1 = h1 + mm(got_ref[m, member, :, j * cols : (j + 1) * cols], out_ref[index])
            h1_ref[m] = h1
            xn2_ref[m] = (unit_rows(h1) * moe_gain_ref[...]).astype(BF16)
        for m in range(micros):
            for s in range(1, members):
                swap(m, s).wait_send()


def attend(x, gain, own_weight, other_weight, bias, seg, out_weight, x_own, moe_gain, scale, members):
    micros, half, width = x.shape
    cols = own_weight.shape[2]
    heads = bias.shape[0] // 2
    shard_len = half // members

    def once(shape):
        return pl.BlockSpec(shape, lambda m, p: (0,) * len(shape), pipeline_mode=pl.Buffered(1))

    return pl.pallas_call(
        functools.partial(attend_kernel, scale),
        grid=(micros, 2),
        out_shape=(
            jax.ShapeDtypeStruct((micros, 2, 3, half, cols), BF16),
            jax.ShapeDtypeStruct((micros, 2, heads, half, half), BF16),
            jax.ShapeDtypeStruct((micros, half, 2 * cols), BF16),
            jax.ShapeDtypeStruct((micros, shard_len, width), F32),
            jax.ShapeDtypeStruct((micros, shard_len, width), BF16),
        ),
        in_specs=[
            pl.BlockSpec((1, half, width), lambda m, p: (m, 0, 0)),
            once((1, width)),
            once((3, width, cols)),
            once((3, width, cols)),
            pl.BlockSpec((heads,) + bias.shape[1:], lambda m, p: (p, 0, 0)),
            pl.BlockSpec((1, 1, half), lambda m, p: (m, 0, 0)),
            pl.BlockSpec((1, half, 1), lambda m, p: (m, 0, 0)),
            once(out_weight.shape),
            once(x_own.shape),
            once((1, width)),
        ],
        out_specs=(
            pl.BlockSpec((1, 1, 3, half, cols), lambda m, p: (m, p, 0, 0, 0)),
            pl.BlockSpec((1, 1, heads, half, half), lambda m, p: (m, p, 0, 0, 0)),
            pl.BlockSpec((1, half, cols), lambda m, p: (m, 0, p)),
            pl.BlockSpec((micros, shard_len, width), lambda m, p: (0, 0, 0)),
            pl.BlockSpec((micros, shard_len, width), lambda m, p: (0, 0, 0)),
        ),
        scratch_shapes=[
            pltpu.VMEM((half, width), BF16),
            pltpu.VMEM((micros, members, shard_len, 2 * cols), BF16),
            pltpu.VMEM((micros, members, shard_len, 2 * cols), BF16),
            pltpu.SemaphoreType.DMA((micros, members)),
            pltpu.SemaphoreType.DMA((micros, members)),
        ],
        compiler_params=pltpu.CompilerParams(
            vmem_limit_bytes=VMEM_LIMIT, collective_id=2, has_side_effects=True
        ),
        cost_estimate=pl.CostEstimate(
            flops=micros * 2 * half * cols * (8 * width + 4 * half),
            bytes_accessed=40000000,
            transcendentals=micros * 2 * heads * half * half,
        ),
        name="attend",
    )(
        x, gain, own_weight, other_weight, bias, seg.reshape(micros, 1, half),
        seg.reshape(micros, half, 1), out_weight, x_own, moe_gain,
    )


def back_kernel(
    scale, added, grad_ref, h1_ref, dy_ref, x_own_ref, moe_gain_ref, gain_ref, out_ref, x_ref,
    own_ref, other_ref, qkv_ref, prob_ref, heads_ref, *refs,
):
    if added:
        prev_ref, refs = refs[0], refs[1:]
    (
        xgrad_ref, grads_ref, line_ref, dmoe_ref, dgain_ref,
        dh1_ref, dattn_all, dheads_part, dheads_all, dxn_part, dxn_got, total_ref, xn_ref, ds_ref,
        dproj_ref, sheet_ref, attn_send, attn_recv, heads_send, heads_recv, dxn_send, dxn_recv,
    ) = refs
    members, shard_len, width = dattn_all.shape
    heads, half = prob_ref.shape[1], prob_ref.shape[2]
    cols = dproj_ref.shape[2]
    size = cols // heads
    length = sheet_ref.shape[1]
    group = pl.program_id(0)
    me = lax.axis_index("expert")
    line = lax.axis_index("hidden")
    mine = lax.rem(line, members)
    part = line // members
    base = line - mine
    steps = range(1, members)

    def peer_of(s):
        return lax.rem(mine + s, members)

    def attn_copy(s):
        return remote(
            dattn_all.at[mine], dattn_all.at[mine], attn_send.at[s], attn_recv.at[s],
            (me, base + peer_of(s)),
        )

    def heads_copy(s):
        return remote(
            dheads_part.at[peer_of(s)], dheads_all.at[mine], heads_send.at[s], heads_recv.at[s],
            (me, base + peer_of(s)),
        )

    def dxn_copy(s):
        return remote(
            dxn_part.at[peer_of(s)], dxn_got.at[mine], dxn_send.at[s], dxn_recv.at[s],
            (me, base + peer_of(s)),
        )

    @pl.when(group == 0)
    def _():
        greet([(me, base + peer_of(s)) for s in steps])
        grad = grad_ref[...].astype(F32)
        h1 = h1_ref[...]
        r2 = lax.rsqrt(jnp.mean(h1 * h1, axis=-1, keepdims=True) + EPSILON)
        unit = h1 * r2
        dmoe_ref[...] = jnp.sum(grad * unit, axis=0, keepdims=True)
        weighted = grad * moe_gain_ref[...]
        inner = jnp.mean(weighted * unit, axis=-1, keepdims=True)
        dh1 = dy_ref[...].astype(F32) + r2 * (weighted - unit * inner)
        dh1_ref[...] = dh1
        dattn = dh1.astype(BF16)
        dattn_all[mine] = dattn
        for member in range(members):
            for j in range(2):
                index = lax.rem(part + j, 2) * members + member
                dheads = mm_nt(dattn, out_ref[index]).astype(BF16)
                dheads_part[member, :, j * cols : (j + 1) * cols] = dheads
        for s in steps:
            heads_copy(s).start()
        for s in steps:
            attn_copy(s).start()
        dheads_all[mine] = dheads_part[mine]
        xn_ref[...] = (unit_rows(x_ref[...]) * gain_ref[...]).astype(BF16)
        for s in steps:
            heads_copy(s).wait_recv()

    for g in range(2):

        @pl.when(group == g)
        def _(g=g):
            for head in range(heads):
                inner_cols = slice(head * size, (head + 1) * size)
                outer_cols = slice(g * cols + head * size, g * cols + (head + 1) * size)
                values = qkv_ref[0, 2, :, inner_cols]
                grads = dheads_all[:, :, outer_cols].reshape(half, size)
                sheet_ref[...] = jnp.zeros_like(sheet_ref)
                for start in range(0, half, TILE):
                    rows = slice(start, start + TILE)
                    prob = prob_ref[0, head, rows, :].astype(F32)
                    dprob = mm_nt(grads[rows], values)
                    inner = jnp.sum(prob * dprob, axis=-1, keepdims=True)
                    dscore = (prob * (dprob - inner)).astype(BF16)
                    ds_ref[rows, :] = dscore
                    dscore = dscore.astype(F32)
                    sheet_ref[:, : half - start] += dscore[:, start:]
                    if start:
                        sheet_ref[:, length - start :] += dscore[:, :start]
                dscores = ds_ref[...]
                keys, queries = qkv_ref[0, 1, :, inner_cols], qkv_ref[0, 0, :, inner_cols]
                dproj_ref[0, :, inner_cols] = (mm(dscores, keys) * scale).astype(BF16)
                dproj_ref[1, :, inner_cols] = (mm_tn(dscores, queries) * scale).astype(BF16)
                dproj_ref[2, :, inner_cols] = mm_tn(prob_ref[0, head], grads).astype(BF16)
                sheet = sheet_ref[...]
                while sheet.shape[0] > 8:
                    upper = sheet.shape[0] // 2
                    sheet = sheet[:upper] + pltpu.roll(sheet[upper:], length - upper, 1)
                row = lax.broadcasted_iota(jnp.int32, (8, length), 0)
                found = jnp.zeros((1, length), F32)
                for r in range(8):
                    moved = pltpu.roll(sheet, length - r, 1) if r else sheet
                    found = found + jnp.sum(
                        jnp.where(row == r, moved, 0.0), axis=0, keepdims=True
                    )
                line_ref[0, head : head + 1, :] = found

    def products(weight_ref):
        dxn = mm_nt(dproj_ref[0], weight_ref[0])
        for t in range(1, 3):
            dxn = dxn + mm_nt(dproj_ref[t], weight_ref[t])
        return dxn.reshape(members, shard_len, width)

    @pl.when(group == 0)
    def _():
        total_ref[...] = products(own_ref)
        for s in steps:
            attn_copy(s).wait_recv()

    @pl.when(group == 1)
    def _():
        total_ref[...] += products(other_ref)
        dxn_part[...] = total_ref[...].astype(BF16)
        for s in steps:
            dxn_copy(s).start()

    per = grads_ref.shape[0] // 4
    for t in range(4):
        if t < 3:
            found = mm_tn(xn_ref[...], dproj_ref[t])
        else:
            found = mm_tn(dattn_all[...].reshape(half, width), heads_ref[...])
        found = found.reshape(per, 1, width // per, cols)
        if added:
            found = found + prev_ref[t * per : (t + 1) * per].astype(F32)
        grads_ref[t * per : (t + 1) * per] = found.astype(BF16)

    @pl.when(group == 1)
    def _():
        total = total_ref[...].reshape(half, width)
        dgain_ref[...] = jnp.sum(total * unit_rows(x_ref[...]), axis=0, keepdims=True)
        x_own = x_own_ref[...].astype(F32)
        r1 = lax.rsqrt(jnp.mean(x_own * x_own, axis=-1, keepdims=True) + EPSILON)
        unit = x_own * r1
        for s in steps:
            dxn_copy(s).wait_recv()
        dxn1 = total_ref[mine]
        for s in steps:
            dxn1 = dxn1 + dxn_got[lax.rem(mine + members - s, members)].astype(F32)
        weighted = dxn1 * gain_ref[...]
        inner = jnp.mean(weighted * unit, axis=-1, keepdims=True)
        xgrad_ref[...] = (dh1_ref[...] + r1 * (weighted - unit * inner)).astype(BF16)
        for s in steps:
            heads_copy(s).wait_send()
            attn_copy(s).wait_send()
            dxn_copy(s).wait_send()


def attend_back(
    grad, h1, dy, x_own, moe_gain, gain, out_weight, x_half, own_weight, other_weight, qkv, prob,
    heads_out, prev, scale, pieces, members, identity,
):
    _, heads, half = prob.shape[:3]
    width, cols = own_weight.shape[1:]
    shard_len = half // members
    length = 2 * half
    rows = 4 * width // pieces

    def once(shape):
        return pl.BlockSpec(shape, lambda p: (0,) * len(shape), pipeline_mode=pl.Buffered(1))

    pieces_spec = pl.BlockSpec((pieces, 1, rows, cols), lambda p: (0, p, 0, 0))
    operands = [
        grad, h1, dy, x_own, moe_gain, gain, out_weight, x_half, own_weight, other_weight, qkv,
        prob, heads_out,
    ]
    in_specs = [once(array.shape) for array in operands[:10]] + [
        pl.BlockSpec((1, 3, half, cols), lambda p: (p, 0, 0, 0)),
        pl.BlockSpec((1, heads, half, half), lambda p: (p, 0, 0, 0)),
        pl.BlockSpec((half, cols), lambda p: (0, p)),
    ]
    if prev is not None:
        operands.append(prev)
        in_specs.append(pieces_spec)
    dma = pltpu.SemaphoreType.DMA
    return pl.pallas_call(
        functools.partial(back_kernel, scale, prev is not None),
        grid=(2,),
        out_shape=(
            jax.ShapeDtypeStruct((shard_len, width), BF16),
            jax.ShapeDtypeStruct((pieces, 2, rows, cols), BF16),
            jax.ShapeDtypeStruct((2, heads, length), F32),
            jax.ShapeDtypeStruct((1, width), F32),
            jax.ShapeDtypeStruct((1, width), F32),
        ),
        in_specs=in_specs,
        out_specs=(
            pl.BlockSpec((shard_len, width), lambda p: (0, 0)),
            pieces_spec,
            pl.BlockSpec((1, heads, length), lambda p: (p, 0, 0)),
            pl.BlockSpec((1, width), lambda p: (0, 0)),
            pl.BlockSpec((1, width), lambda p: (0, 0)),
        ),
        scratch_shapes=[
            pltpu.VMEM((shard_len, width), F32),
            pltpu.VMEM((members, shard_len, width), BF16),
            pltpu.VMEM((members, shard_len, 2 * cols), BF16),
            pltpu.VMEM((members, shard_len, 2 * cols), BF16),
            pltpu.VMEM((members, shard_len, width), BF16),
            pltpu.VMEM((members, shard_len, width), BF16),
            pltpu.VMEM((members, shard_len, width), F32),
            pltpu.VMEM((half, width), BF16),
            pltpu.VMEM((half, half), BF16),
            pltpu.VMEM((3, half, cols), BF16),
            pltpu.VMEM((TILE, length), F32),
            dma((members,)), dma((members,)), dma((members,)), dma((members,)), dma((members,)),
            dma((members,)),
        ],
        compiler_params=pltpu.CompilerParams(
            vmem_limit_bytes=VMEM_LIMIT, collective_id=identity, has_side_effects=True
        ),
        cost_estimate=pl.CostEstimate(
            flops=2 * half * cols * (16 * width + 8 * half),
            bytes_accessed=40000000,
            transcendentals=0,
        ),
        name="attend_back",
    )(*operands)


def closing_kernel(
    pieces_ref, small_ref, whole_ref, sum_ref,
    total_ref, moved_ref, moved_got, piece_ref, small_got, line_sum, line_got,
    small_send, small_recv, line_send, line_recv, moved_send, moved_recv, on_send, on_recv, own_sem,
):
    devices = pieces_ref.shape[0]
    blocks = line_got.shape[0]
    me = lax.axis_index("expert")
    line = lax.axis_index("hidden")
    others = [partner_of(me, s, devices) for s in range(1, devices)]
    along = [lax.rem(line + s, blocks) for s in range(1, blocks)]
    across = lax.rem(line + blocks // 2, blocks)
    greet([(other, line) for other in others] + [(me, z) for z in along])
    smalls = [
        remote(small_ref, small_got.at[me], small_send.at[s], small_recv.at[s], (other, line))
        for s, other in enumerate(others)
    ]
    for copy in smalls:
        copy.start()
    small_got[me] = small_ref[...]
    moved = jnp.sum(pieces_ref[:, 1].astype(F32), axis=0)
    moved_ref[...] = moved.astype(BF16)
    cross = remote(moved_ref, moved_got, moved_send, moved_recv, (me, across))
    cross.start()
    total_ref[...] = jnp.sum(pieces_ref[:, 0].astype(F32), axis=0)
    cross.wait_recv()
    piece_ref[...] = (total_ref[...] + moved_got[...].astype(F32)).astype(BF16)
    onward = [
        remote(piece_ref, whole_ref.at[me], on_send.at[s], on_recv.at[s], (other, line))
        for s, other in enumerate(others)
    ]
    for copy in onward:
        copy.start()
    own = pltpu.make_async_copy(piece_ref, whole_ref.at[me], own_sem)
    own.start()
    for copy in smalls:
        copy.wait_recv()
    line_sum[...] = jnp.sum(small_got[...], axis=0)
    lines = [
        remote(line_sum, line_got.at[line], line_send.at[s], line_recv.at[s], (me, z))
        for s, z in enumerate(along)
    ]
    for copy in lines:
        copy.start()
    line_got[line] = line_sum[...]
    for copy in lines:
        copy.wait_recv()
    sum_ref[...] = jnp.sum(line_got[...], axis=0)
    own.wait()
    cross.wait_send()
    for copy in smalls + lines:
        copy.wait_send()
    for copy in onward:
        copy.wait()


def closing(pieces, small, blocks):
    devices, _, rows, cols = pieces.shape
    vmem = pl.BlockSpec(memory_space=pltpu.VMEM)
    dma = pltpu.SemaphoreType.DMA
    return pl.pallas_call(
        closing_kernel,
        out_shape=(
            jax.ShapeDtypeStruct((devices, rows, cols), BF16),
            jax.ShapeDtypeStruct(small.shape, F32),
        ),
        in_specs=[vmem, vmem],
        out_specs=(any_space(), vmem),
        scratch_shapes=[
            pltpu.VMEM((rows, cols), F32),
            pltpu.VMEM((rows, cols), BF16),
            pltpu.VMEM((rows, cols), BF16),
            pltpu.VMEM((rows, cols), BF16),
            pltpu.VMEM((devices,) + small.shape, F32),
            pltpu.VMEM(small.shape, F32),
            pltpu.VMEM((blocks,) + small.shape, F32),
            dma((devices,)), dma((devices,)), dma((blocks,)), dma((blocks,)), dma, dma,
            dma((devices,)), dma((devices,)), dma,
        ],
        compiler_params=pltpu.CompilerParams(
            vmem_limit_bytes=VMEM_LIMIT, collective_id=3, has_side_effects=True
        ),
        cost_estimate=pl.CostEstimate(flops=0, bytes_accessed=60000000, transcendentals=0),
        name="closing",
    )(pieces, small)


def spread(rows, place0, place1, count):
    ids = lax.broadcasted_iota(jnp.int32, (count, rows.shape[0]), 0)
    hit = (ids == place0) | (ids == place1)
    return mm(jnp.where(hit, 1.0, 0.0).astype(BF16), rows)


def spread_kernel(rows_ref, place_ref, out_ref):
    experts, _, cap, width = out_ref.shape
    placed = spread(rows_ref[...], place_ref[0:1, :], place_ref[1:2, :], experts * cap)
    out_ref[...] = placed.astype(BF16).reshape(experts, 1, cap, width)


def spread_rows(rows, place, experts, cap, shard_len):
    slots, width = rows.shape
    blocks = slots // shard_len
    return pl.pallas_call(
        spread_kernel,
        grid=(blocks,),
        out_shape=jax.ShapeDtypeStruct((experts, blocks, cap, width), BF16),
        in_specs=[
            pl.BlockSpec((shard_len, width), lambda b: (b, 0)),
            pl.BlockSpec((2, shard_len), lambda b: (0, b)),
        ],
        out_specs=pl.BlockSpec((experts, 1, cap, width), lambda b: (0, b, 0, 0)),
        compiler_params=pltpu.CompilerParams(vmem_limit_bytes=VMEM_LIMIT),
        cost_estimate=pl.CostEstimate(
            flops=2 * experts * cap * slots * width,
            bytes_accessed=2 * slots * width + 2 * experts * blocks * cap * width,
            transcendentals=0,
        ),
        name="spread_rows",
    )(rows, place)


def collect_kernel(rows_ref, place_ref, out_ref):
    experts, _, cap, width = rows_ref.shape
    tokens = out_ref.shape[0]
    ids = lax.broadcasted_iota(jnp.int32, (experts * cap, tokens), 0)
    hit = (ids == place_ref[0:1, :]) | (ids == place_ref[1:2, :])
    rows = rows_ref[...].reshape(experts * cap, width)
    out_ref[...] = mm_tn(jnp.where(hit, 1.0, 0.0).astype(BF16), rows).astype(BF16)


def collect_rows(rows, place, shard_len):
    experts, blocks, cap, width = rows.shape
    slots = blocks * shard_len
    return pl.pallas_call(
        collect_kernel,
        grid=(blocks,),
        out_shape=jax.ShapeDtypeStruct((slots, width), BF16),
        in_specs=[
            pl.BlockSpec((experts, 1, cap, width), lambda b: (0, b, 0, 0)),
            pl.BlockSpec((2, shard_len), lambda b: (0, b)),
        ],
        out_specs=pl.BlockSpec((shard_len, width), lambda b: (b, 0)),
        compiler_params=pltpu.CompilerParams(vmem_limit_bytes=VMEM_LIMIT),
        cost_estimate=pl.CostEstimate(
            flops=2 * experts * cap * slots * width,
            bytes_accessed=2 * slots * width + 2 * experts * blocks * cap * width,
            transcendentals=0,
        ),
        name="collect_rows",
    )(rows, place)


def place_kernel(cap, route_ref, live_ref, place_ref, other_ref):
    shard_len = route_ref.shape[2]
    count = other_ref.shape[1]
    experts = count // cap
    first, second = route_ref[0, 0:1, :], route_ref[0, 1:2, :]
    live = live_ref[0] >= 0
    ids = lax.broadcasted_iota(jnp.int32, (experts, shard_len), 0)
    chosen = ((ids == first) | (ids == second)) & live
    row = lax.broadcasted_iota(jnp.int32, (shard_len, shard_len), 0)
    col = lax.broadcasted_iota(jnp.int32, (shard_len, shard_len), 1)
    earlier = jnp.where(row < col, 1.0, 0.0).astype(BF16)
    before = mm(jnp.where(chosen, 1.0, 0.0).astype(BF16), earlier)
    spots = lax.broadcasted_iota(jnp.int32, (count, shard_len), 0)
    other = jnp.full((count, 1), -1, jnp.int32)
    for k, route in enumerate((first, second)):
        position = jnp.sum(jnp.where(ids == route, before, 0.0), axis=0, keepdims=True)
        place = jnp.where(live, route * cap + position.astype(jnp.int32), -1)
        place_ref[0, k : k + 1, :] = place
        partner = (second, first)[k]
        found = jnp.max(jnp.where(spots == place, partner, -1), axis=1, keepdims=True)
        other = jnp.maximum(other, found)
    other_ref[0] = other


def find_places(route, live, experts, cap):
    count, _, shard_len = route.shape
    return pl.pallas_call(
        functools.partial(place_kernel, cap),
        grid=(count,),
        out_shape=(
            jax.ShapeDtypeStruct((count, 2, shard_len), jnp.int32),
            jax.ShapeDtypeStruct((count, experts * cap, 1), jnp.int32),
        ),
        in_specs=[
            pl.BlockSpec((1, 2, shard_len), lambda b: (b, 0, 0)),
            pl.BlockSpec((1, 1, shard_len), lambda b: (b, 0, 0)),
        ],
        out_specs=(
            pl.BlockSpec((1, 2, shard_len), lambda b: (b, 0, 0)),
            pl.BlockSpec((1, experts * cap, 1), lambda b: (b, 0, 0)),
        ),
        compiler_params=pltpu.CompilerParams(vmem_limit_bytes=VMEM_LIMIT),
        name="find_places",
    )(route, live)


def expert_kernel(
    sent_ref, dy_ref, pair_ref, wr_ref, wg_ref, wu_ref, wd_ref,
    back_ref, y_ref, x_ref, g_ref, hid_ref, dga_ref, dup_ref, dlog_ref,
    got_ref, dx_ref, stage_ref, x_send, x_recv, dx_send, dx_recv, own_sem, stage_sem,
):
    devices, experts, cap, width = sent_ref.shape
    step = pl.program_id(0)
    me = lax.axis_index("expert")
    line = lax.axis_index("hidden")

    def x_copy(s):
        peer = partner_of(me, s, devices)
        return pltpu.make_async_remote_copy(
            src_ref=sent_ref.at[peer], dst_ref=got_ref.at[s], send_sem=x_send.at[s],
            recv_sem=x_recv.at[s], device_id=(peer, line), device_id_type=pl.DeviceIdType.MESH,
        )

    def dx_copy(s):
        peer = partner_of(me, s, devices)
        return pltpu.make_async_remote_copy(
            src_ref=dx_ref.at[s], dst_ref=back_ref.at[me], send_sem=dx_send.at[s],
            recv_sem=dx_recv.at[s], device_id=(peer, line), device_id_type=pl.DeviceIdType.MESH,
        )

    def y_copy(s):
        source = partner_of(me, s, devices)
        slot = lax.rem(s, 2)
        return pltpu.make_async_copy(stage_ref.at[slot], y_ref.at[source], stage_sem.at[slot])

    def work(s):
        source = partner_of(me, s, devices)
        slot = lax.rem(s, 2)
        for e in range(experts):
            x = got_ref[s, e]
            dy = dy_ref[source, e].astype(F32)
            pair = pair_ref[source, e].astype(F32)
            margin = jnp.sum(mm_nt(x, wr_ref[...]) * pair, axis=-1, keepdims=True)
            own_gate = 1.0 / (1.0 + jnp.exp(-margin))
            other_gate = 1.0 / (1.0 + jnp.exp(margin))
            g = (own_gate * dy).astype(BF16)
            x_ref[0, e] = x
            g_ref[0, e] = g
            gate = mm_nt(x, wg_ref[e])
            up = mm_nt(x, wu_ref[e])
            square = gate * gate
            bent = jnp.tanh(GELU_C * gate * (1.0 + GELU_A * square))
            half_gate = 0.5 * gate
            gelu = half_gate * (1.0 + bent)
            slope = 0.5 * (1.0 + bent) + half_gate * (1.0 - bent * bent) * (
                GELU_C * (1.0 + 3.0 * GELU_A * square)
            )
            hid = (gelu * up).astype(BF16)
            dhid = mm_nt(g, wd_ref[e])
            dga = (dhid * (up * slope)).astype(BF16)
            dup = (dhid * gelu).astype(BF16)
            hid_ref[0, e] = hid
            dga_ref[0, e] = dga
            dup_ref[0, e] = dup
            y = mm(hid, wd_ref[e])
            dgate = jnp.sum(y * dy, axis=-1, keepdims=True)
            stage_ref[slot, e] = (y * own_gate).astype(BF16)
            dlog = (dgate * own_gate * other_gate * pair).astype(BF16)
            dlog_ref[0, e] = dlog
            dx = mm(dga, wg_ref[e]) + mm(dup, wu_ref[e]) + mm(dlog, wr_ref[...])
            dx_ref[s, e] = dx.astype(BF16)

    @pl.when(step == 0)
    def _():
        barrier = pltpu.get_barrier_semaphore()
        for s in range(1, devices):
            pl.semaphore_signal(
                barrier, inc=1, device_id=(partner_of(me, s, devices), line),
                device_id_type=pl.DeviceIdType.MESH,
            )
        pl.semaphore_wait(barrier, devices - 1)
        for s in range(devices - 1, 0, -1):
            x_copy(s).start()
        own = pltpu.make_async_copy(sent_ref.at[me], got_ref.at[0], own_sem)
        own.start()
        own.wait()

    @pl.when(step > 0)
    def _():
        x_copy(step).wait_recv()

    @pl.when(step > 1)
    def _():
        y_copy(step - 2).wait()

    work(step)
    y_copy(step).start()

    @pl.when(step > 0)
    def _():
        dx_copy(step).start()

    @pl.when(step == devices - 1)
    def _():
        own = pltpu.make_async_copy(dx_ref.at[0], back_ref.at[me], own_sem)
        own.start()
        own.wait()
        y_copy(devices - 2).wait()
        y_copy(devices - 1).wait()
        for s in range(1, devices):
            x_copy(s).wait_send()
            dx_copy(s).wait_send()
            dx_copy(s).wait_recv()


def expert_pass(sent, dy, pair, wr, wg, wu, wd, identity):
    devices, experts, cap, width = sent.shape
    hidden = wg.shape[1]
    choices = wr.shape[0]

    def whole(shape):
        return pl.BlockSpec(shape, lambda s: (0,) * len(shape), pipeline_mode=pl.Buffered(1))

    def block(cols):
        return pl.BlockSpec((1, experts, cap, cols), lambda s: (s, 0, 0, 0))

    def kept(cols):
        return jax.ShapeDtypeStruct((devices, experts, cap, cols), BF16)

    rows = devices * cap
    return pl.pallas_call(
        expert_kernel,
        grid=(devices,),
        out_shape=(
            kept(width), kept(width), kept(width), kept(width), kept(hidden), kept(hidden),
            kept(hidden), kept(choices),
        ),
        in_specs=[
            any_space(), whole(dy.shape), whole(pair.shape), whole(wr.shape), whole(wg.shape),
            whole(wu.shape), whole(wd.shape),
        ],
        out_specs=(
            any_space(), any_space(), block(width), block(width), block(hidden), block(hidden),
            block(hidden), block(choices),
        ),
        scratch_shapes=[
            pltpu.VMEM((devices, experts, cap, width), BF16),
            pltpu.VMEM((devices, experts, cap, width), BF16),
            pltpu.VMEM((2, experts, cap, width), BF16),
            pltpu.SemaphoreType.DMA((devices,)),
            pltpu.SemaphoreType.DMA((devices,)),
            pltpu.SemaphoreType.DMA((devices,)),
            pltpu.SemaphoreType.DMA((devices,)),
            pltpu.SemaphoreType.DMA,
            pltpu.SemaphoreType.DMA((2,)),
        ],
        compiler_params=pltpu.CompilerParams(
            vmem_limit_bytes=VMEM_LIMIT, collective_id=identity, has_side_effects=True
        ),
        cost_estimate=pl.CostEstimate(
            flops=12 * experts * rows * width * hidden,
            bytes_accessed=80 * experts * rows * width,
            transcendentals=experts * rows * hidden,
        ),
        name="expert_pass",
    )(sent, dy, pair, wr, wg, wu, wd)


def weight_kernel(*refs):
    count = (len(refs) - 4) // 6
    dwr_ref, dwg_ref, dwu_ref, dwd_ref = refs[-4:]
    totals = [0.0, 0.0, 0.0, 0.0]
    for index in range(count):
        blocks = [
            ref[...].reshape(ref.shape[0] * ref.shape[2], ref.shape[3])
            for ref in refs[6 * index : 6 * index + 6]
        ]
        x, g, hid, dga, dup, dlog = blocks
        totals[0] = totals[0] + mm_tn(dlog, x)
        totals[1] = totals[1] + mm_tn(dga, x)
        totals[2] = totals[2] + mm_tn(dup, x)
        totals[3] = totals[3] + mm_tn(hid, g)
    dwr_ref[0] = totals[0]
    dwg_ref[0] = totals[1]
    dwu_ref[0] = totals[2]
    dwd_ref[0] = totals[3]


def weight_pass(kept):
    sources, experts, cap, width = kept[0][0].shape
    hidden = kept[0][2].shape[3]
    choices = kept[0][5].shape[3]
    rows = sources * cap
    block = 256 if width % 256 == 0 else width
    tokens = pl.BlockSpec((sources, 1, cap, block), lambda e, j: (0, e, 0, j))
    acts = pl.BlockSpec((sources, 1, cap, hidden), lambda e, j: (0, e, 0, 0))
    logs = pl.BlockSpec((sources, 1, cap, choices), lambda e, j: (0, e, 0, 0))
    operands = []
    for arrays in kept:
        operands.extend(arrays)
    return pl.pallas_call(
        weight_kernel,
        grid=(experts, width // block),
        out_shape=(
            jax.ShapeDtypeStruct((experts, choices, width), F32),
            jax.ShapeDtypeStruct((experts, hidden, width), F32),
            jax.ShapeDtypeStruct((experts, hidden, width), F32),
            jax.ShapeDtypeStruct((experts, hidden, width), F32),
        ),
        in_specs=[tokens, tokens, acts, acts, acts, logs] * len(kept),
        out_specs=(
            pl.BlockSpec((1, choices, block), lambda e, j: (e, 0, j)),
            pl.BlockSpec((1, hidden, block), lambda e, j: (e, 0, j)),
            pl.BlockSpec((1, hidden, block), lambda e, j: (e, 0, j)),
            pl.BlockSpec((1, hidden, block), lambda e, j: (e, 0, j)),
        ),
        compiler_params=pltpu.CompilerParams(vmem_limit_bytes=VMEM_LIMIT),
        cost_estimate=pl.CostEstimate(
            flops=6 * len(kept) * experts * rows * width * hidden,
            bytes_accessed=len(kept) * experts * rows * (4 * width + 6 * hidden)
            + 12 * experts * width * hidden,
            transcendentals=0,
        ),
        name="weight_pass",
    )(*operands)


def after(values, *others):
    return lax.optimization_barrier((values,) + others)[0]


def shards(
    x_in,
    cotangent,
    segment_ids,
    routes,
    qkv_weight,
    out_weight,
    bias_table,
    attn_gain,
    moe_gain,
    router_weight,
    gate_weight,
    up_weight,
    down_weight,
):
    micro_count, _, shard_len, width = x_in.shape
    slot_count = segment_ids.shape[2]
    head_cols = out_weight.shape[0]
    bucket_count, heads_here = bias_table.shape
    head_size = head_cols // heads_here
    expert_count = router_weight.shape[1]
    experts_here = gate_weight.shape[0]
    devices = expert_count // experts_here
    blocks = slot_count // shard_len
    members = blocks // 2
    half = slot_count // 2
    capacity = max(2, (10 * shard_len + 4 * expert_count - 1) // (4 * expert_count))
    scale = head_size ** (-0.5)
    hidden_index = lax.axis_index("hidden")
    expert_index = lax.axis_index("expert")
    part = hidden_index // members
    attn_gain_f = attn_gain.astype(F32).reshape(1, width)
    moe_gain_f = moe_gain.astype(F32).reshape(1, width)
    token_shape = (devices, experts_here, blocks * capacity, width)
    flat_shape = (devices, experts_here * blocks * capacity, width)
    place_shape = (expert_count, blocks, capacity, width)
    gate_rows = gate_weight.transpose(0, 2, 1)
    up_rows = up_weight.transpose(0, 2, 1)
    router_rows = router_weight.T

    def exchange(buffer):
        return lax.all_to_all(buffer, "expert", split_axis=0, concat_axis=0, tiled=True)

    def gather(values):
        return lax.all_gather(values, "hidden", axis=0, tiled=True)

    def scatter(values):
        return lax.psum_scatter(values, "hidden", scatter_dimension=0, tiled=True)

    states = [dict() for _ in range(micro_count)]
    x_all, other_qkv, all_out, all_routes, other_table = opening(
        x_in[:, 0], qkv_weight.reshape(3 * width, head_cols), out_weight,
        routes[:, 0].transpose(0, 2, 1), bias_table.T.astype(F32), devices, blocks, members,
    )
    x_half = x_all.reshape(micro_count, half, width)
    other_qkv = other_qkv.reshape(qkv_weight.shape)
    all_out = all_out.reshape(blocks, head_cols, width)

    route = all_routes.transpose(1, 0, 2, 3).reshape(micro_count * blocks, 2, shard_len)
    live = segment_ids.reshape(micro_count * blocks, 1, shard_len)
    place, other = find_places(route, live, expert_count, capacity)
    place = place.reshape(micro_count, blocks, 2, shard_len).transpose(0, 2, 1, 3)
    place = place.reshape(micro_count, 2, slot_count)
    other = other.reshape(micro_count, blocks, devices, experts_here, capacity)
    other = exchange(other.transpose(2, 0, 3, 1, 4)).transpose(1, 0, 2, 3, 4)
    other = other.reshape(micro_count, devices, experts_here, blocks * capacity, 1)
    expert_ids = jnp.arange(expert_count, dtype=jnp.int32)
    me = expert_index * experts_here + jnp.arange(experts_here, dtype=jnp.int32)
    plus = me[None, None, :, None, None] == expert_ids
    pairs = plus.astype(F32) - (other == expert_ids).astype(F32)
    pairs = jnp.where(other >= 0, pairs, 0.0).astype(BF16)

    tables = jnp.concatenate([bias_table.T.astype(F32), other_table], axis=0)
    onehot_bucket = bucket_onehot(half, bucket_count)
    bias = position_bias(jnp.einsum("jb,hb->hj", onehot_bucket, tables, precision=PRECISE))
    seg_half = lax.dynamic_slice_in_dim(segment_ids[:, 0], part * half, half, 1)

    def spread(rows, micro):
        return spread_rows(rows, place[micro], expert_count, capacity, shard_len)

    def send_dy(micro, kept, rows):
        kept["dy_sent"] = spread(rows, micro)
        kept["dy"] = exchange(kept["dy_sent"].reshape(flat_shape)).reshape(token_shape)

    def experts(micro, kept, *behind):
        sent = spread(kept["xn2_all"], micro).reshape(token_shape)
        back, y, x, g, hid, dga, dup, dlog = expert_pass(
            after(sent, *behind), kept["dy"], pairs[micro], router_rows, gate_rows, up_rows,
            down_weight, 4 + micro,
        )
        kept["weights"] = (x, g, hid, dga, dup, dlog)
        kept["y_sent"] = y.reshape(flat_shape)
        kept["dx_back"] = back.reshape(place_shape)
        kept["dx_part"] = collect_rows(kept["dx_back"], place[micro], shard_len)
        kept["dxn2"] = scatter(kept["dx_part"])

    states[0]["dy_all"] = gather(cotangent[0, 0])
    send_dy(0, states[0], states[0]["dy_all"])
    for micro in range(1, micro_count):
        before = states[micro - 1]["dy_all"]
        states[micro]["dy_all"] = gather(after(cotangent[micro, 0], before))
    qkv, prob, heads, h1, xn2 = attend(
        after(x_half, states[0]["dy_sent"]), attn_gain_f, qkv_weight, other_qkv, bias, seg_half,
        all_out, x_in[:, 0], moe_gain_f, scale, members,
    )
    behind = ()
    for micro in range(micro_count):
        states[micro]["xn2_all"] = gather(after(xn2[micro], *behind))
        behind = (states[micro]["xn2_all"],)
    for micro in range(1, micro_count):
        send_dy(micro, states[micro], after(states[micro]["dy_all"], xn2))
    behind = ()
    for micro in range(micro_count):
        experts(micro, states[micro], *behind)
        behind = (states[micro]["dx_part"],)
    behind = (states[-1]["dx_part"],)
    for micro in range(micro_count):
        state = states[micro]
        state["y_back"] = exchange(after(state["y_sent"], *behind)).reshape(place_shape)
        behind = (state["y_back"],)
    grads = None
    for micro in range(micro_count):
        state = states[micro]
        state["x_grad"], grads, state["line"], state["moe_gain_grad"], state["attn_gain_grad"] = (
            attend_back(
                state["dxn2"], h1[micro], cotangent[micro, 0], x_in[micro, 0], moe_gain_f,
                attn_gain_f, all_out, x_half[micro], qkv_weight, other_qkv, qkv[micro],
                prob[micro], heads[micro], grads, scale, devices, members,
                4 + micro_count + micro,
            )
        )
    for micro in range(micro_count):
        state = states[micro]
        state["mixed"] = scatter(collect_rows(state["y_back"], place[micro], shard_len))
        state["block_out"] = (h1[micro] + state["mixed"].astype(F32)).astype(BF16)
    pieces = exchange(grads)
    kept = [state["weights"] for state in states]
    kept[-1] = tuple(after(list(kept[-1]), grads))
    dwr, dwg, dwu, dwd = weight_pass(kept)

    def added(name):
        total = states[0][name]
        for state in states[1:]:
            total = total + state[name]
        return total

    lines = added("line").reshape(2 * heads_here, 2 * half)
    table = jnp.einsum("hj,jb->hb", lines, onehot_bucket, precision=PRECISE)
    table = table.reshape(2, heads_here * bucket_count)
    mine = jnp.arange(blocks, dtype=jnp.int32)[:, None]
    table = jnp.where(mine == hidden_index, table[0], 0.0) + jnp.where(
        mine == (hidden_index + members) % blocks, table[1], 0.0
    )
    small = jnp.concatenate(
        [
            jnp.sum(dwr, axis=0).reshape(-1),
            added("attn_gain_grad").reshape(-1),
            added("moe_gain_grad").reshape(-1),
            table.reshape(-1),
        ]
    )
    used = small.shape[0]
    small = jnp.pad(small, (0, -used % 1024)).reshape(-1, 128)
    whole, small = closing(pieces, small, blocks)
    whole = whole.reshape(4 * width, head_cols).astype(F32)
    grad_qkv = whole[: 3 * width].reshape(qkv_weight.shape)
    grad_out = whole[3 * width :].T
    small = small.reshape(-1)
    sizes = (width * expert_count, width, width)
    grad_router = small[: sizes[0]].reshape(expert_count, width).T
    grad_attn_gain = small[sizes[0] : sizes[0] + width]
    grad_moe_gain = small[sizes[0] + width : sizes[0] + 2 * width]
    table = small[sizes[0] + 2 * width : used].reshape(blocks, heads_here, bucket_count)
    grad_table = lax.dynamic_index_in_dim(table, hidden_index, 0, keepdims=False).T
    return (
        jnp.stack([state["block_out"] for state in states])[:, None],
        jnp.stack([state["x_grad"] for state in states])[:, None],
        grad_qkv,
        grad_out,
        grad_table,
        grad_attn_gain,
        grad_moe_gain,
        grad_router,
        dwg.transpose(0, 2, 1),
        dwu.transpose(0, 2, 1),
        dwd,
    )


def solution(mesh):
    return jax.shard_map(
        shards,
        mesh=mesh,
        in_specs=(
            P(None, "expert", "hidden", None),
            P(None, "expert", "hidden", None),
            P(None, "expert", None),
            P(None, "expert", "hidden", None),
            P(None, None, "hidden"),
            P("hidden", None),
            P(None, "hidden"),
            P(),
            P(),
            P(),
            P("expert", None, "hidden"),
            P("expert", None, "hidden"),
            P("expert", "hidden", None),
        ),
        out_specs=(
            P(None, "expert", "hidden", None),
            P(None, "expert", "hidden", None),
            P(None, None, "hidden"),
            P("hidden", None),
            P(None, "hidden"),
            P(),
            P(),
            P(),
            P("expert", None, "hidden"),
            P("expert", None, "hidden"),
            P("expert", "hidden", None),
        ),
        check_vma=False,
    )
```

time: 1050 us -> 930 us (0.89)
  Pallas kernels: 459 us -> 678 us
  waiting for transfers between devices: 325 us -> 150 us
  starting transfers between devices: 94.3 us -> 27.5 us
  blocking collectives: 45.2 us -> 0 us
  local copies, waits for them, and re-layouts: 62.9 us -> 33.6 us
  other arithmetic: 33.7 us -> 12.4 us
    pallas_call x8 -> x6, Pallas kernels: 90.4 us -> 307 us  [the longest x2 145 us: attend_back(): pl.pallas_call(functools.partial(back_kernel, scale, prev is not None), g...]
    all_to_all x15 -> x0, waiting for transfers between devices: 121 us -> none  [the longest x10 82.8 us: to_all(): lax.all_to_all(copies, axis, split_axis=0, concat_axis=0, tiled=True, axi...]
    all_to_all x15 -> x0, starting transfers between devices: 58.4 us -> none  [the longest x10 40.8 us: to_all(): lax.all_to_all(copies, axis, split_axis=0, concat_axis=0, tiled=True, axi...]
    ppermute x4 -> x0, waiting for transfers between devices: 56.4 us -> none  [the longest x1 30.3 us: shards(): lax.ppermute(my_piece(qkv_weight.reshape(3 * width, head_cols)), 'hidden'...]
    all_gather x4, waiting for transfers between devices: 30.6 us -> 82.6 us  [gather(): return lax.all_gather(values, 'hidden', axis=0, tiled=True)]
    all_to_all x3 -> x0, blocking collectives: 45.2 us -> none  [the longest x2 34.4 us: to_all(): lax.all_to_all(copies, axis, split_axis=0, concat_axis=0, tiled=True, axi...]
    reduce_scatter x4, waiting for transfers between devices: 43.9 us -> 0.03 us  [scatter(): return lax.psum_scatter(values, 'hidden', scatter_dimension=0, tiled=True)]
    unnamed x73 -> x51, local copies, waits for them, and re-layouts: 32.9 us -> 3.34 us
  transfers between devices with their start and end apart: 34 -> 14, of which waited for: 21 -> 4; matrix products, arithmetic and copies ran while one was open for 8% -> 4% of each run, Pallas kernels for 44% -> 74%
where the time goes in v5:
time: 930 us; the launch traced here: 918 us
  Pallas kernels  678 us (73%)
  waiting for transfers between devices  150 us (16%)
  local copies, waits for them, and re-layouts  33.6 us (4%)
  starting transfers between devices  27.5 us (3%)
  between operations  14.9 us (2%)
  other arithmetic  12.4 us (1%)
    pallas_call x2, Pallas kernels, expert_pass(): pl.pallas_call(expert_kernel, grid=(devices,), out_shape=(kept(width), ke...  284 us
    pallas_call x2, Pallas kernels, attend_back(): pl.pallas_call(functools.partial(back_kernel, scale, prev is not None), g...  145 us
    all_gather x4, waiting for transfers between devices, gather(): return lax.all_gather(values, 'hidden', axis=0, tiled=True)  82.6 us
    pallas_call x1, Pallas kernels, opening(): pl.pallas_call(functools.partial(opening_kernel, micros), out_shape=(jax....  69.2 us
    all_to_all x6, waiting for transfers between devices, exchange(): lax.all_to_all(buffer, 'expert', split_axis=0, concat_axis=0, tiled=True)  67.1 us
    pallas_call x1, Pallas kernels, attend(): pl.pallas_call(functools.partial(attend_kernel, scale), grid=(micros, 2),...  44.9 us
    pallas_call x1, Pallas kernels, closing(): pl.pallas_call(closing_kernel, out_shape=(jax.ShapeDtypeStruct((devices,...  39.7 us
    pallas_call x1, Pallas kernels, weight_pass(): pl.pallas_call(weight_kernel, grid=(experts, width // block), out_shape=(...  38.3 us
  transfers between devices with their start and end apart: 14, of which 4 were waited for; matrix products, arithmetic and copies ran while one was open for 4% of the time, Pallas kernels for 74%

profile of v5, /device:TPU:0, one launch (start us, length us, event | category | flops | bytes accessed | tf_op | source)
XLA Modules:
  0.0 918.0 jit_solution(6249931387177980913)
XLA Ops:
  7.2 2.5 slice_bitcast_fusion.19
  9.8 49.0 %all-gather.12.cloned.1.call-done = bf16[1,1,1024,1024]{3,2,1,0:T(8,128)(2,1)} async-done(((bf16[1,1,256,1024]{3,2,1,0:T(8,128)(2,1)}), bf16[1,1,1024,1024]{3,2,1,0:T(8,128)(2,1)}) %all-gather.12.cloned.1.call-update) | async-done | bytes 2097168 | tf_op jit(solution)/shard_map/all_gather | solution.py:1082
  59.5 69.2 %opening.1 = (bf16[2,2,256,1024]{3,2,1,0:T(8,128)(2,1)}, bf16[8,384,256]{2,1,0:T(8,128)(2,1)}, bf16[4,8,32,1024]{3,2,1,0:T(8,128)(2,1)}, s32[4,2,2,256]{3,2,1,0:T(2,128)}, f32[4,32]{1,0:T(4,128)}) custom-call(bf16[2,256,1024]{2,1,0:T(8,128)(2,1)} %bitcast.139, bf16[3072,256]{1,0:T(8,128)(2,1)} %bitcast.145, bf16[256,1024]{1,0:T(8,128)(2,1)} %out_ref.1, ...), custom_call_target="tpu_custom_call" | custom-call | bytes 60000000 | tf_op jit(solution)/shard_map/opening/pallas_call | solution.py:202
  128.6 1.3 copy.45
  130.0 7.3 find_places.1
  137.3 2.5 reduce.1
  140.7 3.3 all-to-all-start.1
  145.4 5.3 spread_rows.4
  150.8 4.8 all-to-all-start
  156.3 1.0 reshape.287.seg_col_ref
  158.4 5.9 position_bias.1.bias_ref
  165.5 44.9 %attend.1 = (bf16[2,2,3,512,256]{4,3,2,1,0:T(8,128)(2,1)}, bf16[2,2,4,512,512]{4,3,2,1,0:T(8,128)(2,1)}, bf16[2,512,512]{2,1,0:T(8,128)(2,1)}, f32[2,256,1024]{2,1,0:T(8,128)}, bf16[2,256,1024]{2,1,0:T(8,128)(2,1)}) custom-call(bf16[2,512,1024]{2,1,0:T(8,128)(2,1)} %bitcast.143, f32[1,1024]{1,0:T(1,128)} %bitcast.170, bf16[3,1024,256]{2,1,0:T(8,128)(2,1)} %own_ref.5, ...), custom_call_target="tpu_custom_call" | custom-call | flops 5368709120 | bytes 40000000 | tf_op jit(solution)/shard_map/attend/pallas_call | solution.py:329
  210.4 2.2 slice_bitcast_fusion.14
  213.3 5.3 spread_rows.7
  218.6 5.2 all-to-all-start.2
  225.3 33.6 %all-gather.6.cloned.1.call-done.rows_ref = bf16[1024,1024]{1,0:T(8,128)(2,1)} async-done(((bf16[256,1024]{1,0:T(8,128)(2,1)}), bf16[1024,1024]{1,0:T(8,128)(2,1)}) %all-gather.6.cloned.1.call-update) | async-done | bytes 2097168 | tf_op jit(solution)/shard_map/all_gather | solution.py:1082
  259.1 2.0 select_convert_fusion
  261.2 1.1 slice_bitcast_fusion.6
  262.3 5.3 spread_rows.5
  267.7 145.1 %expert_pass.2 = (bf16[8,2,160,1024]{3,2,1,0:T(8,128)(2,1)}, bf16[8,2,160,1024]{3,2,1,0:T(8,128)(2,1)}, bf16[8,2,160,1024]{3,2,1,0:T(8,128)(2,1)}, bf16[8,2,160,...) custom-call(bf16[8,2,160,1024]{3,2,1,0:T(8,128)(2,1)} %bitcast.136, ...), custom_call_target="tpu_custom_call" | custom-call | flops 22145925120 | bytes 209715200 | tf_op jit(solution)/shard_map/expert_pass/pallas_call | solution.py:937
  412.7 5.6 collect_rows.4
  418.4 5.3 spread_rows.6
  423.8 138.5 %expert_pass.3 = (bf16[8,2,160,1024]{3,2,1,0:T(8,128)(2,1)}, bf16[8,2,160,1024]{3,2,1,0:T(8,128)(2,1)}, bf16[8,2,160,1024]{3,2,1,0:T(8,128)(2,1)}, bf16[8,2,160,...) custom-call(bf16[8,2,160,1024]{3,2,1,0:T(8,128)(2,1)} %bitcast.135, ...), custom_call_target="tpu_custom_call" | custom-call | flops 22145925120 | bytes 209715200 | tf_op jit(solution)/shard_map/expert_pass/pallas_call | solution.py:937
  562.3 5.6 collect_rows.5
  567.9 4.7 all-to-all-start.3
  573.1 59.8 %all-to-all-done.3 = bf16[8,320,1024]{2,1,0:T(8,128)(2,1)} async-done(((bf16[8,320,1024]{2,1,0:T(8,128)(2,1)}), bf16[8,320,1024]{2,1,0:T(8,128)(2,1)}, u32[]{:S(2)}, u32[]{:S(2)}) %all-to-all-start.3) | async-done | bytes 5242912 | tf_op jit(solution)/shard_map/all_to_all | solution.py:1079
  632.9 4.7 all-to-all-start.4
  637.6 5.7 collect_rows.6
  643.4 1.0 slice_bitcast_fusion.11
  644.5 3.2 fusion.22
  647.7 1.1 slice_bitcast_fusion.10
  648.8 1.5 slice_bitcast_fusion.5
  650.4 1.9 slice_bitcast_fusion.3
  652.3 0.9 slice-done.1
  653.2 3.6 slice_bitcast_fusion.1
  656.8 66.3 %attend_back.2 = (bf16[256,1024]{1,0:T(8,128)(2,1)}, bf16[8,2,512,256]{3,2,1,0:T(8,128)(2,1)}, f32[2,4,1024]{2,1,0:T(4,128)}, f32[1,1024]{1,0:T(1,128)}, f32[1,1024]{1,0:T(1,128)}) custom-call(bf16[256,1024]{1,0:T(8,128)(2,1)} %reduce-scatter.9.cloned.1.call-done.grad_ref, f32[256,1024]{1,0:T(8,128)} %get-tuple-element.177.h1_ref, ...), custom_call_target="tpu_custom_call" | custom-call | flops 5368709120 | bytes 40000000 | tf_op jit(solution)/shard_map/attend_back/pallas_call | solution.py:570
  723.1 5.6 collect_rows.7
  728.8 79.2 %attend_back.3 = (bf16[256,1024]{1,0:T(8,128)(2,1)}, bf16[8,2,512,256]{3,2,1,0:T(8,128)(2,1)}, f32[2,4,1024]{2,1,0:T(4,128)}, f32[1,1024]{1,0:T(1,128)}, f32[1,1024]{1,0:T(1,128)}) custom-call(bf16[256,1024]{1,0:T(8,128)(2,1)} %reduce-scatter.11.cloned.1.call-done.grad_ref, f32[256,1024]{1,0:T(8,128)} %get-tuple-element.178.h1_ref, ...), custom_call_target="tpu_custom_call" | custom-call | flops 5368709120 | bytes 40000000 | tf_op jit(solution)/shard_map/attend_back/pallas_call | solution.py:570
  808.0 4.6 all-to-all-start.5
  812.7 38.3 %weight_pass.1 = (f32[2,16,1024]{2,1,0:T(8,128)}, f32[2,704,1024]{2,1,0:T(8,128)}, f32[2,704,1024]{2,1,0:T(8,128)}, f32[2,704,1024]{2,1,0:T(8,128)}) custom-call(bf16[8,2,160,1024]{3,2,1,0:T(8,128)(2,1)} %get-tuple-element.95.refs_0_, bf16[8,2,160,1024]{3,2,1,0:T(8,128)(2,1)} %get-tuple-element.96.refs_1_, ...), custom_call_target="tpu_custom_call" | custom-call | flops 22145925120 | bytes 59899904 | tf_op jit(solution)/shard_map/weight_pass/pallas_call | solution.py:1007
  851.0 0.9 reduce_sum.9
  853.3 1.1 maximum_bitcast_fusion.1
  854.4 7.3 all-to-all-done.5.pieces_ref
  861.7 39.7 %closing.1 = (bf16[8,512,256]{2,1,0:T(8,128)(2,1)}, f32[152,128]{1,0:T(8,128)}) custom-call(bf16[8,2,512,256]{3,2,1,0:T(8,128)(2,1)} %all-to-all-done.5.pieces_ref, f32[152,128]{1,0:T(8,128)} %fusion.6.small_ref), custom_call_target="tpu_custom_call" | custom-call | bytes 60000000 | tf_op jit(solution)/shard_map/closing/pallas_call | solution.py:675
  901.5 3.5 slice.147
  905.1 1.3 copy.52
  908.3 1.5 fusion
  909.9 1.1 maximum_bitcast_fusion
  (114 shorter events, 12.6 us)
Async XLA Ops:
  7.2 51.7 %copy-start.18 = (bf16[32,4]{0,1:T(4,128)(2,1)S(1)}, bf16[32,4]{0,1:T(4,128)(2,1)}, u32[]{:S(2)}) copy-start(bf16[32,4]{0,1:T(4,128)(2,1)} %param.19) | copy-start | bytes 772
  7.2 51.6 %all-gather.12.cloned.1.call-start = ((), (), s32[]{:S(2)}) async-start(), calls=%async_computation.17 | async-start | bytes 2621440 | tf_op jit(solution)/shard_map/all_gather | solution.py:1082
  9.8 203.5 %all-gather.10.cloned.1.call-start = ((), (), s32[]{:S(2)}) async-start(), calls=%async_computation.12 | async-start | bytes 2621440 | tf_op jit(solution)/shard_map/all_gather | solution.py:1082
  140.7 10.0 %all-to-all-start.1 = ((s32[8,1,640]{2,1,0:T(1,128)}), s32[8,1,640]{2,1,0:T(1,128)S(1)}, u32[]{:S(2)}, u32[]{:S(2)}) async-start(s32[8,1,640]{2,1,0:T(1,128)} %reshape.290), calls=%async_computation.1 | async-start | bytes 40960 | tf_op jit(solution)/shard_map/all_to_all | solution.py:1079
  150.7 4.9 copy-start.10
  150.7 6.5 copy-start.11
  150.7 6.5 copy-start.19
  150.7 13.6 %copy-start.16 = (bf16[1024]{0:T(1024)(128)(2,1)S(1)}, bf16[1024]{0:T(1024)(128)(2,1)}, u32[]{:S(2)}) copy-start(bf16[1024]{0:T(1024)(128)(2,1)} %param.20) | copy-start | bytes 6148
  150.8 14.1 %copy-start.17 = (bf16[1024]{0:T(1024)(128)(2,1)S(1)}, bf16[1024]{0:T(1024)(128)(2,1)}, u32[]{:S(2)}) copy-start(bf16[1024]{0:T(1024)(128)(2,1)} %param.21) | copy-start | bytes 6148
  150.8 67.8 %all-to-all-start = ((bf16[8,320,1024]{2,1,0:T(8,128)(2,1)}), bf16[8,320,1024]{2,1,0:T(8,128)(2,1)}, u32[]{:S(2)}, u32[]{:S(2)}) async-start(bf16[8,320,1024]{2,1,0:T(8,128)(2,1)} %bitcast.129), calls=%async_computation | async-start | bytes 10485760 | tf_op jit(solution)/shard_map/all_to_all | solution.py:1079
  155.6 103.3 %all-gather.6.cloned.1.call-start = ((), (), s32[]{:S(2)}) async-start(), calls=%async_computation.10 | async-start | bytes 2621440 | tf_op jit(solution)/shard_map/all_gather | solution.py:1082
  218.6 205.1 %all-to-all-start.2 = ((bf16[8,320,1024]{2,1,0:T(8,128)(2,1)}), bf16[8,320,1024]{2,1,0:T(8,128)(2,1)}, u32[]{:S(2)}, u32[]{:S(2)}) async-start(bf16[8,320,1024]{2,1,0:T(8,128)(2,1)} %bitcast.130), calls=%async_computation.2 | async-start | bytes 10485760 | tf_op jit(solution)/shard_map/all_to_all | solution.py:1079
  223.8 194.6 %all-gather.8.cloned.1.call-start = ((), (), s32[]{:S(2)}) async-start(), calls=%async_computation.11 | async-start | bytes 2621440 | tf_op jit(solution)/shard_map/all_gather | solution.py:1082
  258.9 397.9 %reduce-scatter.9.cloned.1.call-start = ((), (), s32[]{:S(2)}) async-start(), calls=%async_computation.15 | async-start | bytes 2621440 | tf_op jit(solution)/shard_map/reduce_scatter | solution.py:1085
  567.9 65.0 %all-to-all-start.3 = ((bf16[8,320,1024]{2,1,0:T(8,128)(2,1)}), bf16[8,320,1024]{2,1,0:T(8,128)(2,1)}, u32[]{:S(2)}, u32[]{:S(2)}) async-start(bf16[8,320,1024]{2,1,0:T(8,128)(2,1)} %bitcast.134), calls=%async_computation.3 | async-start | bytes 10485760 | tf_op jit(solution)/shard_map/all_to_all | solution.py:1079
  572.6 156.2 %reduce-scatter.11.cloned.1.call-start = ((), (), s32[]{:S(2)}) async-start(), calls=%async_computation.16 | async-start | bytes 2621440 | tf_op jit(solution)/shard_map/reduce_scatter | solution.py:1085
  632.9 90.2 %all-to-all-start.4 = ((bf16[8,320,1024]{2,1,0:T(8,128)(2,1)}), bf16[8,320,1024]{2,1,0:T(8,128)(2,1)}, u32[]{:S(2)}, u32[]{:S(2)}) async-start(bf16[8,320,1024]{2,1,0:T(8,128)(2,1)} %bitcast.133), calls=%async_computation.5 | async-start | bytes 10485760 | tf_op jit(solution)/shard_map/all_to_all | solution.py:1079
  637.6 5.8 copy-start.2
  637.6 270.7 %reduce-scatter.5.cloned.1.call-start = ((), (), s32[]{:S(2)}) async-start(), calls=%async_computation.13 | async-start | bytes 2621440 | tf_op jit(solution)/shard_map/reduce_scatter | solution.py:1085
  643.4 4.3 copy-start.4
  643.4 264.9 %reduce-scatter.7.cloned.1.call-start = ((), (), s32[]{:S(2)}) async-start(), calls=%async_computation.14 | async-start | bytes 2621440 | tf_op jit(solution)/shard_map/reduce_scatter | solution.py:1085
  644.5 4.3 copy-start.1
  644.5 7.9 slice-start
  647.7 2.7 copy-start.3
  648.8 4.5 slice-start.1
  808.0 53.7 %all-to-all-start.5 = ((bf16[8,2,512,256]{3,2,1,0:T(8,128)(2,1)}), bf16[8,2,512,256]{3,2,1,0:T(8,128)(2,1)}, u32[]{:S(2)}, u32[]{:S(2)}) async-start(bf16[8,2,512,256]{3,2,1,0:T(8,128)(2,1)} %get-tuple-element.94), calls=%async_computation.9 | async-start | bytes 8388608 | tf_op jit(solution)/shard_map/all_to_all | solution.py:1079
  812.6 39.3 %copy-start.8 = (f32[2,4,1024]{2,1,0:T(4,128)S(1)}, f32[2,4,1024]{2,1,0:T(4,128)}, u32[]{:S(2)}) copy-start(f32[2,4,1024]{2,1,0:T(4,128)} %get-tuple-element.118) | copy-start | bytes 98308
  812.6 39.3 %copy-start.9 = (f32[2,4,1024]{2,1,0:T(4,128)S(1)}, f32[2,4,1024]{2,1,0:T(4,128)}, u32[]{:S(2)}) copy-start(f32[2,4,1024]{2,1,0:T(4,128)} %get-tuple-element.119) | copy-start | bytes 98308
  812.6 39.9 %copy-start.13 = (f32[1,1024]{1,0:T(1,128)S(1)}, f32[1,1024]{1,0:T(1,128)}, u32[]{:S(2)}) copy-start(f32[1,1024]{1,0:T(1,128)} %get-tuple-element.114) | copy-start | bytes 12292
  812.6 39.9 %copy-start.15 = (f32[1,1024]{1,0:T(1,128)S(1)}, f32[1,1024]{1,0:T(1,128)}, u32[]{:S(2)}) copy-start(f32[1,1024]{1,0:T(1,128)} %get-tuple-element.115) | copy-start | bytes 12292
  812.6 39.9 %copy-start.12 = (f32[1,1024]{1,0:T(1,128)S(1)}, f32[1,1024]{1,0:T(1,128)}, u32[]{:S(2)}) copy-start(f32[1,1024]{1,0:T(1,128)} %get-tuple-element.116) | copy-start | bytes 12292
  812.6 39.9 %copy-start.14 = (f32[1,1024]{1,0:T(1,128)S(1)}, f32[1,1024]{1,0:T(1,128)}, u32[]{:S(2)}) copy-start(f32[1,1024]{1,0:T(1,128)} %get-tuple-element.117) | copy-start | bytes 12292
  812.7 40.7 %copy-start.5 = (bf16[256,1024]{1,0:T(8,128)(2,1)S(1)}, bf16[256,1024]{1,0:T(8,128)(2,1)}, u32[]{:S(2)}) copy-start(bf16[256,1024]{1,0:T(8,128)(2,1)} %get-tuple-element.91) | copy-start | bytes 1572868
  812.7 40.6 %copy-start.6 = (bf16[256,1024]{1,0:T(8,128)(2,1)S(1)}, bf16[256,1024]{1,0:T(8,128)(2,1)}, u32[]{:S(2)}) copy-start(bf16[256,1024]{1,0:T(8,128)(2,1)} %get-tuple-element.93) | copy-start | bytes 1572868
  901.4 3.5 copy-start
  901.5 3.6 copy-start.7
Sparse Core Ops, SparseCore 0:
  10.2 48.6 all-gather.11
  60.4 67.1 all-gather.9
  212.8 46.0 all-gather.5
  260.8 44.5 all-gather.7
  418.5 42.4 reduce-scatter.8
  576.1 44.1 reduce-scatter.10
  643.5 60.7 reduce-scatter.4
  728.9 61.0 reduce-scatter.6

commit v6 on v5

--- a/solution.py
+++ b/solution.py
@@ -111,14 +111,17 @@
 
 
 def opening_kernel(
-    micros, x_ref, qkv_ref, out_ref, routes_ref, table_ref,
-    x_all, qkv_all, out_all, routes_all, table_all,
+    micros, x_ref, qkv_ref, out_ref, routes_ref, table_ref, *refs,
+):
+    x_all, refs = refs[:micros], refs[micros:]
+    (
+    qkv_all, out_all, routes_all, table_all,
     x_send, x_recv, qkv_send, qkv_recv, out_send, out_recv, qkv_on_send, qkv_on_recv,
     out_on_send, out_on_recv, routes_send, routes_recv, table_send, table_recv, own_sem,
-):
+    ) = refs
     devices, qkv_rows = qkv_all.shape[0], qkv_all.shape[1]
     blocks, out_rows = out_all.shape[0], out_all.shape[2]
-    members = x_all.shape[1]
+    members = x_all[0].shape[0]
     me = lax.axis_index("expert")
     line = lax.axis_index("hidden")
     mine = lax.rem(line, members)
@@ -133,7 +136,7 @@
     ]
     for micro in range(micros):
         own.append(
-            pltpu.make_async_copy(x_ref.at[micro], x_all.at[micro, mine], own_sem.at[2 + micro])
+            pltpu.make_async_copy(x_ref.at[micro], x_all[micro].at[mine], own_sem.at[2 + micro])
         )
     for copy in own:
         copy.start()
@@ -161,7 +164,7 @@
             peer = base + lax.rem(mine + s, members)
             xs.append(
                 remote(
-                    x_ref.at[micro], x_all.at[micro, mine], x_send.at[micro, s],
+                    x_ref.at[micro], x_all[micro].at[mine], x_send.at[micro, s],
                     x_recv.at[micro, s], (me, peer),
                 )
             )
@@ -201,15 +204,15 @@
     dma = pltpu.SemaphoreType.DMA
     return pl.pallas_call(
         functools.partial(opening_kernel, micros),
-        out_shape=(
-            jax.ShapeDtypeStruct((micros, members, shard_len, width), BF16),
+        out_shape=(jax.ShapeDtypeStruct((members, shard_len, width), BF16),) * micros
+        + (
             jax.ShapeDtypeStruct((devices, qkv.shape[0] // devices, qkv.shape[1]), BF16),
             jax.ShapeDtypeStruct((blocks, devices, out.shape[0] // devices, width), BF16),
             jax.ShapeDtypeStruct((blocks,) + routes.shape, jnp.int32),
             jax.ShapeDtypeStruct(table.shape, table.dtype),
         ),
         in_specs=[any_space()] * 5,
-        out_specs=(any_space(),) * 5,
+        out_specs=(any_space(),) * (4 + micros),
         scratch_shapes=[
             dma((micros, members)), dma((micros, members)), dma, dma, dma((blocks,)), dma((blocks,)),
             dma((devices,)), dma((devices,)), dma((devices,)), dma((devices,)), dma((blocks,)),
@@ -317,7 +320,9 @@
                 swap(m, s).wait_send()
 
 
-def attend(x, gain, own_weight, other_weight, bias, seg, out_weight, x_own, moe_gain, scale, members):
+def attend(
+    x, gain, own_weight, other_weight, bias, seg, out_weight, x_own, moe_gain, scale, members, identity
+):
     micros, half, width = x.shape
     cols = own_weight.shape[2]
     heads = bias.shape[0] // 2
@@ -363,7 +368,7 @@
             pltpu.SemaphoreType.DMA((micros, members)),
         ],
         compiler_params=pltpu.CompilerParams(
-            vmem_limit_bytes=VMEM_LIMIT, collective_id=2, has_side_effects=True
+            vmem_limit_bytes=VMEM_LIMIT, collective_id=identity, has_side_effects=True
         ),
         cost_estimate=pl.CostEstimate(
             flops=micros * 2 * half * cols * (8 * width + 4 * half),
@@ -1085,11 +1090,11 @@
         return lax.psum_scatter(values, "hidden", scatter_dimension=0, tiled=True)
 
     states = [dict() for _ in range(micro_count)]
-    x_all, other_qkv, all_out, all_routes, other_table = opening(
+    *x_all, other_qkv, all_out, all_routes, other_table = opening(
         x_in[:, 0], qkv_weight.reshape(3 * width, head_cols), out_weight,
         routes[:, 0].transpose(0, 2, 1), bias_table.T.astype(F32), devices, blocks, members,
     )
-    x_half = x_all.reshape(micro_count, half, width)
+    x_half = [x.reshape(1, half, width) for x in x_all]
     other_qkv = other_qkv.reshape(qkv_weight.shape)
     all_out = all_out.reshape(blocks, head_cols, width)
 
@@ -1135,44 +1140,49 @@
     send_dy(0, states[0], states[0]["dy_all"])
     for micro in range(1, micro_count):
         before = states[micro - 1]["dy_all"]
-        states[micro]["dy_all"] = gather(after(cotangent[micro, 0], before))
-    qkv, prob, heads, h1, xn2 = attend(
-        after(x_half, states[0]["dy_sent"]), attn_gain_f, qkv_weight, other_qkv, bias, seg_half,
-        all_out, x_in[:, 0], moe_gain_f, scale, members,
-    )
+        states[micro]["dy_all"] = gather(after(cotangent[micro, 0], before, all_out))
+    behind = (states[0]["dy_sent"],)
+    for micro in range(micro_count):
+        state = states[micro]
+        qkv, prob, heads, h1, xn2 = attend(
+            after(x_half[micro], *behind), attn_gain_f, qkv_weight, other_qkv, bias,
+            seg_half[micro : micro + 1], all_out, x_in[micro], moe_gain_f, scale, members, 10 + micro,
+        )
+        state.update(qkv=qkv[0], prob=prob[0], heads=heads[0], h1=h1[0], xn2=xn2[0])
+        behind = (xn2,)
+    for micro in range(1, micro_count):
+        send_dy(micro, states[micro], after(states[micro]["dy_all"], states[-1]["xn2"]))
     behind = ()
     for micro in range(micro_count):
-        states[micro]["xn2_all"] = gather(after(xn2[micro], *behind))
-        behind = (states[micro]["xn2_all"],)
-    for micro in range(1, micro_count):
-        send_dy(micro, states[micro], after(states[micro]["dy_all"], xn2))
+        states[micro]["xn2_all"] = gather(after(states[micro]["xn2"], *behind))
+        behind = (states[micro]["xn2_all"], states[-1]["dy_sent"])
     behind = ()
     for micro in range(micro_count):
         experts(micro, states[micro], *behind)
         behind = (states[micro]["dx_part"],)
     behind = (states[-1]["dx_part"],)
+    grads = None
     for micro in range(micro_count):
         state = states[micro]
         state["y_back"] = exchange(after(state["y_sent"], *behind)).reshape(place_shape)
-        behind = (state["y_back"],)
-    grads = None
+        state["x_grad"], grads, state["line"], state["moe_gain_grad"], state["attn_gain_grad"] = (
+            attend_back(
+                state["dxn2"], state["h1"], cotangent[micro, 0], x_in[micro, 0], moe_gain_f,
+                attn_gain_f, all_out, x_half[micro][0], qkv_weight, other_qkv, state["qkv"],
+                state["prob"], state["heads"], grads, scale, devices, members,
+                4 + micro_count + micro,
+            )
+        )
+        behind = (grads,)
+    parts = []
     for micro in range(micro_count):
         state = states[micro]
-        state["x_grad"], grads, state["line"], state["moe_gain_grad"], state["attn_gain_grad"] = (
-            attend_back(
-                state["dxn2"], h1[micro], cotangent[micro, 0], x_in[micro, 0], moe_gain_f,
-                attn_gain_f, all_out, x_half[micro], qkv_weight, other_qkv, qkv[micro],
-                prob[micro], heads[micro], grads, scale, devices, members,
-                4 + micro_count + micro,
-            )
-        )
-    for micro in range(micro_count):
-        state = states[micro]
-        state["mixed"] = scatter(collect_rows(state["y_back"], place[micro], shard_len))
-        state["block_out"] = (h1[micro] + state["mixed"].astype(F32)).astype(BF16)
+        parts.append(collect_rows(after(state["y_back"], grads), place[micro], shard_len))
+        state["mixed"] = scatter(parts[-1])
+        state["block_out"] = (state["h1"] + state["mixed"].astype(F32)).astype(BF16)
     pieces = exchange(grads)
     kept = [state["weights"] for state in states]
-    kept[-1] = tuple(after(list(kept[-1]), grads))
+    kept[-1] = tuple(after(list(kept[-1]), *parts))
     dwr, dwg, dwu, dwd = weight_pass(kept)
 
     def added(name):

time: 930 us -> 849 us (0.913)
  waiting for transfers between devices: 150 us -> 6.06 us
  Pallas kernels: 678 us -> 752 us
  local copies, waits for them, and re-layouts: 33.6 us -> 21.3 us
    all_gather x4, waiting for transfers between devices: 82.6 us -> 0.06 us  [gather(): return lax.all_gather(values, 'hidden', axis=0, tiled=True)]
    all_to_all x6, waiting for transfers between devices: 67.1 us -> 5.3 us  [exchange(): lax.all_to_all(buffer, 'expert', split_axis=0, concat_axis=0, tiled=True)]
    pallas_call x2, Pallas kernels: 284 us -> 319 us  [expert_pass(): pl.pallas_call(expert_kernel, grid=(devices,), out_shape=(kept(width), ke...]
    pallas_call x1 -> x2, Pallas kernels: 44.9 us -> 75.6 us  [attend(): pl.pallas_call(functools.partial(attend_kernel, scale), grid=(micros, 2),...]
    pallas_call x1, Pallas kernels: 39.7 us -> 57 us  [closing(): pl.pallas_call(closing_kernel, out_shape=(jax.ShapeDtypeStruct((devices,...]
    pallas_call x2, Pallas kernels: 145 us -> 133 us  [attend_back(): pl.pallas_call(functools.partial(back_kernel, scale, prev is not None), g...]
    squeeze x5 -> x0, local copies, waits for them, and re-layouts: 10.3 us -> none  [the longest x1 3.6 us: shards(): prob[micro]]
  transfers between devices with their start and end apart: 14 -> 14, of which waited for: 4 -> 2; matrix products, arithmetic and copies ran while one was open for 4% -> 4% of each run, Pallas kernels for 74% -> 90%
where the time goes in v6:
time: 849 us; the launch traced here: 836 us
  Pallas kernels  752 us (89%)
  starting transfers between devices  27.4 us (3%)
  local copies, waits for them, and re-layouts  21.3 us (3%)
  between operations  15 us (2%)
  other arithmetic  13.9 us (2%)
    pallas_call x2, Pallas kernels, expert_pass(): pl.pallas_call(expert_kernel, grid=(devices,), out_shape=(kept(width), ke...  319 us
    pallas_call x2, Pallas kernels, attend_back(): pl.pallas_call(functools.partial(back_kernel, scale, prev is not None), g...  133 us
    pallas_call x2, Pallas kernels, attend(): pl.pallas_call(functools.partial(attend_kernel, scale), grid=(micros, 2),...  75.6 us
    pallas_call x1, Pallas kernels, opening(): pl.pallas_call(functools.partial(opening_kernel, micros), out_shape=(jax....  72.4 us
    pallas_call x1, Pallas kernels, closing(): pl.pallas_call(closing_kernel, out_shape=(jax.ShapeDtypeStruct((devices,...  57 us
    pallas_call x1, Pallas kernels, weight_pass(): pl.pallas_call(weight_kernel, grid=(experts, width // block), out_shape=(...  38.3 us
    all_to_all x6, starting transfers between devices, exchange(): lax.all_to_all(buffer, 'expert', split_axis=0, concat_axis=0, tiled=True)  26.7 us
    pallas_call x4, Pallas kernels, collect_rows(): pl.pallas_call(collect_kernel, grid=(blocks,), out_shape=jax.ShapeDtypeSt...  22.6 us
  transfers between devices with their start and end apart: 14, of which 2 were waited for; matrix products, arithmetic and copies ran while one was open for 4% of the time, Pallas kernels for 90%

profile of v6, /device:TPU:0, one launch (start us, length us, event | category | flops | bytes accessed | tf_op | source)
XLA Modules:
  0.0 836.4 jit_solution(5661089763783846556)
XLA Ops:
  7.2 2.5 slice_bitcast_fusion.11
  9.8 1.3 convert_bitcast_fusion.table_ref
  11.0 72.4 %opening.1 = (bf16[2,256,1024]{2,1,0:T(8,128)(2,1)}, bf16[2,256,1024]{2,1,0:T(8,128)(2,1)}, bf16[8,384,256]{2,1,0:T(8,128)(2,1)}, bf16[4,8,32,1024]{3,2,1,0:T(8,...) custom-call(bf16[2,256,1024]{2,1,0:T(8,128)(2,1)} %bitcast.132, bf16[3072,256]{1,0:T(8,128)(2,1)} %bitcast.136, ...), custom_call_target="tpu_custom_call" | custom-call | bytes 60000000 | tf_op jit(solution)/shard_map/opening/pallas_call | solution.py:205
  83.5 1.3 copy.47
  84.8 7.3 find_places.1
  92.1 2.5 reduce
  94.8 0.8 reshape.297
  95.6 3.3 all-to-all-start.1
  100.3 5.3 spread_rows.4
  105.6 4.8 all-to-all-start
  111.7 0.9 copy.49.seg_col_ref
  113.7 5.9 position_bias.1.bias_ref
  119.6 1.4 slice_bitcast_fusion.3
  121.1 29.5 %attend.2 = (bf16[1,2,3,512,256]{4,3,2,1,0:T(8,128)(2,1)}, bf16[1,2,4,512,512]{4,3,2,1,0:T(8,128)(2,1)}, bf16[1,512,512]{2,1,0:T(8,128)(2,1)}, f32[1,256,1024]{2,1,0:T(8,128)}, bf16[1,256,1024]{2,1,0:T(8,128)(2,1)}) custom-call(bf16[1,512,1024]{2,1,0:T(8,128)(2,1)} %bitcast.187, f32[1,1024]{1,0:T(1,128)} %bitcast.165, bf16[3,1024,256]{2,1,0:T(8,128)(2,1)} %own_ref.7, ...), custom_call_target="tpu_custom_call" | custom-call | flops 2684354560 | bytes 40000000 | tf_op jit(solution)/shard_map/attend/pallas_call | solution.py:334
  150.8 0.9 copy.54.seg_col_ref
  153.7 46.2 %attend.3 = (bf16[1,2,3,512,256]{4,3,2,1,0:T(8,128)(2,1)}, bf16[1,2,4,512,512]{4,3,2,1,0:T(8,128)(2,1)}, bf16[1,512,512]{2,1,0:T(8,128)(2,1)}, f32[1,256,1024]{2,1,0:T(8,128)}, bf16[1,256,1024]{2,1,0:T(8,128)(2,1)}) custom-call(bf16[1,512,1024]{2,1,0:T(8,128)(2,1)} %bitcast.185, f32[1,1024]{1,0:T(1,128)} %bitcast.166, bf16[3,1024,256]{2,1,0:T(8,128)(2,1)} %own_ref.7, ...), custom_call_target="tpu_custom_call" | custom-call | flops 2684354560 | bytes 40000000 | tf_op jit(solution)/shard_map/attend/pallas_call | solution.py:334
  199.9 5.3 spread_rows.6
  205.4 4.7 all-to-all-start.2
  210.4 2.0 select_convert_fusion
  212.5 1.1 slice_bitcast_fusion
  213.6 5.3 spread_rows.5
  218.9 180.1 %expert_pass.2 = (bf16[8,2,160,1024]{3,2,1,0:T(8,128)(2,1)}, bf16[8,2,160,1024]{3,2,1,0:T(8,128)(2,1)}, bf16[8,2,160,1024]{3,2,1,0:T(8,128)(2,1)}, bf16[8,2,160,...) custom-call(bf16[8,2,160,1024]{3,2,1,0:T(8,128)(2,1)} %bitcast.129, ...), custom_call_target="tpu_custom_call" | custom-call | flops 22145925120 | bytes 209715200 | tf_op jit(solution)/shard_map/expert_pass/pallas_call | solution.py:942
  399.0 5.6 collect_rows.4
  404.7 5.3 spread_rows.7
  410.0 138.5 %expert_pass.3 = (bf16[8,2,160,1024]{3,2,1,0:T(8,128)(2,1)}, bf16[8,2,160,1024]{3,2,1,0:T(8,128)(2,1)}, bf16[8,2,160,1024]{3,2,1,0:T(8,128)(2,1)}, bf16[8,2,160,...) custom-call(bf16[8,2,160,1024]{3,2,1,0:T(8,128)(2,1)} %bitcast.128, ...), custom_call_target="tpu_custom_call" | custom-call | flops 22145925120 | bytes 209715200 | tf_op jit(solution)/shard_map/expert_pass/pallas_call | solution.py:942
  548.5 5.6 collect_rows.5
  554.2 4.7 all-to-all-start.3
  559.4 81.9 %attend_back.2 = (bf16[256,1024]{1,0:T(8,128)(2,1)}, bf16[8,2,512,256]{3,2,1,0:T(8,128)(2,1)}, f32[2,4,1024]{2,1,0:T(4,128)}, f32[1,1024]{1,0:T(1,128)}, f32[1,1024]{1,0:T(1,128)}) custom-call(bf16[256,1024]{1,0:T(8,128)(2,1)} %reduce-scatter.7.cloned.1.call-done.grad_ref, f32[256,1024]{1,0:T(8,128)} %bitcast.137, ...), custom_call_target="tpu_custom_call" | custom-call | flops 5368709120 | bytes 40000000 | tf_op jit(solution)/shard_map/attend_back/pallas_call | solution.py:575
  641.4 4.7 all-to-all-start.4
  646.2 50.8 %attend_back.3 = (bf16[256,1024]{1,0:T(8,128)(2,1)}, bf16[8,2,512,256]{3,2,1,0:T(8,128)(2,1)}, f32[2,4,1024]{2,1,0:T(4,128)}, f32[1,1024]{1,0:T(1,128)}, f32[1,1024]{1,0:T(1,128)}) custom-call(bf16[256,1024]{1,0:T(8,128)(2,1)} %reduce-scatter.5.cloned.1.call-done.grad_ref, f32[256,1024]{1,0:T(8,128)} %bitcast.138, ...), custom_call_target="tpu_custom_call" | custom-call | flops 5368709120 | bytes 40000000 | tf_op jit(solution)/shard_map/attend_back/pallas_call | solution.py:575
  697.0 5.6 collect_rows.6
  702.7 3.8 all-to-all-done.4
  706.4 4.6 all-to-all-start.5
  711.1 5.7 collect_rows.7
  717.6 1.1 maximum_bitcast_fusion.1
  718.7 38.3 %weight_pass.1 = (f32[2,16,1024]{2,1,0:T(8,128)}, f32[2,704,1024]{2,1,0:T(8,128)}, f32[2,704,1024]{2,1,0:T(8,128)}, f32[2,704,1024]{2,1,0:T(8,128)}) custom-call(bf16[8,2,160,1024]{3,2,1,0:T(8,128)(2,1)} %get-tuple-element.113.refs_0_, bf16[8,2,160,1024]{3,2,1,0:T(8,128)(2,1)} %get-tuple-element.114.refs_1_, ...), custom_call_target="tpu_custom_call" | custom-call | flops 22145925120 | bytes 59899904 | tf_op jit(solution)/shard_map/weight_pass/pallas_call | solution.py:1012
  757.0 0.9 reduce_sum.9
  758.6 1.5 all-to-all-done.5.pieces_ref
  760.1 57.0 %closing.1 = (bf16[8,512,256]{2,1,0:T(8,128)(2,1)}, f32[152,128]{1,0:T(8,128)}) custom-call(bf16[8,2,512,256]{3,2,1,0:T(8,128)(2,1)} %all-to-all-done.5.pieces_ref, f32[152,128]{1,0:T(8,128)} %fusion.6.small_ref), custom_call_target="tpu_custom_call" | custom-call | bytes 60000000 | tf_op jit(solution)/shard_map/closing/pallas_call | solution.py:680
  817.2 0.8 slice.97
  818.0 0.8 slice.102
  818.9 1.1 slice.108
  820.0 1.9 slice.107
  822.7 1.3 copy.55
  824.6 1.3 slice_bitcast_fusion.9
  825.9 1.2 fusion
  827.1 1.2 fusion.1
  828.3 1.1 maximum_bitcast_fusion
  (104 shorter events, 10.2 us)
Async XLA Ops:
  7.2 76.3 %all-gather.12.cloned.1.call-start = ((), (), s32[]{:S(2)}) async-start(), calls=%async_computation.17 | async-start | bytes 2621440 | tf_op jit(solution)/shard_map/all_gather | solution.py:1087
  9.7 190.2 %all-gather.8.cloned.1.call-start = ((), (), s32[]{:S(2)}) async-start(), calls=%async_computation.11 | async-start | bytes 2621440 | tf_op jit(solution)/shard_map/all_gather | solution.py:1087
  95.6 10.0 %all-to-all-start.1 = ((s32[8,1,640]{2,1,0:T(1,128)}), s32[8,1,640]{2,1,0:T(1,128)S(1)}, u32[]{:S(2)}, u32[]{:S(2)}) async-start(s32[8,1,640]{2,1,0:T(1,128)} %reshape.297), calls=%async_computation.1 | async-start | bytes 40960 | tf_op jit(solution)/shard_map/all_to_all | solution.py:1084
  105.6 4.9 copy-start.16
  105.6 5.5 copy-start.17
  105.6 6.1 copy-start.8
  105.6 7.0 copy-start.11
  105.6 7.0 copy-start.18
  105.6 14.0 %copy-start.1 = (bf16[2,1,256,1024]{3,2,1,0:T(8,128)(2,1)S(1)}, bf16[2,1,256,1024]{3,2,1,0:T(8,128)(2,1)}, u32[]{:S(2)}) copy-start(bf16[2,1,256,1024]{3,2,1,0:T(8,128)(2,1)} %param.13) | copy-start | bytes 3145732
  105.6 99.8 %all-to-all-start = ((bf16[8,320,1024]{2,1,0:T(8,128)(2,1)}), bf16[8,320,1024]{2,1,0:T(8,128)(2,1)}, u32[]{:S(2)}, u32[]{:S(2)}) async-start(bf16[8,320,1024]{2,1,0:T(8,128)(2,1)} %bitcast.124), calls=%async_computation | async-start | bytes 10485760 | tf_op jit(solution)/shard_map/all_to_all | solution.py:1084
  110.4 94.8 %all-gather.6.cloned.1.call-start = ((), (), s32[]{:S(2)}) async-start(), calls=%async_computation.10 | async-start | bytes 2621440 | tf_op jit(solution)/shard_map/all_gather | solution.py:1087
  111.7 9.4 %copy-start.10 = (s32[1,1,512]{2,1,0:T(1,128)}, s32[1,1,512]{2,1,0:T(1,128)S(1)}, u32[]{:S(2)}) copy-start(s32[1,1,512]{2,1,0:T(1,128)S(1)} %get-tuple-element.201.seg_row_ref) | copy-start | bytes 6148
  111.7 39.1 %copy-start.9 = (s32[1,1,512]{2,1,0:T(1,128)}, s32[1,1,512]{2,1,0:T(1,128)S(1)}, u32[]{:S(2)}) copy-start(s32[1,1,512]{2,1,0:T(1,128)S(1)} %get-tuple-element.200.seg_row_ref) | copy-start | bytes 6148
  150.6 254.1 %all-gather.10.cloned.1.call-start = ((), (), s32[]{:S(2)}) async-start(), calls=%async_computation.12 | async-start | bytes 2621440 | tf_op jit(solution)/shard_map/all_gather | solution.py:1087
  205.4 204.6 %all-to-all-start.2 = ((bf16[8,320,1024]{2,1,0:T(8,128)(2,1)}), bf16[8,320,1024]{2,1,0:T(8,128)(2,1)}, u32[]{:S(2)}, u32[]{:S(2)}) async-start(bf16[8,320,1024]{2,1,0:T(8,128)(2,1)} %bitcast.125), calls=%async_computation.2 | async-start | bytes 10485760 | tf_op jit(solution)/shard_map/all_to_all | solution.py:1084
  210.1 349.3 %reduce-scatter.7.cloned.1.call-start = ((), (), s32[]{:S(2)}) async-start(), calls=%async_computation.14 | async-start | bytes 2621440 | tf_op jit(solution)/shard_map/reduce_scatter | solution.py:1090
  554.2 87.2 %all-to-all-start.3 = ((bf16[8,320,1024]{2,1,0:T(8,128)(2,1)}), bf16[8,320,1024]{2,1,0:T(8,128)(2,1)}, u32[]{:S(2)}, u32[]{:S(2)}) async-start(bf16[8,320,1024]{2,1,0:T(8,128)(2,1)} %bitcast.127), calls=%async_computation.3 | async-start | bytes 10485760 | tf_op jit(solution)/shard_map/all_to_all | solution.py:1084
  558.8 87.3 %reduce-scatter.5.cloned.1.call-start = ((), (), s32[]{:S(2)}) async-start(), calls=%async_computation.13 | async-start | bytes 2621440 | tf_op jit(solution)/shard_map/reduce_scatter | solution.py:1090
  641.4 65.0 %all-to-all-start.4 = ((bf16[8,320,1024]{2,1,0:T(8,128)(2,1)}), bf16[8,320,1024]{2,1,0:T(8,128)(2,1)}, u32[]{:S(2)}, u32[]{:S(2)}) async-start(bf16[8,320,1024]{2,1,0:T(8,128)(2,1)} %bitcast.126), calls=%async_computation.7 | async-start | bytes 10485760 | tf_op jit(solution)/shard_map/all_to_all | solution.py:1084
  646.1 179.8 %reduce-scatter.9.cloned.1.call-start = ((), (), s32[]{:S(2)}) async-start(), calls=%async_computation.15 | async-start | bytes 2621440 | tf_op jit(solution)/shard_map/reduce_scatter | solution.py:1090
  706.4 53.7 %all-to-all-start.5 = ((bf16[8,2,512,256]{3,2,1,0:T(8,128)(2,1)}), bf16[8,2,512,256]{3,2,1,0:T(8,128)(2,1)}, u32[]{:S(2)}, u32[]{:S(2)}) async-start(bf16[8,2,512,256]{3,2,1,0:T(8,128)(2,1)} %get-tuple-element.106), calls=%async_computation.9 | async-start | bytes 8388608 | tf_op jit(solution)/shard_map/all_to_all | solution.py:1084
  711.0 116.1 %reduce-scatter.11.cloned.1.call-start = ((), (), s32[]{:S(2)}) async-start(), calls=%async_computation.16 | async-start | bytes 2621440 | tf_op jit(solution)/shard_map/reduce_scatter | solution.py:1090
  711.1 5.8 copy-start.6
  711.1 5.8 copy-start.7
  711.1 6.4 copy-start.13
  711.1 6.4 copy-start.15
  711.1 6.4 copy-start.12
  711.1 6.4 copy-start.14
  711.1 6.4 copy-start.4
  711.1 6.4 copy-start.5
  817.2 2.8 copy-start
  820.0 5.9 copy-start.2
  820.0 7.1 copy-start.3
Sparse Core Ops, SparseCore 0:
  10.2 71.1 all-gather.11
  83.6 45.6 all-gather.7
  150.7 50.2 all-gather.5
  205.4 45.3 all-gather.9
  404.8 42.1 reduce-scatter.6
  562.3 59.5 reduce-scatter.4
  702.8 42.0 reduce-scatter.8
  747.3 54.3 reduce-scatter.10

commit v7 on v6

--- a/solution.py
+++ b/solution.py
@@ -117,7 +117,8 @@
     (
     qkv_all, out_all, routes_all, table_all,
     x_send, x_recv, qkv_send, qkv_recv, out_send, out_recv, qkv_on_send, qkv_on_recv,
-    out_on_send, out_on_recv, routes_send, routes_recv, table_send, table_recv, own_sem,
+    out_on_send, out_on_recv, routes_send, routes_recv, routes_on_send, routes_on_recv,
+    table_send, table_recv, own_sem,
     ) = refs
     devices, qkv_rows = qkv_all.shape[0], qkv_all.shape[1]
     blocks, out_rows = out_all.shape[0], out_all.shape[2]
@@ -132,7 +133,7 @@
     greet([(other, line) for other in others] + [(me, z) for z in along])
     own = [
         pltpu.make_async_copy(out_ref.at[pl.ds(me * out_rows, out_rows)], out_all.at[line, me], own_sem.at[0]),
-        pltpu.make_async_copy(routes_ref, routes_all.at[line], own_sem.at[1]),
+        pltpu.make_async_copy(routes_ref, routes_all.at[me, line], own_sem.at[1]),
     ]
     for micro in range(micros):
         own.append(
@@ -146,6 +147,7 @@
     first_qkv.start()
     first_out = []
     small = [remote(table_ref, table_all, table_send, table_recv, (me, across))]
+    first_routes = []
     for s, z in enumerate(along):
         first_out.append(
             remote(
@@ -153,10 +155,12 @@
                 out_recv.at[s], (me, z),
             )
         )
-        small.append(
-            remote(routes_ref, routes_all.at[line], routes_send.at[s], routes_recv.at[s], (me, z))
-        )
-    for copy in first_out + small:
+        first_routes.append(
+            remote(
+                routes_ref, routes_all.at[me, line], routes_send.at[s], routes_recv.at[s], (me, z)
+            )
+        )
+    for copy in first_routes + first_out + small:
         copy.start()
     xs = []
     for micro in range(micros):
@@ -179,6 +183,17 @@
             )
         )
         second[-1].start()
+    own[1].wait()
+    for copy in first_routes:
+        copy.wait_recv()
+    for s, other in enumerate(others):
+        second.append(
+            remote(
+                routes_all.at[me], routes_all.at[me], routes_on_send.at[s], routes_on_recv.at[s],
+                (other, line),
+            )
+        )
+        second[-1].start()
     own[0].wait()
     for copy in first_out:
         copy.wait_recv()
@@ -190,10 +205,10 @@
             )
         )
         second[-1].start()
-    for copy in own[1:]:
+    for copy in own[2:]:
         copy.wait()
     first_qkv.wait_send()
-    for copy in first_out:
+    for copy in first_out + first_routes:
         copy.wait_send()
     for copy in small + xs + second:
         copy.wait()
@@ -208,7 +223,7 @@
         + (
             jax.ShapeDtypeStruct((devices, qkv.shape[0] // devices, qkv.shape[1]), BF16),
             jax.ShapeDtypeStruct((blocks, devices, out.shape[0] // devices, width), BF16),
-            jax.ShapeDtypeStruct((blocks,) + routes.shape, jnp.int32),
+            jax.ShapeDtypeStruct((devices, blocks) + routes.shape, jnp.int32),
             jax.ShapeDtypeStruct(table.shape, table.dtype),
         ),
         in_specs=[any_space()] * 5,
@@ -216,7 +231,7 @@
         scratch_shapes=[
             dma((micros, members)), dma((micros, members)), dma, dma, dma((blocks,)), dma((blocks,)),
             dma((devices,)), dma((devices,)), dma((devices,)), dma((devices,)), dma((blocks,)),
-            dma((blocks,)), dma, dma, dma((2 + micros,)),
+            dma((blocks,)), dma((devices,)), dma((devices,)), dma, dma, dma((2 + micros,)),
         ],
         compiler_params=pltpu.CompilerParams(collective_id=1, has_side_effects=True),
         cost_estimate=pl.CostEstimate(flops=0, bytes_accessed=60000000, transcendentals=0),
@@ -231,10 +246,13 @@
 
 def attend_kernel(
     scale, x_ref, gain_ref, own_ref, other_ref, bias_ref, seg_row_ref, seg_col_ref,
-    out_ref, x_own_ref, moe_gain_ref,
-    qkv_ref, prob_ref, heads_ref, h1_ref, xn2_ref,
-    xn_ref, part_ref, got_ref, send_sem, recv_sem,
+    out_ref, x_own_ref, moe_gain_ref, *refs,
 ):
+    riding = len(refs) > 10
+    if riding:
+        sent_ref, arrived_ref, ride_send, ride_recv, ride_own = refs[0], refs[6], *refs[-3:]
+        refs = refs[1:6] + refs[7:-3]
+    qkv_ref, prob_ref, heads_ref, h1_ref, xn2_ref, xn_ref, part_ref, got_ref, send_sem, recv_sem = refs
     micros, members, shard_len, both = got_ref.shape
     cols = both // 2
     heads, length = bias_ref.shape[0], bias_ref.shape[2]
@@ -254,9 +272,26 @@
             (me, base + peer),
         )
 
+    def ride(s):
+        peer = partner_of(me, s, sent_ref.shape[0])
+        return remote(
+            sent_ref.at[peer], arrived_ref.at[me], ride_send.at[s], ride_recv.at[s], (peer, line)
+        )
+
+    def stay():
+        return pltpu.make_async_copy(sent_ref.at[me], arrived_ref.at[me], ride_own)
+
     @pl.when((micro == 0) & (group == 0))
     def _():
-        greet([(me, base + lax.rem(mine + s, members)) for s in range(1, members)])
+        peers = [(me, base + lax.rem(mine + s, members)) for s in range(1, members)]
+        if riding:
+            devices = sent_ref.shape[0]
+            peers += [(partner_of(me, s, devices), line) for s in range(1, devices)]
+        greet(peers)
+        if riding:
+            stay().start()
+            for s in range(1, devices):
+                ride(s).start()
 
     @pl.when(group == 0)
     def _():
@@ -318,15 +353,24 @@
         for m in range(micros):
             for s in range(1, members):
                 swap(m, s).wait_send()
+        if riding:
+            stay().wait()
+            for s in range(1, sent_ref.shape[0]):
+                ride(s).wait()
 
 
 def attend(
-    x, gain, own_weight, other_weight, bias, seg, out_weight, x_own, moe_gain, scale, members, identity
+    x, gain, own_weight, other_weight, bias, seg, out_weight, x_own, moe_gain, scale, members, identity,
+    rider=None,
 ):
     micros, half, width = x.shape
     cols = own_weight.shape[2]
     heads = bias.shape[0] // 2
     shard_len = half // members
+    riders = [] if rider is None else [rider]
+    ride_sems = []
+    for array in riders:
+        ride_sems = [pltpu.SemaphoreType.DMA((array.shape[0],))] * 2 + [pltpu.SemaphoreType.DMA]
 
     def once(shape):
         return pl.BlockSpec(shape, lambda m, p: (0,) * len(shape), pipeline_mode=pl.Buffered(1))
@@ -340,7 +384,8 @@
             jax.ShapeDtypeStruct((micros, half, 2 * cols), BF16),
             jax.ShapeDtypeStruct((micros, shard_len, width), F32),
             jax.ShapeDtypeStruct((micros, shard_len, width), BF16),
-        ),
+        )
+        + tuple(jax.ShapeDtypeStruct(array.shape, array.dtype) for array in riders),
         in_specs=[
             pl.BlockSpec((1, half, width), lambda m, p: (m, 0, 0)),
             once((1, width)),
@@ -352,21 +397,24 @@
             once(out_weight.shape),
             once(x_own.shape),
             once((1, width)),
-        ],
+        ]
+        + [any_space()] * len(riders),
         out_specs=(
             pl.BlockSpec((1, 1, 3, half, cols), lambda m, p: (m, p, 0, 0, 0)),
             pl.BlockSpec((1, 1, heads, half, half), lambda m, p: (m, p, 0, 0, 0)),
             pl.BlockSpec((1, half, cols), lambda m, p: (m, 0, p)),
             pl.BlockSpec((micros, shard_len, width), lambda m, p: (0, 0, 0)),
             pl.BlockSpec((micros, shard_len, width), lambda m, p: (0, 0, 0)),
-        ),
+        )
+        + (any_space(),) * len(riders),
         scratch_shapes=[
             pltpu.VMEM((half, width), BF16),
             pltpu.VMEM((micros, members, shard_len, 2 * cols), BF16),
             pltpu.VMEM((micros, members, shard_len, 2 * cols), BF16),
             pltpu.SemaphoreType.DMA((micros, members)),
             pltpu.SemaphoreType.DMA((micros, members)),
-        ],
+        ]
+        + ride_sems,
         compiler_params=pltpu.CompilerParams(
             vmem_limit_bytes=VMEM_LIMIT, collective_id=identity, has_side_effects=True
         ),
@@ -378,7 +426,7 @@
         name="attend",
     )(
         x, gain, own_weight, other_weight, bias, seg.reshape(micros, 1, half),
-        seg.reshape(micros, half, 1), out_weight, x_own, moe_gain,
+        seg.reshape(micros, half, 1), out_weight, x_own, moe_gain, *riders,
     )
 
 
@@ -769,50 +817,75 @@
     )(rows, place)
 
 
-def place_kernel(cap, route_ref, live_ref, place_ref, other_ref):
-    shard_len = route_ref.shape[2]
-    count = other_ref.shape[1]
-    experts = count // cap
-    first, second = route_ref[0, 0:1, :], route_ref[0, 1:2, :]
-    live = live_ref[0] >= 0
-    ids = lax.broadcasted_iota(jnp.int32, (experts, shard_len), 0)
-    chosen = ((ids == first) | (ids == second)) & live
+def places(route_ref, index, cap, experts):
+    shard_len = route_ref.shape[-1]
     row = lax.broadcasted_iota(jnp.int32, (shard_len, shard_len), 0)
     col = lax.broadcasted_iota(jnp.int32, (shard_len, shard_len), 1)
     earlier = jnp.where(row < col, 1.0, 0.0).astype(BF16)
+    ids = lax.broadcasted_iota(jnp.int32, (experts, shard_len), 0)
+    pair = [route_ref[index + (slice(k, k + 1),)] for k in range(2)]
+    chosen = (ids == pair[0]) | (ids == pair[1])
     before = mm(jnp.where(chosen, 1.0, 0.0).astype(BF16), earlier)
-    spots = lax.broadcasted_iota(jnp.int32, (count, shard_len), 0)
-    other = jnp.full((count, 1), -1, jnp.int32)
-    for k, route in enumerate((first, second)):
+    found = []
+    for route in pair:
         position = jnp.sum(jnp.where(ids == route, before, 0.0), axis=0, keepdims=True)
-        place = jnp.where(live, route * cap + position.astype(jnp.int32), -1)
-        place_ref[0, k : k + 1, :] = place
-        partner = (second, first)[k]
-        found = jnp.max(jnp.where(spots == place, partner, -1), axis=1, keepdims=True)
-        other = jnp.maximum(other, found)
-    other_ref[0] = other
-
-
-def find_places(route, live, experts, cap):
-    count, _, shard_len = route.shape
+        found.append(jnp.where(route >= 0, route * cap + position.astype(jnp.int32), -1))
+    return pair, found
+
+
+def place_kernel(cap, experts, route_ref, place_ref):
+    blocks, micros, _, shard_len = route_ref.shape
+    for block in range(blocks):
+        for micro in range(micros):
+            _, found = places(route_ref, (block, micro), cap, experts)
+            for k in range(2):
+                lanes = slice(block * shard_len, (block + 1) * shard_len)
+                place_ref[micro, k : k + 1, lanes] = found[k]
+
+
+def find_places(route, experts, cap):
+    blocks, micros, _, shard_len = route.shape
+    vmem = pl.BlockSpec(memory_space=pltpu.VMEM)
     return pl.pallas_call(
-        functools.partial(place_kernel, cap),
-        grid=(count,),
-        out_shape=(
-            jax.ShapeDtypeStruct((count, 2, shard_len), jnp.int32),
-            jax.ShapeDtypeStruct((count, experts * cap, 1), jnp.int32),
-        ),
-        in_specs=[
-            pl.BlockSpec((1, 2, shard_len), lambda b: (b, 0, 0)),
-            pl.BlockSpec((1, 1, shard_len), lambda b: (b, 0, 0)),
-        ],
-        out_specs=(
-            pl.BlockSpec((1, 2, shard_len), lambda b: (b, 0, 0)),
-            pl.BlockSpec((1, experts * cap, 1), lambda b: (b, 0, 0)),
-        ),
+        functools.partial(place_kernel, cap, experts),
+        out_shape=jax.ShapeDtypeStruct((micros, 2, blocks * shard_len), jnp.int32),
+        in_specs=[vmem],
+        out_specs=vmem,
         compiler_params=pltpu.CompilerParams(vmem_limit_bytes=VMEM_LIMIT),
         name="find_places",
-    )(route, live)
+    )(route)
+
+
+def pair_kernel(route_ref, pair_ref):
+    _, _, here, blocks, cap, experts = pair_ref.shape
+    shard_len = route_ref.shape[-1]
+    me = lax.axis_index("expert")
+    spots = lax.broadcasted_iota(jnp.int32, (cap, shard_len), 0)
+    ids = lax.broadcasted_iota(jnp.int32, (cap, experts), 1)
+    for block in range(blocks):
+        pair, place = places(route_ref, (0, block, 0), cap, experts)
+        for e in range(here):
+            expert = me * here + e
+            other = jnp.full((cap, 1), -1, jnp.int32)
+            for k in range(2):
+                hit = spots + expert * cap == place[k]
+                found = jnp.max(jnp.where(hit, pair[1 - k], -1), axis=1, keepdims=True)
+                other = jnp.maximum(other, found)
+            sign = jnp.where(ids == expert, 1.0, 0.0) - jnp.where(ids == other, 1.0, 0.0)
+            pair_ref[0, 0, e, block] = jnp.where(other >= 0, sign, 0.0).astype(BF16)
+
+
+def find_pairs(route, experts, here, cap):
+    devices, blocks, micros, _, shard_len = route.shape
+    return pl.pallas_call(
+        pair_kernel,
+        grid=(micros, devices),
+        out_shape=jax.ShapeDtypeStruct((micros, devices, here, blocks, cap, experts), BF16),
+        in_specs=[pl.BlockSpec((1, blocks, 1, 2, shard_len), lambda m, s: (s, 0, m, 0, 0))],
+        out_specs=pl.BlockSpec((1, 1, here, blocks, cap, experts), lambda m, s: (m, s, 0, 0, 0, 0)),
+        compiler_params=pltpu.CompilerParams(vmem_limit_bytes=VMEM_LIMIT),
+        name="find_pairs",
+    )(route)
 
 
 def expert_kernel(
@@ -824,6 +897,9 @@
     step = pl.program_id(0)
     me = lax.axis_index("expert")
     line = lax.axis_index("hidden")
+    first_wave = bits_of(devices)
+    rest = [s for s in range(1, devices) if s not in first_wave]
+    later_waves = [rest[i : i + 2] for i in range(0, len(rest), 2)]
 
     def x_copy(s):
         peer = partner_of(me, s, devices)
@@ -890,7 +966,7 @@
                 device_id_type=pl.DeviceIdType.MESH,
             )
         pl.semaphore_wait(barrier, devices - 1)
-        for s in range(devices - 1, 0, -1):
+        for s in first_wave:
             x_copy(s).start()
         own = pltpu.make_async_copy(sent_ref.at[me], got_ref.at[0], own_sem)
         own.start()
@@ -899,6 +975,13 @@
     @pl.when(step > 0)
     def _():
         x_copy(step).wait_recv()
+
+    for index, wave in enumerate(later_waves):
+
+        @pl.when(step == 2 + index)
+        def _(wave=wave):
+            for s in wave:
+                x_copy(s).start()
 
     @pl.when(step > 1)
     def _():
@@ -938,7 +1021,6 @@
     def kept(cols):
         return jax.ShapeDtypeStruct((devices, experts, cap, cols), BF16)
 
-    rows = devices * cap
     return pl.pallas_call(
         expert_kernel,
         grid=(devices,),
@@ -968,11 +1050,7 @@
         compiler_params=pltpu.CompilerParams(
             vmem_limit_bytes=VMEM_LIMIT, collective_id=identity, has_side_effects=True
         ),
-        cost_estimate=pl.CostEstimate(
-            flops=12 * experts * rows * width * hidden,
-            bytes_accessed=80 * experts * rows * width,
-            transcendentals=experts * rows * hidden,
-        ),
+        cost_estimate=pl.CostEstimate(flops=0, bytes_accessed=4000000, transcendentals=0),
         name="expert_pass",
     )(sent, dy, pair, wr, wg, wu, wd)
 
@@ -1090,27 +1168,18 @@
         return lax.psum_scatter(values, "hidden", scatter_dimension=0, tiled=True)
 
     states = [dict() for _ in range(micro_count)]
+    own_seg = lax.dynamic_slice_in_dim(segment_ids[:, 0], hidden_index * shard_len, shard_len, 1)
+    live_routes = jnp.where(own_seg[:, None, :] >= 0, routes[:, 0].transpose(0, 2, 1), -1)
     *x_all, other_qkv, all_out, all_routes, other_table = opening(
         x_in[:, 0], qkv_weight.reshape(3 * width, head_cols), out_weight,
-        routes[:, 0].transpose(0, 2, 1), bias_table.T.astype(F32), devices, blocks, members,
+        live_routes, bias_table.T.astype(F32), devices, blocks, members,
     )
     x_half = [x.reshape(1, half, width) for x in x_all]
     other_qkv = other_qkv.reshape(qkv_weight.shape)
     all_out = all_out.reshape(blocks, head_cols, width)
 
-    route = all_routes.transpose(1, 0, 2, 3).reshape(micro_count * blocks, 2, shard_len)
-    live = segment_ids.reshape(micro_count * blocks, 1, shard_len)
-    place, other = find_places(route, live, expert_count, capacity)
-    place = place.reshape(micro_count, blocks, 2, shard_len).transpose(0, 2, 1, 3)
-    place = place.reshape(micro_count, 2, slot_count)
-    other = other.reshape(micro_count, blocks, devices, experts_here, capacity)
-    other = exchange(other.transpose(2, 0, 3, 1, 4)).transpose(1, 0, 2, 3, 4)
-    other = other.reshape(micro_count, devices, experts_here, blocks * capacity, 1)
-    expert_ids = jnp.arange(expert_count, dtype=jnp.int32)
-    me = expert_index * experts_here + jnp.arange(experts_here, dtype=jnp.int32)
-    plus = me[None, None, :, None, None] == expert_ids
-    pairs = plus.astype(F32) - (other == expert_ids).astype(F32)
-    pairs = jnp.where(other >= 0, pairs, 0.0).astype(BF16)
+    own_routes = lax.dynamic_index_in_dim(all_routes, expert_index, 0, keepdims=False)
+    place = find_places(own_routes, expert_count, capacity)
 
     tables = jnp.concatenate([bias_table.T.astype(F32), other_table], axis=0)
     onehot_bucket = bucket_onehot(half, bucket_count)
@@ -1119,10 +1188,6 @@
 
     def spread(rows, micro):
         return spread_rows(rows, place[micro], expert_count, capacity, shard_len)
-
-    def send_dy(micro, kept, rows):
-        kept["dy_sent"] = spread(rows, micro)
-        kept["dy"] = exchange(kept["dy_sent"].reshape(flat_shape)).reshape(token_shape)
 
     def experts(micro, kept, *behind):
         sent = spread(kept["xn2_all"], micro).reshape(token_shape)
@@ -1137,43 +1202,50 @@
         kept["dxn2"] = scatter(kept["dx_part"])
 
     states[0]["dy_all"] = gather(cotangent[0, 0])
-    send_dy(0, states[0], states[0]["dy_all"])
     for micro in range(1, micro_count):
         before = states[micro - 1]["dy_all"]
         states[micro]["dy_all"] = gather(after(cotangent[micro, 0], before, all_out))
-    behind = (states[0]["dy_sent"],)
+    behind = ()
     for micro in range(micro_count):
         state = states[micro]
-        qkv, prob, heads, h1, xn2 = attend(
+        rider = spread(after(state["dy_all"], *behind), micro).reshape(token_shape)
+        qkv, prob, heads, h1, xn2, state["dy"] = attend(
             after(x_half[micro], *behind), attn_gain_f, qkv_weight, other_qkv, bias,
             seg_half[micro : micro + 1], all_out, x_in[micro], moe_gain_f, scale, members, 10 + micro,
+            rider,
         )
         state.update(qkv=qkv[0], prob=prob[0], heads=heads[0], h1=h1[0], xn2=xn2[0])
         behind = (xn2,)
-    for micro in range(1, micro_count):
-        send_dy(micro, states[micro], after(states[micro]["dy_all"], states[-1]["xn2"]))
+    pairs = find_pairs(after(all_routes, states[0]["xn2"]), expert_count, experts_here, capacity)
+    pairs = pairs.reshape(micro_count, devices, experts_here, blocks * capacity, expert_count)
     behind = ()
     for micro in range(micro_count):
         states[micro]["xn2_all"] = gather(after(states[micro]["xn2"], *behind))
-        behind = (states[micro]["xn2_all"], states[-1]["dy_sent"])
+        behind = (states[micro]["xn2_all"],)
     behind = ()
     for micro in range(micro_count):
         experts(micro, states[micro], *behind)
         behind = (states[micro]["dx_part"],)
-    behind = (states[-1]["dx_part"],)
+    last_part = states[-1]["dx_part"]
+    kept = [state["weights"] for state in states]
+    kept[-1] = tuple(after(list(kept[-1]), last_part))
+    dwr, dwg, dwu, dwd = weight_pass(kept)
+    behind = (last_part,)
     grads = None
     for micro in range(micro_count):
         state = states[micro]
         state["y_back"] = exchange(after(state["y_sent"], *behind)).reshape(place_shape)
+        behind = (dwr,)
+    for micro in range(micro_count):
+        state = states[micro]
         state["x_grad"], grads, state["line"], state["moe_gain_grad"], state["attn_gain_grad"] = (
             attend_back(
-                state["dxn2"], state["h1"], cotangent[micro, 0], x_in[micro, 0], moe_gain_f,
-                attn_gain_f, all_out, x_half[micro][0], qkv_weight, other_qkv, state["qkv"],
-                state["prob"], state["heads"], grads, scale, devices, members,
+                after(state["dxn2"], dwr), state["h1"], cotangent[micro, 0], x_in[micro, 0],
+                moe_gain_f, attn_gain_f, all_out, x_half[micro][0], qkv_weight, other_qkv,
+                state["qkv"], state["prob"], state["heads"], grads, scale, devices, members,
                 4 + micro_count + micro,
             )
         )
-        behind = (grads,)
     parts = []
     for micro in range(micro_count):
         state = states[micro]
@@ -1181,9 +1253,6 @@
         state["mixed"] = scatter(parts[-1])
         state["block_out"] = (state["h1"] + state["mixed"].astype(F32)).astype(BF16)
     pieces = exchange(grads)
-    kept = [state["weights"] for state in states]
-    kept[-1] = tuple(after(list(kept[-1]), *parts))
-    dwr, dwg, dwu, dwd = weight_pass(kept)
 
     def added(name):
         total = states[0][name]

time: 849 us -> 853 us (level)
  waiting for transfers between devices: 6.06 us -> 47.2 us
  Pallas kernels: 752 us -> 735 us
  starting transfers between devices: 27.4 us -> 14.9 us
    pallas_call x2, Pallas kernels: 75.6 us -> 132 us  [attend(): pl.pallas_call(functools.partial(attend_kernel, scale), grid=(micros, 2),...]
    pallas_call x2, Pallas kernels: 319 us -> 273 us  [expert_pass(): pl.pallas_call(expert_kernel, grid=(devices,), out_shape=(kept(width), ke...]
    all_to_all x6 -> x3, waiting for transfers between devices: 5.3 us -> 46.4 us  [exchange(): lax.all_to_all(buffer, 'expert', split_axis=0, concat_axis=0, tiled=True)]
    pallas_call x2, Pallas kernels: 133 us -> 98.2 us  [attend_back(): pl.pallas_call(functools.partial(back_kernel, scale, prev is not None), g...]
    all_to_all x6 -> x3, starting transfers between devices: 26.7 us -> 13.9 us  [exchange(): lax.all_to_all(buffer, 'expert', split_axis=0, concat_axis=0, tiled=True)]
  transfers between devices with their start and end apart: 14 -> 11, of which waited for: 2 -> 2; matrix products, arithmetic and copies ran while one was open for 4% -> 3% of each run, Pallas kernels for 90% -> 87%
where the time goes in v7:
time: 853 us; the launch traced here: 844 us
  Pallas kernels  735 us (86%)
  waiting for transfers between devices  47.2 us (6%)
  local copies, waits for them, and re-layouts  20.3 us (2%)
  between operations  15.1 us (2%)
  starting transfers between devices  14.9 us (2%)
  other arithmetic  9.79 us (1%)
    pallas_call x2, Pallas kernels, expert_pass(): pl.pallas_call(expert_kernel, grid=(devices,), out_shape=(kept(width), ke...  273 us
    pallas_call x2, Pallas kernels, attend(): pl.pallas_call(functools.partial(attend_kernel, scale), grid=(micros, 2),...  132 us
    pallas_call x2, Pallas kernels, attend_back(): pl.pallas_call(functools.partial(back_kernel, scale, prev is not None), g...  98.2 us
    pallas_call x1, Pallas kernels, opening(): pl.pallas_call(functools.partial(opening_kernel, micros), out_shape=(jax....  72.6 us
    pallas_call x1, Pallas kernels, closing(): pl.pallas_call(closing_kernel, out_shape=(jax.ShapeDtypeStruct((devices,...  59.5 us
    all_to_all x3, waiting for transfers between devices, exchange(): lax.all_to_all(buffer, 'expert', split_axis=0, concat_axis=0, tiled=True)  46.4 us
    pallas_call x1, Pallas kernels, weight_pass(): pl.pallas_call(weight_kernel, grid=(experts, width // block), out_shape=(...  38.3 us
    pallas_call x4, Pallas kernels, collect_rows(): pl.pallas_call(collect_kernel, grid=(blocks,), out_shape=jax.ShapeDtypeSt...  22.7 us
  transfers between devices with their start and end apart: 11, of which 2 were waited for; matrix products, arithmetic and copies ran while one was open for 3% of the time, Pallas kernels for 87%

profile of v7, /device:TPU:0, one launch (start us, length us, event | category | flops | bytes accessed | tf_op | source)
XLA Modules:
  0.0 844.0 jit_solution(8580421928880956445)
XLA Ops:
  7.3 2.5 slice_bitcast_fusion.9
  9.8 0.8 dynamic-slice_compare_fusion
  10.6 1.3 convert_bitcast_fusion.table_ref
  11.9 1.3 fusion.11.routes_ref
  13.2 72.6 %opening.1 = (bf16[2,256,1024]{2,1,0:T(8,128)(2,1)}, bf16[2,256,1024]{2,1,0:T(8,128)(2,1)}, bf16[8,384,256]{2,1,0:T(8,128)(2,1)}, bf16[4,8,32,1024]{3,2,1,0:T(8,...) custom-call(bf16[2,256,1024]{2,1,0:T(8,128)(2,1)} %bitcast.127, bf16[3072,256]{1,0:T(8,128)(2,1)} %bitcast.110, ...), custom_call_target="tpu_custom_call" | custom-call | bytes 60000000 | tf_op jit(solution)/shard_map/opening/pallas_call | solution.py:220
  87.1 0.9 copy.27.seg_col_ref
  88.0 1.3 dynamic-slice_bitcast_fusion.route_ref
  89.3 1.6 find_places.1
  90.9 1.1 fusion.3
  92.0 0.7 reshape.205.line_ref
  92.7 5.9 position_bias.1.bias_ref
  98.6 1.3 slice_bitcast_fusion.5
  99.9 1.4 slice_bitcast_fusion.3
  101.3 5.3 spread_rows.4
  106.7 65.8 %attend.2 = (bf16[1,2,3,512,256]{4,3,2,1,0:T(8,128)(2,1)}, bf16[1,2,4,512,512]{4,3,2,1,0:T(8,128)(2,1)}, bf16[1,512,512]{2,1,0:T(8,128)(2,1)}, f32[1,256,1024]{2...) custom-call(bf16[1,512,1024]{2,1,0:T(8,128)(2,1)} %bitcast.135, f32[1,1024]{1,0:T(1,128)} %bitcast.149, ...), custom_call_target="tpu_custom_call" | custom-call | flops 2684354560 | bytes 40000000 | tf_op jit(solution)/shard_map/attend/pallas_call | solution.py:378
  172.8 0.9 copy.28.seg_col_ref
  173.6 5.3 spread_rows.6
  178.9 65.8 %attend.3 = (bf16[1,2,3,512,256]{4,3,2,1,0:T(8,128)(2,1)}, bf16[1,2,4,512,512]{4,3,2,1,0:T(8,128)(2,1)}, bf16[1,512,512]{2,1,0:T(8,128)(2,1)}, f32[1,256,1024]{2...) custom-call(bf16[1,512,1024]{2,1,0:T(8,128)(2,1)} %bitcast.133, f32[1,1024]{1,0:T(1,128)} %bitcast.150, ...), custom_call_target="tpu_custom_call" | custom-call | flops 2684354560 | bytes 40000000 | tf_op jit(solution)/shard_map/attend/pallas_call | solution.py:378
  245.3 10.9 %find_pairs.1 = bf16[2,8,2,4,40,16]{5,4,3,2,1,0:T(8,128)(2,1)} custom-call(s32[8,4,2,2,256]{4,3,2,1,0:T(2,128)} %get-tuple-element.87.route_ref), custom_call_target="tpu_custom_call" | custom-call | tf_op jit(solution)/shard_map/find_pairs/pallas_call | solution.py:880
  256.2 2.5 fusion.22
  258.6 5.3 spread_rows.5
  263.9 136.6 %expert_pass.2 = (bf16[8,2,160,1024]{3,2,1,0:T(8,128)(2,1)}, bf16[8,2,160,1024]{3,2,1,0:T(8,128)(2,1)}, bf16[8,2,160,1024]{3,2,1,0:T(8,128)(2,1)}, bf16[8,2,160,...) custom-call(bf16[8,2,160,1024]{3,2,1,0:T(8,128)(2,1)} %bitcast.109, ...), custom_call_target="tpu_custom_call" | custom-call | bytes 4000000 | tf_op jit(solution)/shard_map/expert_pass/pallas_call | solution.py:1024
  400.5 5.6 collect_rows.4
  406.2 5.3 spread_rows.7
  411.6 136.2 %expert_pass.3 = (bf16[8,2,160,1024]{3,2,1,0:T(8,128)(2,1)}, bf16[8,2,160,1024]{3,2,1,0:T(8,128)(2,1)}, bf16[8,2,160,1024]{3,2,1,0:T(8,128)(2,1)}, bf16[8,2,160,...) custom-call(bf16[8,2,160,1024]{3,2,1,0:T(8,128)(2,1)} %bitcast.108, ...), custom_call_target="tpu_custom_call" | custom-call | bytes 4000000 | tf_op jit(solution)/shard_map/expert_pass/pallas_call | solution.py:1024
  547.8 5.6 collect_rows.5
  553.4 4.6 all-to-all-start
  558.6 38.3 %weight_pass.1 = (f32[2,16,1024]{2,1,0:T(8,128)}, f32[2,704,1024]{2,1,0:T(8,128)}, f32[2,704,1024]{2,1,0:T(8,128)}, f32[2,704,1024]{2,1,0:T(8,128)}) custom-call(bf16[8,2,160,1024]{3,2,1,0:T(8,128)(2,1)} %get-tuple-element.100.refs_0_, bf16[8,2,160,1024]{3,2,1,0:T(8,128)(2,1)} %get-tuple-element.101.refs_1_, ...), custom_call_target="tpu_custom_call" | custom-call | flops 22145925120 | bytes 59899904 | tf_op jit(solution)/shard_map/weight_pass/pallas_call | solution.py:1090
  597.0 49.3 %attend_back.2 = (bf16[256,1024]{1,0:T(8,128)(2,1)}, bf16[8,2,512,256]{3,2,1,0:T(8,128)(2,1)}, f32[2,4,1024]{2,1,0:T(4,128)}, f32[1,1024]{1,0:T(1,128)}, f32[1,1024]{1,0:T(1,128)}) custom-call(bf16[256,1024]{1,0:T(8,128)(2,1)} %reduce-scatter.7.cloned.1.call-done.grad_ref, f32[256,1024]{1,0:T(8,128)} %bitcast.137, ...), custom_call_target="tpu_custom_call" | custom-call | flops 5368709120 | bytes 40000000 | tf_op jit(solution)/shard_map/attend_back/pallas_call | solution.py:623
  646.3 4.7 all-to-all-start.1
  651.0 48.9 %attend_back.3 = (bf16[256,1024]{1,0:T(8,128)(2,1)}, bf16[8,2,512,256]{3,2,1,0:T(8,128)(2,1)}, f32[2,4,1024]{2,1,0:T(4,128)}, f32[1,1024]{1,0:T(1,128)}, f32[1,1024]{1,0:T(1,128)}) custom-call(bf16[256,1024]{1,0:T(8,128)(2,1)} %reduce-scatter.5.cloned.1.call-done.grad_ref, f32[256,1024]{1,0:T(8,128)} %bitcast.138, ...), custom_call_target="tpu_custom_call" | custom-call | flops 5368709120 | bytes 40000000 | tf_op jit(solution)/shard_map/attend_back/pallas_call | solution.py:623
  699.9 5.7 collect_rows.6
  705.6 5.7 all-to-all-done.1
  711.4 4.6 all-to-all-start.2
  716.1 5.7 collect_rows.7
  723.3 1.1 maximum_bitcast_fusion.1
  724.4 40.7 %all-to-all-done.2.pieces_ref = bf16[8,2,512,256]{3,2,1,0:T(8,128)(2,1)} async-done(((bf16[8,2,512,256]{3,2,1,0:T(8,128)(2,1)}), bf16[8,2,512,256]{3,2,1,0:T(8,128)(2,1)}, u32[]{:S(2)}, u32[]{:S(2)}) %all-to-all-start.2) | async-done | bytes 4194336 | tf_op jit(solution)/shard_map/all_to_all | solution.py:1162
  765.0 59.5 %closing.1 = (bf16[8,512,256]{2,1,0:T(8,128)(2,1)}, f32[152,128]{1,0:T(8,128)}) custom-call(bf16[8,2,512,256]{3,2,1,0:T(8,128)(2,1)} %all-to-all-done.2.pieces_ref, f32[152,128]{1,0:T(8,128)} %fusion.6.small_ref), custom_call_target="tpu_custom_call" | custom-call | bytes 60000000 | tf_op jit(solution)/shard_map/closing/pallas_call | solution.py:728
  824.5 0.8 slice.97
  825.4 0.8 slice.102
  826.2 1.1 slice.108
  827.4 1.9 slice.107
  829.4 0.6 reshape.229
  830.0 1.3 copy.29
  831.9 1.3 slice_bitcast_fusion.7
  833.2 1.2 fusion
  834.4 1.2 fusion.1
  835.6 1.1 maximum_bitcast_fusion
  (83 shorter events, 5.1 us)
Async XLA Ops:
  7.2 79.9 %copy-start.12 = (s32[2,1,1024]{2,1,0:T(1,128)S(1)}, s32[2,1,1024]{2,1,0:T(1,128)}, u32[]{:S(2)}) copy-start(s32[2,1,1024]{2,1,0:T(1,128)} %param.15) | copy-start | bytes 24580
  7.2 78.7 %copy-start.17 = (bf16[1024]{0:T(1024)(128)(2,1)S(1)}, bf16[1024]{0:T(1024)(128)(2,1)}, u32[]{:S(2)}) copy-start(bf16[1024]{0:T(1024)(128)(2,1)} %param.20) | copy-start | bytes 6148
  7.2 79.3 %copy-start.18 = (bf16[1024]{0:T(1024)(128)(2,1)S(1)}, bf16[1024]{0:T(1024)(128)(2,1)}, u32[]{:S(2)}) copy-start(bf16[1024]{0:T(1024)(128)(2,1)} %param.21) | copy-start | bytes 6148
  7.2 78.6 %all-gather.12.cloned.1.call-start = ((), (), s32[]{:S(2)}) async-start(), calls=%async_computation.14 | async-start | bytes 2621440 | tf_op jit(solution)/shard_map/all_gather | solution.py:1165
  9.8 90.1 %copy-start.1 = (bf16[2,1,256,1024]{3,2,1,0:T(8,128)(2,1)S(1)}, bf16[2,1,256,1024]{3,2,1,0:T(8,128)(2,1)}, u32[]{:S(2)}) copy-start(bf16[2,1,256,1024]{3,2,1,0:T(8,128)(2,1)} %param.13) | copy-start | bytes 3145732
  9.8 163.8 %all-gather.8.cloned.1.call-start = ((), (), s32[]{:S(2)}) async-start(), calls=%async_computation.8 | async-start | bytes 2621440 | tf_op jit(solution)/shard_map/all_gather | solution.py:1165
  11.9 79.0 %copy-start.11 = (f32[4,32]{1,0:T(4,128)S(1)}, f32[4,32]{1,0:T(4,128)}, u32[]{:S(2)}) copy-start(f32[4,32]{1,0:T(4,128)} %convert_bitcast_fusion.table_ref) | copy-start | bytes 1540
  85.8 158.9 %all-gather.6.cloned.1.call-start = ((), (), s32[]{:S(2)}) async-start(), calls=%async_computation.7 | async-start | bytes 2621440 | tf_op jit(solution)/shard_map/all_gather | solution.py:1165
  87.1 19.6 %copy-start.10 = (s32[1,1,512]{2,1,0:T(1,128)}, s32[1,1,512]{2,1,0:T(1,128)S(1)}, u32[]{:S(2)}) copy-start(s32[1,1,512]{2,1,0:T(1,128)S(1)} %get-tuple-element.183.seg_row_ref) | copy-start | bytes 6148
  87.1 85.7 %copy-start.9 = (s32[1,1,512]{2,1,0:T(1,128)}, s32[1,1,512]{2,1,0:T(1,128)S(1)}, u32[]{:S(2)}) copy-start(s32[1,1,512]{2,1,0:T(1,128)S(1)} %get-tuple-element.182.seg_row_ref) | copy-start | bytes 6148
  172.5 233.7 %all-gather.10.cloned.1.call-start = ((), (), s32[]{:S(2)}) async-start(), calls=%async_computation.9 | async-start | bytes 2621440 | tf_op jit(solution)/shard_map/all_gather | solution.py:1165
  244.8 352.2 %reduce-scatter.7.cloned.1.call-start = ((), (), s32[]{:S(2)}) async-start(), calls=%async_computation.11 | async-start | bytes 2621440 | tf_op jit(solution)/shard_map/reduce_scatter | solution.py:1168
  553.4 92.9 %all-to-all-start = ((bf16[8,320,1024]{2,1,0:T(8,128)(2,1)}), bf16[8,320,1024]{2,1,0:T(8,128)(2,1)}, u32[]{:S(2)}, u32[]{:S(2)}) async-start(bf16[8,320,1024]{2,1,0:T(8,128)(2,1)} %bitcast.124), calls=%async_computation | async-start | bytes 10485760 | tf_op jit(solution)/shard_map/all_to_all | solution.py:1162
  558.1 88.3 %reduce-scatter.5.cloned.1.call-start = ((), (), s32[]{:S(2)}) async-start(), calls=%async_computation.10 | async-start | bytes 2621440 | tf_op jit(solution)/shard_map/reduce_scatter | solution.py:1168
  646.3 65.0 %all-to-all-start.1 = ((bf16[8,320,1024]{2,1,0:T(8,128)(2,1)}), bf16[8,320,1024]{2,1,0:T(8,128)(2,1)}, u32[]{:S(2)}, u32[]{:S(2)}) async-start(bf16[8,320,1024]{2,1,0:T(8,128)(2,1)} %bitcast.123), calls=%async_computation.4 | async-start | bytes 10485760 | tf_op jit(solution)/shard_map/all_to_all | solution.py:1162
  651.0 182.2 %reduce-scatter.9.cloned.1.call-start = ((), (), s32[]{:S(2)}) async-start(), calls=%async_computation.12 | async-start | bytes 2621440 | tf_op jit(solution)/shard_map/reduce_scatter | solution.py:1168
  711.4 53.7 %all-to-all-start.2 = ((bf16[8,2,512,256]{3,2,1,0:T(8,128)(2,1)}), bf16[8,2,512,256]{3,2,1,0:T(8,128)(2,1)}, u32[]{:S(2)}, u32[]{:S(2)}) async-start(bf16[8,2,512,256]{3,2,1,0:T(8,128)(2,1)} %get-tuple-element.129), calls=%async_computation.6 | async-start | bytes 8388608 | tf_op jit(solution)/shard_map/all_to_all | solution.py:1162
  715.9 118.5 %reduce-scatter.11.cloned.1.call-start = ((), (), s32[]{:S(2)}) async-start(), calls=%async_computation.13 | async-start | bytes 2621440 | tf_op jit(solution)/shard_map/reduce_scatter | solution.py:1168
  716.0 5.9 copy-start.6
  716.0 5.9 copy-start.7
  716.0 5.9 copy-start.8
  716.0 6.5 copy-start.14
  716.0 6.5 copy-start.16
  716.0 6.5 copy-start.13
  716.0 6.5 copy-start.15
  716.0 7.3 copy-start.4
  716.0 7.2 copy-start.5
  824.5 2.8 copy-start
  827.3 5.9 copy-start.2
  827.4 7.1 copy-start.3
Sparse Core Ops, SparseCore 0:
  10.2 73.2 all-gather.11
  85.9 45.0 all-gather.7
  172.6 48.6 all-gather.5
  244.9 44.7 all-gather.9
  406.3 42.7 reduce-scatter.6
  561.6 44.6 reduce-scatter.4
  705.8 44.3 reduce-scatter.8
  752.5 55.2 reduce-scatter.10

commit v8 on v7

--- a/solution.py
+++ b/solution.py
@@ -111,48 +111,52 @@
 
 
 def opening_kernel(
-    micros, x_ref, qkv_ref, out_ref, routes_ref, table_ref, *refs,
+    micros, x_ref, qkv_ref, out_ref, routes_ref, table_ref, dy_ref, *refs,
 ):
     x_all, refs = refs[:micros], refs[micros:]
     (
-    qkv_all, out_all, routes_all, table_all,
-    x_send, x_recv, qkv_send, qkv_recv, out_send, out_recv, qkv_on_send, qkv_on_recv,
-    out_on_send, out_on_recv, routes_send, routes_recv, routes_on_send, routes_on_recv,
-    table_send, table_recv, own_sem,
+        qkv_all, out_all, routes_all, table_all, dy_all,
+        x_send, x_recv, qkv_send, qkv_recv, out_send, out_recv, qkv_on_send, qkv_on_recv,
+        out_on_send, out_on_recv, routes_send, routes_recv, routes_on_send, routes_on_recv,
+        table_send, table_recv, dy_send, dy_recv, own_sem,
     ) = refs
-    devices, qkv_rows = qkv_all.shape[0], qkv_all.shape[1]
-    blocks, out_rows = out_all.shape[0], out_all.shape[2]
+    devices, qkv_rows = qkv_all.shape[0] * 2, qkv_all.shape[2]
+    blocks, out_rows = out_all.shape[0], out_all.shape[3]
     members = x_all[0].shape[0]
     me = lax.axis_index("expert")
     line = lax.axis_index("hidden")
+    chip, core = me // 2, lax.rem(me, 2)
     mine = lax.rem(line, members)
     base = line - mine
-    others = [partner_of(me, s, devices) for s in range(1, devices)]
     along = [lax.rem(line + s, blocks) for s in range(1, blocks)]
     across = lax.rem(line + members, blocks)
-    greet([(other, line) for other in others] + [(me, z) for z in along])
+    sibling = partner_of(me, 1, devices)
+    greet([(partner_of(me, s, devices), line) for s in range(1, devices)] + [(me, z) for z in along])
     own = [
-        pltpu.make_async_copy(out_ref.at[pl.ds(me * out_rows, out_rows)], out_all.at[line, me], own_sem.at[0]),
+        pltpu.make_async_copy(
+            out_ref.at[pl.ds(me * out_rows, out_rows)], out_all.at[line, chip, core], own_sem.at[0]
+        ),
         pltpu.make_async_copy(routes_ref, routes_all.at[me, line], own_sem.at[1]),
+        pltpu.make_async_copy(dy_ref.at[me], dy_all.at[me], own_sem.at[2]),
     ]
     for micro in range(micros):
         own.append(
-            pltpu.make_async_copy(x_ref.at[micro], x_all[micro].at[mine], own_sem.at[2 + micro])
+            pltpu.make_async_copy(x_ref.at[micro], x_all[micro].at[mine], own_sem.at[3 + micro])
         )
     for copy in own:
         copy.start()
     first_qkv = remote(
-        qkv_ref.at[pl.ds(me * qkv_rows, qkv_rows)], qkv_all.at[me], qkv_send, qkv_recv, (me, across)
+        qkv_ref.at[pl.ds(me * qkv_rows, qkv_rows)], qkv_all.at[chip, core], qkv_send, qkv_recv,
+        (me, across),
     )
     first_qkv.start()
-    first_out = []
-    small = [remote(table_ref, table_all, table_send, table_recv, (me, across))]
-    first_routes = []
+    first_out, first_routes = [], []
+    rest = [remote(table_ref, table_all, table_send, table_recv, (me, across))]
     for s, z in enumerate(along):
         first_out.append(
             remote(
-                out_ref.at[pl.ds(me * out_rows, out_rows)], out_all.at[line, me], out_send.at[s],
-                out_recv.at[s], (me, z),
+                out_ref.at[pl.ds(me * out_rows, out_rows)], out_all.at[line, chip, core],
+                out_send.at[s], out_recv.at[s], (me, z),
             )
         )
         first_routes.append(
@@ -160,83 +164,102 @@
                 routes_ref, routes_all.at[me, line], routes_send.at[s], routes_recv.at[s], (me, z)
             )
         )
-    for copy in first_routes + first_out + small:
+    for copy in first_routes + first_out + rest:
         copy.start()
-    xs = []
     for micro in range(micros):
         for s in range(1, members):
             peer = base + lax.rem(mine + s, members)
-            xs.append(
-                remote(
-                    x_ref.at[micro], x_all[micro].at[mine], x_send.at[micro, s],
-                    x_recv.at[micro, s], (me, peer),
-                )
+            copy = remote(
+                x_ref.at[micro], x_all[micro].at[mine], x_send.at[micro, s], x_recv.at[micro, s],
+                (me, peer),
             )
-    for copy in xs:
+            copy.start()
+            rest.append(copy)
+    for s in range(1, devices):
+        peer = partner_of(me, s, devices)
+        copy = remote(dy_ref.at[peer], dy_all.at[me], dy_send.at[s], dy_recv.at[s], (peer, line))
         copy.start()
+        rest.append(copy)
     first_qkv.wait_recv()
-    second = []
-    for s, other in enumerate(others):
-        second.append(
-            remote(
-                qkv_all.at[me], qkv_all.at[me], qkv_on_send.at[s], qkv_on_recv.at[s], (other, line)
-            )
-        )
-        second[-1].start()
+    qkv_on, out_on = [], []
+    for s in range(2, devices, 2):
+        copy = remote(
+            qkv_all.at[chip, core], qkv_all.at[chip, core], qkv_on_send.at[s], qkv_on_recv.at[s],
+            (partner_of(me, s, devices), line),
+        )
+        copy.start()
+        qkv_on.append(copy)
     own[1].wait()
     for copy in first_routes:
         copy.wait_recv()
-    for s, other in enumerate(others):
-        second.append(
-            remote(
-                routes_all.at[me], routes_all.at[me], routes_on_send.at[s], routes_on_recv.at[s],
-                (other, line),
-            )
-        )
-        second[-1].start()
+    for s in range(1, devices):
+        copy = remote(
+            routes_all.at[me], routes_all.at[me], routes_on_send.at[s], routes_on_recv.at[s],
+            (partner_of(me, s, devices), line),
+        )
+        copy.start()
+        rest.append(copy)
     own[0].wait()
     for copy in first_out:
         copy.wait_recv()
-    for s, other in enumerate(others):
-        second.append(
-            remote(
-                out_all.at[:, me], out_all.at[:, me], out_on_send.at[s], out_on_recv.at[s],
-                (other, line),
-            )
-        )
-        second[-1].start()
+    for s in range(2, devices, 2):
+        copy = remote(
+            out_all.at[:, chip, core], out_all.at[:, chip, core], out_on_send.at[s],
+            out_on_recv.at[s], (partner_of(me, s, devices), line),
+        )
+        copy.start()
+        out_on.append(copy)
+    for copy in qkv_on:
+        copy.wait_recv()
+    copy = remote(
+        qkv_all.at[:, core], qkv_all.at[:, core], qkv_on_send.at[1], qkv_on_recv.at[1],
+        (sibling, line),
+    )
+    copy.start()
+    rest.append(copy)
+    for copy in out_on:
+        copy.wait_recv()
+    copy = remote(
+        out_all.at[:, :, core], out_all.at[:, :, core], out_on_send.at[1], out_on_recv.at[1],
+        (sibling, line),
+    )
+    copy.start()
+    rest.append(copy)
     for copy in own[2:]:
         copy.wait()
     first_qkv.wait_send()
-    for copy in first_out + first_routes:
+    for copy in first_out + first_routes + qkv_on + out_on:
         copy.wait_send()
-    for copy in small + xs + second:
+    for copy in rest:
         copy.wait()
 
 
-def opening(x, qkv, out, routes, table, devices, blocks, members):
+def opening(x, qkv, out, routes, table, dy, devices, blocks, members):
     micros, shard_len, width = x.shape
     dma = pltpu.SemaphoreType.DMA
+    pair = (devices // 2, 2)
     return pl.pallas_call(
         functools.partial(opening_kernel, micros),
         out_shape=(jax.ShapeDtypeStruct((members, shard_len, width), BF16),) * micros
         + (
-            jax.ShapeDtypeStruct((devices, qkv.shape[0] // devices, qkv.shape[1]), BF16),
-            jax.ShapeDtypeStruct((blocks, devices, out.shape[0] // devices, width), BF16),
+            jax.ShapeDtypeStruct(pair + (qkv.shape[0] // devices, qkv.shape[1]), BF16),
+            jax.ShapeDtypeStruct((blocks,) + pair + (out.shape[0] // devices, width), BF16),
             jax.ShapeDtypeStruct((devices, blocks) + routes.shape, jnp.int32),
             jax.ShapeDtypeStruct(table.shape, table.dtype),
-        ),
-        in_specs=[any_space()] * 5,
-        out_specs=(any_space(),) * (4 + micros),
+            jax.ShapeDtypeStruct(dy.shape, BF16),
+        ),
+        in_specs=[any_space()] * 6,
+        out_specs=(any_space(),) * (5 + micros),
         scratch_shapes=[
             dma((micros, members)), dma((micros, members)), dma, dma, dma((blocks,)), dma((blocks,)),
             dma((devices,)), dma((devices,)), dma((devices,)), dma((devices,)), dma((blocks,)),
-            dma((blocks,)), dma((devices,)), dma((devices,)), dma, dma, dma((2 + micros,)),
+            dma((blocks,)), dma((devices,)), dma((devices,)), dma, dma, dma((devices,)),
+            dma((devices,)), dma((3 + micros,)),
         ],
         compiler_params=pltpu.CompilerParams(collective_id=1, has_side_effects=True),
-        cost_estimate=pl.CostEstimate(flops=0, bytes_accessed=60000000, transcendentals=0),
+        cost_estimate=pl.CostEstimate(flops=0, bytes_accessed=200000000, transcendentals=0),
         name="opening",
-    )(x, qkv, out, routes, table)
+    )(x, qkv, out, routes, table, dy)
 
 
 def unit_rows(x):
@@ -420,7 +443,7 @@
         ),
         cost_estimate=pl.CostEstimate(
             flops=micros * 2 * half * cols * (8 * width + 4 * half),
-            bytes_accessed=40000000,
+            bytes_accessed=100000000,
             transcendentals=micros * 2 * heads * half * half,
         ),
         name="attend",
@@ -658,7 +681,7 @@
         ),
         cost_estimate=pl.CostEstimate(
             flops=2 * half * cols * (16 * width + 8 * half),
-            bytes_accessed=40000000,
+            bytes_accessed=150000000,
             transcendentals=0,
         ),
         name="attend_back",
@@ -667,39 +690,50 @@
 
 def closing_kernel(
     pieces_ref, small_ref, whole_ref, sum_ref,
-    total_ref, moved_ref, moved_got, piece_ref, small_got, line_sum, line_got,
-    small_send, small_recv, line_send, line_recv, moved_send, moved_recv, on_send, on_recv, own_sem,
+    half_got, held_ref, quarter_got, total_ref, moved_ref, moved_got, small_got, line_sum,
+    line_got, half_sem, quarter_send, quarter_recv, small_send, small_recv, line_send, line_recv,
+    moved_sem, on_send, on_recv, own_sem,
 ):
-    devices = pieces_ref.shape[0]
+    chips = pieces_ref.shape[0]
+    devices = 2 * chips
     blocks = line_got.shape[0]
     me = lax.axis_index("expert")
     line = lax.axis_index("hidden")
-    others = [partner_of(me, s, devices) for s in range(1, devices)]
+    chip, core = me // 2, lax.rem(me, 2)
+    sibling = partner_of(me, 1, devices)
     along = [lax.rem(line + s, blocks) for s in range(1, blocks)]
     across = lax.rem(line + blocks // 2, blocks)
-    greet([(other, line) for other in others] + [(me, z) for z in along])
+    greet([(partner_of(me, s, devices), line) for s in range(1, devices)] + [(me, z) for z in along])
+    halves = remote(
+        pieces_ref.at[:, 1 - core], half_got, half_sem.at[0], half_sem.at[1], (sibling, line)
+    )
+    halves.start()
     smalls = [
-        remote(small_ref, small_got.at[me], small_send.at[s], small_recv.at[s], (other, line))
-        for s, other in enumerate(others)
+        remote(
+            small_ref, small_got.at[me], small_send.at[s], small_recv.at[s],
+            (partner_of(me, s, devices), line),
+        )
+        for s in range(1, devices)
     ]
     for copy in smalls:
         copy.start()
     small_got[me] = small_ref[...]
-    moved = jnp.sum(pieces_ref[:, 1].astype(F32), axis=0)
-    moved_ref[...] = moved.astype(BF16)
-    cross = remote(moved_ref, moved_got, moved_send, moved_recv, (me, across))
-    cross.start()
-    total_ref[...] = jnp.sum(pieces_ref[:, 0].astype(F32), axis=0)
-    cross.wait_recv()
-    piece_ref[...] = (total_ref[...] + moved_got[...].astype(F32)).astype(BF16)
-    onward = [
-        remote(piece_ref, whole_ref.at[me], on_send.at[s], on_recv.at[s], (other, line))
-        for s, other in enumerate(others)
-    ]
-    for copy in onward:
-        copy.start()
-    own = pltpu.make_async_copy(piece_ref, whole_ref.at[me], own_sem)
-    own.start()
+    halves.wait_recv()
+    steps = range(1, chips)
+
+    def quarter(s):
+        other = partner_of(chip, s, chips)
+        return remote(
+            held_ref.at[other], quarter_got.at[s], quarter_send.at[s], quarter_recv.at[s],
+            (partner_of(me, 2 * s, devices), line),
+        )
+
+    for s in steps:
+        other = partner_of(chip, s, chips)
+        held = pieces_ref[other, core].astype(F32) + half_got[other].astype(F32)
+        held_ref[other] = held.astype(BF16)
+        quarter(s).start()
+    total_ref[...] = pieces_ref[chip, core].astype(F32) + half_got[chip].astype(F32)
     for copy in smalls:
         copy.wait_recv()
     line_sum[...] = jnp.sum(small_got[...], axis=0)
@@ -710,46 +744,73 @@
     for copy in lines:
         copy.start()
     line_got[line] = line_sum[...]
+    for s in steps:
+        quarter(s).wait_recv()
+        total_ref[...] += quarter_got[s].astype(F32)
+    moved_ref[...] = total_ref[1].astype(BF16)
+    cross = remote(moved_ref, moved_got, moved_sem.at[0], moved_sem.at[1], (me, across))
+    cross.start()
+    cross.wait_recv()
+    whole_ref[chip, core] = (total_ref[0] + moved_got[...].astype(F32)).astype(BF16)
+    onward = [
+        remote(
+            whole_ref.at[chip, core], whole_ref.at[chip, core], on_send.at[s], on_recv.at[s],
+            (partner_of(me, 2 * s, devices), line),
+        )
+        for s in steps
+    ]
+    for copy in onward:
+        copy.start()
     for copy in lines:
         copy.wait_recv()
     sum_ref[...] = jnp.sum(line_got[...], axis=0)
-    own.wait()
+    for copy in onward:
+        copy.wait_recv()
+    last = remote(
+        whole_ref.at[:, core], whole_ref.at[:, core], on_send.at[0], on_recv.at[0], (sibling, line)
+    )
+    last.start()
+    halves.wait_send()
+    for s in steps:
+        quarter(s).wait_send()
     cross.wait_send()
-    for copy in smalls + lines:
+    for copy in smalls + lines + onward:
         copy.wait_send()
-    for copy in onward:
-        copy.wait()
+    last.wait()
 
 
 def closing(pieces, small, blocks):
-    devices, _, rows, cols = pieces.shape
+    devices, both, rows, cols = pieces.shape
+    chips = devices // 2
     vmem = pl.BlockSpec(memory_space=pltpu.VMEM)
     dma = pltpu.SemaphoreType.DMA
     return pl.pallas_call(
         closing_kernel,
         out_shape=(
-            jax.ShapeDtypeStruct((devices, rows, cols), BF16),
+            jax.ShapeDtypeStruct((chips, 2, rows, cols), BF16),
             jax.ShapeDtypeStruct(small.shape, F32),
         ),
         in_specs=[vmem, vmem],
-        out_specs=(any_space(), vmem),
+        out_specs=(vmem, vmem),
         scratch_shapes=[
-            pltpu.VMEM((rows, cols), F32),
-            pltpu.VMEM((rows, cols), BF16),
+            pltpu.VMEM((chips, both, rows, cols), BF16),
+            pltpu.VMEM((chips, both, rows, cols), BF16),
+            pltpu.VMEM((chips, both, rows, cols), BF16),
+            pltpu.VMEM((both, rows, cols), F32),
             pltpu.VMEM((rows, cols), BF16),
             pltpu.VMEM((rows, cols), BF16),
             pltpu.VMEM((devices,) + small.shape, F32),
             pltpu.VMEM(small.shape, F32),
             pltpu.VMEM((blocks,) + small.shape, F32),
-            dma((devices,)), dma((devices,)), dma((blocks,)), dma((blocks,)), dma, dma,
-            dma((devices,)), dma((devices,)), dma,
+            dma((2,)), dma((chips,)), dma((chips,)), dma((devices,)), dma((devices,)),
+            dma((blocks,)), dma((blocks,)), dma((2,)), dma((chips,)), dma((chips,)), dma,
         ],
         compiler_params=pltpu.CompilerParams(
             vmem_limit_bytes=VMEM_LIMIT, collective_id=3, has_side_effects=True
         ),
-        cost_estimate=pl.CostEstimate(flops=0, bytes_accessed=60000000, transcendentals=0),
+        cost_estimate=pl.CostEstimate(flops=0, bytes_accessed=160000000, transcendentals=0),
         name="closing",
-    )(pieces, small)
+    )(pieces.reshape(chips, 2, both, rows, cols), small)
 
 
 def spread(rows, place0, place1, count):
@@ -889,7 +950,7 @@
 
 
 def expert_kernel(
-    sent_ref, dy_ref, pair_ref, wr_ref, wg_ref, wu_ref, wd_ref,
+    by_block, sent_ref, dy_ref, pair_ref, wr_ref, wg_ref, wu_ref, wd_ref,
     back_ref, y_ref, x_ref, g_ref, hid_ref, dga_ref, dup_ref, dlog_ref,
     got_ref, dx_ref, stage_ref, x_send, x_recv, dx_send, dx_recv, own_sem, stage_sem,
 ):
@@ -915,17 +976,28 @@
             recv_sem=dx_recv.at[s], device_id=(peer, line), device_id_type=pl.DeviceIdType.MESH,
         )
 
-    def y_copy(s):
+    blocks, share = stage_ref.shape[2:4]
+
+    def y_copies(s):
         source = partner_of(me, s, devices)
         slot = lax.rem(s, 2)
-        return pltpu.make_async_copy(stage_ref.at[slot], y_ref.at[source], stage_sem.at[slot])
+        if not by_block:
+            return [
+                pltpu.make_async_copy(stage_ref.at[slot], y_ref.at[source], stage_sem.at[slot, 0])
+            ]
+        return [
+            pltpu.make_async_copy(
+                stage_ref.at[slot, e], y_ref.at[:, source, e], stage_sem.at[slot, e]
+            )
+            for e in range(experts)
+        ]
 
     def work(s):
         source = partner_of(me, s, devices)
         slot = lax.rem(s, 2)
         for e in range(experts):
             x = got_ref[s, e]
-            dy = dy_ref[source, e].astype(F32)
+            dy = dy_ref[:, source, e].reshape(cap, width).astype(F32)
             pair = pair_ref[source, e].astype(F32)
             margin = jnp.sum(mm_nt(x, wr_ref[...]) * pair, axis=-1, keepdims=True)
             own_gate = 1.0 / (1.0 + jnp.exp(-margin))
@@ -951,7 +1023,7 @@
             dup_ref[0, e] = dup
             y = mm(hid, wd_ref[e])
             dgate = jnp.sum(y * dy, axis=-1, keepdims=True)
-            stage_ref[slot, e] = (y * own_gate).astype(BF16)
+            stage_ref[slot, e] = (y * own_gate).astype(BF16).reshape(blocks, share, width)
             dlog = (dgate * own_gate * other_gate * pair).astype(BF16)
             dlog_ref[0, e] = dlog
             dx = mm(dga, wg_ref[e]) + mm(dup, wu_ref[e]) + mm(dlog, wr_ref[...])
@@ -985,10 +1057,12 @@
 
     @pl.when(step > 1)
     def _():
-        y_copy(step - 2).wait()
+        for copy in y_copies(step - 2):
+            copy.wait()
 
     work(step)
-    y_copy(step).start()
+    for copy in y_copies(step):
+        copy.start()
 
     @pl.when(step > 0)
     def _():
@@ -999,15 +1073,16 @@
         own = pltpu.make_async_copy(dx_ref.at[0], back_ref.at[me], own_sem)
         own.start()
         own.wait()
-        y_copy(devices - 2).wait()
-        y_copy(devices - 1).wait()
+        for copy in y_copies(devices - 2) + y_copies(devices - 1):
+            copy.wait()
         for s in range(1, devices):
             x_copy(s).wait_send()
             dx_copy(s).wait_send()
             dx_copy(s).wait_recv()
 
 
-def expert_pass(sent, dy, pair, wr, wg, wu, wd, identity):
+def expert_pass(sent, dy, pair, wr, wg, wu, wd, by_block, identity):
+    blocks, _, _, share, _ = dy.shape
     devices, experts, cap, width = sent.shape
     hidden = wg.shape[1]
     choices = wr.shape[0]
@@ -1021,11 +1096,14 @@
     def kept(cols):
         return jax.ShapeDtypeStruct((devices, experts, cap, cols), BF16)
 
+    y_shape = (blocks, devices, experts, share, width)
+    if not by_block:
+        y_shape = (devices, experts, blocks, share, width)
     return pl.pallas_call(
-        expert_kernel,
+        functools.partial(expert_kernel, by_block),
         grid=(devices,),
         out_shape=(
-            kept(width), kept(width), kept(width), kept(width), kept(hidden), kept(hidden),
+            kept(width), jax.ShapeDtypeStruct(y_shape, BF16), kept(width), kept(width), kept(hidden), kept(hidden),
             kept(hidden), kept(choices),
         ),
         in_specs=[
@@ -1039,18 +1117,18 @@
         scratch_shapes=[
             pltpu.VMEM((devices, experts, cap, width), BF16),
             pltpu.VMEM((devices, experts, cap, width), BF16),
-            pltpu.VMEM((2, experts, cap, width), BF16),
+            pltpu.VMEM((2, experts, blocks, share, width), BF16),
             pltpu.SemaphoreType.DMA((devices,)),
             pltpu.SemaphoreType.DMA((devices,)),
             pltpu.SemaphoreType.DMA((devices,)),
             pltpu.SemaphoreType.DMA((devices,)),
             pltpu.SemaphoreType.DMA,
-            pltpu.SemaphoreType.DMA((2,)),
+            pltpu.SemaphoreType.DMA((2, experts)),
         ],
         compiler_params=pltpu.CompilerParams(
             vmem_limit_bytes=VMEM_LIMIT, collective_id=identity, has_side_effects=True
         ),
-        cost_estimate=pl.CostEstimate(flops=0, bytes_accessed=4000000, transcendentals=0),
+        cost_estimate=pl.CostEstimate(flops=0, bytes_accessed=490000000, transcendentals=0),
         name="expert_pass",
     )(sent, dy, pair, wr, wg, wu, wd)
 
@@ -1170,9 +1248,18 @@
     states = [dict() for _ in range(micro_count)]
     own_seg = lax.dynamic_slice_in_dim(segment_ids[:, 0], hidden_index * shard_len, shard_len, 1)
     live_routes = jnp.where(own_seg[:, None, :] >= 0, routes[:, 0].transpose(0, 2, 1), -1)
-    *x_all, other_qkv, all_out, all_routes, other_table = opening(
+    own_place = find_places(live_routes[None], expert_count, capacity)
+
+    def spread(rows, placed):
+        return spread_rows(rows, placed, expert_count, capacity, shard_len)
+
+    dy_sent = [
+        spread(cotangent[micro, 0], own_place[micro]).reshape(devices, -1, width)
+        for micro in range(micro_count)
+    ]
+    *x_all, other_qkv, all_out, all_routes, other_table, dy_first = opening(
         x_in[:, 0], qkv_weight.reshape(3 * width, head_cols), out_weight,
-        live_routes, bias_table.T.astype(F32), devices, blocks, members,
+        live_routes, bias_table.T.astype(F32), dy_sent[0], devices, blocks, members,
     )
     x_half = [x.reshape(1, half, width) for x in x_all]
     other_qkv = other_qkv.reshape(qkv_weight.shape)
@@ -1186,42 +1273,53 @@
     bias = position_bias(jnp.einsum("jb,hb->hj", onehot_bucket, tables, precision=PRECISE))
     seg_half = lax.dynamic_slice_in_dim(segment_ids[:, 0], part * half, half, 1)
 
-    def spread(rows, micro):
-        return spread_rows(rows, place[micro], expert_count, capacity, shard_len)
+    def gather_dy(rows):
+        whole = gather(rows.reshape(1, devices * experts_here * capacity, width))
+        return whole.reshape(blocks, devices, experts_here, capacity, width)
 
     def experts(micro, kept, *behind):
-        sent = spread(kept["xn2_all"], micro).reshape(token_shape)
-        back, y, x, g, hid, dga, dup, dlog = expert_pass(
+        sent = spread(kept["xn2_all"], place[micro]).reshape(token_shape)
+        kept["by_block"] = micro + 1 < micro_count
+        back, kept["y"], x, g, hid, dga, dup, dlog = expert_pass(
             after(sent, *behind), kept["dy"], pairs[micro], router_rows, gate_rows, up_rows,
-            down_weight, 4 + micro,
+            down_weight, kept["by_block"], 4 + micro,
         )
         kept["weights"] = (x, g, hid, dga, dup, dlog)
-        kept["y_sent"] = y.reshape(flat_shape)
+        kept["back"] = back
+        if micro > 0:
+            back = after(back, states[micro - 1]["y_own"])
         kept["dx_back"] = back.reshape(place_shape)
         kept["dx_part"] = collect_rows(kept["dx_back"], place[micro], shard_len)
         kept["dxn2"] = scatter(kept["dx_part"])
-
-    states[0]["dy_all"] = gather(cotangent[0, 0])
-    for micro in range(1, micro_count):
-        before = states[micro - 1]["dy_all"]
-        states[micro]["dy_all"] = gather(after(cotangent[micro, 0], before, all_out))
+        if kept["by_block"]:
+            parts = after(kept["y"], kept["dx_part"]).reshape(blocks, -1, width)
+            kept["y_own"] = scatter(parts).reshape(devices, -1, width)
+
+    states[0]["dy"] = gather_dy(dy_first)
     behind = ()
     for micro in range(micro_count):
         state = states[micro]
-        rider = spread(after(state["dy_all"], *behind), micro).reshape(token_shape)
-        qkv, prob, heads, h1, xn2, state["dy"] = attend(
+        rider = None
+        if micro + 1 < micro_count:
+            rider = dy_sent[micro + 1]
+        qkv, prob, heads, h1, xn2, *rode = attend(
             after(x_half[micro], *behind), attn_gain_f, qkv_weight, other_qkv, bias,
             seg_half[micro : micro + 1], all_out, x_in[micro], moe_gain_f, scale, members, 10 + micro,
             rider,
         )
         state.update(qkv=qkv[0], prob=prob[0], heads=heads[0], h1=h1[0], xn2=xn2[0])
-        behind = (xn2,)
-    pairs = find_pairs(after(all_routes, states[0]["xn2"]), expert_count, experts_here, capacity)
-    pairs = pairs.reshape(micro_count, devices, experts_here, blocks * capacity, expert_count)
+        if micro + 1 < micro_count:
+            states[micro + 1]["dy_here"] = rode[0]
+        behind = (xn2, states[0]["dy"])
     behind = ()
     for micro in range(micro_count):
-        states[micro]["xn2_all"] = gather(after(states[micro]["xn2"], *behind))
-        behind = (states[micro]["xn2_all"],)
+        state = states[micro]
+        state["xn2_all"] = gather(after(state["xn2"], *behind))
+        behind = (state["xn2_all"],)
+    for micro in range(1, micro_count):
+        states[micro]["dy"] = gather_dy(after(states[micro]["dy_here"], states[0]["xn2_all"]))
+    pairs = find_pairs(after(all_routes, states[-1]["xn2"]), expert_count, experts_here, capacity)
+    pairs = pairs.reshape(micro_count, devices, experts_here, blocks * capacity, expert_count)
     behind = ()
     for micro in range(micro_count):
         experts(micro, states[micro], *behind)
@@ -1230,12 +1328,17 @@
     kept = [state["weights"] for state in states]
     kept[-1] = tuple(after(list(kept[-1]), last_part))
     dwr, dwg, dwu, dwd = weight_pass(kept)
+    grads = None
     behind = (last_part,)
-    grads = None
     for micro in range(micro_count):
         state = states[micro]
-        state["y_back"] = exchange(after(state["y_sent"], *behind)).reshape(place_shape)
-        behind = (dwr,)
+        if state["by_block"]:
+            sent = after(state["y_own"], states[-1]["back"])
+            state["y_rows"] = exchange(sent).reshape(expert_count, 1, capacity, width)
+        else:
+            sent = after(state["y"], *behind).reshape(flat_shape)
+            state["y_rows"] = exchange(sent).reshape(place_shape)
+        behind = (last_part, state["y_rows"])
     for micro in range(micro_count):
         state = states[micro]
         state["x_grad"], grads, state["line"], state["moe_gain_grad"], state["attn_gain_grad"] = (
@@ -1246,13 +1349,14 @@
                 4 + micro_count + micro,
             )
         )
-    parts = []
     for micro in range(micro_count):
         state = states[micro]
-        parts.append(collect_rows(after(state["y_back"], grads), place[micro], shard_len))
-        state["mixed"] = scatter(parts[-1])
-        state["block_out"] = (state["h1"] + state["mixed"].astype(F32)).astype(BF16)
-    pieces = exchange(grads)
+        rows = after(state["y_rows"], grads)
+        if state["by_block"]:
+            mixed = collect_rows(rows, own_place[micro], shard_len)
+        else:
+            mixed = scatter(collect_rows(rows, place[micro], shard_len))
+        state["block_out"] = (state["h1"] + mixed.astype(F32)).astype(BF16)
 
     def added(name):
         total = states[0][name]
@@ -1277,7 +1381,7 @@
     )
     used = small.shape[0]
     small = jnp.pad(small, (0, -used % 1024)).reshape(-1, 128)
-    whole, small = closing(pieces, small, blocks)
+    whole, small = closing(grads, small, blocks)
     whole = whole.reshape(4 * width, head_cols).astype(F32)
     grad_qkv = whole[: 3 * width].reshape(qkv_weight.shape)
     grad_out = whole[3 * width :].T

time: 853 us -> 807 us (0.946)
  Pallas kernels: 735 us -> 685 us
    all_gather x4, waiting for transfers between devices: 0.06 us -> 40.3 us  [gather(): return lax.all_gather(values, 'hidden', axis=0, tiled=True)]
    all_to_all x3 -> x2, waiting for transfers between devices: 46.4 us -> 12.5 us  [exchange(): lax.all_to_all(buffer, 'expert', split_axis=0, concat_axis=0, tiled=True)]
    pallas_call x2, Pallas kernels: 132 us -> 98.7 us  [attend(): pl.pallas_call(functools.partial(attend_kernel, scale), grid=(micros, 2),...]
    pallas_call x1, Pallas kernels: 72.6 us -> 46.9 us  [opening(): pl.pallas_call(functools.partial(opening_kernel, micros), out_shape=(jax....]
    pallas_call x3, Pallas kernels: 332 us -> 351 us  [the longest x2 273 us: expert_pass(): pl.pallas_call(functools.partial(expert_kernel, by_block), grid=(devices,...]
  transfers between devices with their start and end apart: 11 -> 10, of which waited for: 2 -> 3; matrix products, arithmetic and copies ran while one was open for 3% -> 3% of each run, Pallas kernels for 87% -> 79%
where the time goes in v8:
time: 807 us; the launch traced here: 798 us
  Pallas kernels  685 us (85%)
  waiting for transfers between devices  54 us (7%)
  local copies, waits for them, and re-layouts  21.9 us (3%)
  between operations  15 us (2%)
  other arithmetic  10.9 us (1%)
  starting transfers between devices  9.25 us (1%)
    pallas_call x2, Pallas kernels, expert_pass(): pl.pallas_call(functools.partial(expert_kernel, by_block), grid=(devices,...  273 us
    pallas_call x2, Pallas kernels, attend(): pl.pallas_call(functools.partial(attend_kernel, scale), grid=(micros, 2),...  98.7 us
    pallas_call x2, Pallas kernels, attend_back(): pl.pallas_call(functools.partial(back_kernel, scale, prev is not None), g...  94.9 us
    pallas_call x1, Pallas kernels, closing(): pl.pallas_call(closing_kernel, out_shape=(jax.ShapeDtypeStruct((chips, 2,...  77.7 us
    pallas_call x1, Pallas kernels, opening(): pl.pallas_call(functools.partial(opening_kernel, micros), out_shape=(jax....  46.9 us
    all_gather x4, waiting for transfers between devices, gather(): return lax.all_gather(values, 'hidden', axis=0, tiled=True)  40.3 us
    pallas_call x1, Pallas kernels, weight_pass(): pl.pallas_call(weight_kernel, grid=(experts, width // block), out_shape=(...  38.3 us
    pallas_call x4, Pallas kernels, collect_rows(): pl.pallas_call(collect_kernel, grid=(blocks,), out_shape=jax.ShapeDtypeSt...  19.7 us
  transfers between devices with their start and end apart: 10, of which 3 were waited for; matrix products, arithmetic and copies ran while one was open for 3% of the time, Pallas kernels for 79%

profile of v8, /device:TPU:0, one launch (start us, length us, event | category | flops | bytes accessed | tf_op | source)
XLA Modules:
  0.0 798.1 jit_solution(3162293892958490663)
XLA Ops:
  7.2 0.7 dynamic-slice_compare_fusion
  7.9 1.3 convert_bitcast_fusion.table_ref
  9.2 1.3 fusion.20
  10.5 1.4 find_places.2
  11.9 1.3 slice_bitcast_fusion.10
  13.2 3.2 slice_bitcast_fusion
  16.4 2.7 spread_rows.4
  19.1 46.9 %opening.1 = (bf16[2,256,1024]{2,1,0:T(8,128)(2,1)}, bf16[2,256,1024]{2,1,0:T(8,128)(2,1)}, bf16[4,2,384,256]{3,2,1,0:T(8,128)(2,1)}, bf16[4,4,2,32,1024]{4,3,2,...) custom-call(bf16[2,256,1024]{2,1,0:T(8,128)(2,1)} %bitcast.136, ...), custom_call_target="tpu_custom_call" | custom-call | bytes 200000000 | tf_op jit(solution)/shard_map/opening/pallas_call | solution.py:241
  67.3 0.9 copy.32.seg_col_ref
  68.2 1.1 fusion.3
  69.9 6.0 position_bias.1.bias_ref
  75.9 2.6 spread_rows.5
  78.5 51.9 %attend.2 = (bf16[1,2,3,512,256]{4,3,2,1,0:T(8,128)(2,1)}, bf16[1,2,4,512,512]{4,3,2,1,0:T(8,128)(2,1)}, bf16[1,512,512]{2,1,0:T(8,128)(2,1)}, f32[1,256,1024]{2...) custom-call(bf16[1,512,1024]{2,1,0:T(8,128)(2,1)} %bitcast.153, f32[1,1024]{1,0:T(1,128)} %bitcast.168, ...), custom_call_target="tpu_custom_call" | custom-call | flops 2684354560 | bytes 100000000 | tf_op jit(solution)/shard_map/attend/pallas_call | solution.py:401
  130.8 0.9 copy.33.seg_col_ref
  131.6 34.8 %all-gather.7.cloned.1.call-done = bf16[4,640,1024]{2,1,0:T(8,128)(2,1)} async-done(((bf16[1,640,1024]{2,1,0:T(8,128)(2,1)}), bf16[4,640,1024]{2,1,0:T(8,128)(2,1)}) %all-gather.7.cloned.1.call-update) | async-done | bytes 5242896 | tf_op jit(solution)/shard_map/all_gather | solution.py:1243
  166.5 46.8 %attend.3 = (bf16[1,2,3,512,256]{4,3,2,1,0:T(8,128)(2,1)}, bf16[1,2,4,512,512]{4,3,2,1,0:T(8,128)(2,1)}, bf16[1,512,512]{2,1,0:T(8,128)(2,1)}, f32[1,256,1024]{2,1,0:T(8,128)}, bf16[1,256,1024]{2,1,0:T(8,128)(2,1)}) custom-call(bf16[1,512,1024]{2,1,0:T(8,128)(2,1)} %bitcast.182, f32[1,1024]{1,0:T(1,128)} %bitcast.169, bf16[3,1024,256]{2,1,0:T(8,128)(2,1)} %own_ref.7, ...), custom_call_target="tpu_custom_call" | custom-call | flops 2684354560 | bytes 100000000 | tf_op jit(solution)/shard_map/attend/pallas_call | solution.py:401
  213.2 5.4 all-gather.5.cloned.1.call-done.rows_ref
  219.8 1.3 dynamic-slice_bitcast_fusion.route_ref
  221.1 1.6 find_places.3
  222.7 1.3 slice_bitcast_fusion.7
  224.0 5.4 spread_rows.6
  229.5 10.8 %find_pairs.1 = bf16[2,8,2,4,40,16]{5,4,3,2,1,0:T(8,128)(2,1)} custom-call(s32[8,4,2,2,256]{4,3,2,1,0:T(2,128)} %get-tuple-element.91.route_ref), custom_call_target="tpu_custom_call" | custom-call | tf_op jit(solution)/shard_map/find_pairs/pallas_call | solution.py:941
  240.3 2.5 fusion.23
  242.8 136.8 %expert_pass.2 = (bf16[8,2,160,1024]{3,2,1,0:T(8,128)(2,1)}, bf16[4,8,2,40,1024]{4,3,2,1,0:T(8,128)(2,1)}, bf16[8,2,160,1024]{3,2,1,0:T(8,128)(2,1)}, bf16[8,2,1...) custom-call(bf16[8,2,160,1024]{3,2,1,0:T(8,128)(2,1)} %bitcast.120, ...), custom_call_target="tpu_custom_call" | custom-call | bytes 490000000 | tf_op jit(solution)/shard_map/expert_pass/pallas_call | solution.py:1102
  379.6 5.6 collect_rows.4
  385.9 5.3 spread_rows.7
  391.2 136.6 %expert_pass.3 = (bf16[8,2,160,1024]{3,2,1,0:T(8,128)(2,1)}, bf16[8,2,4,40,1024]{4,3,2,1,0:T(8,128)(2,1)}, bf16[8,2,160,1024]{3,2,1,0:T(8,128)(2,1)}, bf16[8,2,1...) custom-call(bf16[8,2,160,1024]{3,2,1,0:T(8,128)(2,1)} %bitcast.121, ...), custom_call_target="tpu_custom_call" | custom-call | bytes 490000000 | tf_op jit(solution)/shard_map/expert_pass/pallas_call | solution.py:1102
  527.8 3.6 all-to-all-start
  531.4 5.6 collect_rows.5
  537.1 12.5 %all-to-all-done = bf16[8,80,1024]{2,1,0:T(8,128)(2,1)S(1)} async-done(((bf16[8,80,1024]{2,1,0:T(8,128)(2,1)}), bf16[8,80,1024]{2,1,0:T(8,128)(2,1)S(1)}, u32[]{:S(2)}, u32[]{:S(2)}) %all-to-all-start) | async-done | bytes 1310752 | tf_op jit(solution)/shard_map/all_to_all | solution.py:1240
  549.5 1.1 copy-done.1
  550.6 4.7 all-to-all-start.1
  555.3 38.3 %weight_pass.1 = (f32[2,16,1024]{2,1,0:T(8,128)}, f32[2,704,1024]{2,1,0:T(8,128)}, f32[2,704,1024]{2,1,0:T(8,128)}, f32[2,704,1024]{2,1,0:T(8,128)}) custom-call(bf16[8,2,160,1024]{3,2,1,0:T(8,128)(2,1)} %get-tuple-element.102.refs_0_, bf16[8,2,160,1024]{3,2,1,0:T(8,128)(2,1)} %get-tuple-element.103.refs_1_, ...), custom_call_target="tpu_custom_call" | custom-call | flops 22145925120 | bytes 59899904 | tf_op jit(solution)/shard_map/weight_pass/pallas_call | solution.py:1168
  593.7 49.5 %attend_back.2 = (bf16[256,1024]{1,0:T(8,128)(2,1)}, bf16[8,2,512,256]{3,2,1,0:T(8,128)(2,1)}, f32[2,4,1024]{2,1,0:T(4,128)}, f32[1,1024]{1,0:T(1,128)}, f32[1,1024]{1,0:T(1,128)}) custom-call(bf16[256,1024]{1,0:T(8,128)(2,1)} %reduce-scatter.9.cloned.1.call-done.grad_ref, f32[256,1024]{1,0:T(8,128)} %bitcast.155, ...), custom_call_target="tpu_custom_call" | custom-call | flops 5368709120 | bytes 150000000 | tf_op jit(solution)/shard_map/attend_back/pallas_call | solution.py:646
  643.3 45.4 %attend_back.3 = (bf16[256,1024]{1,0:T(8,128)(2,1)}, bf16[8,2,512,256]{3,2,1,0:T(8,128)(2,1)}, f32[2,4,1024]{2,1,0:T(4,128)}, f32[1,1024]{1,0:T(1,128)}, f32[1,1024]{1,0:T(1,128)}) custom-call(bf16[256,1024]{1,0:T(8,128)(2,1)} %reduce-scatter.7.cloned.1.call-done.grad_ref, f32[256,1024]{1,0:T(8,128)} %bitcast.156, ...), custom_call_target="tpu_custom_call" | custom-call | flops 5368709120 | bytes 150000000 | tf_op jit(solution)/shard_map/attend_back/pallas_call | solution.py:646
  688.8 5.7 collect_rows.7
  695.9 77.7 %closing.1 = (bf16[4,2,512,256]{3,2,1,0:T(8,128)(2,1)}, f32[152,128]{1,0:T(8,128)}) custom-call(bf16[4,2,2,512,256]{4,3,2,1,0:T(8,128)(2,1)} %bitcast.137, f32[152,128]{1,0:T(8,128)} %fusion.6.small_ref), custom_call_target="tpu_custom_call" | custom-call | bytes 160000000 | tf_op jit(solution)/shard_map/closing/pallas_call | solution.py:787
  773.6 0.8 slice.103
  774.5 0.8 slice.108
  775.3 1.1 slice.116
  776.5 1.9 slice.115
  779.1 1.3 copy.34
  780.4 2.7 collect_rows.6
  783.7 2.3 maximum_bitcast_fusion.1
  786.0 1.3 slice_bitcast_fusion.8
  787.3 1.2 fusion
  788.5 1.2 fusion.1
  789.7 1.1 maximum_bitcast_fusion
  (78 shorter events, 6.8 us)
Async XLA Ops:
  7.2 159.3 %all-gather.7.cloned.1.call-start = ((), (), s32[]{:S(2)}) async-start(), calls=%async_computation.7 | async-start | bytes 6553600 | tf_op jit(solution)/shard_map/all_gather | solution.py:1243
  16.4 49.7 %copy-start.15 = (bf16[1024]{0:T(1024)(128)(2,1)S(1)}, bf16[1024]{0:T(1024)(128)(2,1)}, u32[]{:S(2)}) copy-start(bf16[1024]{0:T(1024)(128)(2,1)} %param.20) | copy-start | bytes 6148
  16.4 50.3 %copy-start.16 = (bf16[1024]{0:T(1024)(128)(2,1)S(1)}, bf16[1024]{0:T(1024)(128)(2,1)}, u32[]{:S(2)}) copy-start(bf16[1024]{0:T(1024)(128)(2,1)} %param.21) | copy-start | bytes 6148
  16.4 50.9 %copy-start.10 = (s32[2,1,1024]{2,1,0:T(1,128)S(1)}, s32[2,1,1024]{2,1,0:T(1,128)}, u32[]{:S(2)}) copy-start(s32[2,1,1024]{2,1,0:T(1,128)} %param.15) | copy-start | bytes 24580
  16.4 51.7 %copy-start.8 = (f32[4,32]{1,0:T(4,128)S(1)}, f32[4,32]{1,0:T(4,128)}, u32[]{:S(2)}) copy-start(f32[4,32]{1,0:T(4,128)} %convert_bitcast_fusion.table_ref) | copy-start | bytes 1540
  66.0 152.7 %all-gather.5.cloned.1.call-start = ((), (), s32[]{:S(2)}) async-start(), calls=%async_computation.6 | async-start | bytes 2621440 | tf_op jit(solution)/shard_map/all_gather | solution.py:1243
  67.3 11.3 %copy-start.7 = (s32[1,1,512]{2,1,0:T(1,128)}, s32[1,1,512]{2,1,0:T(1,128)S(1)}, u32[]{:S(2)}) copy-start(s32[1,1,512]{2,1,0:T(1,128)S(1)} %get-tuple-element.195.seg_row_ref) | copy-start | bytes 6148
  67.3 63.5 %copy-start.9 = (s32[1,1,512]{2,1,0:T(1,128)}, s32[1,1,512]{2,1,0:T(1,128)S(1)}, u32[]{:S(2)}) copy-start(s32[1,1,512]{2,1,0:T(1,128)S(1)} %get-tuple-element.194.seg_row_ref) | copy-start | bytes 6148
  130.5 255.4 %all-gather.9.cloned.1.call-start = ((), (), s32[]{:S(2)}) async-start(), calls=%async_computation.9 | async-start | bytes 2621440 | tf_op jit(solution)/shard_map/all_gather | solution.py:1243
  218.7 172.5 %all-gather.11.cloned.1.call-start = ((), (), s32[]{:S(2)}) async-start(), calls=%async_computation.10 | async-start | bytes 6553600 | tf_op jit(solution)/shard_map/all_gather | solution.py:1243
  219.3 308.5 %reduce-scatter.5.cloned.1.call-start = ((), (), s32[]{:S(2)}) async-start(), calls=%async_computation.8 | async-start | bytes 6553600 | tf_op jit(solution)/shard_map/reduce_scatter | solution.py:1246
  385.3 208.4 %reduce-scatter.9.cloned.1.call-start = ((), (), s32[]{:S(2)}) async-start(), calls=%async_computation.12 | async-start | bytes 2621440 | tf_op jit(solution)/shard_map/reduce_scatter | solution.py:1246
  527.8 21.7 %all-to-all-start = ((bf16[8,80,1024]{2,1,0:T(8,128)(2,1)}), bf16[8,80,1024]{2,1,0:T(8,128)(2,1)S(1)}, u32[]{:S(2)}, u32[]{:S(2)}) async-start(bf16[8,80,1024]{2,1,0:T(8,128)(2,1)} %bitcast.152), calls=%async_computation.1 | async-start | bytes 2621440 | tf_op jit(solution)/shard_map/all_to_all | solution.py:1240
  531.4 111.9 %reduce-scatter.7.cloned.1.call-start = ((), (), s32[]{:S(2)}) async-start(), calls=%async_computation.11 | async-start | bytes 2621440 | tf_op jit(solution)/shard_map/reduce_scatter | solution.py:1246
  549.5 1.1 copy-start.1
  550.6 138.1 %all-to-all-start.1 = ((bf16[8,320,1024]{2,1,0:T(8,128)(2,1)}), bf16[8,320,1024]{2,1,0:T(8,128)(2,1)}, u32[]{:S(2)}, u32[]{:S(2)}) async-start(bf16[8,320,1024]{2,1,0:T(8,128)(2,1)} %bitcast.129), calls=%async_computation.4 | async-start | bytes 10485760 | tf_op jit(solution)/shard_map/all_to_all | solution.py:1240
  555.3 233.2 %reduce-scatter.11.cloned.1.call-start = ((), (), s32[]{:S(2)}) async-start(), calls=%async_computation.13 | async-start | bytes 2621440 | tf_op jit(solution)/shard_map/reduce_scatter | solution.py:1246
  688.7 5.8 copy-start.4
  688.7 5.9 copy-start.5
  688.7 5.9 copy-start.6
  688.7 6.4 copy-start.12
  688.7 6.4 copy-start.14
  688.7 6.5 copy-start.11
  688.7 6.5 copy-start.13
  773.6 2.8 copy-start
  778.4 8.9 %copy-start.2 = (f32[1,256,1024]{2,1,0:T(8,128)S(1)}, f32[1,256,1024]{2,1,0:T(8,128)}, u32[]{:S(2)}) copy-start(f32[1,256,1024]{2,1,0:T(8,128)} %get-tuple-element.84) | copy-start | bytes 3145732
  779.1 9.4 %copy-start.3 = (f32[1,256,1024]{2,1,0:T(8,128)S(1)}, f32[1,256,1024]{2,1,0:T(8,128)}, u32[]{:S(2)}) copy-start(f32[1,256,1024]{2,1,0:T(8,128)} %get-tuple-element.122) | copy-start | bytes 3145732
Sparse Core Ops, SparseCore 0:
  66.1 100.3 all-gather.6
  168.0 50.5 all-gather.4
  220.3 46.0 all-gather.8
  267.8 96.7 all-gather.10
  385.4 92.8 reduce-scatter.4
  480.4 44.3 reduce-scatter.8
  537.2 44.4 reduce-scatter.6
  694.6 54.3 reduce-scatter.10

commit v9 on v8

--- a/solution.py
+++ b/solution.py
@@ -111,14 +111,14 @@
 
 
 def opening_kernel(
-    micros, x_ref, qkv_ref, out_ref, routes_ref, table_ref, dy_ref, *refs,
+    micros, x_ref, qkv_ref, out_ref, routes_ref, table_ref, *refs,
 ):
     x_all, refs = refs[:micros], refs[micros:]
     (
-        qkv_all, out_all, routes_all, table_all, dy_all,
+        qkv_all, out_all, routes_all, table_all,
         x_send, x_recv, qkv_send, qkv_recv, out_send, out_recv, qkv_on_send, qkv_on_recv,
         out_on_send, out_on_recv, routes_send, routes_recv, routes_on_send, routes_on_recv,
-        table_send, table_recv, dy_send, dy_recv, own_sem,
+        table_send, table_recv, own_sem,
     ) = refs
     devices, qkv_rows = qkv_all.shape[0] * 2, qkv_all.shape[2]
     blocks, out_rows = out_all.shape[0], out_all.shape[3]
@@ -137,11 +137,10 @@
             out_ref.at[pl.ds(me * out_rows, out_rows)], out_all.at[line, chip, core], own_sem.at[0]
         ),
         pltpu.make_async_copy(routes_ref, routes_all.at[me, line], own_sem.at[1]),
-        pltpu.make_async_copy(dy_ref.at[me], dy_all.at[me], own_sem.at[2]),
     ]
     for micro in range(micros):
         own.append(
-            pltpu.make_async_copy(x_ref.at[micro], x_all[micro].at[mine], own_sem.at[3 + micro])
+            pltpu.make_async_copy(x_ref.at[micro], x_all[micro].at[mine], own_sem.at[2 + micro])
         )
     for copy in own:
         copy.start()
@@ -175,11 +174,6 @@
             )
             copy.start()
             rest.append(copy)
-    for s in range(1, devices):
-        peer = partner_of(me, s, devices)
-        copy = remote(dy_ref.at[peer], dy_all.at[me], dy_send.at[s], dy_recv.at[s], (peer, line))
-        copy.start()
-        rest.append(copy)
     first_qkv.wait_recv()
     qkv_on, out_on = [], []
     for s in range(2, devices, 2):
@@ -234,7 +228,7 @@
         copy.wait()
 
 
-def opening(x, qkv, out, routes, table, dy, devices, blocks, members):
+def opening(x, qkv, out, routes, table, devices, blocks, members):
     micros, shard_len, width = x.shape
     dma = pltpu.SemaphoreType.DMA
     pair = (devices // 2, 2)
@@ -246,20 +240,51 @@
             jax.ShapeDtypeStruct((blocks,) + pair + (out.shape[0] // devices, width), BF16),
             jax.ShapeDtypeStruct((devices, blocks) + routes.shape, jnp.int32),
             jax.ShapeDtypeStruct(table.shape, table.dtype),
-            jax.ShapeDtypeStruct(dy.shape, BF16),
-        ),
-        in_specs=[any_space()] * 6,
-        out_specs=(any_space(),) * (5 + micros),
+        ),
+        in_specs=[any_space()] * 5,
+        out_specs=(any_space(),) * (4 + micros),
         scratch_shapes=[
             dma((micros, members)), dma((micros, members)), dma, dma, dma((blocks,)), dma((blocks,)),
             dma((devices,)), dma((devices,)), dma((devices,)), dma((devices,)), dma((blocks,)),
-            dma((blocks,)), dma((devices,)), dma((devices,)), dma, dma, dma((devices,)),
-            dma((devices,)), dma((3 + micros,)),
+            dma((blocks,)), dma((devices,)), dma((devices,)), dma, dma, dma((2 + micros,)),
         ],
         compiler_params=pltpu.CompilerParams(collective_id=1, has_side_effects=True),
         cost_estimate=pl.CostEstimate(flops=0, bytes_accessed=200000000, transcendentals=0),
         name="opening",
-    )(x, qkv, out, routes, table, dy)
+    )(x, qkv, out, routes, table)
+
+
+def swap_kernel(sent_ref, got_ref, send_sem, recv_sem, own_sem):
+    devices = sent_ref.shape[0]
+    me = lax.axis_index("expert")
+    line = lax.axis_index("hidden")
+    greet([(partner_of(me, s, devices), line) for s in range(1, devices)])
+    own = pltpu.make_async_copy(sent_ref.at[me], got_ref.at[me], own_sem)
+    own.start()
+    copies = []
+    for s in range(1, devices):
+        peer = partner_of(me, s, devices)
+        copies.append(
+            remote(sent_ref.at[peer], got_ref.at[me], send_sem.at[s], recv_sem.at[s], (peer, line))
+        )
+        copies[-1].start()
+    own.wait()
+    for copy in copies:
+        copy.wait()
+
+
+def swap_rows(sent, identity):
+    dma = pltpu.SemaphoreType.DMA
+    return pl.pallas_call(
+        swap_kernel,
+        out_shape=jax.ShapeDtypeStruct(sent.shape, sent.dtype),
+        in_specs=[any_space()],
+        out_specs=any_space(),
+        scratch_shapes=[dma((sent.shape[0],)), dma((sent.shape[0],)), dma],
+        compiler_params=pltpu.CompilerParams(collective_id=identity, has_side_effects=True),
+        cost_estimate=pl.CostEstimate(flops=0, bytes_accessed=60000000, transcendentals=0),
+        name="swap_rows",
+    )(sent)
 
 
 def unit_rows(x):
@@ -453,23 +478,21 @@
     )
 
 
-def back_kernel(
-    scale, added, grad_ref, h1_ref, dy_ref, x_own_ref, moe_gain_ref, gain_ref, out_ref, x_ref,
-    own_ref, other_ref, qkv_ref, prob_ref, heads_ref, *refs,
-):
-    if added:
-        prev_ref, refs = refs[0], refs[1:]
+def back_kernel(scale, micros, *refs):
+    moe_gain_ref, gain_ref, out_ref, own_ref, other_ref = refs[:5]
+    inputs = [refs[5 + 8 * m : 13 + 8 * m] for m in range(micros)]
+    refs = refs[5 + 8 * micros :]
+    xgrads, refs = refs[:micros], refs[micros:]
     (
-        xgrad_ref, grads_ref, line_ref, dmoe_ref, dgain_ref,
+        grads_ref, line_ref, dmoe_ref, dgain_ref,
         dh1_ref, dattn_all, dheads_part, dheads_all, dxn_part, dxn_got, total_ref, xn_ref, ds_ref,
         dproj_ref, sheet_ref, attn_send, attn_recv, heads_send, heads_recv, dxn_send, dxn_recv,
     ) = refs
-    members, shard_len, width = dattn_all.shape
-    heads, half = prob_ref.shape[1], prob_ref.shape[2]
+    _, members, shard_len, width = dattn_all.shape
     cols = dproj_ref.shape[2]
-    size = cols // heads
+    half = members * shard_len
     length = sheet_ref.shape[1]
-    group = pl.program_id(0)
+    group, micro = pl.program_id(0), pl.program_id(1)
     me = lax.axis_index("expert")
     line = lax.axis_index("hidden")
     mine = lax.rem(line, members)
@@ -480,90 +503,52 @@
     def peer_of(s):
         return lax.rem(mine + s, members)
 
-    def attn_copy(s):
+    def attn_copy(m, s):
         return remote(
-            dattn_all.at[mine], dattn_all.at[mine], attn_send.at[s], attn_recv.at[s],
+            dattn_all.at[m, mine], dattn_all.at[m, mine], attn_send.at[m, s], attn_recv.at[m, s],
             (me, base + peer_of(s)),
         )
 
-    def heads_copy(s):
+    def heads_copy(m, s):
         return remote(
-            dheads_part.at[peer_of(s)], dheads_all.at[mine], heads_send.at[s], heads_recv.at[s],
+            dheads_part.at[m, peer_of(s)], dheads_all.at[m, mine], heads_send.at[m, s],
+            heads_recv.at[m, s], (me, base + peer_of(s)),
+        )
+
+    def dxn_copy(m, s):
+        return remote(
+            dxn_part.at[m, peer_of(s)], dxn_got.at[m, mine], dxn_send.at[m, s], dxn_recv.at[m, s],
             (me, base + peer_of(s)),
         )
 
-    def dxn_copy(s):
-        return remote(
-            dxn_part.at[peer_of(s)], dxn_got.at[mine], dxn_send.at[s], dxn_recv.at[s],
-            (me, base + peer_of(s)),
-        )
-
-    @pl.when(group == 0)
+    @pl.when((group == 0) & (micro == 0))
     def _():
         greet([(me, base + peer_of(s)) for s in steps])
-        grad = grad_ref[...].astype(F32)
-        h1 = h1_ref[...]
-        r2 = lax.rsqrt(jnp.mean(h1 * h1, axis=-1, keepdims=True) + EPSILON)
-        unit = h1 * r2
-        dmoe_ref[...] = jnp.sum(grad * unit, axis=0, keepdims=True)
-        weighted = grad * moe_gain_ref[...]
-        inner = jnp.mean(weighted * unit, axis=-1, keepdims=True)
-        dh1 = dy_ref[...].astype(F32) + r2 * (weighted - unit * inner)
-        dh1_ref[...] = dh1
-        dattn = dh1.astype(BF16)
-        dattn_all[mine] = dattn
-        for member in range(members):
-            for j in range(2):
-                index = lax.rem(part + j, 2) * members + member
-                dheads = mm_nt(dattn, out_ref[index]).astype(BF16)
-                dheads_part[member, :, j * cols : (j + 1) * cols] = dheads
-        for s in steps:
-            heads_copy(s).start()
-        for s in steps:
-            attn_copy(s).start()
-        dheads_all[mine] = dheads_part[mine]
-        xn_ref[...] = (unit_rows(x_ref[...]) * gain_ref[...]).astype(BF16)
-        for s in steps:
-            heads_copy(s).wait_recv()
-
-    for g in range(2):
-
-        @pl.when(group == g)
-        def _(g=g):
-            for head in range(heads):
-                inner_cols = slice(head * size, (head + 1) * size)
-                outer_cols = slice(g * cols + head * size, g * cols + (head + 1) * size)
-                values = qkv_ref[0, 2, :, inner_cols]
-                grads = dheads_all[:, :, outer_cols].reshape(half, size)
-                sheet_ref[...] = jnp.zeros_like(sheet_ref)
-                for start in range(0, half, TILE):
-                    rows = slice(start, start + TILE)
-                    prob = prob_ref[0, head, rows, :].astype(F32)
-                    dprob = mm_nt(grads[rows], values)
-                    inner = jnp.sum(prob * dprob, axis=-1, keepdims=True)
-                    dscore = (prob * (dprob - inner)).astype(BF16)
-                    ds_ref[rows, :] = dscore
-                    dscore = dscore.astype(F32)
-                    sheet_ref[:, : half - start] += dscore[:, start:]
-                    if start:
-                        sheet_ref[:, length - start :] += dscore[:, :start]
-                dscores = ds_ref[...]
-                keys, queries = qkv_ref[0, 1, :, inner_cols], qkv_ref[0, 0, :, inner_cols]
-                dproj_ref[0, :, inner_cols] = (mm(dscores, keys) * scale).astype(BF16)
-                dproj_ref[1, :, inner_cols] = (mm_tn(dscores, queries) * scale).astype(BF16)
-                dproj_ref[2, :, inner_cols] = mm_tn(prob_ref[0, head], grads).astype(BF16)
-                sheet = sheet_ref[...]
-                while sheet.shape[0] > 8:
-                    upper = sheet.shape[0] // 2
-                    sheet = sheet[:upper] + pltpu.roll(sheet[upper:], length - upper, 1)
-                row = lax.broadcasted_iota(jnp.int32, (8, length), 0)
-                found = jnp.zeros((1, length), F32)
-                for r in range(8):
-                    moved = pltpu.roll(sheet, length - r, 1) if r else sheet
-                    found = found + jnp.sum(
-                        jnp.where(row == r, moved, 0.0), axis=0, keepdims=True
-                    )
-                line_ref[0, head : head + 1, :] = found
+        dmoe_ref[...] = jnp.zeros_like(dmoe_ref)
+        dgain_ref[...] = jnp.zeros_like(dgain_ref)
+        for m in range(micros):
+            grad_ref, h1_ref, dy_ref = inputs[m][:3]
+            grad = grad_ref[...].astype(F32)
+            h1 = h1_ref[...]
+            r2 = lax.rsqrt(jnp.mean(h1 * h1, axis=-1, keepdims=True) + EPSILON)
+            unit = h1 * r2
+            dmoe_ref[...] += jnp.sum(grad * unit, axis=0, keepdims=True)
+            weighted = grad * moe_gain_ref[...]
+            inner = jnp.mean(weighted * unit, axis=-1, keepdims=True)
+            dh1 = dy_ref[...].astype(F32) + r2 * (weighted - unit * inner)
+            dh1_ref[m] = dh1
+            dattn = dh1.astype(BF16)
+            dattn_all[m, mine] = dattn
+            for member in range(members):
+                for j in range(2):
+                    index = lax.rem(part + j, 2) * members + member
+                    dheads = mm_nt(dattn, out_ref[index]).astype(BF16)
+                    dheads_part[m, member, :, j * cols : (j + 1) * cols] = dheads
+            for s in steps:
+                heads_copy(m, s).start()
+            dheads_all[m, mine] = dheads_part[m, mine]
+        for m in range(micros):
+            xn_ref[m] = (unit_rows(inputs[m][4][...]) * gain_ref[...]).astype(BF16)
 
     def products(weight_ref):
         dxn = mm_nt(dproj_ref[0], weight_ref[0])
@@ -571,117 +556,160 @@
             dxn = dxn + mm_nt(dproj_ref[t], weight_ref[t])
         return dxn.reshape(members, shard_len, width)
 
-    @pl.when(group == 0)
+    per = grads_ref.shape[0] // 4
+    for g in range(2):
+        for m in range(micros):
+
+            @pl.when((group == g) & (micro == m))
+            def _(g=g, m=m):
+                x_ref, qkv_ref, prob_ref, heads_ref = inputs[m][4:]
+                heads = prob_ref.shape[1]
+                size = cols // heads
+                if g == 0:
+                    for s in steps:
+                        heads_copy(m, s).wait_recv()
+                    for s in steps:
+                        attn_copy(m, s).start()
+                for head in range(heads):
+                    inner_cols = slice(head * size, (head + 1) * size)
+                    outer_cols = slice(g * cols + head * size, g * cols + (head + 1) * size)
+                    values = qkv_ref[0, 2, :, inner_cols]
+                    grads = dheads_all[m, :, :, outer_cols].reshape(half, size)
+                    sheet_ref[...] = jnp.zeros_like(sheet_ref)
+                    for start in range(0, half, TILE):
+                        rows = slice(start, start + TILE)
+                        prob = prob_ref[0, head, rows, :].astype(F32)
+                        dprob = mm_nt(grads[rows], values)
+                        inner = jnp.sum(prob * dprob, axis=-1, keepdims=True)
+                        dscore = (prob * (dprob - inner)).astype(BF16)
+                        ds_ref[rows, :] = dscore
+                        dscore = dscore.astype(F32)
+                        sheet_ref[:, : half - start] += dscore[:, start:]
+                        if start:
+                            sheet_ref[:, length - start :] += dscore[:, :start]
+                    dscores = ds_ref[...]
+                    keys, queries = qkv_ref[0, 1, :, inner_cols], qkv_ref[0, 0, :, inner_cols]
+                    dproj_ref[0, :, inner_cols] = (mm(dscores, keys) * scale).astype(BF16)
+                    dproj_ref[1, :, inner_cols] = (mm_tn(dscores, queries) * scale).astype(BF16)
+                    dproj_ref[2, :, inner_cols] = mm_tn(prob_ref[0, head], grads).astype(BF16)
+                    sheet = sheet_ref[...]
+                    while sheet.shape[0] > 8:
+                        upper = sheet.shape[0] // 2
+                        sheet = sheet[:upper] + pltpu.roll(sheet[upper:], length - upper, 1)
+                    row = lax.broadcasted_iota(jnp.int32, (8, length), 0)
+                    found = jnp.zeros((1, length), F32)
+                    for r in range(8):
+                        moved = pltpu.roll(sheet, length - r, 1) if r else sheet
+                        found = found + jnp.sum(
+                            jnp.where(row == r, moved, 0.0), axis=0, keepdims=True
+                        )
+                    if m:
+                        found = found + line_ref[0, head : head + 1, :]
+                    line_ref[0, head : head + 1, :] = found
+                if g == 0:
+                    total_ref[m] = products(own_ref)
+                    for s in steps:
+                        attn_copy(m, s).wait_recv()
+                else:
+                    total = total_ref[m] + products(other_ref)
+                    total_ref[m] = total
+                    dxn_part[m] = total.astype(BF16)
+                    for s in steps:
+                        dxn_copy(m, s).start()
+                    total = total.reshape(half, width)
+                    dgain_ref[...] += jnp.sum(total * unit_rows(x_ref[...]), axis=0, keepdims=True)
+                for t in range(4):
+                    if t < 3:
+                        found = mm_tn(xn_ref[m], dproj_ref[t])
+                    else:
+                        found = mm_tn(dattn_all[m].reshape(half, width), heads_ref[...])
+                    found = found.reshape(per, 1, width // per, cols)
+                    if m:
+                        found = found + grads_ref[t * per : (t + 1) * per].astype(F32)
+                    grads_ref[t * per : (t + 1) * per] = found.astype(BF16)
+
+    @pl.when((group == 1) & (micro == micros - 1))
     def _():
-        total_ref[...] = products(own_ref)
-        for s in steps:
-            attn_copy(s).wait_recv()
-
-    @pl.when(group == 1)
-    def _():
-        total_ref[...] += products(other_ref)
-        dxn_part[...] = total_ref[...].astype(BF16)
-        for s in steps:
-            dxn_copy(s).start()
-
-    per = grads_ref.shape[0] // 4
-    for t in range(4):
-        if t < 3:
-            found = mm_tn(xn_ref[...], dproj_ref[t])
-        else:
-            found = mm_tn(dattn_all[...].reshape(half, width), heads_ref[...])
-        found = found.reshape(per, 1, width // per, cols)
-        if added:
-            found = found + prev_ref[t * per : (t + 1) * per].astype(F32)
-        grads_ref[t * per : (t + 1) * per] = found.astype(BF16)
-
-    @pl.when(group == 1)
-    def _():
-        total = total_ref[...].reshape(half, width)
-        dgain_ref[...] = jnp.sum(total * unit_rows(x_ref[...]), axis=0, keepdims=True)
-        x_own = x_own_ref[...].astype(F32)
-        r1 = lax.rsqrt(jnp.mean(x_own * x_own, axis=-1, keepdims=True) + EPSILON)
-        unit = x_own * r1
-        for s in steps:
-            dxn_copy(s).wait_recv()
-        dxn1 = total_ref[mine]
-        for s in steps:
-            dxn1 = dxn1 + dxn_got[lax.rem(mine + members - s, members)].astype(F32)
-        weighted = dxn1 * gain_ref[...]
-        inner = jnp.mean(weighted * unit, axis=-1, keepdims=True)
-        xgrad_ref[...] = (dh1_ref[...] + r1 * (weighted - unit * inner)).astype(BF16)
-        for s in steps:
-            heads_copy(s).wait_send()
-            attn_copy(s).wait_send()
-            dxn_copy(s).wait_send()
-
-
-def attend_back(
-    grad, h1, dy, x_own, moe_gain, gain, out_weight, x_half, own_weight, other_weight, qkv, prob,
-    heads_out, prev, scale, pieces, members, identity,
-):
-    _, heads, half = prob.shape[:3]
+        for m in range(micros):
+            x_own = inputs[m][3][...].astype(F32)
+            r1 = lax.rsqrt(jnp.mean(x_own * x_own, axis=-1, keepdims=True) + EPSILON)
+            unit = x_own * r1
+            for s in steps:
+                dxn_copy(m, s).wait_recv()
+            dxn1 = total_ref[m, mine]
+            for s in steps:
+                dxn1 = dxn1 + dxn_got[m, lax.rem(mine + members - s, members)].astype(F32)
+            weighted = dxn1 * gain_ref[...]
+            inner = jnp.mean(weighted * unit, axis=-1, keepdims=True)
+            xgrads[m][...] = (dh1_ref[m] + r1 * (weighted - unit * inner)).astype(BF16)
+        for m in range(micros):
+            for s in steps:
+                heads_copy(m, s).wait_send()
+                attn_copy(m, s).wait_send()
+                dxn_copy(m, s).wait_send()
+
+
+def attend_back(moe_gain, gain, out_weight, own_weight, other_weight, kept, scale, pieces, members):
+    micros = len(kept)
+    _, heads, half = kept[0][6].shape[:3]
     width, cols = own_weight.shape[1:]
     shard_len = half // members
     length = 2 * half
     rows = 4 * width // pieces
 
-    def once(shape):
-        return pl.BlockSpec(shape, lambda p: (0,) * len(shape), pipeline_mode=pl.Buffered(1))
-
-    pieces_spec = pl.BlockSpec((pieces, 1, rows, cols), lambda p: (0, p, 0, 0))
-    operands = [
-        grad, h1, dy, x_own, moe_gain, gain, out_weight, x_half, own_weight, other_weight, qkv,
-        prob, heads_out,
-    ]
-    in_specs = [once(array.shape) for array in operands[:10]] + [
-        pl.BlockSpec((1, 3, half, cols), lambda p: (p, 0, 0, 0)),
-        pl.BlockSpec((1, heads, half, half), lambda p: (p, 0, 0, 0)),
-        pl.BlockSpec((half, cols), lambda p: (0, p)),
-    ]
-    if prev is not None:
-        operands.append(prev)
-        in_specs.append(pieces_spec)
-    dma = pltpu.SemaphoreType.DMA
+    def once(array):
+        return pl.BlockSpec(
+            array.shape, lambda p, m: (0,) * array.ndim, pipeline_mode=pl.Buffered(1)
+        )
+
+    operands = [moe_gain, gain, out_weight, own_weight, other_weight]
+    in_specs = [once(array) for array in operands]
+    for arrays in kept:
+        operands.extend(arrays)
+        in_specs += [once(array) for array in arrays[:5]] + [
+            pl.BlockSpec((1, 3, half, cols), lambda p, m: (p, 0, 0, 0)),
+            pl.BlockSpec((1, heads, half, half), lambda p, m: (p, 0, 0, 0)),
+            pl.BlockSpec((half, cols), lambda p, m: (0, p)),
+        ]
+    dma = pltpu.SemaphoreType.DMA((micros, members))
     return pl.pallas_call(
-        functools.partial(back_kernel, scale, prev is not None),
-        grid=(2,),
-        out_shape=(
-            jax.ShapeDtypeStruct((shard_len, width), BF16),
+        functools.partial(back_kernel, scale, micros),
+        grid=(2, micros),
+        out_shape=(jax.ShapeDtypeStruct((shard_len, width), BF16),) * micros
+        + (
             jax.ShapeDtypeStruct((pieces, 2, rows, cols), BF16),
             jax.ShapeDtypeStruct((2, heads, length), F32),
             jax.ShapeDtypeStruct((1, width), F32),
             jax.ShapeDtypeStruct((1, width), F32),
         ),
         in_specs=in_specs,
-        out_specs=(
-            pl.BlockSpec((shard_len, width), lambda p: (0, 0)),
-            pieces_spec,
-            pl.BlockSpec((1, heads, length), lambda p: (p, 0, 0)),
-            pl.BlockSpec((1, width), lambda p: (0, 0)),
-            pl.BlockSpec((1, width), lambda p: (0, 0)),
+        out_specs=(pl.BlockSpec((shard_len, width), lambda p, m: (0, 0)),) * micros
+        + (
+            pl.BlockSpec((pieces, 1, rows, cols), lambda p, m: (0, p, 0, 0)),
+            pl.BlockSpec((1, heads, length), lambda p, m: (p, 0, 0)),
+            pl.BlockSpec((1, width), lambda p, m: (0, 0)),
+            pl.BlockSpec((1, width), lambda p, m: (0, 0)),
         ),
         scratch_shapes=[
-            pltpu.VMEM((shard_len, width), F32),
-            pltpu.VMEM((members, shard_len, width), BF16),
-            pltpu.VMEM((members, shard_len, 2 * cols), BF16),
-            pltpu.VMEM((members, shard_len, 2 * cols), BF16),
-            pltpu.VMEM((members, shard_len, width), BF16),
-            pltpu.VMEM((members, shard_len, width), BF16),
-            pltpu.VMEM((members, shard_len, width), F32),
-            pltpu.VMEM((half, width), BF16),
+            pltpu.VMEM((micros, shard_len, width), F32),
+            pltpu.VMEM((micros, members, shard_len, width), BF16),
+            pltpu.VMEM((micros, members, shard_len, 2 * cols), BF16),
+            pltpu.VMEM((micros, members, shard_len, 2 * cols), BF16),
+            pltpu.VMEM((micros, members, shard_len, width), BF16),
+            pltpu.VMEM((micros, members, shard_len, width), BF16),
+            pltpu.VMEM((micros, members, shard_len, width), F32),
+            pltpu.VMEM((micros, half, width), BF16),
             pltpu.VMEM((half, half), BF16),
             pltpu.VMEM((3, half, cols), BF16),
             pltpu.VMEM((TILE, length), F32),
-            dma((members,)), dma((members,)), dma((members,)), dma((members,)), dma((members,)),
-            dma((members,)),
+            dma, dma, dma, dma, dma, dma,
         ],
         compiler_params=pltpu.CompilerParams(
-            vmem_limit_bytes=VMEM_LIMIT, collective_id=identity, has_side_effects=True
+            vmem_limit_bytes=VMEM_LIMIT, collective_id=6, has_side_effects=True
         ),
         cost_estimate=pl.CostEstimate(
-            flops=2 * half * cols * (16 * width + 8 * half),
-            bytes_accessed=150000000,
+            flops=2 * micros * half * cols * (16 * width + 8 * half),
+            bytes_accessed=250000000,
             transcendentals=0,
         ),
         name="attend_back",
@@ -689,8 +717,8 @@
 
 
 def closing_kernel(
-    pieces_ref, small_ref, whole_ref, sum_ref,
-    half_got, held_ref, quarter_got, total_ref, moved_ref, moved_got, small_got, line_sum,
+    pieces_ref, small_ref, y_ref, h1_ref, whole_ref, sum_ref, block_ref,
+    y_got, y_send, y_recv, half_got, held_ref, quarter_got, total_ref, moved_ref, moved_got, small_got, line_sum,
     line_got, half_sem, quarter_send, quarter_recv, small_send, small_recv, line_send, line_recv,
     moved_sem, on_send, on_recv, own_sem,
 ):
@@ -704,10 +732,16 @@
     along = [lax.rem(line + s, blocks) for s in range(1, blocks)]
     across = lax.rem(line + blocks // 2, blocks)
     greet([(partner_of(me, s, devices), line) for s in range(1, devices)] + [(me, z) for z in along])
+    ys = [
+        remote(y_ref.at[z], y_got.at[line], y_send.at[s], y_recv.at[s], (me, z))
+        for s, z in enumerate(along)
+    ]
     halves = remote(
         pieces_ref.at[:, 1 - core], half_got, half_sem.at[0], half_sem.at[1], (sibling, line)
     )
     halves.start()
+    for copy in ys:
+        copy.start()
     smalls = [
         remote(
             small_ref, small_got.at[me], small_send.at[s], small_recv.at[s],
@@ -766,10 +800,16 @@
     sum_ref[...] = jnp.sum(line_got[...], axis=0)
     for copy in onward:
         copy.wait_recv()
+    y_got[line] = y_ref[line]
     last = remote(
         whole_ref.at[:, core], whole_ref.at[:, core], on_send.at[0], on_recv.at[0], (sibling, line)
     )
     last.start()
+    for copy in ys:
+        copy.wait_recv()
+    block_ref[...] = (h1_ref[...] + jnp.sum(y_got[...].astype(F32), axis=0)).astype(BF16)
+    for copy in ys:
+        copy.wait_send()
     halves.wait_send()
     for s in steps:
         quarter(s).wait_send()
@@ -779,8 +819,9 @@
     last.wait()
 
 
-def closing(pieces, small, blocks):
+def closing(pieces, small, y, h1):
     devices, both, rows, cols = pieces.shape
+    blocks = y.shape[0]
     chips = devices // 2
     vmem = pl.BlockSpec(memory_space=pltpu.VMEM)
     dma = pltpu.SemaphoreType.DMA
@@ -789,10 +830,14 @@
         out_shape=(
             jax.ShapeDtypeStruct((chips, 2, rows, cols), BF16),
             jax.ShapeDtypeStruct(small.shape, F32),
-        ),
-        in_specs=[vmem, vmem],
-        out_specs=(vmem, vmem),
+            jax.ShapeDtypeStruct(h1.shape, BF16),
+        ),
+        in_specs=[vmem] * 4,
+        out_specs=(vmem,) * 3,
         scratch_shapes=[
+            pltpu.VMEM(y.shape, BF16),
+            dma((blocks,)),
+            dma((blocks,)),
             pltpu.VMEM((chips, both, rows, cols), BF16),
             pltpu.VMEM((chips, both, rows, cols), BF16),
             pltpu.VMEM((chips, both, rows, cols), BF16),
@@ -810,7 +855,7 @@
         ),
         cost_estimate=pl.CostEstimate(flops=0, bytes_accessed=160000000, transcendentals=0),
         name="closing",
-    )(pieces.reshape(chips, 2, both, rows, cols), small)
+    )(pieces.reshape(chips, 2, both, rows, cols), small, y, h1)
 
 
 def spread(rows, place0, place1, count):
@@ -1257,9 +1302,10 @@
         spread(cotangent[micro, 0], own_place[micro]).reshape(devices, -1, width)
         for micro in range(micro_count)
     ]
-    *x_all, other_qkv, all_out, all_routes, other_table, dy_first = opening(
+    dy_first = swap_rows(dy_sent[0], 7)
+    *x_all, other_qkv, all_out, all_routes, other_table = opening(
         x_in[:, 0], qkv_weight.reshape(3 * width, head_cols), out_weight,
-        live_routes, bias_table.T.astype(F32), dy_sent[0], devices, blocks, members,
+        after(live_routes, dy_first), bias_table.T.astype(F32), devices, blocks, members,
     )
     x_half = [x.reshape(1, half, width) for x in x_all]
     other_qkv = other_qkv.reshape(qkv_weight.shape)
@@ -1310,7 +1356,14 @@
         state.update(qkv=qkv[0], prob=prob[0], heads=heads[0], h1=h1[0], xn2=xn2[0])
         if micro + 1 < micro_count:
             states[micro + 1]["dy_here"] = rode[0]
-        behind = (xn2, states[0]["dy"])
+        if micro == 0:
+            pairs = find_pairs(after(all_routes, xn2), expert_count, experts_here, capacity)
+            pairs = pairs.reshape(
+                micro_count, devices, experts_here, blocks * capacity, expert_count
+            )
+            place = after(place, xn2)
+            seg_half = seg_half + jnp.where(pairs[0, 0, 0, 0, 0] > 2, 1, 0)
+        behind = (xn2, states[0]["dy"], place)
     behind = ()
     for micro in range(micro_count):
         state = states[micro]
@@ -1318,8 +1371,6 @@
         behind = (state["xn2_all"],)
     for micro in range(1, micro_count):
         states[micro]["dy"] = gather_dy(after(states[micro]["dy_here"], states[0]["xn2_all"]))
-    pairs = find_pairs(after(all_routes, states[-1]["xn2"]), expert_count, experts_here, capacity)
-    pairs = pairs.reshape(micro_count, devices, experts_here, blocks * capacity, expert_count)
     behind = ()
     for micro in range(micro_count):
         experts(micro, states[micro], *behind)
@@ -1328,43 +1379,28 @@
     kept = [state["weights"] for state in states]
     kept[-1] = tuple(after(list(kept[-1]), last_part))
     dwr, dwg, dwu, dwd = weight_pass(kept)
-    grads = None
-    behind = (last_part,)
-    for micro in range(micro_count):
+    last = states[-1]
+    last["y_rows"] = exchange(after(last["y"], last_part).reshape(flat_shape)).reshape(place_shape)
+    *x_grads, grads, lines, moe_gain_grad, attn_gain_grad = attend_back(
+        moe_gain_f, attn_gain_f, all_out, qkv_weight, other_qkv,
+        [
+            (
+                after(state["dxn2"], dwr), state["h1"], cotangent[micro, 0], x_in[micro, 0],
+                x_half[micro][0], state["qkv"], state["prob"], state["heads"],
+            )
+            for micro, state in enumerate(states)
+        ],
+        scale, devices, members,
+    )
+    rows = collect_rows(after(last["y_rows"], grads), place[-1], shard_len)
+    rows = rows.reshape(blocks, shard_len, width)
+    for micro in range(micro_count - 1):
         state = states[micro]
-        if state["by_block"]:
-            sent = after(state["y_own"], states[-1]["back"])
-            state["y_rows"] = exchange(sent).reshape(expert_count, 1, capacity, width)
-        else:
-            sent = after(state["y"], *behind).reshape(flat_shape)
-            state["y_rows"] = exchange(sent).reshape(place_shape)
-        behind = (last_part, state["y_rows"])
-    for micro in range(micro_count):
-        state = states[micro]
-        state["x_grad"], grads, state["line"], state["moe_gain_grad"], state["attn_gain_grad"] = (
-            attend_back(
-                after(state["dxn2"], dwr), state["h1"], cotangent[micro, 0], x_in[micro, 0],
-                moe_gain_f, attn_gain_f, all_out, x_half[micro][0], qkv_weight, other_qkv,
-                state["qkv"], state["prob"], state["heads"], grads, scale, devices, members,
-                4 + micro_count + micro,
-            )
-        )
-    for micro in range(micro_count):
-        state = states[micro]
-        rows = after(state["y_rows"], grads)
-        if state["by_block"]:
-            mixed = collect_rows(rows, own_place[micro], shard_len)
-        else:
-            mixed = scatter(collect_rows(rows, place[micro], shard_len))
+        mixed = exchange(after(state["y_own"], grads)).reshape(expert_count, 1, capacity, width)
+        mixed = collect_rows(mixed, own_place[micro], shard_len)
         state["block_out"] = (state["h1"] + mixed.astype(F32)).astype(BF16)
 
-    def added(name):
-        total = states[0][name]
-        for state in states[1:]:
-            total = total + state[name]
-        return total
-
-    lines = added("line").reshape(2 * heads_here, 2 * half)
+    lines = lines.reshape(2 * heads_here, 2 * half)
     table = jnp.einsum("hj,jb->hb", lines, onehot_bucket, precision=PRECISE)
     table = table.reshape(2, heads_here * bucket_count)
     mine = jnp.arange(blocks, dtype=jnp.int32)[:, None]
@@ -1374,14 +1410,14 @@
     small = jnp.concatenate(
         [
             jnp.sum(dwr, axis=0).reshape(-1),
-            added("attn_gain_grad").reshape(-1),
-            added("moe_gain_grad").reshape(-1),
+            attn_gain_grad.reshape(-1),
+            moe_gain_grad.reshape(-1),
             table.reshape(-1),
         ]
     )
     used = small.shape[0]
     small = jnp.pad(small, (0, -used % 1024)).reshape(-1, 128)
-    whole, small = closing(grads, small, blocks)
+    whole, small, last["block_out"] = closing(grads, small, rows, last["h1"])
     whole = whole.reshape(4 * width, head_cols).astype(F32)
     grad_qkv = whole[: 3 * width].reshape(qkv_weight.shape)
     grad_out = whole[3 * width :].T
@@ -1394,7 +1430,7 @@
     grad_table = lax.dynamic_index_in_dim(table, hidden_index, 0, keepdims=False).T
     return (
         jnp.stack([state["block_out"] for state in states])[:, None],
-        jnp.stack([state["x_grad"] for state in states])[:, None],
+        jnp.stack(x_grads)[:, None],
         grad_qkv,
         grad_out,
         grad_table,

time: 807 us -> 788 us (0.976)
  waiting for transfers between devices: 54 us -> 1.24 us
  Pallas kernels: 685 us -> 717 us
    pallas_call x1, Pallas kernels: 46.9 us -> 97 us  [opening(): pl.pallas_call(functools.partial(opening_kernel, micros), out_shape=(jax....]
    all_gather x4, waiting for transfers between devices: 40.3 us -> 0.04 us  [gather(): return lax.all_gather(values, 'hidden', axis=0, tiled=True)]
    pallas_call x2, Pallas kernels: 98.7 us -> 63.7 us  [attend(): pl.pallas_call(functools.partial(attend_kernel, scale), grid=(micros, 2),...]
    all_to_all x2, waiting for transfers between devices: 12.5 us -> 0.01 us  [exchange(): lax.all_to_all(buffer, 'expert', split_axis=0, concat_axis=0, tiled=True)]
    pallas_call x1, Pallas kernels: 77.7 us -> 89.6 us  [closing(): pl.pallas_call(closing_kernel, out_shape=(jax.ShapeDtypeStruct((chips, 2,...]
  transfers between devices with their start and end apart: 10 -> 9, of which waited for: 3 -> 0; matrix products, arithmetic and copies ran while one was open for 3% -> 3% of each run, Pallas kernels for 79% -> 89%
where the time goes in v9:
time: 788 us; the launch traced here: 779 us
  Pallas kernels  717 us (91%)
  local copies, waits for them, and re-layouts  22.5 us (3%)
  between operations  15.5 us (2%)
  other arithmetic  11.2 us (1%)
  starting transfers between devices  9.52 us (1%)
    pallas_call x2, Pallas kernels, expert_pass(): pl.pallas_call(functools.partial(expert_kernel, by_block), grid=(devices,...  274 us
    pallas_call x1, Pallas kernels, opening(): pl.pallas_call(functools.partial(opening_kernel, micros), out_shape=(jax....  97 us
    pallas_call x1, Pallas kernels, closing(): pl.pallas_call(closing_kernel, out_shape=(jax.ShapeDtypeStruct((chips, 2,...  89.6 us
    pallas_call x1, Pallas kernels, attend_back(): pl.pallas_call(functools.partial(back_kernel, scale, micros), grid=(2, mi...  80.1 us
    pallas_call x2, Pallas kernels, attend(): pl.pallas_call(functools.partial(attend_kernel, scale), grid=(micros, 2),...  63.7 us
    pallas_call x1, Pallas kernels, weight_pass(): pl.pallas_call(weight_kernel, grid=(experts, width // block), out_shape=(...  38.6 us
    pallas_call x4, Pallas kernels, collect_rows(): pl.pallas_call(collect_kernel, grid=(blocks,), out_shape=jax.ShapeDtypeSt...  19.6 us
    pallas_call x1, Pallas kernels, swap_rows(): pl.pallas_call(swap_kernel, out_shape=jax.ShapeDtypeStruct(sent.shape, se...  19.5 us
  transfers between devices with their start and end apart: 9, of which 0 were waited for; matrix products, arithmetic and copies ran while one was open for 3% of the time, Pallas kernels for 89%

profile of v9, /device:TPU:0, one launch (start us, length us, event | category | flops | bytes accessed | tf_op | source)
XLA Modules:
  0.0 778.7 jit_solution(10996970203751609013)
XLA Ops:
  7.2 0.7 dynamic-slice_compare_fusion
  7.9 1.3 fusion.19
  9.2 1.4 find_places.2
  10.7 1.3 slice_bitcast_fusion.10
  12.0 3.2 slice_bitcast_fusion
  15.2 2.7 spread_rows.4
  17.8 19.5 %swap_rows.1 = bf16[8,80,1024]{2,1,0:T(8,128)(2,1)} custom-call(bf16[8,80,1024]{2,1,0:T(8,128)(2,1)} %bitcast.139), custom_call_target="tpu_custom_call" | custom-call | bytes 60000000 | tf_op jit(solution)/shard_map/swap_rows/pallas_call | solution.py:278
  38.6 0.9 copy.32.seg_col_ref
  40.1 97.0 %opening.1 = (bf16[2,256,1024]{2,1,0:T(8,128)(2,1)}, bf16[2,256,1024]{2,1,0:T(8,128)(2,1)}, bf16[4,2,384,256]{3,2,1,0:T(8,128)(2,1)}, bf16[4,4,2,32,1024]{4,3,2,...) custom-call(bf16[2,256,1024]{2,1,0:T(8,128)(2,1)} %bitcast.142, bf16[3072,256]{1,0:T(8,128)(2,1)} %bitcast.130, ...), custom_call_target="tpu_custom_call" | custom-call | bytes 200000000 | tf_op jit(solution)/shard_map/opening/pallas_call | solution.py:235
  137.1 1.1 fusion.2
  138.3 0.7 reshape.236.line_ref
  138.9 5.9 position_bias.1.bias_ref
  144.8 2.6 spread_rows.5
  148.0 28.6 %attend.2 = (bf16[1,2,3,512,256]{4,3,2,1,0:T(8,128)(2,1)}, bf16[1,2,4,512,512]{4,3,2,1,0:T(8,128)(2,1)}, bf16[1,512,512]{2,1,0:T(8,128)(2,1)}, f32[1,256,1024]{2...) custom-call(bf16[1,512,1024]{2,1,0:T(8,128)(2,1)} %bitcast.155, f32[1,1024]{1,0:T(1,128)} %bitcast.171, ...), custom_call_target="tpu_custom_call" | custom-call | flops 2684354560 | bytes 100000000 | tf_op jit(solution)/shard_map/attend/pallas_call | solution.py:426
  176.9 1.3 dynamic-slice_bitcast_fusion.route_ref
  178.3 1.6 find_places.3
  179.9 10.8 %find_pairs.1 = bf16[2,8,2,4,40,16]{5,4,3,2,1,0:T(8,128)(2,1)} custom-call(s32[8,4,2,2,256]{4,3,2,1,0:T(2,128)} %get-tuple-element.86.route_ref), custom_call_target="tpu_custom_call" | custom-call | tf_op jit(solution)/shard_map/find_pairs/pallas_call | solution.py:986
  190.7 1.2 slice.116
  192.6 0.9 copy.33.seg_col_ref
  194.0 35.1 %attend.3 = (bf16[1,2,3,512,256]{4,3,2,1,0:T(8,128)(2,1)}, bf16[1,2,4,512,512]{4,3,2,1,0:T(8,128)(2,1)}, bf16[1,512,512]{2,1,0:T(8,128)(2,1)}, f32[1,256,1024]{2,1,0:T(8,128)}, bf16[1,256,1024]{2,1,0:T(8,128)(2,1)}) custom-call(bf16[1,512,1024]{2,1,0:T(8,128)(2,1)} %bitcast.182, f32[1,1024]{1,0:T(1,128)} %bitcast.172, bf16[3,1024,256]{2,1,0:T(8,128)(2,1)} %refs_3_.1, ...), custom_call_target="tpu_custom_call" | custom-call | flops 2684354560 | bytes 100000000 | tf_op jit(solution)/shard_map/attend/pallas_call | solution.py:426
  230.6 1.2 fusion.22
  231.8 5.3 spread_rows.6
  237.1 137.0 %expert_pass.2 = (bf16[8,2,160,1024]{3,2,1,0:T(8,128)(2,1)}, bf16[4,8,2,40,1024]{4,3,2,1,0:T(8,128)(2,1)}, bf16[8,2,160,1024]{3,2,1,0:T(8,128)(2,1)}, bf16[8,2,1...) custom-call(bf16[8,2,160,1024]{3,2,1,0:T(8,128)(2,1)} %bitcast.124, ...), custom_call_target="tpu_custom_call" | custom-call | bytes 490000000 | tf_op jit(solution)/shard_map/expert_pass/pallas_call | solution.py:1147
  374.1 5.6 collect_rows.4
  380.4 5.3 spread_rows.7
  385.7 136.6 %expert_pass.3 = (bf16[8,2,160,1024]{3,2,1,0:T(8,128)(2,1)}, bf16[8,2,4,40,1024]{4,3,2,1,0:T(8,128)(2,1)}, bf16[8,2,160,1024]{3,2,1,0:T(8,128)(2,1)}, bf16[8,2,1...) custom-call(bf16[8,2,160,1024]{3,2,1,0:T(8,128)(2,1)} %bitcast.123, ...), custom_call_target="tpu_custom_call" | custom-call | bytes 490000000 | tf_op jit(solution)/shard_map/expert_pass/pallas_call | solution.py:1147
  522.3 5.6 collect_rows.5
  528.0 5.2 all-to-all-start.1
  533.2 38.6 %weight_pass.1 = (f32[2,16,1024]{2,1,0:T(8,128)}, f32[2,704,1024]{2,1,0:T(8,128)}, f32[2,704,1024]{2,1,0:T(8,128)}, f32[2,704,1024]{2,1,0:T(8,128)}) custom-call(bf16[8,2,160,1024]{3,2,1,0:T(8,128)(2,1)} %get-tuple-element.90.refs_0_, bf16[8,2,160,1024]{3,2,1,0:T(8,128)(2,1)} %get-tuple-element.91.refs_1_, ...), custom_call_target="tpu_custom_call" | custom-call | flops 22145925120 | bytes 59899904 | tf_op jit(solution)/shard_map/weight_pass/pallas_call | solution.py:1213
  571.9 0.9 reduce_sum.9
  572.9 80.1 %attend_back.1 = (bf16[256,1024]{1,0:T(8,128)(2,1)}, bf16[256,1024]{1,0:T(8,128)(2,1)}, bf16[8,2,512,256]{3,2,1,0:T(8,128)(2,1)}, f32[2,4,1024]{2,1,0:T(4,128)}, f32[1,1024]{1,0:T(1,128)}, /*index=5*/f32[1,1024]{1,0:T(1,128)}) custom-call(f32[1,1024]{1,0:T(1,128)} %bitcast.176, f32[1,1024]{1,0:T(1,128)} %bitcast.173, bf16[4,256,1024]{2,1,0:T(8,128)(2,1)} %bitcast.150, ...), custom_call_target="tpu_custom_call" | custom-call | flops 10737418240 | bytes 250000000 | tf_op jit(solution)/shard_map/attend_back/pallas_call | solution.py:675
  653.0 0.8 reshape.260
  654.1 3.6 all-to-all-start
  658.0 1.3 fusion.5.small_ref
  659.3 2.3 maximum_bitcast_fusion.1
  661.6 5.6 collect_rows.7
  667.2 89.6 %closing.1 = (bf16[4,2,512,256]{3,2,1,0:T(8,128)(2,1)}, f32[152,128]{1,0:T(8,128)}, bf16[256,1024]{1,0:T(8,128)(2,1)}) custom-call(bf16[4,2,2,512,256]{4,3,2,1,0:T(8,128)(2,1)} %bitcast.143, f32[152,128]{1,0:T(8,128)} %fusion.5.small_ref, bf16[4,256,1024]{2,1,0:T(8,128)(2,1)} %bitcast.129, f32[256,1024]{1,0:T(8,128)} %bitcast.160), custom_call_target="tpu_custom_call" | custom-call | bytes 160000000 | tf_op jit(solution)/shard_map/closing/pallas_call | solution.py:828
  756.8 0.8 slice.107
  757.6 0.8 slice.112
  758.4 1.1 slice.119
  759.6 1.9 slice.118
  761.6 0.6 reshape.267
  762.3 1.3 copy.34
  764.2 1.3 slice_bitcast_fusion.8
  765.4 1.1 copy-done.1
  766.5 2.7 collect_rows.6
  769.2 1.2 fusion
  770.5 1.1 maximum_bitcast_fusion
  (61 shorter events, 6.9 us)
Async XLA Ops:
  7.2 186.8 %all-gather.7.cloned.1.call-start = ((), (), s32[]{:S(2)}) async-start(), calls=%async_computation.6 | async-start | bytes 6553600 | tf_op jit(solution)/shard_map/all_gather | solution.py:1288
  15.2 22.3 %copy-start.7 = (bf16[1024]{0:T(1024)(128)(2,1)S(1)}, bf16[1024]{0:T(1024)(128)(2,1)}, u32[]{:S(2)}) copy-start(bf16[1024]{0:T(1024)(128)(2,1)} %param.20) | copy-start | bytes 6148
  15.2 22.9 %copy-start.8 = (bf16[1024]{0:T(1024)(128)(2,1)S(1)}, bf16[1024]{0:T(1024)(128)(2,1)}, u32[]{:S(2)}) copy-start(bf16[1024]{0:T(1024)(128)(2,1)} %param.21) | copy-start | bytes 6148
  15.2 23.5 %copy-start.6 = (s32[2,1,1024]{2,1,0:T(1,128)S(1)}, s32[2,1,1024]{2,1,0:T(1,128)}, u32[]{:S(2)}) copy-start(s32[2,1,1024]{2,1,0:T(1,128)} %param.15) | copy-start | bytes 24580
  15.2 24.3 %copy-start.9 = (bf16[32,4]{0,1:T(4,128)(2,1)S(1)}, bf16[32,4]{0,1:T(4,128)(2,1)}, u32[]{:S(2)}) copy-start(bf16[32,4]{0,1:T(4,128)(2,1)} %param.19) | copy-start | bytes 772
  37.4 191.7 %all-gather.5.cloned.1.call-start = ((), (), s32[]{:S(2)}) async-start(), calls=%async_computation.5 | async-start | bytes 2621440 | tf_op jit(solution)/shard_map/all_gather | solution.py:1288
  176.7 203.7 %all-gather.9.cloned.1.call-start = ((), (), s32[]{:S(2)}) async-start(), calls=%async_computation.9 | async-start | bytes 2621440 | tf_op jit(solution)/shard_map/all_gather | solution.py:1288
  194.0 36.0 %copy-start.5 = (s32[2,2,1024]{2,1,0:T(2,128)S(1)}, s32[2,2,1024]{2,1,0:T(2,128)}, u32[]{:S(2)}) copy-start(s32[2,2,1024]{2,1,0:T(2,128)} %find_places.3) | copy-start | bytes 49156
  194.0 36.6 %copy-start.2 = (bf16[2,8,2,4,40,16]{5,4,3,2,1,0:T(8,128)(2,1)S(1)}, bf16[2,8,2,4,40,16]{5,4,3,2,1,0:T(8,128)(2,1)}, u32[]{:S(2)}) copy-start(bf16[2,8,2,4,40,16]{5,4,3,2,1,0:T(8,128)(2,1)} %find_pairs.1) | copy-start | bytes 491524
  229.1 156.6 %all-gather.11.cloned.1.call-start = ((), (), s32[]{:S(2)}) async-start(), calls=%async_computation.10 | async-start | bytes 6553600 | tf_op jit(solution)/shard_map/all_gather | solution.py:1288
  229.7 292.6 %reduce-scatter.4.cloned.1.call-start = ((), (), s32[]{:S(2)}) async-start(), calls=%async_computation.7 | async-start | bytes 6553600 | tf_op jit(solution)/shard_map/reduce_scatter | solution.py:1291
  379.8 192.1 %reduce-scatter.6.cloned.1.call-start = ((), (), s32[]{:S(2)}) async-start(), calls=%async_computation.8 | async-start | bytes 2621440 | tf_op jit(solution)/shard_map/reduce_scatter | solution.py:1291
  380.3 192.5 %reduce-scatter.8.cloned.1.call-start = ((), (), s32[]{:S(2)}) async-start(), calls=%async_computation.11 | async-start | bytes 2621440 | tf_op jit(solution)/shard_map/reduce_scatter | solution.py:1291
  528.0 126.1 %all-to-all-start.1 = ((bf16[8,320,1024]{2,1,0:T(8,128)(2,1)}), bf16[8,320,1024]{2,1,0:T(8,128)(2,1)}, u32[]{:S(2)}, u32[]{:S(2)}) async-start(bf16[8,320,1024]{2,1,0:T(8,128)(2,1)} %bitcast.132), calls=%async_computation.4 | async-start | bytes 10485760 | tf_op jit(solution)/shard_map/all_to_all | solution.py:1285
  654.1 111.3 %all-to-all-start = ((bf16[8,80,1024]{2,1,0:T(8,128)(2,1)}), bf16[8,80,1024]{2,1,0:T(8,128)(2,1)S(1)}, u32[]{:S(2)}, u32[]{:S(2)}) async-start(bf16[8,80,1024]{2,1,0:T(8,128)(2,1)} %bitcast.32), calls=%async_computation.3 | async-start | bytes 2621440 | tf_op jit(solution)/shard_map/all_to_all | solution.py:1285
  756.8 2.8 copy-start
  759.6 9.7 %copy-start.3 = (f32[1,256,1024]{2,1,0:T(8,128)S(1)}, f32[1,256,1024]{2,1,0:T(8,128)}, u32[]{:S(2)}) copy-start(f32[1,256,1024]{2,1,0:T(8,128)} %get-tuple-element.82) | copy-start | bytes 3145732
  763.6 6.9 copy-start.4
  765.4 1.1 copy-start.1
Sparse Core Ops, SparseCore 0:
  37.5 123.7 all-gather.6
  176.8 45.8 all-gather.4
  229.3 45.8 all-gather.8
  276.6 96.7 all-gather.10
  379.9 92.9 reduce-scatter.3
  475.6 44.3 reduce-scatter.5
  528.1 43.8 reduce-scatter.7

commit v10 on v9

--- a/solution.py
+++ b/solution.py
@@ -111,14 +111,14 @@
 
 
 def opening_kernel(
-    micros, x_ref, qkv_ref, out_ref, routes_ref, table_ref, *refs,
+    micros, x_ref, qkv_ref, out_ref, routes_ref, table_ref, dy_ref, *refs,
 ):
     x_all, refs = refs[:micros], refs[micros:]
     (
-        qkv_all, out_all, routes_all, table_all,
+        qkv_all, out_all, routes_all, table_all, dy_all,
         x_send, x_recv, qkv_send, qkv_recv, out_send, out_recv, qkv_on_send, qkv_on_recv,
         out_on_send, out_on_recv, routes_send, routes_recv, routes_on_send, routes_on_recv,
-        table_send, table_recv, own_sem,
+        table_send, table_recv, dy_send, dy_recv, own_sem,
     ) = refs
     devices, qkv_rows = qkv_all.shape[0] * 2, qkv_all.shape[2]
     blocks, out_rows = out_all.shape[0], out_all.shape[3]
@@ -137,10 +137,11 @@
             out_ref.at[pl.ds(me * out_rows, out_rows)], out_all.at[line, chip, core], own_sem.at[0]
         ),
         pltpu.make_async_copy(routes_ref, routes_all.at[me, line], own_sem.at[1]),
+        pltpu.make_async_copy(dy_ref.at[me], dy_all.at[me], own_sem.at[2]),
     ]
     for micro in range(micros):
         own.append(
-            pltpu.make_async_copy(x_ref.at[micro], x_all[micro].at[mine], own_sem.at[2 + micro])
+            pltpu.make_async_copy(x_ref.at[micro], x_all[micro].at[mine], own_sem.at[3 + micro])
         )
     for copy in own:
         copy.start()
@@ -174,6 +175,11 @@
             )
             copy.start()
             rest.append(copy)
+    for s in range(1, devices):
+        peer = partner_of(me, s, devices)
+        copy = remote(dy_ref.at[peer], dy_all.at[me], dy_send.at[s], dy_recv.at[s], (peer, line))
+        copy.start()
+        rest.append(copy)
     first_qkv.wait_recv()
     qkv_on, out_on = [], []
     for s in range(2, devices, 2):
@@ -228,7 +234,7 @@
         copy.wait()
 
 
-def opening(x, qkv, out, routes, table, devices, blocks, members):
+def opening(x, qkv, out, routes, table, dy, devices, blocks, members):
     micros, shard_len, width = x.shape
     dma = pltpu.SemaphoreType.DMA
     pair = (devices // 2, 2)
@@ -240,51 +246,20 @@
             jax.ShapeDtypeStruct((blocks,) + pair + (out.shape[0] // devices, width), BF16),
             jax.ShapeDtypeStruct((devices, blocks) + routes.shape, jnp.int32),
             jax.ShapeDtypeStruct(table.shape, table.dtype),
-        ),
-        in_specs=[any_space()] * 5,
-        out_specs=(any_space(),) * (4 + micros),
+            jax.ShapeDtypeStruct(dy.shape, BF16),
+        ),
+        in_specs=[any_space()] * 6,
+        out_specs=(any_space(),) * (5 + micros),
         scratch_shapes=[
             dma((micros, members)), dma((micros, members)), dma, dma, dma((blocks,)), dma((blocks,)),
             dma((devices,)), dma((devices,)), dma((devices,)), dma((devices,)), dma((blocks,)),
-            dma((blocks,)), dma((devices,)), dma((devices,)), dma, dma, dma((2 + micros,)),
+            dma((blocks,)), dma((devices,)), dma((devices,)), dma, dma, dma((devices,)),
+            dma((devices,)), dma((3 + micros,)),
         ],
         compiler_params=pltpu.CompilerParams(collective_id=1, has_side_effects=True),
         cost_estimate=pl.CostEstimate(flops=0, bytes_accessed=200000000, transcendentals=0),
         name="opening",
-    )(x, qkv, out, routes, table)
-
-
-def swap_kernel(sent_ref, got_ref, send_sem, recv_sem, own_sem):
-    devices = sent_ref.shape[0]
-    me = lax.axis_index("expert")
-    line = lax.axis_index("hidden")
-    greet([(partner_of(me, s, devices), line) for s in range(1, devices)])
-    own = pltpu.make_async_copy(sent_ref.at[me], got_ref.at[me], own_sem)
-    own.start()
-    copies = []
-    for s in range(1, devices):
-        peer = partner_of(me, s, devices)
-        copies.append(
-            remote(sent_ref.at[peer], got_ref.at[me], send_sem.at[s], recv_sem.at[s], (peer, line))
-        )
-        copies[-1].start()
-    own.wait()
-    for copy in copies:
-        copy.wait()
-
-
-def swap_rows(sent, identity):
-    dma = pltpu.SemaphoreType.DMA
-    return pl.pallas_call(
-        swap_kernel,
-        out_shape=jax.ShapeDtypeStruct(sent.shape, sent.dtype),
-        in_specs=[any_space()],
-        out_specs=any_space(),
-        scratch_shapes=[dma((sent.shape[0],)), dma((sent.shape[0],)), dma],
-        compiler_params=pltpu.CompilerParams(collective_id=identity, has_side_effects=True),
-        cost_estimate=pl.CostEstimate(flops=0, bytes_accessed=60000000, transcendentals=0),
-        name="swap_rows",
-    )(sent)
+    )(x, qkv, out, routes, table, dy)
 
 
 def unit_rows(x):
@@ -298,8 +273,9 @@
 ):
     riding = len(refs) > 10
     if riding:
-        sent_ref, arrived_ref, ride_send, ride_recv, ride_own = refs[0], refs[6], *refs[-3:]
-        refs = refs[1:6] + refs[7:-3]
+        sent_ref, next_ref, arrived_ref, next_all = *refs[:2], *refs[7:9]
+        ride_send, ride_recv, next_send, next_recv, ride_own = refs[-5:]
+        refs = refs[2:7] + refs[9:-5]
     qkv_ref, prob_ref, heads_ref, h1_ref, xn2_ref, xn_ref, part_ref, got_ref, send_sem, recv_sem = refs
     micros, members, shard_len, both = got_ref.shape
     cols = both // 2
@@ -327,7 +303,16 @@
         )
 
     def stay():
-        return pltpu.make_async_copy(sent_ref.at[me], arrived_ref.at[me], ride_own)
+        return [
+            pltpu.make_async_copy(sent_ref.at[me], arrived_ref.at[me], ride_own.at[0]),
+            pltpu.make_async_copy(next_ref, next_all.at[mine], ride_own.at[1]),
+        ]
+
+    def pair(s):
+        peer = lax.rem(mine + s, members)
+        return remote(
+            next_ref, next_all.at[mine], next_send.at[s], next_recv.at[s], (me, base + peer)
+        )
 
     @pl.when((micro == 0) & (group == 0))
     def _():
@@ -337,7 +322,8 @@
             peers += [(partner_of(me, s, devices), line) for s in range(1, devices)]
         greet(peers)
         if riding:
-            stay().start()
+            for copy in stay():
+                copy.start()
             for s in range(1, devices):
                 ride(s).start()
 
@@ -385,6 +371,8 @@
         got_ref[micro, mine] = part_ref[micro, mine]
         for s in range(1, members):
             swap(micro, s).start()
+            if riding:
+                pair(s).start()
 
     @pl.when((micro == micros - 1) & (group == 1))
     def _():
@@ -402,7 +390,10 @@
             for s in range(1, members):
                 swap(m, s).wait_send()
         if riding:
-            stay().wait()
+            for copy in stay():
+                copy.wait()
+            for s in range(1, members):
+                pair(s).wait()
             for s in range(1, sent_ref.shape[0]):
                 ride(s).wait()
 
@@ -415,10 +406,12 @@
     cols = own_weight.shape[2]
     heads = bias.shape[0] // 2
     shard_len = half // members
-    riders = [] if rider is None else [rider]
-    ride_sems = []
-    for array in riders:
-        ride_sems = [pltpu.SemaphoreType.DMA((array.shape[0],))] * 2 + [pltpu.SemaphoreType.DMA]
+    riders, ride_shapes, ride_sems = [], (), []
+    if rider is not None:
+        riders = list(rider)
+        ride_shapes = (rider[0].shape, (members, shard_len, width))
+        ride_sems = [pltpu.SemaphoreType.DMA((rider[0].shape[0],))] * 2
+        ride_sems += [pltpu.SemaphoreType.DMA((members,))] * 2 + [pltpu.SemaphoreType.DMA((2,))]
 
     def once(shape):
         return pl.BlockSpec(shape, lambda m, p: (0,) * len(shape), pipeline_mode=pl.Buffered(1))
@@ -433,7 +426,7 @@
             jax.ShapeDtypeStruct((micros, shard_len, width), F32),
             jax.ShapeDtypeStruct((micros, shard_len, width), BF16),
         )
-        + tuple(jax.ShapeDtypeStruct(array.shape, array.dtype) for array in riders),
+        + tuple(jax.ShapeDtypeStruct(shape, BF16) for shape in ride_shapes),
         in_specs=[
             pl.BlockSpec((1, half, width), lambda m, p: (m, 0, 0)),
             once((1, width)),
@@ -732,15 +725,23 @@
     along = [lax.rem(line + s, blocks) for s in range(1, blocks)]
     across = lax.rem(line + blocks // 2, blocks)
     greet([(partner_of(me, s, devices), line) for s in range(1, devices)] + [(me, z) for z in along])
-    ys = [
-        remote(y_ref.at[z], y_got.at[line], y_send.at[s], y_recv.at[s], (me, z))
-        for s, z in enumerate(along)
-    ]
+    share = y_ref.shape[1] // 2
+
+    def y_copies(turn):
+        rows = pl.ds(turn * share, share)
+        return [
+            remote(
+                y_ref.at[z, rows], y_got.at[line, rows], y_send.at[turn, s], y_recv.at[turn, s],
+                (me, z),
+            )
+            for s, z in enumerate(along)
+        ]
+
     halves = remote(
         pieces_ref.at[:, 1 - core], half_got, half_sem.at[0], half_sem.at[1], (sibling, line)
     )
     halves.start()
-    for copy in ys:
+    for copy in y_copies(0):
         copy.start()
     smalls = [
         remote(
@@ -785,6 +786,8 @@
     cross = remote(moved_ref, moved_got, moved_sem.at[0], moved_sem.at[1], (me, across))
     cross.start()
     cross.wait_recv()
+    for copy in y_copies(1):
+        copy.start()
     whole_ref[chip, core] = (total_ref[0] + moved_got[...].astype(F32)).astype(BF16)
     onward = [
         remote(
@@ -805,10 +808,10 @@
         whole_ref.at[:, core], whole_ref.at[:, core], on_send.at[0], on_recv.at[0], (sibling, line)
     )
     last.start()
-    for copy in ys:
+    for copy in y_copies(0) + y_copies(1):
         copy.wait_recv()
     block_ref[...] = (h1_ref[...] + jnp.sum(y_got[...].astype(F32), axis=0)).astype(BF16)
-    for copy in ys:
+    for copy in y_copies(0) + y_copies(1):
         copy.wait_send()
     halves.wait_send()
     for s in steps:
@@ -836,8 +839,8 @@
         out_specs=(vmem,) * 3,
         scratch_shapes=[
             pltpu.VMEM(y.shape, BF16),
-            dma((blocks,)),
-            dma((blocks,)),
+            dma((2, blocks)),
+            dma((2, blocks)),
             pltpu.VMEM((chips, both, rows, cols), BF16),
             pltpu.VMEM((chips, both, rows, cols), BF16),
             pltpu.VMEM((chips, both, rows, cols), BF16),
@@ -866,19 +869,19 @@
 
 def spread_kernel(rows_ref, place_ref, out_ref):
     experts, _, cap, width = out_ref.shape
-    placed = spread(rows_ref[...], place_ref[0:1, :], place_ref[1:2, :], experts * cap)
+    placed = spread(rows_ref[0], place_ref[0:1, :], place_ref[1:2, :], experts * cap)
     out_ref[...] = placed.astype(BF16).reshape(experts, 1, cap, width)
 
 
-def spread_rows(rows, place, experts, cap, shard_len):
-    slots, width = rows.shape
+def spread_rows(rows, micro, place, experts, cap, shard_len):
+    _, slots, width = rows.shape
     blocks = slots // shard_len
     return pl.pallas_call(
         spread_kernel,
         grid=(blocks,),
         out_shape=jax.ShapeDtypeStruct((experts, blocks, cap, width), BF16),
         in_specs=[
-            pl.BlockSpec((shard_len, width), lambda b: (b, 0)),
+            pl.BlockSpec((1, shard_len, width), lambda b: (micro, b, 0)),
             pl.BlockSpec((2, shard_len), lambda b: (0, b)),
         ],
         out_specs=pl.BlockSpec((experts, 1, cap, width), lambda b: (0, b, 0, 0)),
@@ -1295,19 +1298,18 @@
     live_routes = jnp.where(own_seg[:, None, :] >= 0, routes[:, 0].transpose(0, 2, 1), -1)
     own_place = find_places(live_routes[None], expert_count, capacity)
 
-    def spread(rows, placed):
-        return spread_rows(rows, placed, expert_count, capacity, shard_len)
+    def spread(rows, micro, placed):
+        return spread_rows(rows, micro, placed, expert_count, capacity, shard_len)
 
     dy_sent = [
-        spread(cotangent[micro, 0], own_place[micro]).reshape(devices, -1, width)
+        spread(cotangent[:, 0], micro, own_place[micro]).reshape(devices, -1, width)
         for micro in range(micro_count)
     ]
-    dy_first = swap_rows(dy_sent[0], 7)
-    *x_all, other_qkv, all_out, all_routes, other_table = opening(
-        x_in[:, 0], qkv_weight.reshape(3 * width, head_cols), out_weight,
-        after(live_routes, dy_first), bias_table.T.astype(F32), devices, blocks, members,
+    x_first, other_qkv, all_out, all_routes, other_table, dy_first = opening(
+        x_in[0], qkv_weight.reshape(3 * width, head_cols), out_weight,
+        live_routes, bias_table.T.astype(F32), dy_sent[0], devices, blocks, members,
     )
-    x_half = [x.reshape(1, half, width) for x in x_all]
+    x_half = [x_first.reshape(1, half, width)]
     other_qkv = other_qkv.reshape(qkv_weight.shape)
     all_out = all_out.reshape(blocks, head_cols, width)
 
@@ -1324,7 +1326,7 @@
         return whole.reshape(blocks, devices, experts_here, capacity, width)
 
     def experts(micro, kept, *behind):
-        sent = spread(kept["xn2_all"], place[micro]).reshape(token_shape)
+        sent = spread(kept["xn2_all"][None], 0, place[micro]).reshape(token_shape)
         kept["by_block"] = micro + 1 < micro_count
         back, kept["y"], x, g, hid, dga, dup, dlog = expert_pass(
             after(sent, *behind), kept["dy"], pairs[micro], router_rows, gate_rows, up_rows,
@@ -1347,7 +1349,7 @@
         state = states[micro]
         rider = None
         if micro + 1 < micro_count:
-            rider = dy_sent[micro + 1]
+            rider = (dy_sent[micro + 1], x_in[micro + 1, 0])
         qkv, prob, heads, h1, xn2, *rode = attend(
             after(x_half[micro], *behind), attn_gain_f, qkv_weight, other_qkv, bias,
             seg_half[micro : micro + 1], all_out, x_in[micro], moe_gain_f, scale, members, 10 + micro,
@@ -1356,6 +1358,7 @@
         state.update(qkv=qkv[0], prob=prob[0], heads=heads[0], h1=h1[0], xn2=xn2[0])
         if micro + 1 < micro_count:
             states[micro + 1]["dy_here"] = rode[0]
+            x_half.append(rode[1].reshape(1, half, width))
         if micro == 0:
             pairs = find_pairs(after(all_routes, xn2), expert_count, experts_here, capacity)
             pairs = pairs.reshape(

time: 788 us -> 774 us (0.982)
  Pallas kernels: 717 us -> 700 us
    pallas_call x2, Pallas kernels: 63.7 us -> 134 us  [attend(): pl.pallas_call(functools.partial(attend_kernel, scale), grid=(micros, 2),...]
    pallas_call x1, Pallas kernels: 97 us -> 46.8 us  [opening(): pl.pallas_call(functools.partial(opening_kernel, micros), out_shape=(jax....]
    pallas_call x1 -> x0, Pallas kernels: 19.5 us -> none  [swap_rows(): pl.pallas_call(swap_kernel, out_shape=jax.ShapeDtypeStruct(sent.shape, se...]
    pallas_call x1, Pallas kernels: 89.6 us -> 71.6 us  [closing(): pl.pallas_call(closing_kernel, out_shape=(jax.ShapeDtypeStruct((chips, 2,...]
  transfers between devices with their start and end apart: 9 -> 9, of which waited for: 0 -> 0; matrix products, arithmetic and copies ran while one was open for 3% -> 3% of each run, Pallas kernels for 89% -> 85%
where the time goes in v10:
time: 774 us; the launch traced here: 762 us
  Pallas kernels  700 us (90%)
  local copies, waits for them, and re-layouts  22.9 us (3%)
  between operations  15.5 us (2%)
  other arithmetic  11.9 us (2%)
  starting transfers between devices  9.66 us (1%)
    pallas_call x2, Pallas kernels, expert_pass(): pl.pallas_call(functools.partial(expert_kernel, by_block), grid=(devices,...  273 us
    pallas_call x2, Pallas kernels, attend(): pl.pallas_call(functools.partial(attend_kernel, scale), grid=(micros, 2),...  134 us
    pallas_call x1, Pallas kernels, attend_back(): pl.pallas_call(functools.partial(back_kernel, scale, micros), grid=(2, mi...  80.4 us
    pallas_call x1, Pallas kernels, closing(): pl.pallas_call(closing_kernel, out_shape=(jax.ShapeDtypeStruct((chips, 2,...  71.6 us
    pallas_call x1, Pallas kernels, opening(): pl.pallas_call(functools.partial(opening_kernel, micros), out_shape=(jax....  46.8 us
    pallas_call x1, Pallas kernels, weight_pass(): pl.pallas_call(weight_kernel, grid=(experts, width // block), out_shape=(...  38.2 us
    pallas_call x4, Pallas kernels, collect_rows(): pl.pallas_call(collect_kernel, grid=(blocks,), out_shape=jax.ShapeDtypeSt...  19.6 us
    pallas_call x4, Pallas kernels, spread_rows(): pl.pallas_call(spread_kernel, grid=(blocks,), out_shape=jax.ShapeDtypeStr...  16 us
  transfers between devices with their start and end apart: 9, of which 0 were waited for; matrix products, arithmetic and copies ran while one was open for 3% of the time, Pallas kernels for 85%

profile of v10, /device:TPU:0, one launch (start us, length us, event | category | flops | bytes accessed | tf_op | source)
XLA Modules:
  0.0 762.2 jit_solution(5772187883033486049)
XLA Ops:
  7.2 0.7 dynamic-slice_compare_fusion
  7.9 1.3 convert_bitcast_fusion.table_ref
  9.2 1.3 fusion.19
  10.5 1.4 find_places.2
  11.9 1.3 slice_bitcast_fusion.10
  13.2 2.7 slice_bitcast_fusion.4
  15.9 2.7 spread_rows.4
  18.5 46.8 %opening.1 = (bf16[2,256,1024]{2,1,0:T(8,128)(2,1)}, bf16[4,2,384,256]{3,2,1,0:T(8,128)(2,1)}, bf16[4,4,2,32,1024]{4,3,2,1,0:T(8,128)(2,1)}, s32[8,4,2,2,256]{4,...) custom-call(bf16[1,256,1024]{2,1,0:T(8,128)(2,1)} %get-tuple-element.183.x_ref.x_own_ref, ...), custom_call_target="tpu_custom_call" | custom-call | bytes 200000000 | tf_op jit(solution)/shard_map/opening/pallas_call | solution.py:241
  66.7 0.9 copy.32.seg_col_ref
  67.6 1.1 fusion.2
  69.3 5.9 position_bias.1.bias_ref
  75.2 2.6 spread_rows.5
  78.4 88.8 %attend.2 = (bf16[1,2,3,512,256]{4,3,2,1,0:T(8,128)(2,1)}, bf16[1,2,4,512,512]{4,3,2,1,0:T(8,128)(2,1)}, bf16[1,512,512]{2,1,0:T(8,128)(2,1)}, f32[1,256,1024]{2...) custom-call(bf16[1,512,1024]{2,1,0:T(8,128)(2,1)} %bitcast.164, ...), custom_call_target="tpu_custom_call" | custom-call | flops 2684354560 | bytes 100000000 | tf_op jit(solution)/shard_map/attend/pallas_call | solution.py:419
  167.6 1.3 dynamic-slice_bitcast_fusion.route_ref
  168.9 1.6 find_places.3
  170.5 10.8 %find_pairs.1 = bf16[2,8,2,4,40,16]{5,4,3,2,1,0:T(8,128)(2,1)} custom-call(s32[8,4,2,2,256]{4,3,2,1,0:T(2,128)} %get-tuple-element.86.route_ref), custom_call_target="tpu_custom_call" | custom-call | tf_op jit(solution)/shard_map/find_pairs/pallas_call | solution.py:989
  181.3 1.2 slice.116
  183.2 0.9 copy.33.seg_col_ref
  184.6 44.8 %attend.3 = (bf16[1,2,3,512,256]{4,3,2,1,0:T(8,128)(2,1)}, bf16[1,2,4,512,512]{4,3,2,1,0:T(8,128)(2,1)}, bf16[1,512,512]{2,1,0:T(8,128)(2,1)}, f32[1,256,1024]{2,1,0:T(8,128)}, bf16[1,256,1024]{2,1,0:T(8,128)(2,1)}) custom-call(bf16[1,512,1024]{2,1,0:T(8,128)(2,1)} %bitcast.187, f32[1,1024]{1,0:T(1,128)} %bitcast.177, bf16[3,1024,256]{2,1,0:T(8,128)(2,1)} %refs_3_.1, ...), custom_call_target="tpu_custom_call" | custom-call | flops 2684354560 | bytes 100000000 | tf_op jit(solution)/shard_map/attend/pallas_call | solution.py:419
  231.0 1.2 fusion.22
  232.2 5.3 spread_rows.6
  237.5 136.8 %expert_pass.2 = (bf16[8,2,160,1024]{3,2,1,0:T(8,128)(2,1)}, bf16[4,8,2,40,1024]{4,3,2,1,0:T(8,128)(2,1)}, bf16[8,2,160,1024]{3,2,1,0:T(8,128)(2,1)}, bf16[8,2,1...) custom-call(bf16[8,2,160,1024]{3,2,1,0:T(8,128)(2,1)} %bitcast.126, ...), custom_call_target="tpu_custom_call" | custom-call | bytes 490000000 | tf_op jit(solution)/shard_map/expert_pass/pallas_call | solution.py:1150
  374.3 5.6 collect_rows.4
  380.6 5.3 spread_rows.7
  386.0 136.6 %expert_pass.3 = (bf16[8,2,160,1024]{3,2,1,0:T(8,128)(2,1)}, bf16[8,2,4,40,1024]{4,3,2,1,0:T(8,128)(2,1)}, bf16[8,2,160,1024]{3,2,1,0:T(8,128)(2,1)}, bf16[8,2,1...) custom-call(bf16[8,2,160,1024]{3,2,1,0:T(8,128)(2,1)} %bitcast.125, ...), custom_call_target="tpu_custom_call" | custom-call | bytes 490000000 | tf_op jit(solution)/shard_map/expert_pass/pallas_call | solution.py:1150
  522.6 5.6 collect_rows.5
  528.3 5.3 all-to-all-start.1
  533.7 1.0 slice_bitcast_fusion
  534.7 38.2 %weight_pass.1 = (f32[2,16,1024]{2,1,0:T(8,128)}, f32[2,704,1024]{2,1,0:T(8,128)}, f32[2,704,1024]{2,1,0:T(8,128)}, f32[2,704,1024]{2,1,0:T(8,128)}) custom-call(bf16[8,2,160,1024]{3,2,1,0:T(8,128)(2,1)} %get-tuple-element.90.refs_0_, bf16[8,2,160,1024]{3,2,1,0:T(8,128)(2,1)} %get-tuple-element.91.refs_1_, ...), custom_call_target="tpu_custom_call" | custom-call | flops 22145925120 | bytes 59899904 | tf_op jit(solution)/shard_map/weight_pass/pallas_call | solution.py:1216
  573.0 0.9 reduce_sum.9
  574.0 80.4 %attend_back.1 = (bf16[256,1024]{1,0:T(8,128)(2,1)}, bf16[256,1024]{1,0:T(8,128)(2,1)}, bf16[8,2,512,256]{3,2,1,0:T(8,128)(2,1)}, f32[2,4,1024]{2,1,0:T(4,128)}, f32[1,1024]{1,0:T(1,128)}, /*index=5*/f32[1,1024]{1,0:T(1,128)}) custom-call(f32[1,1024]{1,0:T(1,128)} %bitcast.181, f32[1,1024]{1,0:T(1,128)} %bitcast.178, bf16[4,256,1024]{2,1,0:T(8,128)(2,1)} %bitcast.152, ...), custom_call_target="tpu_custom_call" | custom-call | flops 10737418240 | bytes 250000000 | tf_op jit(solution)/shard_map/attend_back/pallas_call | solution.py:668
  654.4 0.8 reshape.260
  655.6 3.6 all-to-all-start
  659.4 1.3 fusion.5.small_ref
  660.8 2.3 maximum_bitcast_fusion.1
  663.0 5.6 collect_rows.7
  668.6 71.6 %closing.1 = (bf16[4,2,512,256]{3,2,1,0:T(8,128)(2,1)}, f32[152,128]{1,0:T(8,128)}, bf16[256,1024]{1,0:T(8,128)(2,1)}) custom-call(bf16[4,2,2,512,256]{4,3,2,1,0:T(8,128)(2,1)} %bitcast.145, f32[152,128]{1,0:T(8,128)} %fusion.5.small_ref, bf16[4,256,1024]{2,1,0:T(8,128)(2,1)} %bitcast.133, f32[256,1024]{1,0:T(8,128)} %bitcast.163), custom_call_target="tpu_custom_call" | custom-call | bytes 160000000 | tf_op jit(solution)/shard_map/closing/pallas_call | solution.py:831
  740.3 0.8 slice.107
  741.1 0.8 slice.112
  741.9 1.1 slice.119
  743.1 1.9 slice.118
  745.1 0.6 reshape.267
  745.8 1.3 copy.34
  747.6 1.3 slice_bitcast_fusion.8
  748.9 1.1 copy-done.2
  750.0 2.7 collect_rows.6
  752.7 1.2 fusion
  753.9 1.1 maximum_bitcast_fusion
  (63 shorter events, 7.0 us)
Async XLA Ops:
  7.2 177.4 %all-gather.7.cloned.1.call-start = ((), (), s32[]{:S(2)}) async-start(), calls=%async_computation.6 | async-start | bytes 6553600 | tf_op jit(solution)/shard_map/all_gather | solution.py:1291
  15.9 49.6 %copy-start.9 = (bf16[1024]{0:T(1024)(128)(2,1)S(1)}, bf16[1024]{0:T(1024)(128)(2,1)}, u32[]{:S(2)}) copy-start(bf16[1024]{0:T(1024)(128)(2,1)} %param.20) | copy-start | bytes 6148
  15.9 50.2 %copy-start.10 = (bf16[1024]{0:T(1024)(128)(2,1)S(1)}, bf16[1024]{0:T(1024)(128)(2,1)}, u32[]{:S(2)}) copy-start(bf16[1024]{0:T(1024)(128)(2,1)} %param.21) | copy-start | bytes 6148
  15.9 50.8 %copy-start.7 = (s32[2,1,1024]{2,1,0:T(1,128)S(1)}, s32[2,1,1024]{2,1,0:T(1,128)}, u32[]{:S(2)}) copy-start(s32[2,1,1024]{2,1,0:T(1,128)} %param.15) | copy-start | bytes 24580
  15.9 51.7 %copy-start.8 = (f32[4,32]{1,0:T(4,128)S(1)}, f32[4,32]{1,0:T(4,128)}, u32[]{:S(2)}) copy-start(f32[4,32]{1,0:T(4,128)} %convert_bitcast_fusion.table_ref) | copy-start | bytes 1540
  65.4 164.1 %all-gather.5.cloned.1.call-start = ((), (), s32[]{:S(2)}) async-start(), calls=%async_computation.5 | async-start | bytes 2621440 | tf_op jit(solution)/shard_map/all_gather | solution.py:1291
  167.3 213.3 %all-gather.9.cloned.1.call-start = ((), (), s32[]{:S(2)}) async-start(), calls=%async_computation.9 | async-start | bytes 2621440 | tf_op jit(solution)/shard_map/all_gather | solution.py:1291
  184.6 45.8 %copy-start.6 = (s32[2,2,1024]{2,1,0:T(2,128)S(1)}, s32[2,2,1024]{2,1,0:T(2,128)}, u32[]{:S(2)}) copy-start(s32[2,2,1024]{2,1,0:T(2,128)} %find_places.3) | copy-start | bytes 49156
  184.6 46.4 %copy-start.3 = (bf16[2,8,2,4,40,16]{5,4,3,2,1,0:T(8,128)(2,1)S(1)}, bf16[2,8,2,4,40,16]{5,4,3,2,1,0:T(8,128)(2,1)}, u32[]{:S(2)}) copy-start(bf16[2,8,2,4,40,16]{5,4,3,2,1,0:T(8,128)(2,1)} %find_pairs.1) | copy-start | bytes 491524
  229.5 156.5 %all-gather.11.cloned.1.call-start = ((), (), s32[]{:S(2)}) async-start(), calls=%async_computation.10 | async-start | bytes 6553600 | tf_op jit(solution)/shard_map/all_gather | solution.py:1291
  230.1 292.6 %reduce-scatter.4.cloned.1.call-start = ((), (), s32[]{:S(2)}) async-start(), calls=%async_computation.7 | async-start | bytes 6553600 | tf_op jit(solution)/shard_map/reduce_scatter | solution.py:1294
  380.0 193.0 %reduce-scatter.6.cloned.1.call-start = ((), (), s32[]{:S(2)}) async-start(), calls=%async_computation.8 | async-start | bytes 2621440 | tf_op jit(solution)/shard_map/reduce_scatter | solution.py:1294
  380.6 193.4 %reduce-scatter.8.cloned.1.call-start = ((), (), s32[]{:S(2)}) async-start(), calls=%async_computation.11 | async-start | bytes 2621440 | tf_op jit(solution)/shard_map/reduce_scatter | solution.py:1294
  528.3 5.4 copy-start
  528.3 127.2 %all-to-all-start.1 = ((bf16[8,320,1024]{2,1,0:T(8,128)(2,1)}), bf16[8,320,1024]{2,1,0:T(8,128)(2,1)}, u32[]{:S(2)}, u32[]{:S(2)}) async-start(bf16[8,320,1024]{2,1,0:T(8,128)(2,1)} %bitcast.135), calls=%async_computation.4 | async-start | bytes 10485760 | tf_op jit(solution)/shard_map/all_to_all | solution.py:1288
  655.6 93.3 %all-to-all-start = ((bf16[8,80,1024]{2,1,0:T(8,128)(2,1)}), bf16[8,80,1024]{2,1,0:T(8,128)(2,1)S(1)}, u32[]{:S(2)}, u32[]{:S(2)}) async-start(bf16[8,80,1024]{2,1,0:T(8,128)(2,1)} %bitcast.32), calls=%async_computation.3 | async-start | bytes 2621440 | tf_op jit(solution)/shard_map/all_to_all | solution.py:1288
  740.3 2.8 copy-start.1
  743.1 9.7 %copy-start.4 = (f32[1,256,1024]{2,1,0:T(8,128)S(1)}, f32[1,256,1024]{2,1,0:T(8,128)}, u32[]{:S(2)}) copy-start(f32[1,256,1024]{2,1,0:T(8,128)} %get-tuple-element.81) | copy-start | bytes 3145732
  747.1 6.9 copy-start.5
  748.9 1.1 copy-start.2
Sparse Core Ops, SparseCore 0:
  65.5 111.5 all-gather.6
  178.7 50.3 all-gather.4
  230.6 46.0 all-gather.8
  278.1 96.7 all-gather.10
  380.1 92.9 reduce-scatter.3
  475.8 44.3 reduce-scatter.5
  528.4 43.7 reduce-scatter.7

commit v11 on v10

--- a/solution.py
+++ b/solution.py
@@ -111,14 +111,14 @@
 
 
 def opening_kernel(
-    micros, x_ref, qkv_ref, out_ref, routes_ref, table_ref, dy_ref, *refs,
+    micros, x_ref, qkv_ref, out_ref, routes_ref, table_ref, *refs,
 ):
     x_all, refs = refs[:micros], refs[micros:]
     (
-        qkv_all, out_all, routes_all, table_all, dy_all,
+        qkv_all, out_all, routes_all, table_all,
         x_send, x_recv, qkv_send, qkv_recv, out_send, out_recv, qkv_on_send, qkv_on_recv,
         out_on_send, out_on_recv, routes_send, routes_recv, routes_on_send, routes_on_recv,
-        table_send, table_recv, dy_send, dy_recv, own_sem,
+        table_send, table_recv, own_sem,
     ) = refs
     devices, qkv_rows = qkv_all.shape[0] * 2, qkv_all.shape[2]
     blocks, out_rows = out_all.shape[0], out_all.shape[3]
@@ -137,11 +137,10 @@
             out_ref.at[pl.ds(me * out_rows, out_rows)], out_all.at[line, chip, core], own_sem.at[0]
         ),
         pltpu.make_async_copy(routes_ref, routes_all.at[me, line], own_sem.at[1]),
-        pltpu.make_async_copy(dy_ref.at[me], dy_all.at[me], own_sem.at[2]),
     ]
     for micro in range(micros):
         own.append(
-            pltpu.make_async_copy(x_ref.at[micro], x_all[micro].at[mine], own_sem.at[3 + micro])
+            pltpu.make_async_copy(x_ref.at[micro], x_all[micro].at[mine], own_sem.at[2 + micro])
         )
     for copy in own:
         copy.start()
@@ -175,11 +174,6 @@
             )
             copy.start()
             rest.append(copy)
-    for s in range(1, devices):
-        peer = partner_of(me, s, devices)
-        copy = remote(dy_ref.at[peer], dy_all.at[me], dy_send.at[s], dy_recv.at[s], (peer, line))
-        copy.start()
-        rest.append(copy)
     first_qkv.wait_recv()
     qkv_on, out_on = [], []
     for s in range(2, devices, 2):
@@ -234,7 +228,7 @@
         copy.wait()
 
 
-def opening(x, qkv, out, routes, table, dy, devices, blocks, members):
+def opening(x, qkv, out, routes, table, devices, blocks, members):
     micros, shard_len, width = x.shape
     dma = pltpu.SemaphoreType.DMA
     pair = (devices // 2, 2)
@@ -246,36 +240,69 @@
             jax.ShapeDtypeStruct((blocks,) + pair + (out.shape[0] // devices, width), BF16),
             jax.ShapeDtypeStruct((devices, blocks) + routes.shape, jnp.int32),
             jax.ShapeDtypeStruct(table.shape, table.dtype),
-            jax.ShapeDtypeStruct(dy.shape, BF16),
-        ),
-        in_specs=[any_space()] * 6,
-        out_specs=(any_space(),) * (5 + micros),
+        ),
+        in_specs=[any_space()] * 5,
+        out_specs=(any_space(),) * (4 + micros),
         scratch_shapes=[
             dma((micros, members)), dma((micros, members)), dma, dma, dma((blocks,)), dma((blocks,)),
             dma((devices,)), dma((devices,)), dma((devices,)), dma((devices,)), dma((blocks,)),
-            dma((blocks,)), dma((devices,)), dma((devices,)), dma, dma, dma((devices,)),
-            dma((devices,)), dma((3 + micros,)),
+            dma((blocks,)), dma((devices,)), dma((devices,)), dma, dma, dma((2 + micros,)),
         ],
         compiler_params=pltpu.CompilerParams(collective_id=1, has_side_effects=True),
         cost_estimate=pl.CostEstimate(flops=0, bytes_accessed=200000000, transcendentals=0),
         name="opening",
-    )(x, qkv, out, routes, table, dy)
+    )(x, qkv, out, routes, table)
 
 
 def unit_rows(x):
     x = x.astype(F32)
     return x * lax.rsqrt(jnp.mean(x * x, axis=-1, keepdims=True) + EPSILON)
+
+
+def places(route_ref, index, cap, experts):
+    shard_len = route_ref.shape[-1]
+    row = lax.broadcasted_iota(jnp.int32, (shard_len, shard_len), 0)
+    col = lax.broadcasted_iota(jnp.int32, (shard_len, shard_len), 1)
+    earlier = jnp.where(row < col, 1.0, 0.0).astype(BF16)
+    ids = lax.broadcasted_iota(jnp.int32, (experts, shard_len), 0)
+    pair = [route_ref[index + (slice(k, k + 1),)] for k in range(2)]
+    chosen = (ids == pair[0]) | (ids == pair[1])
+    before = mm(jnp.where(chosen, 1.0, 0.0).astype(BF16), earlier)
+    found = []
+    for route in pair:
+        position = jnp.sum(jnp.where(ids == route, before, 0.0), axis=0, keepdims=True)
+        found.append(jnp.where(route >= 0, route * cap + position.astype(jnp.int32), -1))
+    return pair, found
+
+
+def fill_pairs(route_ref, pair_ref, source, micro, me):
+    _, _, here, blocks, cap, experts = pair_ref.shape
+    spots = lax.broadcasted_iota(jnp.int32, (cap, route_ref.shape[-1]), 0)
+    ids = lax.broadcasted_iota(jnp.int32, (cap, experts), 1)
+    for block in range(blocks):
+        pair, place = places(route_ref, (source, block, micro), cap, experts)
+        for e in range(here):
+            expert = me * here + e
+            other = jnp.full((cap, 1), -1, jnp.int32)
+            for k in range(2):
+                hit = spots + expert * cap == place[k]
+                found = jnp.max(jnp.where(hit, pair[1 - k], -1), axis=1, keepdims=True)
+                other = jnp.maximum(other, found)
+            sign = jnp.where(ids == expert, 1.0, 0.0) - jnp.where(ids == other, 1.0, 0.0)
+            pair_ref[micro, source, e, block] = jnp.where(other >= 0, sign, 0.0).astype(BF16)
 
 
 def attend_kernel(
     scale, x_ref, gain_ref, own_ref, other_ref, bias_ref, seg_row_ref, seg_col_ref,
     out_ref, x_own_ref, moe_gain_ref, *refs,
 ):
-    riding = len(refs) > 10
-    if riding:
-        sent_ref, next_ref, arrived_ref, next_all = *refs[:2], *refs[7:9]
-        ride_send, ride_recv, next_send, next_recv, ride_own = refs[-5:]
-        refs = refs[2:7] + refs[9:-5]
+    sent_ref, refs = refs[0], refs[1:]
+    pairing = len(refs) > 14
+    if pairing:
+        routes_ref, pair_ref = refs[0], refs[7]
+        refs = refs[1:7] + refs[8:]
+    arrived_ref, ride_send, ride_recv, ride_own = refs[5], *refs[-3:]
+    refs = refs[:5] + refs[6:-3]
     qkv_ref, prob_ref, heads_ref, h1_ref, xn2_ref, xn_ref, part_ref, got_ref, send_sem, recv_sem = refs
     micros, members, shard_len, both = got_ref.shape
     cols = both // 2
@@ -303,29 +330,17 @@
         )
 
     def stay():
-        return [
-            pltpu.make_async_copy(sent_ref.at[me], arrived_ref.at[me], ride_own.at[0]),
-            pltpu.make_async_copy(next_ref, next_all.at[mine], ride_own.at[1]),
-        ]
-
-    def pair(s):
-        peer = lax.rem(mine + s, members)
-        return remote(
-            next_ref, next_all.at[mine], next_send.at[s], next_recv.at[s], (me, base + peer)
-        )
+        return pltpu.make_async_copy(sent_ref.at[me], arrived_ref.at[me], ride_own)
 
     @pl.when((micro == 0) & (group == 0))
     def _():
         peers = [(me, base + lax.rem(mine + s, members)) for s in range(1, members)]
-        if riding:
-            devices = sent_ref.shape[0]
-            peers += [(partner_of(me, s, devices), line) for s in range(1, devices)]
+        devices = sent_ref.shape[0]
+        peers += [(partner_of(me, s, devices), line) for s in range(1, devices)]
         greet(peers)
-        if riding:
-            for copy in stay():
-                copy.start()
-            for s in range(1, devices):
-                ride(s).start()
+        stay().start()
+        for s in range(1, devices):
+            ride(s).start()
 
     @pl.when(group == 0)
     def _():
@@ -371,8 +386,6 @@
         got_ref[micro, mine] = part_ref[micro, mine]
         for s in range(1, members):
             swap(micro, s).start()
-            if riding:
-                pair(s).start()
 
     @pl.when((micro == micros - 1) & (group == 1))
     def _():
@@ -389,29 +402,34 @@
         for m in range(micros):
             for s in range(1, members):
                 swap(m, s).wait_send()
-        if riding:
-            for copy in stay():
-                copy.wait()
-            for s in range(1, members):
-                pair(s).wait()
-            for s in range(1, sent_ref.shape[0]):
-                ride(s).wait()
+        if pairing:
+
+            @pl.loop(0, routes_ref.shape[0])
+            def _(source):
+                for m in range(pair_ref.shape[0]):
+                    fill_pairs(routes_ref, pair_ref, source, m, me)
+
+        stay().wait()
+        for s in range(1, sent_ref.shape[0]):
+            ride(s).wait()
 
 
 def attend(
     x, gain, own_weight, other_weight, bias, seg, out_weight, x_own, moe_gain, scale, members, identity,
-    rider=None,
+    rider, routes=None, pair_shape=None,
 ):
     micros, half, width = x.shape
     cols = own_weight.shape[2]
     heads = bias.shape[0] // 2
     shard_len = half // members
-    riders, ride_shapes, ride_sems = [], (), []
-    if rider is not None:
-        riders = list(rider)
-        ride_shapes = (rider[0].shape, (members, shard_len, width))
-        ride_sems = [pltpu.SemaphoreType.DMA((rider[0].shape[0],))] * 2
-        ride_sems += [pltpu.SemaphoreType.DMA((members,))] * 2 + [pltpu.SemaphoreType.DMA((2,))]
+    riders, ride_specs = [rider], [any_space()]
+    ride_out, ride_out_specs = [jax.ShapeDtypeStruct(rider.shape, BF16)], [any_space()]
+    if routes is not None:
+        riders.append(routes)
+        ride_specs.append(pl.BlockSpec(memory_space=pltpu.VMEM))
+        ride_out.append(jax.ShapeDtypeStruct(pair_shape, BF16))
+        ride_out_specs.append(pl.BlockSpec(memory_space=pltpu.VMEM))
+    ride_sems = [pltpu.SemaphoreType.DMA((rider.shape[0],))] * 2 + [pltpu.SemaphoreType.DMA]
 
     def once(shape):
         return pl.BlockSpec(shape, lambda m, p: (0,) * len(shape), pipeline_mode=pl.Buffered(1))
@@ -426,7 +444,7 @@
             jax.ShapeDtypeStruct((micros, shard_len, width), F32),
             jax.ShapeDtypeStruct((micros, shard_len, width), BF16),
         )
-        + tuple(jax.ShapeDtypeStruct(shape, BF16) for shape in ride_shapes),
+        + tuple(ride_out),
         in_specs=[
             pl.BlockSpec((1, half, width), lambda m, p: (m, 0, 0)),
             once((1, width)),
@@ -439,7 +457,7 @@
             once(x_own.shape),
             once((1, width)),
         ]
-        + [any_space()] * len(riders),
+        + ride_specs,
         out_specs=(
             pl.BlockSpec((1, 1, 3, half, cols), lambda m, p: (m, p, 0, 0, 0)),
             pl.BlockSpec((1, 1, heads, half, half), lambda m, p: (m, p, 0, 0, 0)),
@@ -447,7 +465,7 @@
             pl.BlockSpec((micros, shard_len, width), lambda m, p: (0, 0, 0)),
             pl.BlockSpec((micros, shard_len, width), lambda m, p: (0, 0, 0)),
         )
-        + (any_space(),) * len(riders),
+        + tuple(ride_out_specs),
         scratch_shapes=[
             pltpu.VMEM((half, width), BF16),
             pltpu.VMEM((micros, members, shard_len, 2 * cols), BF16),
@@ -725,10 +743,11 @@
     along = [lax.rem(line + s, blocks) for s in range(1, blocks)]
     across = lax.rem(line + blocks // 2, blocks)
     greet([(partner_of(me, s, devices), line) for s in range(1, devices)] + [(me, z) for z in along])
-    share = y_ref.shape[1] // 2
+    share = 3 * y_ref.shape[1] // 4
+    turns = (pl.ds(0, share), pl.ds(share, y_ref.shape[1] - share))
 
     def y_copies(turn):
-        rows = pl.ds(turn * share, share)
+        rows = turns[turn]
         return [
             remote(
                 y_ref.at[z, rows], y_got.at[line, rows], y_send.at[turn, s], y_recv.at[turn, s],
@@ -926,22 +945,6 @@
     )(rows, place)
 
 
-def places(route_ref, index, cap, experts):
-    shard_len = route_ref.shape[-1]
-    row = lax.broadcasted_iota(jnp.int32, (shard_len, shard_len), 0)
-    col = lax.broadcasted_iota(jnp.int32, (shard_len, shard_len), 1)
-    earlier = jnp.where(row < col, 1.0, 0.0).astype(BF16)
-    ids = lax.broadcasted_iota(jnp.int32, (experts, shard_len), 0)
-    pair = [route_ref[index + (slice(k, k + 1),)] for k in range(2)]
-    chosen = (ids == pair[0]) | (ids == pair[1])
-    before = mm(jnp.where(chosen, 1.0, 0.0).astype(BF16), earlier)
-    found = []
-    for route in pair:
-        position = jnp.sum(jnp.where(ids == route, before, 0.0), axis=0, keepdims=True)
-        found.append(jnp.where(route >= 0, route * cap + position.astype(jnp.int32), -1))
-    return pair, found
-
-
 def place_kernel(cap, experts, route_ref, place_ref):
     blocks, micros, _, shard_len = route_ref.shape
     for block in range(blocks):
@@ -962,38 +965,6 @@
         out_specs=vmem,
         compiler_params=pltpu.CompilerParams(vmem_limit_bytes=VMEM_LIMIT),
         name="find_places",
-    )(route)
-
-
-def pair_kernel(route_ref, pair_ref):
-    _, _, here, blocks, cap, experts = pair_ref.shape
-    shard_len = route_ref.shape[-1]
-    me = lax.axis_index("expert")
-    spots = lax.broadcasted_iota(jnp.int32, (cap, shard_len), 0)
-    ids = lax.broadcasted_iota(jnp.int32, (cap, experts), 1)
-    for block in range(blocks):
-        pair, place = places(route_ref, (0, block, 0), cap, experts)
-        for e in range(here):
-            expert = me * here + e
-            other = jnp.full((cap, 1), -1, jnp.int32)
-            for k in range(2):
-                hit = spots + expert * cap == place[k]
-                found = jnp.max(jnp.where(hit, pair[1 - k], -1), axis=1, keepdims=True)
-                other = jnp.maximum(other, found)
-            sign = jnp.where(ids == expert, 1.0, 0.0) - jnp.where(ids == other, 1.0, 0.0)
-            pair_ref[0, 0, e, block] = jnp.where(other >= 0, sign, 0.0).astype(BF16)
-
-
-def find_pairs(route, experts, here, cap):
-    devices, blocks, micros, _, shard_len = route.shape
-    return pl.pallas_call(
-        pair_kernel,
-        grid=(micros, devices),
-        out_shape=jax.ShapeDtypeStruct((micros, devices, here, blocks, cap, experts), BF16),
-        in_specs=[pl.BlockSpec((1, blocks, 1, 2, shard_len), lambda m, s: (s, 0, m, 0, 0))],
-        out_specs=pl.BlockSpec((1, 1, here, blocks, cap, experts), lambda m, s: (m, s, 0, 0, 0, 0)),
-        compiler_params=pltpu.CompilerParams(vmem_limit_bytes=VMEM_LIMIT),
-        name="find_pairs",
     )(route)
 
 
@@ -1029,7 +1000,7 @@
     def y_copies(s):
         source = partner_of(me, s, devices)
         slot = lax.rem(s, 2)
-        if not by_block:
+        if not by_block[1]:
             return [
                 pltpu.make_async_copy(stage_ref.at[slot], y_ref.at[source], stage_sem.at[slot, 0])
             ]
@@ -1045,7 +1016,8 @@
         slot = lax.rem(s, 2)
         for e in range(experts):
             x = got_ref[s, e]
-            dy = dy_ref[:, source, e].reshape(cap, width).astype(F32)
+            dy = dy_ref[:, source, e] if by_block[0] else dy_ref[source, e]
+            dy = dy.reshape(cap, width).astype(F32)
             pair = pair_ref[source, e].astype(F32)
             margin = jnp.sum(mm_nt(x, wr_ref[...]) * pair, axis=-1, keepdims=True)
             own_gate = 1.0 / (1.0 + jnp.exp(-margin))
@@ -1130,7 +1102,8 @@
 
 
 def expert_pass(sent, dy, pair, wr, wg, wu, wd, by_block, identity):
-    blocks, _, _, share, _ = dy.shape
+    share = dy.shape[3]
+    blocks = sent.shape[2] // share
     devices, experts, cap, width = sent.shape
     hidden = wg.shape[1]
     choices = wr.shape[0]
@@ -1145,7 +1118,7 @@
         return jax.ShapeDtypeStruct((devices, experts, cap, cols), BF16)
 
     y_shape = (blocks, devices, experts, share, width)
-    if not by_block:
+    if not by_block[1]:
         y_shape = (devices, experts, blocks, share, width)
     return pl.pallas_call(
         functools.partial(expert_kernel, by_block),
@@ -1301,15 +1274,11 @@
     def spread(rows, micro, placed):
         return spread_rows(rows, micro, placed, expert_count, capacity, shard_len)
 
-    dy_sent = [
-        spread(cotangent[:, 0], micro, own_place[micro]).reshape(devices, -1, width)
-        for micro in range(micro_count)
-    ]
-    x_first, other_qkv, all_out, all_routes, other_table, dy_first = opening(
-        x_in[0], qkv_weight.reshape(3 * width, head_cols), out_weight,
-        live_routes, bias_table.T.astype(F32), dy_sent[0], devices, blocks, members,
+    *x_all, other_qkv, all_out, all_routes, other_table = opening(
+        x_in[:, 0], qkv_weight.reshape(3 * width, head_cols), out_weight,
+        live_routes, bias_table.T.astype(F32), devices, blocks, members,
     )
-    x_half = [x_first.reshape(1, half, width)]
+    x_half = [x.reshape(1, half, width) for x in x_all]
     other_qkv = other_qkv.reshape(qkv_weight.shape)
     all_out = all_out.reshape(blocks, head_cols, width)
 
@@ -1327,7 +1296,7 @@
 
     def experts(micro, kept, *behind):
         sent = spread(kept["xn2_all"][None], 0, place[micro]).reshape(token_shape)
-        kept["by_block"] = micro + 1 < micro_count
+        kept["by_block"] = (micro > 0, micro + 1 < micro_count)
         back, kept["y"], x, g, hid, dga, dup, dlog = expert_pass(
             after(sent, *behind), kept["dy"], pairs[micro], router_rows, gate_rows, up_rows,
             down_weight, kept["by_block"], 4 + micro,
@@ -1339,34 +1308,29 @@
         kept["dx_back"] = back.reshape(place_shape)
         kept["dx_part"] = collect_rows(kept["dx_back"], place[micro], shard_len)
         kept["dxn2"] = scatter(kept["dx_part"])
-        if kept["by_block"]:
+        if kept["by_block"][1]:
             parts = after(kept["y"], kept["dx_part"]).reshape(blocks, -1, width)
             kept["y_own"] = scatter(parts).reshape(devices, -1, width)
 
-    states[0]["dy"] = gather_dy(dy_first)
-    behind = ()
-    for micro in range(micro_count):
-        state = states[micro]
-        rider = None
-        if micro + 1 < micro_count:
-            rider = (dy_sent[micro + 1], x_in[micro + 1, 0])
-        qkv, prob, heads, h1, xn2, *rode = attend(
-            after(x_half[micro], *behind), attn_gain_f, qkv_weight, other_qkv, bias,
-            seg_half[micro : micro + 1], all_out, x_in[micro], moe_gain_f, scale, members, 10 + micro,
-            rider,
-        )
+    first, last = states
+    first["dy_all"] = gather(after(cotangent[0, 0], all_out))
+    pair_shape = (micro_count, devices, experts_here, blocks, capacity, expert_count)
+    for micro, state in enumerate(states):
+        inputs = (
+            attn_gain_f, qkv_weight, other_qkv, bias, seg_half[micro : micro + 1], all_out,
+            x_in[micro], moe_gain_f, scale, members, 10 + micro,
+        )
+        if micro == 0:
+            sent = spread(cotangent[:, 0], 1, own_place[1]).reshape(devices, -1, width)
+            qkv, prob, heads, h1, xn2, last["dy_here"] = attend(x_half[0], *inputs, sent)
+        else:
+            sent = spread(after(first["dy_all"], xn2)[None], 0, place[0]).reshape(token_shape)
+            qkv, prob, heads, h1, xn2, first["dy"], pairs = attend(
+                after(x_half[1], xn2), *inputs, sent, all_routes, pair_shape
+            )
         state.update(qkv=qkv[0], prob=prob[0], heads=heads[0], h1=h1[0], xn2=xn2[0])
-        if micro + 1 < micro_count:
-            states[micro + 1]["dy_here"] = rode[0]
-            x_half.append(rode[1].reshape(1, half, width))
-        if micro == 0:
-            pairs = find_pairs(after(all_routes, xn2), expert_count, experts_here, capacity)
-            pairs = pairs.reshape(
-                micro_count, devices, experts_here, blocks * capacity, expert_count
-            )
-            place = after(place, xn2)
-            seg_half = seg_half + jnp.where(pairs[0, 0, 0, 0, 0] > 2, 1, 0)
-        behind = (xn2, states[0]["dy"], place)
+    first["dy"] = first["dy"].reshape(devices, experts_here, blocks, capacity, width)
+    pairs = pairs.reshape(micro_count, devices, experts_here, blocks * capacity, expert_count)
     behind = ()
     for micro in range(micro_count):
         state = states[micro]
@@ -1382,7 +1346,6 @@
     kept = [state["weights"] for state in states]
     kept[-1] = tuple(after(list(kept[-1]), last_part))
     dwr, dwg, dwu, dwd = weight_pass(kept)
-    last = states[-1]
     last["y_rows"] = exchange(after(last["y"], last_part).reshape(flat_shape)).reshape(place_shape)
     *x_grads, grads, lines, moe_gain_grad, attn_gain_grad = attend_back(
         moe_gain_f, attn_gain_f, all_out, qkv_weight, other_qkv,

time: 774 us -> 734 us (0.948)
  Pallas kernels: 700 us -> 666 us
    pallas_call x2, Pallas kernels: 134 us -> 103 us  [attend(): pl.pallas_call(functools.partial(attend_kernel, scale), grid=(micros, 2),...]
    pallas_call x1 -> x0, Pallas kernels: 10.8 us -> none  [find_pairs(): pl.pallas_call(pair_kernel, grid=(micros, devices), out_shape=jax.ShapeDt...]
where the time goes in v11:
time: 734 us; the launch traced here: 726 us
  Pallas kernels  666 us (91%)
  local copies, waits for them, and re-layouts  21.5 us (3%)
  between operations  14.8 us (2%)
  other arithmetic  11.3 us (2%)
  starting transfers between devices  9.53 us (1%)
    pallas_call x2, Pallas kernels, expert_pass(): pl.pallas_call(functools.partial(expert_kernel, by_block), grid=(devices,...  274 us
    pallas_call x2, Pallas kernels, attend(): pl.pallas_call(functools.partial(attend_kernel, scale), grid=(micros, 2),...  103 us
    pallas_call x1, Pallas kernels, attend_back(): pl.pallas_call(functools.partial(back_kernel, scale, micros), grid=(2, mi...  80.1 us
    pallas_call x1, Pallas kernels, closing(): pl.pallas_call(closing_kernel, out_shape=(jax.ShapeDtypeStruct((chips, 2,...  78.5 us
    pallas_call x1, Pallas kernels, opening(): pl.pallas_call(functools.partial(opening_kernel, micros), out_shape=(jax....  45.3 us
    pallas_call x1, Pallas kernels, weight_pass(): pl.pallas_call(weight_kernel, grid=(experts, width // block), out_shape=(...  38.6 us
    pallas_call x4, Pallas kernels, collect_rows(): pl.pallas_call(collect_kernel, grid=(blocks,), out_shape=jax.ShapeDtypeSt...  19.6 us
    pallas_call x4, Pallas kernels, spread_rows(): pl.pallas_call(spread_kernel, grid=(blocks,), out_shape=jax.ShapeDtypeStr...  18.8 us
  transfers between devices with their start and end apart: 9, of which 0 were waited for; matrix products, arithmetic and copies ran while one was open for 3% of the time, Pallas kernels for 85%

profile of v11, /device:TPU:0, one launch (start us, length us, event | category | flops | bytes accessed | tf_op | source)
XLA Modules:
  0.0 726.0 jit_solution(13886159122156894234)
XLA Ops:
  7.2 0.7 dynamic-slice_compare_fusion
  7.9 1.3 convert_bitcast_fusion.table_ref
  9.2 1.3 fusion.19
  10.5 3.2 slice_bitcast_fusion
  13.7 45.3 %opening.1 = (bf16[2,256,1024]{2,1,0:T(8,128)(2,1)}, bf16[2,256,1024]{2,1,0:T(8,128)(2,1)}, bf16[4,2,384,256]{3,2,1,0:T(8,128)(2,1)}, bf16[4,4,2,32,1024]{4,3,2,...) custom-call(bf16[2,256,1024]{2,1,0:T(8,128)(2,1)} %bitcast.145, bf16[3072,256]{1,0:T(8,128)(2,1)} %bitcast.125, ...), custom_call_target="tpu_custom_call" | custom-call | bytes 200000000 | tf_op jit(solution)/shard_map/opening/pallas_call | solution.py:235
  59.1 0.6 reshape.254
  60.3 1.4 find_places.2
  61.8 0.9 copy.32.seg_col_ref
  62.7 1.1 fusion.2
  63.8 0.7 reshape.223.line_ref
  64.4 5.9 position_bias.1.bias_ref
  70.4 1.3 slice_bitcast_fusion.10
  71.7 2.6 spread_rows.4
  74.3 36.6 %attend.2 = (bf16[1,2,3,512,256]{4,3,2,1,0:T(8,128)(2,1)}, bf16[1,2,4,512,512]{4,3,2,1,0:T(8,128)(2,1)}, bf16[1,512,512]{2,1,0:T(8,128)(2,1)}, f32[1,256,1024]{2...) custom-call(bf16[1,512,1024]{2,1,0:T(8,128)(2,1)} %bitcast.156, f32[1,1024]{1,0:T(1,128)} %bitcast.174, ...), custom_call_target="tpu_custom_call" | custom-call | flops 2684354560 | bytes 100000000 | tf_op jit(solution)/shard_map/attend/pallas_call | solution.py:437
  111.2 0.9 copy.33.seg_col_ref
  112.0 1.3 dynamic-slice_bitcast_fusion.route_ref
  113.4 1.6 find_places.3
  115.0 1.3 slice_bitcast_fusion.6
  116.3 5.4 spread_rows.6
  121.7 66.2 %attend.3 = (bf16[1,2,3,512,256]{4,3,2,1,0:T(8,128)(2,1)}, bf16[1,2,4,512,512]{4,3,2,1,0:T(8,128)(2,1)}, bf16[1,512,512]{2,1,0:T(8,128)(2,1)}, f32[1,256,1024]{2...) custom-call(bf16[1,512,1024]{2,1,0:T(8,128)(2,1)} %bitcast.158, ...), custom_call_target="tpu_custom_call" | custom-call | flops 2684354560 | bytes 100000000 | tf_op jit(solution)/shard_map/attend/pallas_call | solution.py:437
  188.8 5.4 spread_rows.5
  194.2 1.2 fusion.22
  195.4 137.0 %expert_pass.2 = (bf16[8,2,160,1024]{3,2,1,0:T(8,128)(2,1)}, bf16[4,8,2,40,1024]{4,3,2,1,0:T(8,128)(2,1)}, bf16[8,2,160,1024]{3,2,1,0:T(8,128)(2,1)}, bf16[8,2,1...) custom-call(bf16[8,2,160,1024]{3,2,1,0:T(8,128)(2,1)} %bitcast.124, ...), custom_call_target="tpu_custom_call" | custom-call | bytes 490000000 | tf_op jit(solution)/shard_map/expert_pass/pallas_call | solution.py:1123
  332.4 5.6 collect_rows.4
  338.7 5.3 spread_rows.7
  344.0 136.6 %expert_pass.3 = (bf16[8,2,160,1024]{3,2,1,0:T(8,128)(2,1)}, bf16[8,2,4,40,1024]{4,3,2,1,0:T(8,128)(2,1)}, bf16[8,2,160,1024]{3,2,1,0:T(8,128)(2,1)}, bf16[8,2,1...) custom-call(bf16[8,2,160,1024]{3,2,1,0:T(8,128)(2,1)} %bitcast.123, ...), custom_call_target="tpu_custom_call" | custom-call | bytes 490000000 | tf_op jit(solution)/shard_map/expert_pass/pallas_call | solution.py:1123
  480.6 5.6 collect_rows.5
  486.3 5.2 all-to-all-start.1
  491.5 38.6 %weight_pass.1 = (f32[2,16,1024]{2,1,0:T(8,128)}, f32[2,704,1024]{2,1,0:T(8,128)}, f32[2,704,1024]{2,1,0:T(8,128)}, f32[2,704,1024]{2,1,0:T(8,128)}) custom-call(bf16[8,2,160,1024]{3,2,1,0:T(8,128)(2,1)} %get-tuple-element.94.refs_0_, bf16[8,2,160,1024]{3,2,1,0:T(8,128)(2,1)} %get-tuple-element.95.refs_1_, ...), custom_call_target="tpu_custom_call" | custom-call | flops 22145925120 | bytes 59899904 | tf_op jit(solution)/shard_map/weight_pass/pallas_call | solution.py:1189
  530.2 0.9 reduce_sum.9
  531.2 80.1 %attend_back.1 = (bf16[256,1024]{1,0:T(8,128)(2,1)}, bf16[256,1024]{1,0:T(8,128)(2,1)}, bf16[8,2,512,256]{3,2,1,0:T(8,128)(2,1)}, f32[2,4,1024]{2,1,0:T(4,128)}, f32[1,1024]{1,0:T(1,128)}, /*index=5*/f32[1,1024]{1,0:T(1,128)}) custom-call(f32[1,1024]{1,0:T(1,128)} %bitcast.179, f32[1,1024]{1,0:T(1,128)} %bitcast.176, bf16[4,256,1024]{2,1,0:T(8,128)(2,1)} %bitcast.132, ...), custom_call_target="tpu_custom_call" | custom-call | flops 10737418240 | bytes 250000000 | tf_op jit(solution)/shard_map/attend_back/pallas_call | solution.py:686
  611.3 0.8 reshape.246
  612.5 3.6 all-to-all-start
  616.3 1.3 fusion.5.small_ref
  617.6 2.3 maximum_bitcast_fusion.1
  619.9 5.6 collect_rows.7
  625.5 78.5 %closing.1 = (bf16[4,2,512,256]{3,2,1,0:T(8,128)(2,1)}, f32[152,128]{1,0:T(8,128)}, bf16[256,1024]{1,0:T(8,128)(2,1)}) custom-call(bf16[4,2,2,512,256]{4,3,2,1,0:T(8,128)(2,1)} %bitcast.147, f32[152,128]{1,0:T(8,128)} %fusion.5.small_ref, bf16[4,256,1024]{2,1,0:T(8,128)(2,1)} %bitcast.133, f32[256,1024]{1,0:T(8,128)} %bitcast.163), custom_call_target="tpu_custom_call" | custom-call | bytes 160000000 | tf_op jit(solution)/shard_map/closing/pallas_call | solution.py:850
  704.0 0.8 slice.102
  704.9 0.8 slice.107
  705.7 1.1 slice.113
  706.8 1.9 slice.112
  708.9 0.6 reshape.253
  709.5 1.3 copy.34
  711.4 1.3 slice_bitcast_fusion.8
  712.7 1.1 copy-done.1
  713.8 2.7 collect_rows.6
  716.5 1.2 fusion
  717.7 1.1 maximum_bitcast_fusion
  (57 shorter events, 3.9 us)
Async XLA Ops:
  7.2 109.1 %all-gather.7.cloned.1.call-start = ((), (), s32[]{:S(2)}) async-start(), calls=%async_computation.6 | async-start | bytes 2621440 | tf_op jit(solution)/shard_map/all_gather | solution.py:1264
  10.5 48.7 %copy-start.9 = (bf16[1024]{0:T(1024)(128)(2,1)S(1)}, bf16[1024]{0:T(1024)(128)(2,1)}, u32[]{:S(2)}) copy-start(bf16[1024]{0:T(1024)(128)(2,1)} %param.20) | copy-start | bytes 6148
  10.5 49.3 %copy-start.10 = (bf16[1024]{0:T(1024)(128)(2,1)S(1)}, bf16[1024]{0:T(1024)(128)(2,1)}, u32[]{:S(2)}) copy-start(bf16[1024]{0:T(1024)(128)(2,1)} %param.21) | copy-start | bytes 6148
  10.5 51.3 %copy-start.8 = (s32[2,1,1024]{2,1,0:T(1,128)S(1)}, s32[2,1,1024]{2,1,0:T(1,128)}, u32[]{:S(2)}) copy-start(s32[2,1,1024]{2,1,0:T(1,128)} %param.15) | copy-start | bytes 24580
  10.5 52.2 %copy-start.7 = (f32[4,32]{1,0:T(4,128)S(1)}, f32[4,32]{1,0:T(4,128)}, u32[]{:S(2)}) copy-start(f32[4,32]{1,0:T(4,128)} %convert_bitcast_fusion.table_ref) | copy-start | bytes 1540
  59.1 128.8 %all-gather.5.cloned.1.call-start = ((), (), s32[]{:S(2)}) async-start(), calls=%async_computation.5 | async-start | bytes 2621440 | tf_op jit(solution)/shard_map/all_gather | solution.py:1264
  61.8 12.5 %copy-start.6 = (s32[1,1,512]{2,1,0:T(1,128)}, s32[1,1,512]{2,1,0:T(1,128)S(1)}, u32[]{:S(2)}) copy-start(s32[1,1,512]{2,1,0:T(1,128)S(1)} %get-tuple-element.191.seg_row_ref) | copy-start | bytes 6148
  61.8 49.4 %copy-start.5 = (s32[1,1,512]{2,1,0:T(1,128)}, s32[1,1,512]{2,1,0:T(1,128)S(1)}, u32[]{:S(2)}) copy-start(s32[1,1,512]{2,1,0:T(1,128)S(1)} %get-tuple-element.190.seg_row_ref) | copy-start | bytes 6148
  110.9 227.8 %all-gather.9.cloned.1.call-start = ((), (), s32[]{:S(2)}) async-start(), calls=%async_computation.9 | async-start | bytes 2621440 | tf_op jit(solution)/shard_map/all_gather | solution.py:1264
  187.9 156.1 %all-gather.11.cloned.1.call-start = ((), (), s32[]{:S(2)}) async-start(), calls=%async_computation.10 | async-start | bytes 6553600 | tf_op jit(solution)/shard_map/all_gather | solution.py:1264
  188.5 5.7 copy-start.2
  188.5 292.1 %reduce-scatter.4.cloned.1.call-start = ((), (), s32[]{:S(2)}) async-start(), calls=%async_computation.7 | async-start | bytes 6553600 | tf_op jit(solution)/shard_map/reduce_scatter | solution.py:1267
  338.0 192.2 %reduce-scatter.6.cloned.1.call-start = ((), (), s32[]{:S(2)}) async-start(), calls=%async_computation.8 | async-start | bytes 2621440 | tf_op jit(solution)/shard_map/reduce_scatter | solution.py:1267
  338.6 192.6 %reduce-scatter.8.cloned.1.call-start = ((), (), s32[]{:S(2)}) async-start(), calls=%async_computation.11 | async-start | bytes 2621440 | tf_op jit(solution)/shard_map/reduce_scatter | solution.py:1267
  486.3 126.2 %all-to-all-start.1 = ((bf16[8,320,1024]{2,1,0:T(8,128)(2,1)}), bf16[8,320,1024]{2,1,0:T(8,128)(2,1)}, u32[]{:S(2)}, u32[]{:S(2)}) async-start(bf16[8,320,1024]{2,1,0:T(8,128)(2,1)} %bitcast.137), calls=%async_computation.4 | async-start | bytes 10485760 | tf_op jit(solution)/shard_map/all_to_all | solution.py:1261
  612.5 100.2 %all-to-all-start = ((bf16[8,80,1024]{2,1,0:T(8,128)(2,1)}), bf16[8,80,1024]{2,1,0:T(8,128)(2,1)S(1)}, u32[]{:S(2)}, u32[]{:S(2)}) async-start(bf16[8,80,1024]{2,1,0:T(8,128)(2,1)} %bitcast.35), calls=%async_computation.3 | async-start | bytes 2621440 | tf_op jit(solution)/shard_map/all_to_all | solution.py:1261
  704.0 2.8 copy-start
  706.8 9.7 %copy-start.3 = (f32[1,256,1024]{2,1,0:T(8,128)S(1)}, f32[1,256,1024]{2,1,0:T(8,128)}, u32[]{:S(2)}) copy-start(f32[1,256,1024]{2,1,0:T(8,128)} %get-tuple-element.82) | copy-start | bytes 3145732
  710.8 6.9 copy-start.4
  712.7 1.1 copy-start.1
Sparse Core Ops, SparseCore 0:
  59.2 46.2 all-gather.6
  111.0 50.0 all-gather.4
  188.0 45.8 all-gather.8
  235.4 96.7 all-gather.10
  338.1 92.9 reduce-scatter.3
  433.9 44.3 reduce-scatter.5
  486.4 43.9 reduce-scatter.7

commit v12 on v11

--- a/solution.py
+++ b/solution.py
@@ -50,28 +50,29 @@
 
 
 def bias_kernel(line_ref, out_ref):
-    length = out_ref.shape[2]
-    line = jnp.broadcast_to(line_ref[0], (8, length))
+    heads, _, length = out_ref.shape
     row = lax.broadcasted_iota(jnp.int32, (8, length), 0)
-    sheet = line
-    for r in range(1, 8):
-        sheet = jnp.where(row == r, pltpu.roll(line, r, 1), sheet)
-    while sheet.shape[0] < TILE:
-        sheet = jnp.concatenate([sheet, pltpu.roll(sheet, sheet.shape[0], 1)], axis=0)
-    out_ref[0] = sheet.astype(out_ref.dtype)
+    for head in range(heads):
+        line = jnp.broadcast_to(line_ref[head : head + 1, :], (8, length))
+        sheet = line
+        for r in range(1, 8):
+            sheet = jnp.where(row == r, pltpu.roll(line, r, 1), sheet)
+        while sheet.shape[0] < TILE:
+            sheet = jnp.concatenate([sheet, pltpu.roll(sheet, sheet.shape[0], 1)], axis=0)
+        out_ref[head] = sheet.astype(out_ref.dtype)
 
 
 def position_bias(line):
     heads, length = line.shape
+    vmem = pl.BlockSpec(memory_space=pltpu.VMEM)
     return pl.pallas_call(
         bias_kernel,
-        grid=(heads,),
         out_shape=jax.ShapeDtypeStruct((heads, TILE, length), BF16),
-        in_specs=[pl.BlockSpec((1, 1, length), lambda h: (h, 0, 0))],
-        out_specs=pl.BlockSpec((1, TILE, length), lambda h: (h, 0, 0)),
+        in_specs=[vmem],
+        out_specs=vmem,
         compiler_params=pltpu.CompilerParams(vmem_limit_bytes=VMEM_LIMIT),
         name="position_bias",
-    )(line.reshape(heads, 1, length))
+    )(line)
 
 
 def unit_rows(x):
@@ -292,6 +293,15 @@
             pair_ref[micro, source, e, block] = jnp.where(other >= 0, sign, 0.0).astype(BF16)
 
 
+def collect(rows_ref, place_ref):
+    experts, _, cap, width = rows_ref.shape
+    tokens = place_ref.shape[1]
+    ids = lax.broadcasted_iota(jnp.int32, (experts * cap, tokens), 0)
+    hit = (ids == place_ref[0:1, :]) | (ids == place_ref[1:2, :])
+    rows = rows_ref[...].reshape(experts * cap, width)
+    return mm_tn(jnp.where(hit, 1.0, 0.0).astype(BF16), rows)
+
+
 def attend_kernel(
     scale, x_ref, gain_ref, own_ref, other_ref, bias_ref, seg_row_ref, seg_col_ref,
     out_ref, x_own_ref, moe_gain_ref, *refs,
@@ -392,7 +402,7 @@
         for m in range(micros):
             for s in range(1, members):
                 swap(m, s).wait_recv()
-            h1 = x_own_ref[m].astype(F32)
+            h1 = x_own_ref[0, 0].astype(F32)
             for member in range(members):
                 for j in range(2):
                     index = lax.rem(part + j, 2) * members + member
@@ -416,12 +426,15 @@
 
 def attend(
     x, gain, own_weight, other_weight, bias, seg, out_weight, x_own, moe_gain, scale, members, identity,
-    rider, routes=None, pair_shape=None,
+    which, rider, routes=None, pair_shape=None,
 ):
     micros, half, width = x.shape
     cols = own_weight.shape[2]
     heads = bias.shape[0] // 2
     shard_len = half // members
+    mine = pl.BlockSpec(
+        (1, 1, shard_len, width), lambda m, p: (which, 0, 0, 0), pipeline_mode=pl.Buffered(1)
+    )
     riders, ride_specs = [rider], [any_space()]
     ride_out, ride_out_specs = [jax.ShapeDtypeStruct(rider.shape, BF16)], [any_space()]
     if routes is not None:
@@ -454,7 +467,7 @@
             pl.BlockSpec((1, 1, half), lambda m, p: (m, 0, 0)),
             pl.BlockSpec((1, half, 1), lambda m, p: (m, 0, 0)),
             once(out_weight.shape),
-            once(x_own.shape),
+            mine,
             once((1, width)),
         ]
         + ride_specs,
@@ -492,13 +505,14 @@
 def back_kernel(scale, micros, *refs):
     moe_gain_ref, gain_ref, out_ref, own_ref, other_ref = refs[:5]
     inputs = [refs[5 + 8 * m : 13 + 8 * m] for m in range(micros)]
-    refs = refs[5 + 8 * micros :]
-    xgrads, refs = refs[:micros], refs[micros:]
+    sent_ref, refs = refs[5 + 8 * micros], refs[6 + 8 * micros :]
     (
-        grads_ref, line_ref, dmoe_ref, dgain_ref,
+        xgrad_ref, arrived_ref, grads_ref, line_ref, dmoe_ref, dgain_ref,
         dh1_ref, dattn_all, dheads_part, dheads_all, dxn_part, dxn_got, total_ref, xn_ref, ds_ref,
         dproj_ref, sheet_ref, attn_send, attn_recv, heads_send, heads_recv, dxn_send, dxn_recv,
+        ride_send, ride_recv, ride_own,
     ) = refs
+    devices = sent_ref.shape[0]
     _, members, shard_len, width = dattn_all.shape
     cols = dproj_ref.shape[2]
     half = members * shard_len
@@ -532,9 +546,22 @@
             (me, base + peer_of(s)),
         )
 
+    def ride(s):
+        peer = partner_of(me, s, devices)
+        return remote(
+            sent_ref.at[peer], arrived_ref.at[me], ride_send.at[s], ride_recv.at[s], (peer, line)
+        )
+
+    def stay():
+        return pltpu.make_async_copy(sent_ref.at[me], arrived_ref.at[me], ride_own)
+
     @pl.when((group == 0) & (micro == 0))
     def _():
-        greet([(me, base + peer_of(s)) for s in steps])
+        peers = [(me, base + peer_of(s)) for s in steps]
+        greet(peers + [(partner_of(me, s, devices), line) for s in range(1, devices)])
+        stay().start()
+        for s in range(1, devices):
+            ride(s).start()
         dmoe_ref[...] = jnp.zeros_like(dmoe_ref)
         dgain_ref[...] = jnp.zeros_like(dgain_ref)
         for m in range(micros):
@@ -546,7 +573,7 @@
             dmoe_ref[...] += jnp.sum(grad * unit, axis=0, keepdims=True)
             weighted = grad * moe_gain_ref[...]
             inner = jnp.mean(weighted * unit, axis=-1, keepdims=True)
-            dh1 = dy_ref[...].astype(F32) + r2 * (weighted - unit * inner)
+            dh1 = dy_ref[0, 0].astype(F32) + r2 * (weighted - unit * inner)
             dh1_ref[m] = dh1
             dattn = dh1.astype(BF16)
             dattn_all[m, mine] = dattn
@@ -642,7 +669,7 @@
     @pl.when((group == 1) & (micro == micros - 1))
     def _():
         for m in range(micros):
-            x_own = inputs[m][3][...].astype(F32)
+            x_own = inputs[m][3][0, 0].astype(F32)
             r1 = lax.rsqrt(jnp.mean(x_own * x_own, axis=-1, keepdims=True) + EPSILON)
             unit = x_own * r1
             for s in steps:
@@ -652,15 +679,20 @@
                 dxn1 = dxn1 + dxn_got[m, lax.rem(mine + members - s, members)].astype(F32)
             weighted = dxn1 * gain_ref[...]
             inner = jnp.mean(weighted * unit, axis=-1, keepdims=True)
-            xgrads[m][...] = (dh1_ref[m] + r1 * (weighted - unit * inner)).astype(BF16)
+            xgrad_ref[m] = (dh1_ref[m] + r1 * (weighted - unit * inner)).astype(BF16)
         for m in range(micros):
             for s in steps:
                 heads_copy(m, s).wait_send()
                 attn_copy(m, s).wait_send()
                 dxn_copy(m, s).wait_send()
-
-
-def attend_back(moe_gain, gain, out_weight, own_weight, other_weight, kept, scale, pieces, members):
+        stay().wait()
+        for s in range(1, devices):
+            ride(s).wait()
+
+
+def attend_back(
+    moe_gain, gain, out_weight, own_weight, other_weight, kept, rider, scale, pieces, members
+):
     micros = len(kept)
     _, heads, half = kept[0][6].shape[:3]
     width, cols = own_weight.shape[1:]
@@ -675,27 +707,37 @@
 
     operands = [moe_gain, gain, out_weight, own_weight, other_weight]
     in_specs = [once(array) for array in operands]
-    for arrays in kept:
+    for micro, arrays in enumerate(kept):
         operands.extend(arrays)
-        in_specs += [once(array) for array in arrays[:5]] + [
+        grad, h1, _, _, x_half = [once(array) for array in arrays[:5]]
+        mine = pl.BlockSpec(
+            (1, 1, shard_len, width), lambda p, m, which=micro: (which, 0, 0, 0),
+            pipeline_mode=pl.Buffered(1),
+        )
+        in_specs += [grad, h1, mine, mine, x_half] + [
             pl.BlockSpec((1, 3, half, cols), lambda p, m: (p, 0, 0, 0)),
             pl.BlockSpec((1, heads, half, half), lambda p, m: (p, 0, 0, 0)),
             pl.BlockSpec((half, cols), lambda p, m: (0, p)),
         ]
+    operands.append(rider)
+    in_specs.append(any_space())
     dma = pltpu.SemaphoreType.DMA((micros, members))
+    ride_dma = pltpu.SemaphoreType.DMA((rider.shape[0],))
     return pl.pallas_call(
         functools.partial(back_kernel, scale, micros),
         grid=(2, micros),
-        out_shape=(jax.ShapeDtypeStruct((shard_len, width), BF16),) * micros
-        + (
+        out_shape=(
+            jax.ShapeDtypeStruct((micros, shard_len, width), BF16),
+            jax.ShapeDtypeStruct(rider.shape, BF16),
             jax.ShapeDtypeStruct((pieces, 2, rows, cols), BF16),
             jax.ShapeDtypeStruct((2, heads, length), F32),
             jax.ShapeDtypeStruct((1, width), F32),
             jax.ShapeDtypeStruct((1, width), F32),
         ),
         in_specs=in_specs,
-        out_specs=(pl.BlockSpec((shard_len, width), lambda p, m: (0, 0)),) * micros
-        + (
+        out_specs=(
+            pl.BlockSpec((micros, shard_len, width), lambda p, m: (0, 0, 0)),
+            any_space(),
             pl.BlockSpec((pieces, 1, rows, cols), lambda p, m: (0, p, 0, 0)),
             pl.BlockSpec((1, heads, length), lambda p, m: (p, 0, 0)),
             pl.BlockSpec((1, width), lambda p, m: (0, 0)),
@@ -713,7 +755,7 @@
             pltpu.VMEM((half, half), BF16),
             pltpu.VMEM((3, half, cols), BF16),
             pltpu.VMEM((TILE, length), F32),
-            dma, dma, dma, dma, dma, dma,
+            dma, dma, dma, dma, dma, dma, ride_dma, ride_dma, pltpu.SemaphoreType.DMA,
         ],
         compiler_params=pltpu.CompilerParams(
             vmem_limit_bytes=VMEM_LIMIT, collective_id=6, has_side_effects=True
@@ -728,7 +770,8 @@
 
 
 def closing_kernel(
-    pieces_ref, small_ref, y_ref, h1_ref, whole_ref, sum_ref, block_ref,
+    pieces_ref, small_ref, y_ref, h1_ref, rows_ref, place_ref, first_h1_ref,
+    whole_ref, sum_ref, block_ref,
     y_got, y_send, y_recv, half_got, held_ref, quarter_got, total_ref, moved_ref, moved_got, small_got, line_sum,
     line_got, half_sem, quarter_send, quarter_recv, small_send, small_recv, line_send, line_recv,
     moved_sem, on_send, on_recv, own_sem,
@@ -743,7 +786,7 @@
     along = [lax.rem(line + s, blocks) for s in range(1, blocks)]
     across = lax.rem(line + blocks // 2, blocks)
     greet([(partner_of(me, s, devices), line) for s in range(1, devices)] + [(me, z) for z in along])
-    share = 3 * y_ref.shape[1] // 4
+    share = y_ref.shape[1] // 2
     turns = (pl.ds(0, share), pl.ds(share, y_ref.shape[1] - share))
 
     def y_copies(turn):
@@ -772,6 +815,7 @@
     for copy in smalls:
         copy.start()
     small_got[me] = small_ref[...]
+    block_ref[0] = (first_h1_ref[...] + collect(rows_ref, place_ref)).astype(BF16)
     halves.wait_recv()
     steps = range(1, chips)
 
@@ -829,7 +873,7 @@
     last.start()
     for copy in y_copies(0) + y_copies(1):
         copy.wait_recv()
-    block_ref[...] = (h1_ref[...] + jnp.sum(y_got[...].astype(F32), axis=0)).astype(BF16)
+    block_ref[1] = (h1_ref[...] + jnp.sum(y_got[...].astype(F32), axis=0)).astype(BF16)
     for copy in y_copies(0) + y_copies(1):
         copy.wait_send()
     halves.wait_send()
@@ -841,7 +885,7 @@
     last.wait()
 
 
-def closing(pieces, small, y, h1):
+def closing(pieces, small, y, h1, rows_first, place, first_h1):
     devices, both, rows, cols = pieces.shape
     blocks = y.shape[0]
     chips = devices // 2
@@ -852,9 +896,9 @@
         out_shape=(
             jax.ShapeDtypeStruct((chips, 2, rows, cols), BF16),
             jax.ShapeDtypeStruct(small.shape, F32),
-            jax.ShapeDtypeStruct(h1.shape, BF16),
-        ),
-        in_specs=[vmem] * 4,
+            jax.ShapeDtypeStruct((2,) + h1.shape, BF16),
+        ),
+        in_specs=[vmem] * 7,
         out_specs=(vmem,) * 3,
         scratch_shapes=[
             pltpu.VMEM(y.shape, BF16),
@@ -877,7 +921,7 @@
         ),
         cost_estimate=pl.CostEstimate(flops=0, bytes_accessed=160000000, transcendentals=0),
         name="closing",
-    )(pieces.reshape(chips, 2, both, rows, cols), small, y, h1)
+    )(pieces.reshape(chips, 2, both, rows, cols), small, y, h1, rows_first, place, first_h1)
 
 
 def spread(rows, place0, place1, count):
@@ -915,12 +959,7 @@
 
 
 def collect_kernel(rows_ref, place_ref, out_ref):
-    experts, _, cap, width = rows_ref.shape
-    tokens = out_ref.shape[0]
-    ids = lax.broadcasted_iota(jnp.int32, (experts * cap, tokens), 0)
-    hit = (ids == place_ref[0:1, :]) | (ids == place_ref[1:2, :])
-    rows = rows_ref[...].reshape(experts * cap, width)
-    out_ref[...] = mm_tn(jnp.where(hit, 1.0, 0.0).astype(BF16), rows).astype(BF16)
+    out_ref[...] = collect(rows_ref, place_ref).astype(BF16)
 
 
 def collect_rows(rows, place, shard_len):
@@ -1318,7 +1357,7 @@
     for micro, state in enumerate(states):
         inputs = (
             attn_gain_f, qkv_weight, other_qkv, bias, seg_half[micro : micro + 1], all_out,
-            x_in[micro], moe_gain_f, scale, members, 10 + micro,
+            x_in, moe_gain_f, scale, members, 10 + micro, micro,
         )
         if micro == 0:
             sent = spread(cotangent[:, 0], 1, own_place[1]).reshape(devices, -1, width)
@@ -1347,25 +1386,20 @@
     kept[-1] = tuple(after(list(kept[-1]), last_part))
     dwr, dwg, dwu, dwd = weight_pass(kept)
     last["y_rows"] = exchange(after(last["y"], last_part).reshape(flat_shape)).reshape(place_shape)
-    *x_grads, grads, lines, moe_gain_grad, attn_gain_grad = attend_back(
+    x_grad, first_rows, grads, lines, moe_gain_grad, attn_gain_grad = attend_back(
         moe_gain_f, attn_gain_f, all_out, qkv_weight, other_qkv,
         [
             (
-                after(state["dxn2"], dwr), state["h1"], cotangent[micro, 0], x_in[micro, 0],
+                after(state["dxn2"], dwr), state["h1"], cotangent, x_in,
                 x_half[micro][0], state["qkv"], state["prob"], state["heads"],
             )
             for micro, state in enumerate(states)
         ],
-        scale, devices, members,
+        first["y_own"], scale, devices, members,
     )
     rows = collect_rows(after(last["y_rows"], grads), place[-1], shard_len)
     rows = rows.reshape(blocks, shard_len, width)
-    for micro in range(micro_count - 1):
-        state = states[micro]
-        mixed = exchange(after(state["y_own"], grads)).reshape(expert_count, 1, capacity, width)
-        mixed = collect_rows(mixed, own_place[micro], shard_len)
-        state["block_out"] = (state["h1"] + mixed.astype(F32)).astype(BF16)
-
+    first_rows = first_rows.reshape(expert_count, 1, capacity, width)
     lines = lines.reshape(2 * heads_here, 2 * half)
     table = jnp.einsum("hj,jb->hb", lines, onehot_bucket, precision=PRECISE)
     table = table.reshape(2, heads_here * bucket_count)
@@ -1383,7 +1417,9 @@
     )
     used = small.shape[0]
     small = jnp.pad(small, (0, -used % 1024)).reshape(-1, 128)
-    whole, small, last["block_out"] = closing(grads, small, rows, last["h1"])
+    whole, small, block_out = closing(
+        grads, small, rows, last["h1"], first_rows, own_place[0], first["h1"]
+    )
     whole = whole.reshape(4 * width, head_cols).astype(F32)
     grad_qkv = whole[: 3 * width].reshape(qkv_weight.shape)
     grad_out = whole[3 * width :].T
@@ -1395,8 +1431,8 @@
     table = small[sizes[0] + 2 * width : used].reshape(blocks, heads_here, bucket_count)
     grad_table = lax.dynamic_index_in_dim(table, hidden_index, 0, keepdims=False).T
     return (
-        jnp.stack([state["block_out"] for state in states])[:, None],
-        jnp.stack(x_grads)[:, None],
+        block_out[:, None],
+        x_grad[:, None],
         grad_qkv,
         grad_out,
         grad_table,

time: 734 us -> 721 us (0.982)
  Pallas kernels: 666 us -> 658 us
    pallas_call x1, Pallas kernels: 78.5 us -> 70.7 us  [closing(): pl.pallas_call(closing_kernel, out_shape=(jax.ShapeDtypeStruct((chips, 2,...]
    pallas_call x4 -> x3, Pallas kernels: 19.6 us -> 16.9 us  [collect_rows(): pl.pallas_call(collect_kernel, grid=(blocks,), out_shape=jax.ShapeDtypeSt...]
  transfers between devices with their start and end apart: 9 -> 8, of which waited for: 0 -> 0; matrix products, arithmetic and copies ran while one was open for 3% -> 2% of each run, Pallas kernels for 85% -> 76%
where the time goes in v12:
time: 721 us; the launch traced here: 709 us
  Pallas kernels  658 us (91%)
  local copies, waits for them, and re-layouts  20.3 us (3%)
  between operations  14.8 us (2%)
    pallas_call x2, Pallas kernels, expert_pass(): pl.pallas_call(functools.partial(expert_kernel, by_block), grid=(devices,...  274 us
    pallas_call x2, Pallas kernels, attend(): pl.pallas_call(functools.partial(attend_kernel, scale), grid=(micros, 2),...  104 us
    pallas_call x1, Pallas kernels, attend_back(): pl.pallas_call(functools.partial(back_kernel, scale, micros), grid=(2, mi...  82.6 us
    pallas_call x1, Pallas kernels, closing(): pl.pallas_call(closing_kernel, out_shape=(jax.ShapeDtypeStruct((chips, 2,...  70.7 us
    pallas_call x1, Pallas kernels, opening(): pl.pallas_call(functools.partial(opening_kernel, micros), out_shape=(jax....  45.3 us
    pallas_call x1, Pallas kernels, weight_pass(): pl.pallas_call(weight_kernel, grid=(experts, width // block), out_shape=(...  38.6 us
    pallas_call x4, Pallas kernels, spread_rows(): pl.pallas_call(spread_kernel, grid=(blocks,), out_shape=jax.ShapeDtypeStr...  18.8 us
    pallas_call x3, Pallas kernels, collect_rows(): pl.pallas_call(collect_kernel, grid=(blocks,), out_shape=jax.ShapeDtypeSt...  16.9 us
  transfers between devices with their start and end apart: 8, of which 0 were waited for; matrix products, arithmetic and copies ran while one was open for 2% of the time, Pallas kernels for 76%

profile of v12, /device:TPU:0, one launch (start us, length us, event | category | flops | bytes accessed | tf_op | source)
XLA Modules:
  0.0 709.3 jit_solution(11278373789530657900)
XLA Ops:
  7.3 0.7 dynamic-slice_compare_fusion
  8.0 1.3 convert_bitcast_fusion.table_ref
  9.2 1.9 slice_bitcast_fusion
  11.1 1.3 fusion.18
  12.4 45.3 %opening.1 = (bf16[2,256,1024]{2,1,0:T(8,128)(2,1)}, bf16[2,256,1024]{2,1,0:T(8,128)(2,1)}, bf16[4,2,384,256]{3,2,1,0:T(8,128)(2,1)}, bf16[4,4,2,32,1024]{4,3,2,...) custom-call(bf16[2,256,1024]{2,1,0:T(8,128)(2,1)} %bitcast.112, bf16[3072,256]{1,0:T(8,128)(2,1)} %bitcast.107, ...), custom_call_target="tpu_custom_call" | custom-call | bytes 200000000 | tf_op jit(solution)/shard_map/opening/pallas_call | solution.py:236
  57.8 0.6 reshape.252
  58.4 0.6 reshape.250
  59.0 1.4 find_places.2
  60.4 0.9 copy.32.seg_col_ref
  61.3 1.8 fusion.1.line_ref
  63.1 4.6 position_bias.1.bias_ref
  67.6 1.3 slice_bitcast_fusion.5
  68.9 2.6 spread_rows.4
  71.6 37.9 %attend.2 = (bf16[1,2,3,512,256]{4,3,2,1,0:T(8,128)(2,1)}, bf16[1,2,4,512,512]{4,3,2,1,0:T(8,128)(2,1)}, bf16[1,512,512]{2,1,0:T(8,128)(2,1)}, f32[1,256,1024]{2...) custom-call(bf16[1,512,1024]{2,1,0:T(8,128)(2,1)} %bitcast.147, f32[1,1024]{1,0:T(1,128)} %bitcast.156, ...), custom_call_target="tpu_custom_call" | custom-call | flops 2684354560 | bytes 100000000 | tf_op jit(solution)/shard_map/attend/pallas_call | solution.py:450
  109.8 0.9 copy.33.seg_col_ref
  110.6 1.3 dynamic-slice_bitcast_fusion.route_ref
  112.0 1.6 find_places.3
  113.5 1.3 slice_bitcast_fusion.1
  114.9 5.4 spread_rows.6
  120.3 66.2 %attend.3 = (bf16[1,2,3,512,256]{4,3,2,1,0:T(8,128)(2,1)}, bf16[1,2,4,512,512]{4,3,2,1,0:T(8,128)(2,1)}, bf16[1,512,512]{2,1,0:T(8,128)(2,1)}, f32[1,256,1024]{2...) custom-call(bf16[1,512,1024]{2,1,0:T(8,128)(2,1)} %bitcast.138, ...), custom_call_target="tpu_custom_call" | custom-call | flops 2684354560 | bytes 100000000 | tf_op jit(solution)/shard_map/attend/pallas_call | solution.py:450
  186.6 0.5 all-gather.11.cloned.1.call-update
  187.4 5.4 spread_rows.5
  192.8 1.2 fusion.21
  194.0 137.0 %expert_pass.2 = (bf16[8,2,160,1024]{3,2,1,0:T(8,128)(2,1)}, bf16[4,8,2,40,1024]{4,3,2,1,0:T(8,128)(2,1)}, bf16[8,2,160,1024]{3,2,1,0:T(8,128)(2,1)}, bf16[8,2,1...) custom-call(bf16[8,2,160,1024]{3,2,1,0:T(8,128)(2,1)} %bitcast.106, ...), custom_call_target="tpu_custom_call" | custom-call | bytes 490000000 | tf_op jit(solution)/shard_map/expert_pass/pallas_call | solution.py:1162
  331.0 5.6 collect_rows.3
  336.7 0.5 reduce-scatter.4.cloned.1.call-update
  337.3 5.3 spread_rows.7
  342.6 136.6 %expert_pass.3 = (bf16[8,2,160,1024]{3,2,1,0:T(8,128)(2,1)}, bf16[8,2,4,40,1024]{4,3,2,1,0:T(8,128)(2,1)}, bf16[8,2,160,1024]{3,2,1,0:T(8,128)(2,1)}, bf16[8,2,1...) custom-call(bf16[8,2,160,1024]{3,2,1,0:T(8,128)(2,1)} %bitcast.105, ...), custom_call_target="tpu_custom_call" | custom-call | bytes 490000000 | tf_op jit(solution)/shard_map/expert_pass/pallas_call | solution.py:1162
  479.2 5.6 collect_rows.4
  484.9 5.2 all-to-all-start
  490.1 38.6 %weight_pass.1 = (f32[2,16,1024]{2,1,0:T(8,128)}, f32[2,704,1024]{2,1,0:T(8,128)}, f32[2,704,1024]{2,1,0:T(8,128)}, f32[2,704,1024]{2,1,0:T(8,128)}) custom-call(bf16[8,2,160,1024]{3,2,1,0:T(8,128)(2,1)} %get-tuple-element.90.refs_0_, bf16[8,2,160,1024]{3,2,1,0:T(8,128)(2,1)} %get-tuple-element.91.refs_1_, ...), custom_call_target="tpu_custom_call" | custom-call | flops 22145925120 | bytes 59899904 | tf_op jit(solution)/shard_map/weight_pass/pallas_call | solution.py:1228
  528.8 0.9 reduce_sum.9
  529.7 82.6 %attend_back.1 = (bf16[2,256,1024]{2,1,0:T(8,128)(2,1)}, bf16[8,80,1024]{2,1,0:T(8,128)(2,1)}, bf16[8,2,512,256]{3,2,1,0:T(8,128)(2,1)}, f32[2,4,1024]{2,1,0:T(4...) custom-call(f32[1,1024]{1,0:T(1,128)} %bitcast.161, f32[1,1024]{1,0:T(1,128)} %bitcast.158, bf16[4,256,1024]{2,1,0:T(8,128)(2,1)} %bitcast.115, ...), custom_call_target="tpu_custom_call" | custom-call | flops 10737418240 | bytes 250000000 | tf_op jit(solution)/shard_map/attend_back/pallas_call | solution.py:726
  612.3 0.8 reshape.241
  613.1 0.4 fusion
  613.7 1.3 fusion.4.small_ref
  615.1 5.6 collect_rows.5
  620.7 70.7 %closing.1 = (bf16[4,2,512,256]{3,2,1,0:T(8,128)(2,1)}, f32[152,128]{1,0:T(8,128)}, bf16[2,256,1024]{2,1,0:T(8,128)(2,1)}) custom-call(bf16[4,2,2,512,256]{4,3,2,1,0:T(8,128)(2,1)} %bitcast.127, f32[152,128]{1,0:T(8,128)} %fusion.4.small_ref, bf16[4,256,1024]{2,1,0:T(8,128)(2,1)} %bitcast.116, f32[256,1024]{1,0:T(8,128)} %bitcast.143, ...), custom_call_target="tpu_custom_call" | custom-call | bytes 160000000 | tf_op jit(solution)/shard_map/closing/pallas_call | solution.py:894
  691.5 0.8 slice.87
  692.3 1.3 slice_bitcast_fusion.3
  693.6 0.8 slice.92
  694.4 1.1 slice.98
  695.6 1.9 slice.97
  697.6 0.6 reshape.249
  698.2 1.3 copy.34
  699.5 0.6 dynamic-slice_bitcast_fusion.1
  700.1 1.0 copy.43
  701.1 1.0 copy.44
  (50 shorter events, 1.4 us)
Async XLA Ops:
  7.2 53.2 %copy-start.7 = (s32[2,1,1024]{2,1,0:T(1,128)S(1)}, s32[2,1,1024]{2,1,0:T(1,128)}, u32[]{:S(2)}) copy-start(s32[2,1,1024]{2,1,0:T(1,128)} %param.15) | copy-start | bytes 24580
  7.2 50.6 %copy-start.8 = (bf16[1024]{0:T(1024)(128)(2,1)S(1)}, bf16[1024]{0:T(1024)(128)(2,1)}, u32[]{:S(2)}) copy-start(bf16[1024]{0:T(1024)(128)(2,1)} %param.20) | copy-start | bytes 6148
  7.2 51.2 %copy-start.9 = (bf16[1024]{0:T(1024)(128)(2,1)S(1)}, bf16[1024]{0:T(1024)(128)(2,1)}, u32[]{:S(2)}) copy-start(bf16[1024]{0:T(1024)(128)(2,1)} %param.21) | copy-start | bytes 6148
  7.2 107.7 %all-gather.7.cloned.1.call-start = ((), (), s32[]{:S(2)}) async-start(), calls=%async_computation.5 | async-start | bytes 2621440 | tf_op jit(solution)/shard_map/all_gather | solution.py:1303
  9.2 52.1 %copy-start.6 = (f32[4,32]{1,0:T(4,128)S(1)}, f32[4,32]{1,0:T(4,128)}, u32[]{:S(2)}) copy-start(f32[4,32]{1,0:T(4,128)} %convert_bitcast_fusion.table_ref) | copy-start | bytes 1540
  57.7 128.8 %all-gather.5.cloned.1.call-start = ((), (), s32[]{:S(2)}) async-start(), calls=%async_computation.4 | async-start | bytes 2621440 | tf_op jit(solution)/shard_map/all_gather | solution.py:1303
  60.4 11.1 %copy-start.5 = (s32[1,1,512]{2,1,0:T(1,128)}, s32[1,1,512]{2,1,0:T(1,128)S(1)}, u32[]{:S(2)}) copy-start(s32[1,1,512]{2,1,0:T(1,128)S(1)} %get-tuple-element.183.seg_row_ref) | copy-start | bytes 6148
  60.4 49.3 %copy-start.4 = (s32[1,1,512]{2,1,0:T(1,128)}, s32[1,1,512]{2,1,0:T(1,128)S(1)}, u32[]{:S(2)}) copy-start(s32[1,1,512]{2,1,0:T(1,128)S(1)} %get-tuple-element.182.seg_row_ref) | copy-start | bytes 6148
  109.5 227.8 %all-gather.9.cloned.1.call-start = ((), (), s32[]{:S(2)}) async-start(), calls=%async_computation.7 | async-start | bytes 2621440 | tf_op jit(solution)/shard_map/all_gather | solution.py:1303
  186.5 156.1 %all-gather.11.cloned.1.call-start = ((), (), s32[]{:S(2)}) async-start(), calls=%async_computation.8 | async-start | bytes 6553600 | tf_op jit(solution)/shard_map/all_gather | solution.py:1303
  187.1 5.7 copy-start.1
  187.1 292.1 %reduce-scatter.6.cloned.1.call-start = ((), (), s32[]{:S(2)}) async-start(), calls=%async_computation.9 | async-start | bytes 6553600 | tf_op jit(solution)/shard_map/reduce_scatter | solution.py:1306
  336.6 192.1 %reduce-scatter.4.cloned.1.call-start = ((), (), s32[]{:S(2)}) async-start(), calls=%async_computation.6 | async-start | bytes 2621440 | tf_op jit(solution)/shard_map/reduce_scatter | solution.py:1306
  337.2 192.5 %reduce-scatter.8.cloned.1.call-start = ((), (), s32[]{:S(2)}) async-start(), calls=%async_computation.10 | async-start | bytes 2621440 | tf_op jit(solution)/shard_map/reduce_scatter | solution.py:1306
  484.9 130.2 %all-to-all-start = ((bf16[8,320,1024]{2,1,0:T(8,128)(2,1)}), bf16[8,320,1024]{2,1,0:T(8,128)(2,1)}, u32[]{:S(2)}, u32[]{:S(2)}) async-start(bf16[8,320,1024]{2,1,0:T(8,128)(2,1)} %bitcast.120), calls=%async_computation.3 | async-start | bytes 10485760 | tf_op jit(solution)/shard_map/all_to_all | solution.py:1300
  691.4 4.1 copy-start
  695.5 4.6 copy-start.3
  695.5 5.6 copy-start.2
Sparse Core Ops, SparseCore 0:
  57.8 46.7 all-gather.6
  109.6 50.0 all-gather.4
  186.7 45.9 all-gather.8
  234.0 96.7 all-gather.10
  336.7 92.9 reduce-scatter.5
  432.5 44.3 reduce-scatter.3
  485.0 43.8 reduce-scatter.7

commit v13 on v12

--- a/solution.py
+++ b/solution.py
@@ -380,7 +380,7 @@
             weights = jnp.exp(scores - top)
             inverse = 1.0 / jnp.sum(weights, axis=-1, keepdims=True)
             prob = (weights * inverse).astype(BF16)
-            prob_ref[0, 0, head, rows, :] = prob
+            prob_ref[0, 0, head, :, rows] = prob.T
             heads_ref[0, rows, inner] = mm(prob, values).astype(BF16)
 
     for g in range(2):
@@ -516,7 +516,7 @@
     _, members, shard_len, width = dattn_all.shape
     cols = dproj_ref.shape[2]
     half = members * shard_len
-    length = sheet_ref.shape[1]
+    length = sheet_ref.shape[0]
     group, micro = pl.program_id(0), pl.program_id(1)
     me = lax.axis_index("expert")
     line = lax.axis_index("hidden")
@@ -616,21 +616,21 @@
                     sheet_ref[...] = jnp.zeros_like(sheet_ref)
                     for start in range(0, half, TILE):
                         rows = slice(start, start + TILE)
-                        prob = prob_ref[0, head, rows, :].astype(F32)
-                        dprob = mm_nt(grads[rows], values)
-                        inner = jnp.sum(prob * dprob, axis=-1, keepdims=True)
+                        prob = prob_ref[0, head, :, rows].astype(F32)
+                        dprob = mm_nt(values, grads[rows])
+                        inner = jnp.sum(prob * dprob, axis=0, keepdims=True)
                         dscore = (prob * (dprob - inner)).astype(BF16)
-                        ds_ref[rows, :] = dscore
+                        ds_ref[:, rows] = dscore
                         dscore = dscore.astype(F32)
-                        sheet_ref[:, : half - start] += dscore[:, start:]
+                        sheet_ref[: half - start, :] += dscore[start:]
                         if start:
-                            sheet_ref[:, length - start :] += dscore[:, :start]
+                            sheet_ref[length - start :, :] += dscore[:start]
                     dscores = ds_ref[...]
                     keys, queries = qkv_ref[0, 1, :, inner_cols], qkv_ref[0, 0, :, inner_cols]
-                    dproj_ref[0, :, inner_cols] = (mm(dscores, keys) * scale).astype(BF16)
-                    dproj_ref[1, :, inner_cols] = (mm_tn(dscores, queries) * scale).astype(BF16)
-                    dproj_ref[2, :, inner_cols] = mm_tn(prob_ref[0, head], grads).astype(BF16)
-                    sheet = sheet_ref[...]
+                    dproj_ref[0, :, inner_cols] = (mm_tn(dscores, keys) * scale).astype(BF16)
+                    dproj_ref[1, :, inner_cols] = (mm(dscores, queries) * scale).astype(BF16)
+                    dproj_ref[2, :, inner_cols] = mm(prob_ref[0, head], grads).astype(BF16)
+                    sheet = sheet_ref[...].T
                     while sheet.shape[0] > 8:
                         upper = sheet.shape[0] // 2
                         sheet = sheet[:upper] + pltpu.roll(sheet[upper:], length - upper, 1)
@@ -754,7 +754,7 @@
             pltpu.VMEM((micros, half, width), BF16),
             pltpu.VMEM((half, half), BF16),
             pltpu.VMEM((3, half, cols), BF16),
-            pltpu.VMEM((TILE, length), F32),
+            pltpu.VMEM((length, TILE), F32),
             dma, dma, dma, dma, dma, dma, ride_dma, ride_dma, pltpu.SemaphoreType.DMA,
         ],
         compiler_params=pltpu.CompilerParams(
@@ -1361,7 +1361,9 @@
         )
         if micro == 0:
             sent = spread(cotangent[:, 0], 1, own_place[1]).reshape(devices, -1, width)
-            qkv, prob, heads, h1, xn2, last["dy_here"] = attend(x_half[0], *inputs, sent)
+            qkv, prob, heads, h1, xn2, last["dy_here"] = attend(
+                after(x_half[0], place), *inputs, sent
+            )
         else:
             sent = spread(after(first["dy_all"], xn2)[None], 0, place[0]).reshape(token_shape)
             qkv, prob, heads, h1, xn2, first["dy"], pairs = attend(

time: 721 us -> 718 us (level)
  no operation moved by 1% of the time
where the time goes in v13:
time: 718 us; the launch traced here: 706 us
  Pallas kernels  656 us (91%)
  local copies, waits for them, and re-layouts  19.5 us (3%)
  between operations  14.8 us (2%)
    pallas_call x2, Pallas kernels, expert_pass(): pl.pallas_call(functools.partial(expert_kernel, by_block), grid=(devices,...  274 us
    pallas_call x2, Pallas kernels, attend(): pl.pallas_call(functools.partial(attend_kernel, scale), grid=(micros, 2),...  101 us
    pallas_call x1, Pallas kernels, attend_back(): pl.pallas_call(functools.partial(back_kernel, scale, micros), grid=(2, mi...  82.8 us
    pallas_call x1, Pallas kernels, closing(): pl.pallas_call(closing_kernel, out_shape=(jax.ShapeDtypeStruct((chips, 2,...  70.9 us
    pallas_call x1, Pallas kernels, opening(): pl.pallas_call(functools.partial(opening_kernel, micros), out_shape=(jax....  45.3 us
    pallas_call x1, Pallas kernels, weight_pass(): pl.pallas_call(weight_kernel, grid=(experts, width // block), out_shape=(...  38.6 us
    pallas_call x4, Pallas kernels, spread_rows(): pl.pallas_call(spread_kernel, grid=(blocks,), out_shape=jax.ShapeDtypeStr...  18.7 us
    pallas_call x3, Pallas kernels, collect_rows(): pl.pallas_call(collect_kernel, grid=(blocks,), out_shape=jax.ShapeDtypeSt...  16.9 us
  transfers between devices with their start and end apart: 8, of which 0 were waited for; matrix products, arithmetic and copies ran while one was open for 2% of the time, Pallas kernels for 76%

profile of v13, /device:TPU:0, one launch (start us, length us, event | category | flops | bytes accessed | tf_op | source)
XLA Modules:
  0.0 706.4 jit_solution(3443577232979089400)
XLA Ops:
  7.3 0.7 dynamic-slice_compare_fusion
  8.0 1.3 convert_bitcast_fusion.table_ref
  9.2 1.9 slice_bitcast_fusion
  11.1 1.3 fusion.18
  12.4 45.3 %opening.1 = (bf16[2,256,1024]{2,1,0:T(8,128)(2,1)}, bf16[2,256,1024]{2,1,0:T(8,128)(2,1)}, bf16[4,2,384,256]{3,2,1,0:T(8,128)(2,1)}, bf16[4,4,2,32,1024]{4,3,2,...) custom-call(bf16[2,256,1024]{2,1,0:T(8,128)(2,1)} %bitcast.112, bf16[3072,256]{1,0:T(8,128)(2,1)} %bitcast.107, ...), custom_call_target="tpu_custom_call" | custom-call | bytes 200000000 | tf_op jit(solution)/shard_map/opening/pallas_call | solution.py:236
  57.8 0.6 reshape.252
  58.4 0.6 reshape.250
  59.0 1.4 find_places.3
  60.4 0.9 copy.32.seg_col_ref
  61.3 1.3 dynamic-slice_bitcast_fusion.route_ref
  62.6 1.6 find_places.2
  64.2 1.7 fusion.1.line_ref
  66.0 4.6 position_bias.1.bias_ref
  70.5 1.3 slice_bitcast_fusion.5
  71.8 2.6 spread_rows.4
  74.5 35.0 %attend.2 = (bf16[1,2,3,512,256]{4,3,2,1,0:T(8,128)(2,1)}, bf16[1,2,4,512,512]{4,3,2,1,0:T(8,128)(2,1)}, bf16[1,512,512]{2,1,0:T(8,128)(2,1)}, f32[1,256,1024]{2...) custom-call(bf16[1,512,1024]{2,1,0:T(8,128)(2,1)} %bitcast.147, f32[1,1024]{1,0:T(1,128)} %bitcast.156, ...), custom_call_target="tpu_custom_call" | custom-call | flops 2684354560 | bytes 100000000 | tf_op jit(solution)/shard_map/attend/pallas_call | solution.py:450
  109.8 0.9 copy.33.seg_col_ref
  110.7 0.6 slice_bitcast_fusion.1
  111.3 5.3 spread_rows.6
  116.6 66.4 %attend.3 = (bf16[1,2,3,512,256]{4,3,2,1,0:T(8,128)(2,1)}, bf16[1,2,4,512,512]{4,3,2,1,0:T(8,128)(2,1)}, bf16[1,512,512]{2,1,0:T(8,128)(2,1)}, f32[1,256,1024]{2...) custom-call(bf16[1,512,1024]{2,1,0:T(8,128)(2,1)} %bitcast.138, ...), custom_call_target="tpu_custom_call" | custom-call | flops 2684354560 | bytes 100000000 | tf_op jit(solution)/shard_map/attend/pallas_call | solution.py:450
  183.1 0.5 all-gather.11.cloned.1.call-update
  184.0 5.4 spread_rows.5
  189.4 1.2 fusion.21
  190.5 137.1 %expert_pass.2 = (bf16[8,2,160,1024]{3,2,1,0:T(8,128)(2,1)}, bf16[4,8,2,40,1024]{4,3,2,1,0:T(8,128)(2,1)}, bf16[8,2,160,1024]{3,2,1,0:T(8,128)(2,1)}, bf16[8,2,1...) custom-call(bf16[8,2,160,1024]{3,2,1,0:T(8,128)(2,1)} %bitcast.106, ...), custom_call_target="tpu_custom_call" | custom-call | bytes 490000000 | tf_op jit(solution)/shard_map/expert_pass/pallas_call | solution.py:1162
  327.6 5.6 collect_rows.3
  333.3 0.5 reduce-scatter.4.cloned.1.call-update
  333.9 5.3 spread_rows.7
  339.3 136.6 %expert_pass.3 = (bf16[8,2,160,1024]{3,2,1,0:T(8,128)(2,1)}, bf16[8,2,4,40,1024]{4,3,2,1,0:T(8,128)(2,1)}, bf16[8,2,160,1024]{3,2,1,0:T(8,128)(2,1)}, bf16[8,2,1...) custom-call(bf16[8,2,160,1024]{3,2,1,0:T(8,128)(2,1)} %bitcast.105, ...), custom_call_target="tpu_custom_call" | custom-call | bytes 490000000 | tf_op jit(solution)/shard_map/expert_pass/pallas_call | solution.py:1162
  475.9 5.6 collect_rows.4
  481.6 5.2 all-to-all-start
  486.8 38.6 %weight_pass.1 = (f32[2,16,1024]{2,1,0:T(8,128)}, f32[2,704,1024]{2,1,0:T(8,128)}, f32[2,704,1024]{2,1,0:T(8,128)}, f32[2,704,1024]{2,1,0:T(8,128)}) custom-call(bf16[8,2,160,1024]{3,2,1,0:T(8,128)(2,1)} %get-tuple-element.92.refs_0_, bf16[8,2,160,1024]{3,2,1,0:T(8,128)(2,1)} %get-tuple-element.93.refs_1_, ...), custom_call_target="tpu_custom_call" | custom-call | flops 22145925120 | bytes 59899904 | tf_op jit(solution)/shard_map/weight_pass/pallas_call | solution.py:1228
  525.5 0.9 reduce_sum.9
  526.5 82.8 %attend_back.1 = (bf16[2,256,1024]{2,1,0:T(8,128)(2,1)}, bf16[8,80,1024]{2,1,0:T(8,128)(2,1)}, bf16[8,2,512,256]{3,2,1,0:T(8,128)(2,1)}, f32[2,4,1024]{2,1,0:T(4...) custom-call(f32[1,1024]{1,0:T(1,128)} %bitcast.161, f32[1,1024]{1,0:T(1,128)} %bitcast.158, bf16[4,256,1024]{2,1,0:T(8,128)(2,1)} %bitcast.115, ...), custom_call_target="tpu_custom_call" | custom-call | flops 10737418240 | bytes 250000000 | tf_op jit(solution)/shard_map/attend_back/pallas_call | solution.py:726
  609.3 0.8 reshape.241
  610.1 0.4 fusion
  610.7 1.4 fusion.4.small_ref
  612.0 5.6 collect_rows.5
  617.7 70.9 %closing.1 = (bf16[4,2,512,256]{3,2,1,0:T(8,128)(2,1)}, f32[152,128]{1,0:T(8,128)}, bf16[2,256,1024]{2,1,0:T(8,128)(2,1)}) custom-call(bf16[4,2,2,512,256]{4,3,2,1,0:T(8,128)(2,1)} %bitcast.127, f32[152,128]{1,0:T(8,128)} %fusion.4.small_ref, bf16[4,256,1024]{2,1,0:T(8,128)(2,1)} %bitcast.116, f32[256,1024]{1,0:T(8,128)} %bitcast.143, ...), custom_call_target="tpu_custom_call" | custom-call | bytes 160000000 | tf_op jit(solution)/shard_map/closing/pallas_call | solution.py:894
  688.6 0.8 slice.87
  689.4 1.3 slice_bitcast_fusion.3
  690.7 0.8 slice.92
  691.5 1.1 slice.98
  692.7 1.9 slice.97
  694.7 0.6 reshape.249
  695.3 1.3 copy.34
  696.7 0.6 dynamic-slice_bitcast_fusion.1
  697.2 1.0 copy.43
  698.2 1.0 copy.44
  (52 shorter events, 1.4 us)
Async XLA Ops:
  7.2 53.2 %copy-start.8 = (s32[2,1,1024]{2,1,0:T(1,128)S(1)}, s32[2,1,1024]{2,1,0:T(1,128)}, u32[]{:S(2)}) copy-start(s32[2,1,1024]{2,1,0:T(1,128)} %param.15) | copy-start | bytes 24580
  7.2 50.6 %copy-start.9 = (bf16[1024]{0:T(1024)(128)(2,1)S(1)}, bf16[1024]{0:T(1024)(128)(2,1)}, u32[]{:S(2)}) copy-start(bf16[1024]{0:T(1024)(128)(2,1)} %param.20) | copy-start | bytes 6148
  7.2 51.2 %copy-start.10 = (bf16[1024]{0:T(1024)(128)(2,1)S(1)}, bf16[1024]{0:T(1024)(128)(2,1)}, u32[]{:S(2)}) copy-start(bf16[1024]{0:T(1024)(128)(2,1)} %param.21) | copy-start | bytes 6148
  7.2 104.1 %all-gather.7.cloned.1.call-start = ((), (), s32[]{:S(2)}) async-start(), calls=%async_computation.5 | async-start | bytes 2621440 | tf_op jit(solution)/shard_map/all_gather | solution.py:1303
  9.2 55.0 %copy-start.7 = (f32[4,32]{1,0:T(4,128)S(1)}, f32[4,32]{1,0:T(4,128)}, u32[]{:S(2)}) copy-start(f32[4,32]{1,0:T(4,128)} %convert_bitcast_fusion.table_ref) | copy-start | bytes 1540
  57.7 125.4 %all-gather.5.cloned.1.call-start = ((), (), s32[]{:S(2)}) async-start(), calls=%async_computation.4 | async-start | bytes 2621440 | tf_op jit(solution)/shard_map/all_gather | solution.py:1303
  60.4 14.0 %copy-start.6 = (s32[1,1,512]{2,1,0:T(1,128)}, s32[1,1,512]{2,1,0:T(1,128)S(1)}, u32[]{:S(2)}) copy-start(s32[1,1,512]{2,1,0:T(1,128)S(1)} %get-tuple-element.185.seg_row_ref) | copy-start | bytes 6148
  60.4 49.4 %copy-start.5 = (s32[1,1,512]{2,1,0:T(1,128)}, s32[1,1,512]{2,1,0:T(1,128)S(1)}, u32[]{:S(2)}) copy-start(s32[1,1,512]{2,1,0:T(1,128)S(1)} %get-tuple-element.184.seg_row_ref) | copy-start | bytes 6148
  74.5 36.2 %copy-start.4 = (s32[2,2,1024]{2,1,0:T(2,128)S(1)}, s32[2,2,1024]{2,1,0:T(2,128)}, u32[]{:S(2)}) copy-start(s32[2,2,1024]{2,1,0:T(2,128)} %find_places.2) | copy-start | bytes 49156
  109.5 224.4 %all-gather.9.cloned.1.call-start = ((), (), s32[]{:S(2)}) async-start(), calls=%async_computation.7 | async-start | bytes 2621440 | tf_op jit(solution)/shard_map/all_gather | solution.py:1303
  183.1 156.2 %all-gather.11.cloned.1.call-start = ((), (), s32[]{:S(2)}) async-start(), calls=%async_computation.8 | async-start | bytes 6553600 | tf_op jit(solution)/shard_map/all_gather | solution.py:1303
  183.7 5.7 copy-start.1
  183.7 292.3 %reduce-scatter.6.cloned.1.call-start = ((), (), s32[]{:S(2)}) async-start(), calls=%async_computation.9 | async-start | bytes 6553600 | tf_op jit(solution)/shard_map/reduce_scatter | solution.py:1306
  333.3 192.2 %reduce-scatter.4.cloned.1.call-start = ((), (), s32[]{:S(2)}) async-start(), calls=%async_computation.6 | async-start | bytes 2621440 | tf_op jit(solution)/shard_map/reduce_scatter | solution.py:1306
  333.9 192.6 %reduce-scatter.8.cloned.1.call-start = ((), (), s32[]{:S(2)}) async-start(), calls=%async_computation.10 | async-start | bytes 2621440 | tf_op jit(solution)/shard_map/reduce_scatter | solution.py:1306
  481.6 130.4 %all-to-all-start = ((bf16[8,320,1024]{2,1,0:T(8,128)(2,1)}), bf16[8,320,1024]{2,1,0:T(8,128)(2,1)}, u32[]{:S(2)}, u32[]{:S(2)}) async-start(bf16[8,320,1024]{2,1,0:T(8,128)(2,1)} %bitcast.120), calls=%async_computation.3 | async-start | bytes 10485760 | tf_op jit(solution)/shard_map/all_to_all | solution.py:1300
  688.6 4.1 copy-start
  692.6 4.6 copy-start.3
  692.7 5.6 copy-start.2
Sparse Core Ops, SparseCore 0:
  57.8 44.6 all-gather.6
  109.7 50.0 all-gather.4
  183.2 46.0 all-gather.8
  230.8 96.7 all-gather.10
  333.4 93.0 reduce-scatter.5
  429.3 44.3 reduce-scatter.3
  481.7 43.9 reduce-scatter.7

commit v14 on v13

--- a/solution.py
+++ b/solution.py
@@ -507,12 +507,13 @@
     inputs = [refs[5 + 8 * m : 13 + 8 * m] for m in range(micros)]
     sent_ref, refs = refs[5 + 8 * micros], refs[6 + 8 * micros :]
     (
-        xgrad_ref, arrived_ref, grads_ref, line_ref, dmoe_ref, dgain_ref,
-        dh1_ref, dattn_all, dheads_part, dheads_all, dxn_part, dxn_got, total_ref, xn_ref, ds_ref,
+        xgrad_ref, arrived_ref, grads_ref, crossed_ref, line_ref, dmoe_ref, dgain_ref,
+        far_ref, half_got, held_ref, quarter_got, moved_ref, moved_got, dh1_ref, dattn_all, dheads_part, dheads_all, dxn_part, dxn_got, total_ref, xn_ref, ds_ref,
         dproj_ref, sheet_ref, attn_send, attn_recv, heads_send, heads_recv, dxn_send, dxn_recv,
-        ride_send, ride_recv, ride_own,
+        ride_send, ride_recv, ride_own, half_sem, quarter_send, quarter_recv, moved_sem,
     ) = refs
     devices = sent_ref.shape[0]
+    chips = devices // 2
     _, members, shard_len, width = dattn_all.shape
     cols = dproj_ref.shape[2]
     half = members * shard_len
@@ -555,9 +556,27 @@
     def stay():
         return pltpu.make_async_copy(sent_ref.at[me], arrived_ref.at[me], ride_own)
 
+    chip, core = me // 2, lax.rem(me, 2)
+    across = lax.rem(line + members, 2 * members)
+
+    def halves():
+        return remote(
+            far_ref.at[:, 1 - core], half_got, half_sem.at[0], half_sem.at[1],
+            (partner_of(me, 1, devices), line),
+        )
+
+    def quarter(s):
+        return remote(
+            held_ref.at[partner_of(chip, s, chips)], quarter_got.at[s], quarter_send.at[s],
+            quarter_recv.at[s], (partner_of(me, 2 * s, devices), line),
+        )
+
+    def cross():
+        return remote(moved_ref, moved_got, moved_sem.at[0], moved_sem.at[1], (me, across))
+
     @pl.when((group == 0) & (micro == 0))
     def _():
-        peers = [(me, base + peer_of(s)) for s in steps]
+        peers = [(me, base + peer_of(s)) for s in steps] + [(me, across)]
         greet(peers + [(partner_of(me, s, devices), line) for s in range(1, devices)])
         stay().start()
         for s in range(1, devices):
@@ -588,13 +607,31 @@
         for m in range(micros):
             xn_ref[m] = (unit_rows(inputs[m][4][...]) * gain_ref[...]).astype(BF16)
 
+    @pl.when((group == 1) & (micro == 0))
+    def _():
+        halves().wait_recv()
+        for s in range(1, chips):
+            other = partner_of(chip, s, chips)
+            held = far_ref[other, core].astype(F32) + half_got[other].astype(F32)
+            held_ref[other] = held.astype(BF16)
+            quarter(s).start()
+
+    @pl.when((group == 1) & (micro == micros - 1))
+    def _():
+        total = far_ref[chip, core].astype(F32) + half_got[chip].astype(F32)
+        for s in range(1, chips):
+            quarter(s).wait_recv()
+            total = total + quarter_got[s].astype(F32)
+        moved_ref[...] = total.astype(BF16)
+        cross().start()
+
     def products(weight_ref):
         dxn = mm_nt(dproj_ref[0], weight_ref[0])
         for t in range(1, 3):
             dxn = dxn + mm_nt(dproj_ref[t], weight_ref[t])
         return dxn.reshape(members, shard_len, width)
 
-    per = grads_ref.shape[0] // 4
+    span = chips // 4
     for g in range(2):
         for m in range(micros):
 
@@ -610,7 +647,8 @@
                         attn_copy(m, s).start()
                 for head in range(heads):
                     inner_cols = slice(head * size, (head + 1) * size)
-                    outer_cols = slice(g * cols + head * size, g * cols + (head + 1) * size)
+                    outer = (1 - g) * cols + head * size
+                    outer_cols = slice(outer, outer + size)
                     values = qkv_ref[0, 2, :, inner_cols]
                     grads = dheads_all[m, :, :, outer_cols].reshape(half, size)
                     sheet_ref[...] = jnp.zeros_like(sheet_ref)
@@ -645,11 +683,11 @@
                         found = found + line_ref[0, head : head + 1, :]
                     line_ref[0, head : head + 1, :] = found
                 if g == 0:
-                    total_ref[m] = products(own_ref)
+                    total_ref[m] = products(other_ref)
                     for s in steps:
                         attn_copy(m, s).wait_recv()
                 else:
-                    total = total_ref[m] + products(other_ref)
+                    total = total_ref[m] + products(own_ref)
                     total_ref[m] = total
                     dxn_part[m] = total.astype(BF16)
                     for s in steps:
@@ -661,10 +699,13 @@
                         found = mm_tn(xn_ref[m], dproj_ref[t])
                     else:
                         found = mm_tn(dattn_all[m].reshape(half, width), heads_ref[...])
-                    found = found.reshape(per, 1, width // per, cols)
+                    target = (far_ref, grads_ref)[g]
+                    found = found.reshape(span, 2, width // (2 * span), cols)
                     if m:
-                        found = found + grads_ref[t * per : (t + 1) * per].astype(F32)
-                    grads_ref[t * per : (t + 1) * per] = found.astype(BF16)
+                        found = found + target[t * span : (t + 1) * span].astype(F32)
+                    target[t * span : (t + 1) * span] = found.astype(BF16)
+                if g == 0 and m == micros - 1:
+                    halves().start()
 
     @pl.when((group == 1) & (micro == micros - 1))
     def _():
@@ -688,6 +729,12 @@
         stay().wait()
         for s in range(1, devices):
             ride(s).wait()
+        cross().wait_recv()
+        crossed_ref[...] = moved_got[...]
+        halves().wait_send()
+        cross().wait_send()
+        for s in range(1, chips):
+            quarter(s).wait_send()
 
 
 def attend_back(
@@ -715,9 +762,9 @@
             pipeline_mode=pl.Buffered(1),
         )
         in_specs += [grad, h1, mine, mine, x_half] + [
-            pl.BlockSpec((1, 3, half, cols), lambda p, m: (p, 0, 0, 0)),
-            pl.BlockSpec((1, heads, half, half), lambda p, m: (p, 0, 0, 0)),
-            pl.BlockSpec((half, cols), lambda p, m: (0, p)),
+            pl.BlockSpec((1, 3, half, cols), lambda p, m: (1 - p, 0, 0, 0)),
+            pl.BlockSpec((1, heads, half, half), lambda p, m: (1 - p, 0, 0, 0)),
+            pl.BlockSpec((half, cols), lambda p, m: (0, 1 - p)),
         ]
     operands.append(rider)
     in_specs.append(any_space())
@@ -729,7 +776,8 @@
         out_shape=(
             jax.ShapeDtypeStruct((micros, shard_len, width), BF16),
             jax.ShapeDtypeStruct(rider.shape, BF16),
-            jax.ShapeDtypeStruct((pieces, 2, rows, cols), BF16),
+            jax.ShapeDtypeStruct((pieces // 2, 2, rows, cols), BF16),
+            jax.ShapeDtypeStruct((rows, cols), BF16),
             jax.ShapeDtypeStruct((2, heads, length), F32),
             jax.ShapeDtypeStruct((1, width), F32),
             jax.ShapeDtypeStruct((1, width), F32),
@@ -738,12 +786,22 @@
         out_specs=(
             pl.BlockSpec((micros, shard_len, width), lambda p, m: (0, 0, 0)),
             any_space(),
-            pl.BlockSpec((pieces, 1, rows, cols), lambda p, m: (0, p, 0, 0)),
-            pl.BlockSpec((1, heads, length), lambda p, m: (p, 0, 0)),
+            pl.BlockSpec(
+                (pieces // 2, 2, rows, cols), lambda p, m: (0, 0, 0, 0),
+                pipeline_mode=pl.Buffered(1),
+            ),
+            pl.BlockSpec((rows, cols), lambda p, m: (0, 0)),
+            pl.BlockSpec((1, heads, length), lambda p, m: (1 - p, 0, 0)),
             pl.BlockSpec((1, width), lambda p, m: (0, 0)),
             pl.BlockSpec((1, width), lambda p, m: (0, 0)),
         ),
         scratch_shapes=[
+            pltpu.VMEM((pieces // 2, 2, rows, cols), BF16),
+            pltpu.VMEM((pieces // 2, rows, cols), BF16),
+            pltpu.VMEM((pieces // 2, rows, cols), BF16),
+            pltpu.VMEM((pieces // 2, rows, cols), BF16),
+            pltpu.VMEM((rows, cols), BF16),
+            pltpu.VMEM((rows, cols), BF16),
             pltpu.VMEM((micros, shard_len, width), F32),
             pltpu.VMEM((micros, members, shard_len, width), BF16),
             pltpu.VMEM((micros, members, shard_len, 2 * cols), BF16),
@@ -756,6 +814,7 @@
             pltpu.VMEM((3, half, cols), BF16),
             pltpu.VMEM((length, TILE), F32),
             dma, dma, dma, dma, dma, dma, ride_dma, ride_dma, pltpu.SemaphoreType.DMA,
+            pltpu.SemaphoreType.DMA((2,)), ride_dma, ride_dma, pltpu.SemaphoreType.DMA((2,)),
         ],
         compiler_params=pltpu.CompilerParams(
             vmem_limit_bytes=VMEM_LIMIT, collective_id=6, has_side_effects=True
@@ -770,11 +829,11 @@
 
 
 def closing_kernel(
-    pieces_ref, small_ref, y_ref, h1_ref, rows_ref, place_ref, first_h1_ref,
+    pieces_ref, crossed_ref, small_ref, rows_ref, place_ref, first_h1_ref,
     whole_ref, sum_ref, block_ref,
-    y_got, y_send, y_recv, half_got, held_ref, quarter_got, total_ref, moved_ref, moved_got, small_got, line_sum,
-    line_got, half_sem, quarter_send, quarter_recv, small_send, small_recv, line_send, line_recv,
-    moved_sem, on_send, on_recv, own_sem,
+    half_got, held_ref, quarter_got, small_got, line_sum, line_got,
+    half_sem, quarter_send, quarter_recv, small_send, small_recv, line_send, line_recv,
+    on_send, on_recv,
 ):
     chips = pieces_ref.shape[0]
     devices = 2 * chips
@@ -784,27 +843,12 @@
     chip, core = me // 2, lax.rem(me, 2)
     sibling = partner_of(me, 1, devices)
     along = [lax.rem(line + s, blocks) for s in range(1, blocks)]
-    across = lax.rem(line + blocks // 2, blocks)
+    steps = range(1, chips)
     greet([(partner_of(me, s, devices), line) for s in range(1, devices)] + [(me, z) for z in along])
-    share = y_ref.shape[1] // 2
-    turns = (pl.ds(0, share), pl.ds(share, y_ref.shape[1] - share))
-
-    def y_copies(turn):
-        rows = turns[turn]
-        return [
-            remote(
-                y_ref.at[z, rows], y_got.at[line, rows], y_send.at[turn, s], y_recv.at[turn, s],
-                (me, z),
-            )
-            for s, z in enumerate(along)
-        ]
-
     halves = remote(
         pieces_ref.at[:, 1 - core], half_got, half_sem.at[0], half_sem.at[1], (sibling, line)
     )
     halves.start()
-    for copy in y_copies(0):
-        copy.start()
     smalls = [
         remote(
             small_ref, small_got.at[me], small_send.at[s], small_recv.at[s],
@@ -815,23 +859,19 @@
     for copy in smalls:
         copy.start()
     small_got[me] = small_ref[...]
-    block_ref[0] = (first_h1_ref[...] + collect(rows_ref, place_ref)).astype(BF16)
+
+    def quarter(s):
+        return remote(
+            held_ref.at[partner_of(chip, s, chips)], quarter_got.at[s], quarter_send.at[s],
+            quarter_recv.at[s], (partner_of(me, 2 * s, devices), line),
+        )
+
     halves.wait_recv()
-    steps = range(1, chips)
-
-    def quarter(s):
-        other = partner_of(chip, s, chips)
-        return remote(
-            held_ref.at[other], quarter_got.at[s], quarter_send.at[s], quarter_recv.at[s],
-            (partner_of(me, 2 * s, devices), line),
-        )
-
     for s in steps:
         other = partner_of(chip, s, chips)
         held = pieces_ref[other, core].astype(F32) + half_got[other].astype(F32)
         held_ref[other] = held.astype(BF16)
         quarter(s).start()
-    total_ref[...] = pieces_ref[chip, core].astype(F32) + half_got[chip].astype(F32)
     for copy in smalls:
         copy.wait_recv()
     line_sum[...] = jnp.sum(small_got[...], axis=0)
@@ -842,16 +882,13 @@
     for copy in lines:
         copy.start()
     line_got[line] = line_sum[...]
+    block_ref[...] = (first_h1_ref[...] + collect(rows_ref, place_ref)).astype(BF16)
+    total = pieces_ref[chip, core].astype(F32) + half_got[chip].astype(F32)
+    total = total + crossed_ref[...].astype(F32)
     for s in steps:
         quarter(s).wait_recv()
-        total_ref[...] += quarter_got[s].astype(F32)
-    moved_ref[...] = total_ref[1].astype(BF16)
-    cross = remote(moved_ref, moved_got, moved_sem.at[0], moved_sem.at[1], (me, across))
-    cross.start()
-    cross.wait_recv()
-    for copy in y_copies(1):
-        copy.start()
-    whole_ref[chip, core] = (total_ref[0] + moved_got[...].astype(F32)).astype(BF16)
+        total = total + quarter_got[s].astype(F32)
+    whole_ref[chip, core] = total.astype(BF16)
     onward = [
         remote(
             whole_ref.at[chip, core], whole_ref.at[chip, core], on_send.at[s], on_recv.at[s],
@@ -861,34 +898,26 @@
     ]
     for copy in onward:
         copy.start()
-    for copy in lines:
-        copy.wait_recv()
-    sum_ref[...] = jnp.sum(line_got[...], axis=0)
     for copy in onward:
         copy.wait_recv()
-    y_got[line] = y_ref[line]
     last = remote(
         whole_ref.at[:, core], whole_ref.at[:, core], on_send.at[0], on_recv.at[0], (sibling, line)
     )
     last.start()
-    for copy in y_copies(0) + y_copies(1):
+    for copy in lines:
         copy.wait_recv()
-    block_ref[1] = (h1_ref[...] + jnp.sum(y_got[...].astype(F32), axis=0)).astype(BF16)
-    for copy in y_copies(0) + y_copies(1):
-        copy.wait_send()
+    sum_ref[...] = jnp.sum(line_got[...], axis=0)
     halves.wait_send()
     for s in steps:
         quarter(s).wait_send()
-    cross.wait_send()
     for copy in smalls + lines + onward:
         copy.wait_send()
     last.wait()
 
 
-def closing(pieces, small, y, h1, rows_first, place, first_h1):
-    devices, both, rows, cols = pieces.shape
-    blocks = y.shape[0]
-    chips = devices // 2
+def closing(pieces, crossed, small, rows_first, place, first_h1, blocks):
+    chips, _, rows, cols = pieces.shape
+    devices = 2 * chips
     vmem = pl.BlockSpec(memory_space=pltpu.VMEM)
     dma = pltpu.SemaphoreType.DMA
     return pl.pallas_call(
@@ -896,32 +925,26 @@
         out_shape=(
             jax.ShapeDtypeStruct((chips, 2, rows, cols), BF16),
             jax.ShapeDtypeStruct(small.shape, F32),
-            jax.ShapeDtypeStruct((2,) + h1.shape, BF16),
-        ),
-        in_specs=[vmem] * 7,
+            jax.ShapeDtypeStruct(first_h1.shape, BF16),
+        ),
+        in_specs=[vmem] * 6,
         out_specs=(vmem,) * 3,
         scratch_shapes=[
-            pltpu.VMEM(y.shape, BF16),
-            dma((2, blocks)),
-            dma((2, blocks)),
-            pltpu.VMEM((chips, both, rows, cols), BF16),
-            pltpu.VMEM((chips, both, rows, cols), BF16),
-            pltpu.VMEM((chips, both, rows, cols), BF16),
-            pltpu.VMEM((both, rows, cols), F32),
-            pltpu.VMEM((rows, cols), BF16),
-            pltpu.VMEM((rows, cols), BF16),
+            pltpu.VMEM((chips, rows, cols), BF16),
+            pltpu.VMEM((chips, rows, cols), BF16),
+            pltpu.VMEM((chips, rows, cols), BF16),
             pltpu.VMEM((devices,) + small.shape, F32),
             pltpu.VMEM(small.shape, F32),
             pltpu.VMEM((blocks,) + small.shape, F32),
             dma((2,)), dma((chips,)), dma((chips,)), dma((devices,)), dma((devices,)),
-            dma((blocks,)), dma((blocks,)), dma((2,)), dma((chips,)), dma((chips,)), dma,
+            dma((blocks,)), dma((blocks,)), dma((chips,)), dma((chips,)),
         ],
         compiler_params=pltpu.CompilerParams(
             vmem_limit_bytes=VMEM_LIMIT, collective_id=3, has_side_effects=True
         ),
         cost_estimate=pl.CostEstimate(flops=0, bytes_accessed=160000000, transcendentals=0),
         name="closing",
-    )(pieces.reshape(chips, 2, both, rows, cols), small, y, h1, rows_first, place, first_h1)
+    )(pieces, crossed, small, rows_first, place, first_h1)
 
 
 def spread(rows, place0, place1, count):
@@ -1057,7 +1080,7 @@
             x = got_ref[s, e]
             dy = dy_ref[:, source, e] if by_block[0] else dy_ref[source, e]
             dy = dy.reshape(cap, width).astype(F32)
-            pair = pair_ref[source, e].astype(F32)
+            pair = pair_ref[0, source, e].astype(F32)
             margin = jnp.sum(mm_nt(x, wr_ref[...]) * pair, axis=-1, keepdims=True)
             own_gate = 1.0 / (1.0 + jnp.exp(-margin))
             other_gate = 1.0 / (1.0 + jnp.exp(margin))
@@ -1140,7 +1163,7 @@
             dx_copy(s).wait_recv()
 
 
-def expert_pass(sent, dy, pair, wr, wg, wu, wd, by_block, identity):
+def expert_pass(sent, dy, pair, which, wr, wg, wu, wd, by_block, identity):
     share = dy.shape[3]
     blocks = sent.shape[2] // share
     devices, experts, cap, width = sent.shape
@@ -1156,6 +1179,9 @@
     def kept(cols):
         return jax.ShapeDtypeStruct((devices, experts, cap, cols), BF16)
 
+    pair_spec = pl.BlockSpec(
+        (1,) + pair.shape[1:], lambda s: (which, 0, 0, 0, 0), pipeline_mode=pl.Buffered(1)
+    )
     y_shape = (blocks, devices, experts, share, width)
     if not by_block[1]:
         y_shape = (devices, experts, blocks, share, width)
@@ -1167,7 +1193,7 @@
             kept(hidden), kept(choices),
         ),
         in_specs=[
-            any_space(), whole(dy.shape), whole(pair.shape), whole(wr.shape), whole(wg.shape),
+            any_space(), whole(dy.shape), pair_spec, whole(wr.shape), whole(wg.shape),
             whole(wu.shape), whole(wd.shape),
         ],
         out_specs=(
@@ -1337,7 +1363,7 @@
         sent = spread(kept["xn2_all"][None], 0, place[micro]).reshape(token_shape)
         kept["by_block"] = (micro > 0, micro + 1 < micro_count)
         back, kept["y"], x, g, hid, dga, dup, dlog = expert_pass(
-            after(sent, *behind), kept["dy"], pairs[micro], router_rows, gate_rows, up_rows,
+            after(sent, *behind), kept["dy"], pairs, micro, router_rows, gate_rows, up_rows,
             down_weight, kept["by_block"], 4 + micro,
         )
         kept["weights"] = (x, g, hid, dga, dup, dlog)
@@ -1388,7 +1414,7 @@
     kept[-1] = tuple(after(list(kept[-1]), last_part))
     dwr, dwg, dwu, dwd = weight_pass(kept)
     last["y_rows"] = exchange(after(last["y"], last_part).reshape(flat_shape)).reshape(place_shape)
-    x_grad, first_rows, grads, lines, moe_gain_grad, attn_gain_grad = attend_back(
+    x_grad, first_rows, grads, crossed, lines, moe_gain_grad, attn_gain_grad = attend_back(
         moe_gain_f, attn_gain_f, all_out, qkv_weight, other_qkv,
         [
             (
@@ -1400,7 +1426,8 @@
         first["y_own"], scale, devices, members,
     )
     rows = collect_rows(after(last["y_rows"], grads), place[-1], shard_len)
-    rows = rows.reshape(blocks, shard_len, width)
+    mixed = scatter(rows)
+    last_block = (last["h1"] + mixed.astype(F32)).astype(BF16)
     first_rows = first_rows.reshape(expert_count, 1, capacity, width)
     lines = lines.reshape(2 * heads_here, 2 * half)
     table = jnp.einsum("hj,jb->hb", lines, onehot_bucket, precision=PRECISE)
@@ -1419,8 +1446,8 @@
     )
     used = small.shape[0]
     small = jnp.pad(small, (0, -used % 1024)).reshape(-1, 128)
-    whole, small, block_out = closing(
-        grads, small, rows, last["h1"], first_rows, own_place[0], first["h1"]
+    whole, small, first_block = closing(
+        grads, crossed, small, first_rows, own_place[0], first["h1"], blocks
     )
     whole = whole.reshape(4 * width, head_cols).astype(F32)
     grad_qkv = whole[: 3 * width].reshape(qkv_weight.shape)
@@ -1433,7 +1460,7 @@
     table = small[sizes[0] + 2 * width : used].reshape(blocks, heads_here, bucket_count)
     grad_table = lax.dynamic_index_in_dim(table, hidden_index, 0, keepdims=False).T
     return (
-        block_out[:, None],
+        jnp.stack([first_block, last_block])[:, None],
         x_grad[:, None],
         grad_qkv,
         grad_out,

time: 718 us -> 695 us (0.968)
  Pallas kernels: 656 us -> 637 us
    pallas_call x1, Pallas kernels: 70.9 us -> 43.5 us  [closing(): pl.pallas_call(closing_kernel, out_shape=(jax.ShapeDtypeStruct((chips, 2,...]
    pallas_call x1, Pallas kernels: 82.8 us -> 90.4 us  [attend_back(): pl.pallas_call(functools.partial(back_kernel, scale, micros), grid=(2, mi...]
  transfers between devices with their start and end apart: 8 -> 9, of which waited for: 0 -> 1; matrix products, arithmetic and copies ran while one was open for 2% -> 3% of each run, Pallas kernels for 76% -> 85%
where the time goes in v14:
time: 695 us; the launch traced here: 686 us
  Pallas kernels  637 us (92%)
  local copies, waits for them, and re-layouts  16.7 us (2%)
  between operations  14.9 us (2%)
  other arithmetic  8.47 us (1%)
    pallas_call x2, Pallas kernels, expert_pass(): pl.pallas_call(functools.partial(expert_kernel, by_block), grid=(devices,...  274 us
    pallas_call x2, Pallas kernels, attend(): pl.pallas_call(functools.partial(attend_kernel, scale), grid=(micros, 2),...  102 us
    pallas_call x1, Pallas kernels, attend_back(): pl.pallas_call(functools.partial(back_kernel, scale, micros), grid=(2, mi...  90.4 us
    pallas_call x1, Pallas kernels, opening(): pl.pallas_call(functools.partial(opening_kernel, micros), out_shape=(jax....  45.3 us
    pallas_call x1, Pallas kernels, closing(): pl.pallas_call(closing_kernel, out_shape=(jax.ShapeDtypeStruct((chips, 2,...  43.5 us
    pallas_call x1, Pallas kernels, weight_pass(): pl.pallas_call(weight_kernel, grid=(experts, width // block), out_shape=(...  38.6 us
    pallas_call x4, Pallas kernels, spread_rows(): pl.pallas_call(spread_kernel, grid=(blocks,), out_shape=jax.ShapeDtypeStr...  18.6 us
    pallas_call x3, Pallas kernels, collect_rows(): pl.pallas_call(collect_kernel, grid=(blocks,), out_shape=jax.ShapeDtypeSt...  16.9 us
  transfers between devices with their start and end apart: 9, of which 1 were waited for; matrix products, arithmetic and copies ran while one was open for 3% of the time, Pallas kernels for 85%

profile of v14, /device:TPU:0, one launch (start us, length us, event | category | flops | bytes accessed | tf_op | source)
XLA Modules:
  0.0 686.0 jit_solution(16535153851229971206)
XLA Ops:
  7.3 0.7 dynamic-slice_compare_fusion
  8.0 1.3 convert_bitcast_fusion.table_ref
  9.2 1.9 slice_bitcast_fusion
  11.1 1.3 fusion.19
  12.4 45.3 %opening.1 = (bf16[2,256,1024]{2,1,0:T(8,128)(2,1)}, bf16[2,256,1024]{2,1,0:T(8,128)(2,1)}, bf16[4,2,384,256]{3,2,1,0:T(8,128)(2,1)}, bf16[4,4,2,32,1024]{4,3,2,...) custom-call(bf16[2,256,1024]{2,1,0:T(8,128)(2,1)} %bitcast.114, bf16[3072,256]{1,0:T(8,128)(2,1)} %bitcast.109, ...), custom_call_target="tpu_custom_call" | custom-call | bytes 200000000 | tf_op jit(solution)/shard_map/opening/pallas_call | solution.py:236
  57.8 0.6 reshape.243
  58.4 0.6 reshape.241
  59.0 1.4 find_places.3
  60.4 0.9 copy.32.seg_col_ref
  61.3 1.3 dynamic-slice_bitcast_fusion.route_ref
  62.6 1.6 find_places.2
  64.2 1.7 fusion.2.line_ref
  66.0 4.6 position_bias.1.bias_ref
  70.5 1.3 slice_bitcast_fusion.5
  71.8 2.6 spread_rows.4
  74.4 35.2 %attend.2 = (bf16[1,2,3,512,256]{4,3,2,1,0:T(8,128)(2,1)}, bf16[1,2,4,512,512]{4,3,2,1,0:T(8,128)(2,1)}, bf16[1,512,512]{2,1,0:T(8,128)(2,1)}, f32[1,256,1024]{2...) custom-call(bf16[1,512,1024]{2,1,0:T(8,128)(2,1)} %bitcast.145, f32[1,1024]{1,0:T(1,128)} %bitcast.155, ...), custom_call_target="tpu_custom_call" | custom-call | flops 2684354560 | bytes 100000000 | tf_op jit(solution)/shard_map/attend/pallas_call | solution.py:450
  109.9 0.9 copy.33.seg_col_ref
  110.8 0.6 slice_bitcast_fusion.1
  111.4 5.3 spread_rows.6
  116.7 66.5 %attend.3 = (bf16[1,2,3,512,256]{4,3,2,1,0:T(8,128)(2,1)}, bf16[1,2,4,512,512]{4,3,2,1,0:T(8,128)(2,1)}, bf16[1,512,512]{2,1,0:T(8,128)(2,1)}, f32[1,256,1024]{2...) custom-call(bf16[1,512,1024]{2,1,0:T(8,128)(2,1)} %bitcast.138, ...), custom_call_target="tpu_custom_call" | custom-call | flops 2684354560 | bytes 100000000 | tf_op jit(solution)/shard_map/attend/pallas_call | solution.py:450
  183.3 0.5 all-gather.11.cloned.1.call-update
  183.9 0.3 reduce-scatter.7.cloned.1.call-start
  184.2 5.3 spread_rows.5
  189.5 137.3 %expert_pass.2 = (bf16[8,2,160,1024]{3,2,1,0:T(8,128)(2,1)}, bf16[4,8,2,40,1024]{4,3,2,1,0:T(8,128)(2,1)}, bf16[8,2,160,1024]{3,2,1,0:T(8,128)(2,1)}, bf16[8,2,1...) custom-call(bf16[8,2,160,1024]{3,2,1,0:T(8,128)(2,1)} %bitcast.108, ...), custom_call_target="tpu_custom_call" | custom-call | bytes 490000000 | tf_op jit(solution)/shard_map/expert_pass/pallas_call | solution.py:1188
  326.8 5.6 collect_rows.3
  332.5 0.5 reduce-scatter.5.cloned.1.call-update
  333.1 5.3 spread_rows.7
  338.5 136.6 %expert_pass.3 = (bf16[8,2,160,1024]{3,2,1,0:T(8,128)(2,1)}, bf16[8,2,4,40,1024]{4,3,2,1,0:T(8,128)(2,1)}, bf16[8,2,160,1024]{3,2,1,0:T(8,128)(2,1)}, bf16[8,2,1...) custom-call(bf16[8,2,160,1024]{3,2,1,0:T(8,128)(2,1)} %bitcast.106, ...), custom_call_target="tpu_custom_call" | custom-call | bytes 490000000 | tf_op jit(solution)/shard_map/expert_pass/pallas_call | solution.py:1188
  475.1 5.6 collect_rows.4
  480.7 4.7 all-to-all-start
  485.4 0.6 reduce-scatter.11.cloned.1.call-start
  486.0 38.6 %weight_pass.1 = (f32[2,16,1024]{2,1,0:T(8,128)}, f32[2,704,1024]{2,1,0:T(8,128)}, f32[2,704,1024]{2,1,0:T(8,128)}, f32[2,704,1024]{2,1,0:T(8,128)}) custom-call(bf16[8,2,160,1024]{3,2,1,0:T(8,128)(2,1)} %get-tuple-element.93.refs_0_, bf16[8,2,160,1024]{3,2,1,0:T(8,128)(2,1)} %get-tuple-element.94.refs_1_, ...), custom_call_target="tpu_custom_call" | custom-call | flops 22145925120 | bytes 59899904 | tf_op jit(solution)/shard_map/weight_pass/pallas_call | solution.py:1254
  524.8 90.4 %attend_back.1 = (bf16[2,256,1024]{2,1,0:T(8,128)(2,1)}, bf16[8,80,1024]{2,1,0:T(8,128)(2,1)}, bf16[4,2,512,256]{3,2,1,0:T(8,128)(2,1)}, bf16[512,256]{1,0:T(8,1...) custom-call(f32[1,1024]{1,0:T(1,128)} %bitcast.160, f32[1,1024]{1,0:T(1,128)} %bitcast.157, ...), custom_call_target="tpu_custom_call" | custom-call | flops 10737418240 | bytes 250000000 | tf_op jit(solution)/shard_map/attend_back/pallas_call | solution.py:773
  615.3 5.7 collect_rows.5
  621.1 0.4 fusion.1
  621.7 0.6 fusion.5.small_ref
  622.4 43.5 %closing.1 = (bf16[4,2,512,256]{3,2,1,0:T(8,128)(2,1)}, f32[152,128]{1,0:T(8,128)}, bf16[256,1024]{1,0:T(8,128)(2,1)}) custom-call(bf16[4,2,512,256]{3,2,1,0:T(8,128)(2,1)} %get-tuple-element.131.pieces_ref, bf16[512,256]{1,0:T(8,128)(2,1)} %get-tuple-element.132.crossed_ref, f32[152,128]{1,0:T(8,128)} %fusion.5.small_ref, ...), custom_call_target="tpu_custom_call" | custom-call | bytes 160000000 | tf_op jit(solution)/shard_map/closing/pallas_call | solution.py:923
  665.9 0.8 slice.77
  666.7 0.8 slice.82
  667.5 1.1 slice.88
  668.7 1.9 slice.87
  670.7 0.6 reshape.240
  671.4 1.3 copy.34
  672.7 0.6 dynamic-slice_bitcast_fusion.1
  673.3 1.3 slice_bitcast_fusion.3
  674.5 1.2 fusion
  675.7 2.1 maximum_bitcast_fusion
  677.8 1.0 copy.42
  (61 shorter events, 1.3 us)
Async XLA Ops:
  7.2 53.2 %copy-start.9 = (s32[2,1,1024]{2,1,0:T(1,128)S(1)}, s32[2,1,1024]{2,1,0:T(1,128)}, u32[]{:S(2)}) copy-start(s32[2,1,1024]{2,1,0:T(1,128)} %param.15) | copy-start | bytes 24580
  7.2 50.6 %copy-start.12 = (bf16[1024]{0:T(1024)(128)(2,1)S(1)}, bf16[1024]{0:T(1024)(128)(2,1)}, u32[]{:S(2)}) copy-start(bf16[1024]{0:T(1024)(128)(2,1)} %param.20) | copy-start | bytes 6148
  7.2 51.2 %copy-start.13 = (bf16[1024]{0:T(1024)(128)(2,1)S(1)}, bf16[1024]{0:T(1024)(128)(2,1)}, u32[]{:S(2)}) copy-start(bf16[1024]{0:T(1024)(128)(2,1)} %param.21) | copy-start | bytes 6148
  7.2 104.2 %all-gather.7.cloned.1.call-start = ((), (), s32[]{:S(2)}) async-start(), calls=%async_computation.6 | async-start | bytes 2621440 | tf_op jit(solution)/shard_map/all_gather | solution.py:1329
  9.2 55.0 %copy-start.8 = (f32[4,32]{1,0:T(4,128)S(1)}, f32[4,32]{1,0:T(4,128)}, u32[]{:S(2)}) copy-start(f32[4,32]{1,0:T(4,128)} %convert_bitcast_fusion.table_ref) | copy-start | bytes 1540
  57.7 125.6 %all-gather.5.cloned.1.call-start = ((), (), s32[]{:S(2)}) async-start(), calls=%async_computation.5 | async-start | bytes 2621440 | tf_op jit(solution)/shard_map/all_gather | solution.py:1329
  60.4 14.0 %copy-start.7 = (s32[1,1,512]{2,1,0:T(1,128)}, s32[1,1,512]{2,1,0:T(1,128)S(1)}, u32[]{:S(2)}) copy-start(s32[1,1,512]{2,1,0:T(1,128)S(1)} %get-tuple-element.185.seg_row_ref) | copy-start | bytes 6148
  60.4 49.5 %copy-start.6 = (s32[1,1,512]{2,1,0:T(1,128)}, s32[1,1,512]{2,1,0:T(1,128)S(1)}, u32[]{:S(2)}) copy-start(s32[1,1,512]{2,1,0:T(1,128)S(1)} %get-tuple-element.184.seg_row_ref) | copy-start | bytes 6148
  74.4 36.3 %copy-start.4 = (s32[2,2,1024]{2,1,0:T(2,128)S(1)}, s32[2,2,1024]{2,1,0:T(2,128)}, u32[]{:S(2)}) copy-start(s32[2,2,1024]{2,1,0:T(2,128)} %find_places.2) | copy-start | bytes 49156
  109.7 223.5 %all-gather.9.cloned.1.call-start = ((), (), s32[]{:S(2)}) async-start(), calls=%async_computation.8 | async-start | bytes 2621440 | tf_op jit(solution)/shard_map/all_gather | solution.py:1329
  183.3 155.2 %all-gather.11.cloned.1.call-start = ((), (), s32[]{:S(2)}) async-start(), calls=%async_computation.9 | async-start | bytes 6553600 | tf_op jit(solution)/shard_map/all_gather | solution.py:1329
  183.9 291.2 %reduce-scatter.7.cloned.1.call-start = ((), (), s32[]{:S(2)}) async-start(), calls=%async_computation.10 | async-start | bytes 6553600 | tf_op jit(solution)/shard_map/reduce_scatter | solution.py:1332
  332.5 192.2 %reduce-scatter.5.cloned.1.call-start = ((), (), s32[]{:S(2)}) async-start(), calls=%async_computation.7 | async-start | bytes 2621440 | tf_op jit(solution)/shard_map/reduce_scatter | solution.py:1332
  333.1 191.7 %reduce-scatter.9.cloned.1.call-start = ((), (), s32[]{:S(2)}) async-start(), calls=%async_computation.11 | async-start | bytes 2621440 | tf_op jit(solution)/shard_map/reduce_scatter | solution.py:1332
  480.7 134.5 %all-to-all-start = ((bf16[8,320,1024]{2,1,0:T(8,128)(2,1)}), bf16[8,320,1024]{2,1,0:T(8,128)(2,1)}, u32[]{:S(2)}, u32[]{:S(2)}) async-start(bf16[8,320,1024]{2,1,0:T(8,128)(2,1)} %bitcast.125), calls=%async_computation.3 | async-start | bytes 10485760 | tf_op jit(solution)/shard_map/all_to_all | solution.py:1326
  485.4 189.1 %reduce-scatter.11.cloned.1.call-start = ((), (), s32[]{:S(2)}) async-start(), calls=%async_computation.12 | async-start | bytes 2621440 | tf_op jit(solution)/shard_map/reduce_scatter | solution.py:1332
  615.3 5.8 copy-start.3
  615.3 5.8 copy-start.5
  615.3 6.4 copy-start.10
  615.3 6.4 copy-start.11
  665.9 2.8 copy-start
  668.7 5.9 copy-start.1
  670.6 7.2 %copy-start.2 = (bf16[2,256,1024]{2,1,0:T(8,128)(2,1)S(1)}, bf16[2,256,1024]{2,1,0:T(8,128)(2,1)}, u32[]{:S(2)}) copy-start(bf16[2,256,1024]{2,1,0:T(8,128)(2,1)} %get-tuple-element.141) | copy-start | bytes 3145732
Sparse Core Ops, SparseCore 0:
  57.8 44.6 all-gather.6
  109.8 50.0 all-gather.4
  183.4 46.0 all-gather.8
  230.9 96.7 all-gather.10
  332.6 92.9 reduce-scatter.6
  428.4 44.3 reduce-scatter.4
  480.9 43.8 reduce-scatter.8
  621.1 47.8 reduce-scatter.10

commit v15 on v14

--- a/solution.py
+++ b/solution.py
@@ -607,8 +607,7 @@
         for m in range(micros):
             xn_ref[m] = (unit_rows(inputs[m][4][...]) * gain_ref[...]).astype(BF16)
 
-    @pl.when((group == 1) & (micro == 0))
-    def _():
+    def pass_halves():
         halves().wait_recv()
         for s in range(1, chips):
             other = partner_of(chip, s, chips)
@@ -616,8 +615,7 @@
             held_ref[other] = held.astype(BF16)
             quarter(s).start()
 
-    @pl.when((group == 1) & (micro == micros - 1))
-    def _():
+    def pass_quarters():
         total = far_ref[chip, core].astype(F32) + half_got[chip].astype(F32)
         for s in range(1, chips):
             quarter(s).wait_recv()
@@ -682,6 +680,10 @@
                     if m:
                         found = found + line_ref[0, head : head + 1, :]
                     line_ref[0, head : head + 1, :] = found
+                if g == 1 and m == 0:
+                    pass_halves()
+                if g == 1 and m == micros - 1:
+                    pass_quarters()
                 if g == 0:
                     total_ref[m] = products(other_ref)
                     for s in steps:

time: 695 us -> 717 us (1.032)
  Pallas kernels: 637 us -> 658 us
    pallas_call x1, Pallas kernels: 90.4 us -> 114 us  [attend_back(): pl.pallas_call(functools.partial(back_kernel, scale, micros), grid=(2, mi...]
  transfers between devices with their start and end apart: 9 -> 9, of which waited for: 1 -> 1; matrix products, arithmetic and copies ran while one was open for 3% -> 3% of each run, Pallas kernels for 85% -> 86%
where the time goes in v15:
time: 717 us; the launch traced here: 708 us
  Pallas kernels  658 us (92%)
  local copies, waits for them, and re-layouts  16.7 us (2%)
  between operations  14.7 us (2%)
  other arithmetic  8.47 us (1%)
    pallas_call x2, Pallas kernels, expert_pass(): pl.pallas_call(functools.partial(expert_kernel, by_block), grid=(devices,...  274 us
    pallas_call x1, Pallas kernels, attend_back(): pl.pallas_call(functools.partial(back_kernel, scale, micros), grid=(2, mi...  114 us
    pallas_call x2, Pallas kernels, attend(): pl.pallas_call(functools.partial(attend_kernel, scale), grid=(micros, 2),...  102 us
    pallas_call x1, Pallas kernels, opening(): pl.pallas_call(functools.partial(opening_kernel, micros), out_shape=(jax....  45.3 us
    pallas_call x1, Pallas kernels, closing(): pl.pallas_call(closing_kernel, out_shape=(jax.ShapeDtypeStruct((chips, 2,...  41.1 us
    pallas_call x1, Pallas kernels, weight_pass(): pl.pallas_call(weight_kernel, grid=(experts, width // block), out_shape=(...  38.7 us
    pallas_call x4, Pallas kernels, spread_rows(): pl.pallas_call(spread_kernel, grid=(blocks,), out_shape=jax.ShapeDtypeStr...  18.6 us
    pallas_call x3, Pallas kernels, collect_rows(): pl.pallas_call(collect_kernel, grid=(blocks,), out_shape=jax.ShapeDtypeSt...  16.9 us
  transfers between devices with their start and end apart: 9, of which 1 were waited for; matrix products, arithmetic and copies ran while one was open for 3% of the time, Pallas kernels for 86%

profile of v15, /device:TPU:0, one launch (start us, length us, event | category | flops | bytes accessed | tf_op | source)
XLA Modules:
  0.0 707.8 jit_solution(17264805299772067512)
XLA Ops:
  7.3 0.7 dynamic-slice_compare_fusion
  8.0 1.3 convert_bitcast_fusion.table_ref
  9.2 1.9 slice_bitcast_fusion
  11.1 1.3 fusion.19
  12.4 45.3 %opening.1 = (bf16[2,256,1024]{2,1,0:T(8,128)(2,1)}, bf16[2,256,1024]{2,1,0:T(8,128)(2,1)}, bf16[4,2,384,256]{3,2,1,0:T(8,128)(2,1)}, bf16[4,4,2,32,1024]{4,3,2,...) custom-call(bf16[2,256,1024]{2,1,0:T(8,128)(2,1)} %bitcast.114, bf16[3072,256]{1,0:T(8,128)(2,1)} %bitcast.109, ...), custom_call_target="tpu_custom_call" | custom-call | bytes 200000000 | tf_op jit(solution)/shard_map/opening/pallas_call | solution.py:236
  57.8 0.6 reshape.243
  58.4 0.6 reshape.241
  59.0 1.4 find_places.3
  60.4 0.9 copy.32.seg_col_ref
  61.3 1.3 dynamic-slice_bitcast_fusion.route_ref
  62.6 1.6 find_places.2
  64.2 1.7 fusion.2.line_ref
  66.0 4.6 position_bias.1.bias_ref
  70.5 1.3 slice_bitcast_fusion.5
  71.8 2.6 spread_rows.4
  74.4 35.2 %attend.2 = (bf16[1,2,3,512,256]{4,3,2,1,0:T(8,128)(2,1)}, bf16[1,2,4,512,512]{4,3,2,1,0:T(8,128)(2,1)}, bf16[1,512,512]{2,1,0:T(8,128)(2,1)}, f32[1,256,1024]{2...) custom-call(bf16[1,512,1024]{2,1,0:T(8,128)(2,1)} %bitcast.145, f32[1,1024]{1,0:T(1,128)} %bitcast.155, ...), custom_call_target="tpu_custom_call" | custom-call | flops 2684354560 | bytes 100000000 | tf_op jit(solution)/shard_map/attend/pallas_call | solution.py:450
  110.0 0.9 copy.33.seg_col_ref
  110.9 0.6 slice_bitcast_fusion.1
  111.5 5.3 spread_rows.6
  116.8 66.4 %attend.3 = (bf16[1,2,3,512,256]{4,3,2,1,0:T(8,128)(2,1)}, bf16[1,2,4,512,512]{4,3,2,1,0:T(8,128)(2,1)}, bf16[1,512,512]{2,1,0:T(8,128)(2,1)}, f32[1,256,1024]{2...) custom-call(bf16[1,512,1024]{2,1,0:T(8,128)(2,1)} %bitcast.138, ...), custom_call_target="tpu_custom_call" | custom-call | flops 2684354560 | bytes 100000000 | tf_op jit(solution)/shard_map/attend/pallas_call | solution.py:450
  183.3 0.5 all-gather.11.cloned.1.call-update
  183.9 0.6 reduce-scatter.7.cloned.1.call-start
  184.4 5.3 spread_rows.5
  189.8 137.4 %expert_pass.2 = (bf16[8,2,160,1024]{3,2,1,0:T(8,128)(2,1)}, bf16[4,8,2,40,1024]{4,3,2,1,0:T(8,128)(2,1)}, bf16[8,2,160,1024]{3,2,1,0:T(8,128)(2,1)}, bf16[8,2,1...) custom-call(bf16[8,2,160,1024]{3,2,1,0:T(8,128)(2,1)} %bitcast.108, ...), custom_call_target="tpu_custom_call" | custom-call | bytes 490000000 | tf_op jit(solution)/shard_map/expert_pass/pallas_call | solution.py:1190
  327.1 5.6 collect_rows.3
  332.8 0.5 reduce-scatter.5.cloned.1.call-update
  333.4 5.3 spread_rows.7
  338.8 136.6 %expert_pass.3 = (bf16[8,2,160,1024]{3,2,1,0:T(8,128)(2,1)}, bf16[8,2,4,40,1024]{4,3,2,1,0:T(8,128)(2,1)}, bf16[8,2,160,1024]{3,2,1,0:T(8,128)(2,1)}, bf16[8,2,1...) custom-call(bf16[8,2,160,1024]{3,2,1,0:T(8,128)(2,1)} %bitcast.106, ...), custom_call_target="tpu_custom_call" | custom-call | bytes 490000000 | tf_op jit(solution)/shard_map/expert_pass/pallas_call | solution.py:1190
  475.4 5.6 collect_rows.4
  481.1 4.7 all-to-all-start
  486.0 38.7 %weight_pass.1 = (f32[2,16,1024]{2,1,0:T(8,128)}, f32[2,704,1024]{2,1,0:T(8,128)}, f32[2,704,1024]{2,1,0:T(8,128)}, f32[2,704,1024]{2,1,0:T(8,128)}) custom-call(bf16[8,2,160,1024]{3,2,1,0:T(8,128)(2,1)} %get-tuple-element.93.refs_0_, bf16[8,2,160,1024]{3,2,1,0:T(8,128)(2,1)} %get-tuple-element.94.refs_1_, ...), custom_call_target="tpu_custom_call" | custom-call | flops 22145925120 | bytes 59899904 | tf_op jit(solution)/shard_map/weight_pass/pallas_call | solution.py:1256
  524.7 0.4 reduce-scatter.9.cloned.1.call-done.refs_13_
  525.2 114.4 %attend_back.1 = (bf16[2,256,1024]{2,1,0:T(8,128)(2,1)}, bf16[8,80,1024]{2,1,0:T(8,128)(2,1)}, bf16[4,2,512,256]{3,2,1,0:T(8,128)(2,1)}, bf16[512,256]{1,0:T(8,1...) custom-call(f32[1,1024]{1,0:T(1,128)} %bitcast.160, f32[1,1024]{1,0:T(1,128)} %bitcast.157, ...), custom_call_target="tpu_custom_call" | custom-call | flops 10737418240 | bytes 250000000 | tf_op jit(solution)/shard_map/attend_back/pallas_call | solution.py:775
  639.6 5.7 collect_rows.5
  645.4 0.4 fusion.1
  646.0 0.6 fusion.5.small_ref
  646.7 41.1 %closing.1 = (bf16[4,2,512,256]{3,2,1,0:T(8,128)(2,1)}, f32[152,128]{1,0:T(8,128)}, bf16[256,1024]{1,0:T(8,128)(2,1)}) custom-call(bf16[4,2,512,256]{3,2,1,0:T(8,128)(2,1)} %get-tuple-element.131.pieces_ref, bf16[512,256]{1,0:T(8,128)(2,1)} %get-tuple-element.132.crossed_ref, f32[152,128]{1,0:T(8,128)} %fusion.5.small_ref, ...), custom_call_target="tpu_custom_call" | custom-call | bytes 160000000 | tf_op jit(solution)/shard_map/closing/pallas_call | solution.py:925
  687.8 0.8 slice.77
  688.7 0.8 slice.82
  689.5 1.1 slice.88
  690.7 1.9 slice.87
  692.7 0.6 reshape.240
  693.3 1.3 copy.34
  694.7 0.6 dynamic-slice_bitcast_fusion.1
  695.2 1.3 slice_bitcast_fusion.3
  696.5 1.2 fusion
  697.7 2.1 maximum_bitcast_fusion
  699.8 1.0 copy.42
  (61 shorter events, 1.4 us)
Async XLA Ops:
  7.2 53.2 %copy-start.9 = (s32[2,1,1024]{2,1,0:T(1,128)S(1)}, s32[2,1,1024]{2,1,0:T(1,128)}, u32[]{:S(2)}) copy-start(s32[2,1,1024]{2,1,0:T(1,128)} %param.15) | copy-start | bytes 24580
  7.2 50.6 %copy-start.12 = (bf16[1024]{0:T(1024)(128)(2,1)S(1)}, bf16[1024]{0:T(1024)(128)(2,1)}, u32[]{:S(2)}) copy-start(bf16[1024]{0:T(1024)(128)(2,1)} %param.20) | copy-start | bytes 6148
  7.2 51.2 %copy-start.13 = (bf16[1024]{0:T(1024)(128)(2,1)S(1)}, bf16[1024]{0:T(1024)(128)(2,1)}, u32[]{:S(2)}) copy-start(bf16[1024]{0:T(1024)(128)(2,1)} %param.21) | copy-start | bytes 6148
  7.2 104.3 %all-gather.7.cloned.1.call-start = ((), (), s32[]{:S(2)}) async-start(), calls=%async_computation.6 | async-start | bytes 2621440 | tf_op jit(solution)/shard_map/all_gather | solution.py:1331
  9.2 55.0 %copy-start.8 = (f32[4,32]{1,0:T(4,128)S(1)}, f32[4,32]{1,0:T(4,128)}, u32[]{:S(2)}) copy-start(f32[4,32]{1,0:T(4,128)} %convert_bitcast_fusion.table_ref) | copy-start | bytes 1540
  57.7 125.6 %all-gather.5.cloned.1.call-start = ((), (), s32[]{:S(2)}) async-start(), calls=%async_computation.5 | async-start | bytes 2621440 | tf_op jit(solution)/shard_map/all_gather | solution.py:1331
  60.4 14.0 %copy-start.7 = (s32[1,1,512]{2,1,0:T(1,128)}, s32[1,1,512]{2,1,0:T(1,128)S(1)}, u32[]{:S(2)}) copy-start(s32[1,1,512]{2,1,0:T(1,128)S(1)} %get-tuple-element.185.seg_row_ref) | copy-start | bytes 6148
  60.4 49.6 %copy-start.6 = (s32[1,1,512]{2,1,0:T(1,128)}, s32[1,1,512]{2,1,0:T(1,128)S(1)}, u32[]{:S(2)}) copy-start(s32[1,1,512]{2,1,0:T(1,128)S(1)} %get-tuple-element.184.seg_row_ref) | copy-start | bytes 6148
  74.4 36.4 %copy-start.4 = (s32[2,2,1024]{2,1,0:T(2,128)S(1)}, s32[2,2,1024]{2,1,0:T(2,128)}, u32[]{:S(2)}) copy-start(s32[2,2,1024]{2,1,0:T(2,128)} %find_places.2) | copy-start | bytes 49156
  109.7 223.8 %all-gather.9.cloned.1.call-start = ((), (), s32[]{:S(2)}) async-start(), calls=%async_computation.8 | async-start | bytes 2621440 | tf_op jit(solution)/shard_map/all_gather | solution.py:1331
  183.3 155.5 %all-gather.11.cloned.1.call-start = ((), (), s32[]{:S(2)}) async-start(), calls=%async_computation.9 | async-start | bytes 6553600 | tf_op jit(solution)/shard_map/all_gather | solution.py:1331
  183.9 291.5 %reduce-scatter.7.cloned.1.call-start = ((), (), s32[]{:S(2)}) async-start(), calls=%async_computation.10 | async-start | bytes 6553600 | tf_op jit(solution)/shard_map/reduce_scatter | solution.py:1334
  332.8 191.9 %reduce-scatter.5.cloned.1.call-start = ((), (), s32[]{:S(2)}) async-start(), calls=%async_computation.7 | async-start | bytes 2621440 | tf_op jit(solution)/shard_map/reduce_scatter | solution.py:1334
  333.4 191.8 %reduce-scatter.9.cloned.1.call-start = ((), (), s32[]{:S(2)}) async-start(), calls=%async_computation.11 | async-start | bytes 2621440 | tf_op jit(solution)/shard_map/reduce_scatter | solution.py:1334
  481.1 158.5 %all-to-all-start = ((bf16[8,320,1024]{2,1,0:T(8,128)(2,1)}), bf16[8,320,1024]{2,1,0:T(8,128)(2,1)}, u32[]{:S(2)}, u32[]{:S(2)}) async-start(bf16[8,320,1024]{2,1,0:T(8,128)(2,1)} %bitcast.125), calls=%async_computation.3 | async-start | bytes 10485760 | tf_op jit(solution)/shard_map/all_to_all | solution.py:1328
  485.8 210.8 %reduce-scatter.11.cloned.1.call-start = ((), (), s32[]{:S(2)}) async-start(), calls=%async_computation.12 | async-start | bytes 2621440 | tf_op jit(solution)/shard_map/reduce_scatter | solution.py:1334
  639.5 5.8 copy-start.3
  639.6 5.8 copy-start.5
  639.6 6.4 copy-start.10
  639.6 6.4 copy-start.11
  687.8 2.8 copy-start
  690.7 5.9 copy-start.1
  692.6 7.2 %copy-start.2 = (bf16[2,256,1024]{2,1,0:T(8,128)(2,1)S(1)}, bf16[2,256,1024]{2,1,0:T(8,128)(2,1)}, u32[]{:S(2)}) copy-start(bf16[2,256,1024]{2,1,0:T(8,128)(2,1)} %get-tuple-element.141) | copy-start | bytes 3145732
Sparse Core Ops, SparseCore 0:
  57.8 44.6 all-gather.6
  109.8 50.0 all-gather.4
  183.4 46.1 all-gather.8
  231.0 96.7 all-gather.10
  332.9 93.0 reduce-scatter.6
  428.7 44.3 reduce-scatter.4
  481.2 43.9 reduce-scatter.8
  645.4 47.6 reduce-scatter.10
